TPU v7x, 256 devices: a whole 4x4x8 slice. The times are simulated.
256 devices in a mesh: ctx: 64 (over z, y, core), tp: 4 (over x).
Axes of the slice: x: 4, y: 4, z: 8, core: 2. Of those that a mesh axis runs over, the one named last changes fastest.
Arguments:
- query: bfloat16 [2, 8192, 2048], P(None, 'ctx', 'tp'), may hold values from -64 to 64
- key_states: bfloat16 [2, 8192, 1024], P(None, 'ctx', 'tp'), may hold values from -6 to 6
- value_state_rows: bfloat16 [2, 8192, 1024], P(None, 'ctx', 'tp'), may hold values from -6 to 6
- d_out: bfloat16 [2, 8192, 5376], P(None, ('ctx', 'tp')), may hold values from -24 to 24
- o_weight: bfloat16 [5376, 2048], P(None, 'tp'), may hold values from -0.125 to 0.125
- doc_start: int32 [2, 8192], P(None, 'ctx'), may hold values from 0 to 8191, as said below
Outputs:
- d_query: bfloat16 [2, 8192, 2048], P(None, 'ctx', 'tp')
- d_key: bfloat16 [2, 8192, 1024], P(None, 'ctx', 'tp')
- d_value: bfloat16 [2, 8192, 1024], P(None, 'ctx', 'tp')
- d_o_weight: float32 [5376, 2048], P('ctx', 'tp')
Inputs may be any that keep to these rules, and one draw needn't show every extreme that they name: doc_start[s, t] is the position of the first token of the document holding token t of sequence s: it never falls along t, is at most t, equals t exactly where a document begins, and is 0 for the first document; the last token of every sequence begins a document of its own.
All inputs are finite; a program needn't handle non-finite values.
Results may differ from a plain program's by a relative error of at most 0.039.
Values may be sent and summed in bfloat16 or wider, within the bound.
No kernel may reach another device: no remote copies, remote signals or barrier semaphores. Data moves between devices by JAX's collectives and lax.ppermute only.
A program may use at most 128 MiB of HBM per device.

v0:
```python
from functools import reduce

import jax
import jax.numpy as jnp
from jax import lax
from jax.sharding import PartitionSpec as P

HEAD_SIZE = 128
WIN = 1024


score_scale = 168.0 ** (-0.5)


def from_behind(block, axis, distance):
    devices = range(lax.axis_size(axis))
    route = [(i - distance, i) for i in devices if i - distance in devices]
    return lax.ppermute(block, axis, route)


def attend(query, all_keys, all_values, d_attn, doc_start, first_pos):
    seq_count, shard_rows, query_width = query.shape
    key_total_count = all_keys.shape[1]
    kv_heads = all_keys.shape[2] // HEAD_SIZE
    query_group_count = query_width // HEAD_SIZE // kv_heads
    query_heads = query.reshape(seq_count, shard_rows, kv_heads, query_group_count, HEAD_SIZE)
    key_heads = all_keys.reshape(seq_count, key_total_count, kv_heads, HEAD_SIZE)
    value_heads = all_values.reshape(seq_count, key_total_count, kv_heads, HEAD_SIZE)
    d_attn_heads = d_attn.reshape(seq_count, shard_rows, kv_heads, query_group_count, HEAD_SIZE)
    query_pos = first_pos + jnp.arange(shard_rows, dtype=jnp.int32)
    key_pos = (
        first_pos + shard_rows - key_total_count + jnp.arange(key_total_count, dtype=jnp.int32)
    )
    visible = (
        (key_pos[None, None, :] <= query_pos[None, :, None])
        & (key_pos[None, None, :] > query_pos[None, :, None] - WIN)
        & (key_pos[None, None, :] >= doc_start[:, :, None])
    )
    scores = (
        jnp.einsum("sqhgd,skhd->shgqk", query_heads, key_heads, preferred_element_type=jnp.float32)
        * score_scale
    )
    scores = jnp.where(visible[:, None, None], scores, -jnp.inf)
    row_max = jnp.max(scores, axis=-1, keepdims=True)
    expo = jnp.exp(scores - row_max)
    attn_weights = expo / jnp.sum(expo, axis=-1, keepdims=True)
    weights_b = attn_weights.astype(jnp.bfloat16)
    attn = jnp.einsum(
        "shgqk,skhd->sqhgd", weights_b, value_heads, preferred_element_type=jnp.float32
    ).astype(jnp.bfloat16)
    d_probs = jnp.einsum(
        "sqhgd,skhd->shgqk", d_attn_heads, value_heads, preferred_element_type=jnp.float32
    )
    row_delta = jnp.sum(d_attn_heads.astype(jnp.float32) * attn.astype(jnp.float32), axis=-1)
    row_delta = jnp.transpose(row_delta, (0, 2, 3, 1))[..., None]
    d_scores = (attn_weights * (d_probs - row_delta)).astype(jnp.bfloat16)
    d_query = (
        jnp.einsum("shgqk,skhd->sqhgd", d_scores, key_heads, preferred_element_type=jnp.float32)
        * score_scale
    ).astype(jnp.bfloat16)
    d_keys = (
        jnp.einsum("shgqk,sqhgd->skhd", d_scores, query_heads, preferred_element_type=jnp.float32)
        * score_scale
    )
    d_values = jnp.einsum(
        "shgqk,sqhgd->skhd", weights_b, d_attn_heads, preferred_element_type=jnp.float32
    )
    kv_width = kv_heads * HEAD_SIZE
    return (
        d_query.reshape(seq_count, shard_rows, query_width),
        attn.reshape(seq_count, shard_rows, query_width),
        d_keys.reshape(seq_count, key_total_count, kv_width),
        d_values.reshape(seq_count, key_total_count, kv_width),
    )


def local(query, key_states, value_state_rows, d_out, o_weight, doc_start):
    seq_count, shard_rows, query_width = query.shape
    nhalo = (WIN - 1) // shard_rows + 1
    first_pos = lax.axis_index("ctx") * shard_rows
    halo_keys = []
    halo_values = []
    for distance in range(nhalo, 0, -1):
        arrived = from_behind((key_states, value_state_rows), "ctx", distance)
        halo_keys.append(arrived[0])
        halo_values.append(arrived[1])
    all_keys = jnp.concatenate(halo_keys + [key_states], axis=1)
    all_values = jnp.concatenate(halo_values + [value_state_rows], axis=1)
    d_rows = lax.all_gather(d_out, "tp", axis=1, tiled=True)
    d_attn = jnp.einsum("std,dc->stc", d_rows, o_weight, preferred_element_type=jnp.float32).astype(
        jnp.bfloat16
    )
    d_query, attn, d_keys, d_values = attend(
        query, all_keys, all_values, d_attn, doc_start, first_pos
    )

    def back_piece(grads, behind):
        return grads[:, (nhalo - behind) * shard_rows : (nhalo - behind + 1) * shard_rows]

    summed_keys = back_piece(d_keys, 0)
    summed_values = back_piece(d_values, 0)
    for distance in range(1, nhalo + 1):
        arrived = from_behind(
            (back_piece(d_keys, distance), back_piece(d_values, distance)), "ctx", -distance
        )
        summed_keys = summed_keys + arrived[0]
        summed_values = summed_values + arrived[1]
    partials = []
    for seq_id in range(seq_count):
        columns = d_rows[seq_id]
        partials.append(
            lax.psum_scatter(
                jnp.dot(columns.T, attn[seq_id], preferred_element_type=jnp.float32),
                "ctx",
                scatter_dimension=0,
                tiled=True,
            )
        )
    d_o_weight = reduce(jnp.add, partials)
    return (
        d_query,
        summed_keys.astype(jnp.bfloat16),
        summed_values.astype(jnp.bfloat16),
        d_o_weight,
    )


def solution(mesh):
    return jax.shard_map(
        local,
        mesh=mesh,
        in_specs=(
            P(None, "ctx", "tp"),
            P(None, "ctx", "tp"),
            P(None, "ctx", "tp"),
            P(None, ("ctx", "tp"), None),
            P(None, "tp"),
            P(None, "ctx"),
        ),
        out_specs=(
            P(None, "ctx", "tp"),
            P(None, "ctx", "tp"),
            P(None, "ctx", "tp"),
            P("ctx", "tp"),
        ),
        check_vma=False,
    )
```

profile of v0, /device:TPU:1, one launch (start us, length us, event | category | flops | bytes accessed | tf_op | source)
XLA Modules:
  0.0 359.6 jit_solution(5256550249442685030)
XLA Ops:
  8.3 4.4 %collective-permute-start = (bf16[2,128,256]{1,2,0:T(8,128)(2,1)S(1)}, bf16[2,128,256]{1,2,0:T(8,128)(2,1)S(1)}, u32[]{:S(2)}, u32[]{:S(2)}) collective-permute-start(bf16[2,128,256]{1,2,0:T(8,128)(2,1)S(1)} %copy.90), channel_id=1, source_target_pairs={{0,32},{4,36},{8,40},{12,44},{16,48},{20,52},{24,56},{28,60},{32,6... | collective-permute-start | bytes 393224 | tf_op jit(solution)/shard_map/ppermute | solution.py:18
  12.7 4.4 %collective-permute-start.1 = (bf16[2,128,256]{1,2,0:T(8,128)(2,1)S(1)}, bf16[2,128,256]{1,2,0:T(8,128)(2,1)S(1)}, u32[]{:S(2)}, u32[]{:S(2)}) collective-permute-start(bf16[2,128,256]{1,2,0:T(8,128)(2,1)S(1)} %copy.90), channel_id=1, source_target_pairs={{0,28},{4,32},{8,36},{12,40},{16,44},{20,48},{24,52},{28,56},{32,6... | collective-permute-start | bytes 393224 | tf_op jit(solution)/shard_map/ppermute | solution.py:18
  17.1 4.6 %collective-permute-start.2 = (bf16[2,128,256]{1,2,0:T(8,128)(2,1)S(1)}, bf16[2,128,256]{1,2,0:T(8,128)(2,1)S(1)}, u32[]{:S(2)}, u32[]{:S(2)}) collective-permute-start(bf16[2,128,256]{1,2,0:T(8,128)(2,1)S(1)} %copy.90), channel_id=1, source_target_pairs={{0,24},{4,28},{8,32},{12,36},{16,40},{20,44},{24,48},{28,52},{32,5... | collective-permute-start | bytes 393224 | tf_op jit(solution)/shard_map/ppermute | solution.py:18
  21.7 3.3 collective-permute-start.3
  25.1 4.5 %collective-permute-start.4 = (bf16[2,128,256]{1,2,0:T(8,128)(2,1)S(1)}, bf16[2,128,256]{1,2,0:T(8,128)(2,1)S(1)}, u32[]{:S(2)}, u32[]{:S(2)}) collective-permute-start(bf16[2,128,256]{1,2,0:T(8,128)(2,1)S(1)} %copy.90), channel_id=1, source_target_pairs={{0,16},{4,20},{8,24},{12,28},{16,32},{20,36},{24,40},{28,44},{32,4... | collective-permute-start | bytes 393224 | tf_op jit(solution)/shard_map/ppermute | solution.py:18
  31.3 5.7 %collective-permute-start.5 = (bf16[2,128,256]{1,2,0:T(8,128)(2,1)S(1)}, bf16[2,128,256]{1,2,0:T(8,128)(2,1)S(1)}, u32[]{:S(2)}, u32[]{:S(2)}) collective-permute-start(bf16[2,128,256]{1,2,0:T(8,128)(2,1)S(1)} %copy.90), channel_id=1, source_target_pairs={{0,12},{4,16},{8,20},{12,24},{16,28},{20,32},{24,36},{28,40},{32,4... | collective-permute-start | bytes 393224 | tf_op jit(solution)/shard_map/ppermute | solution.py:18
  37.0 2.6 collective-permute-start.6
  39.6 2.5 collective-permute-start.7
  42.2 2.6 collective-permute-start.8
  44.9 2.7 collective-permute-start.9
  47.7 4.3 %collective-permute-start.10 = (bf16[2,128,256]{1,2,0:T(8,128)(2,1)S(1)}, bf16[2,128,256]{1,2,0:T(8,128)(2,1)S(1)}, u32[]{:S(2)}, u32[]{:S(2)}) collective-permute-start(bf16[2,128,256]{1,2,0:T(8,128)(2,1)S(1)} %copy.101), channel_id=1, source_target_pairs={{0,24},{4,28},{8,32},{12,36},{16,40},{20,44},{24,48},{28,52},{32,5... | collective-permute-start | bytes 393224 | tf_op jit(solution)/shard_map/ppermute | solution.py:18
  52.1 3.8 %collective-permute-start.11 = (bf16[2,128,256]{1,2,0:T(8,128)(2,1)S(1)}, bf16[2,128,256]{1,2,0:T(8,128)(2,1)S(1)}, u32[]{:S(2)}, u32[]{:S(2)}) collective-permute-start(bf16[2,128,256]{1,2,0:T(8,128)(2,1)S(1)} %copy.101), channel_id=1, source_target_pairs={{0,20},{4,24},{8,28},{12,32},{16,36},{20,40},{24,44},{28,48},{32,5... | collective-permute-start | bytes 393224 | tf_op jit(solution)/shard_map/ppermute | solution.py:18
  56.0 2.7 collective-permute-start.12
  58.8 3.8 %collective-permute-start.13 = (bf16[2,128,256]{1,2,0:T(8,128)(2,1)S(1)}, bf16[2,128,256]{1,2,0:T(8,128)(2,1)S(1)}, u32[]{:S(2)}, u32[]{:S(2)}) collective-permute-start(bf16[2,128,256]{1,2,0:T(8,128)(2,1)S(1)} %copy.101), channel_id=1, source_target_pairs={{0,12},{4,16},{8,20},{12,24},{16,28},{20,32},{24,36},{28,40},{32,4... | collective-permute-start | bytes 393224 | tf_op jit(solution)/shard_map/ppermute | solution.py:18
  63.3 1.9 collective-permute-start.14
  65.9 3.3 collective-permute-start.15
  74.0 3.8 %exponential_reduce_fusion = (f32[2,2,2,128]{3,2,1,0:T(2,128)S(1)}, f32[2,2,2,128,1152]{3,4,2,1,0:T(8,128)}) fusion(pred[2,128,1152]{1,2,0:T(8,128)(4,1)S(1)} %compare_and_fusion, bf16[2,1152,2,128,1]{1,3,4,2,0:T(8,128)(2,1)S(1)} %bitcast.89, bf16[2,128,2,2,128]{1,4,3,2,0:T(8,128)(2,1)S(1)} %bitcast.91), kind=kOutput, calls=%fused_computation.12 | convolution fusion | flops 306709632 | bytes 6459392 | tf_op jit(solution)/shard_map/sub | solution.py:45
  77.8 3.0 fusion.10
  80.8 5.0 %fusion.13 = bf16[2,128,512]{2,1,0:T(8,128)(2,1)S(1)} fusion(bf16[2,128,5376]{2,1,0:T(8,128)(2,1)} %all-gather.2.cloned.1.call-done, bf16[5376,512]{1,0:T(8,128)(2,1)} %param.10), kind=kOutput, calls=%fused_computation.24 | convolution fusion | flops 1409417216 | bytes 8519680 | tf_op jit(solution)/shard_map/std,dc->stc/dot_general | solution.py:90
  86.0 2.0 multiply_reduce_fusion
  88.1 1.6 fusion.11
  89.7 5.6 %add_bitcast_fusion = f32[5376,512]{0,1:T(8,128)} fusion(f32[512,5376]{1,0:T(8,128)S(1)} %fusion.11, bf16[128,512]{0,1:T(8,128)(2,1)S(1)} %bitcast.94, bf16[2,128,5376]{2,1,0:T(8,128)(2,1)S(1)} %copy-done.2), kind=kOutput, calls=%fused_computation.1 | convolution fusion | flops 707395584 | bytes 23527424 | tf_op jit(solution)/shard_map/dot_general | solution.py:113
  97.2 3.9 %fusion.5 = bf16[2,2,2,128,1152]{3,4,2,1,0:T(8,128)(2,1)S(1)} fusion(bf16[2,1152,2,128,1]{1,3,4,2,0:T(8,128)(2,1)} %bitcast.37, bf16[2,128,2,2,128]{1,4,3,2,0:T(8,128)(2,1)S(1)} %bitcast.87, f32[2,2,2,128]{3,2,1,0:T(2,128)S(1)} %bitcast.96, f32[2,2,2,128]{3,2,1,0:T(2,128)S(1)} %get-tuple-element.36, f32[2,2,2,128,1152]{3,4,2,1,0:T(8,128)} %get-tuple-element.37), kind=kOutput, calls=%fused_computation.8 | convolution fusion | flops 306708480 | bytes 8527872 | tf_op jit(solution)/shard_map/sqhgd,skhd->shgqk/dot_general | solution.py:51
  103.8 1.8 copy.163
  106.9 1.8 copy.162
  108.7 1.5 collective-permute-start.22
  110.1 1.8 copy.161
  113.2 1.8 copy.160
  116.3 1.8 copy.159
  124.1 1.4 fusion.19
  125.5 1.9 copy.172
  127.4 1.8 copy.171
  129.2 1.8 copy.170
  132.3 1.9 collective-permute-start.16
  134.3 4.7 %collective-permute-done.20 = f32[2,128,256]{2,1,0:T(8,128)} collective-permute-done((f32[2,128,256]{2,1,0:T(8,128)}, f32[2,128,256]{2,1,0:T(8,128)}, u32[]{:S(2)}, u32[]{:S(2)}) %collective-permute-start.20) | collective-permute-done | bytes 262176 | tf_op jit(solution)/shard_map/ppermute | solution.py:18
  140.3 2.9 collective-permute-done.19
  144.5 1.7 collective-permute-done.18
  147.5 1.3 fusion.12
  148.8 1.9 copy.137
  154.9 2.6 collective-permute-done.16
  158.9 18.7 %collective-permute-done.31 = f32[2,128,256]{2,1,0:T(8,128)} collective-permute-done((f32[2,128,256]{2,1,0:T(8,128)}, f32[2,128,256]{2,1,0:T(8,128)}, u32[]{:S(2)}, u32[]{:S(2)}) %collective-permute-start.31) | collective-permute-done | bytes 262176 | tf_op jit(solution)/shard_map/ppermute | solution.py:18
  178.8 16.4 %collective-permute-done.30 = f32[2,128,256]{2,1,0:T(8,128)} collective-permute-done((f32[2,128,256]{2,1,0:T(8,128)}, f32[2,128,256]{2,1,0:T(8,128)}, u32[]{:S(2)}, u32[]{:S(2)}) %collective-permute-start.30) | collective-permute-done | bytes 262176 | tf_op jit(solution)/shard_map/ppermute | solution.py:18
  196.5 1.9 collective-permute-start.24
  198.4 2.3 add_convert_fusion.1
  200.7 5.6 %collective-permute-done.25 = f32[2,128,256]{2,1,0:T(8,128)S(1)} collective-permute-done((f32[2,128,256]{2,1,0:T(8,128)S(1)}, f32[2,128,256]{2,1,0:T(8,128)S(1)}, u32[]{:S(2)}, u32[]{:S(2)}) %collective-permute-start.25) | collective-permute-done | bytes 262176 | tf_op jit(solution)/shard_map/ppermute | solution.py:18
  206.3 4.8 %collective-permute-done.24 = f32[2,128,256]{2,1,0:T(8,128)S(1)} collective-permute-done((f32[2,128,256]{2,1,0:T(8,128)S(1)}, f32[2,128,256]{2,1,0:T(8,128)S(1)}, u32[]{:S(2)}, u32[]{:S(2)}) %collective-permute-start.24) | collective-permute-done | bytes 262176 | tf_op jit(solution)/shard_map/ppermute | solution.py:18
  211.1 1.9 add_convert_fusion
  213.0 137.7 %all-reduce.3.cloned.1.call-done = f32[5376,512]{0,1:T(8,128)} async-done(((f32[5376,512]{0,1:T(8,128)}), f32[5376,512]{0,1:T(8,128)}) %all-reduce.3.cloned.1.call-update) | async-done | bytes 11010064
  (111 shorter events, 38.3 us)
Async XLA Ops:
  7.2 23.8 %copy-start.11 = (bf16[2,128,256]{2,1,0:T(8,128)(2,1)S(1)}, bf16[2,128,256]{2,1,0:T(8,128)(2,1)}, u32[]{:S(2)}) copy-start(bf16[2,128,256]{2,1,0:T(8,128)(2,1)} %param.8) | copy-start | bytes 393220
  7.2 23.9 %copy-start.10 = (bf16[2,128,512]{2,1,0:T(8,128)(2,1)S(1)}, bf16[2,128,512]{2,1,0:T(8,128)(2,1)}, u32[]{:S(2)}) copy-start(bf16[2,128,512]{2,1,0:T(8,128)(2,1)} %param.6) | copy-start | bytes 786436
  7.2 73.6 %all-gather.2.cloned.1.call-start = ((), (), s32[]{:S(2)}) async-start(), calls=%async_computation | async-start | bytes 3440640 | tf_op jit(solution)/shard_map/all_gather | solution.py:89
  8.3 22.9 %collective-permute-start = (bf16[2,128,256]{1,2,0:T(8,128)(2,1)S(1)}, bf16[2,128,256]{1,2,0:T(8,128)(2,1)S(1)}, u32[]{:S(2)}, u32[]{:S(2)}) collective-permute-start(bf16[2,128,256]{1,2,0:T(8,128)(2,1)S(1)} %copy.90), channel_id=1, source_target_pairs={{0,32},{4,36},{8,40},{12,44},{16,48},{20,52},{24,56},{28,60},{32,6... | collective-permute-start | bytes 393224 | tf_op jit(solution)/shard_map/ppermute | solution.py:18
  12.7 24.3 %collective-permute-start.1 = (bf16[2,128,256]{1,2,0:T(8,128)(2,1)S(1)}, bf16[2,128,256]{1,2,0:T(8,128)(2,1)S(1)}, u32[]{:S(2)}, u32[]{:S(2)}) collective-permute-start(bf16[2,128,256]{1,2,0:T(8,128)(2,1)S(1)} %copy.90), channel_id=1, source_target_pairs={{0,28},{4,32},{8,36},{12,40},{16,44},{20,48},{24,52},{28,56},{32,6... | collective-permute-start | bytes 393224 | tf_op jit(solution)/shard_map/ppermute | solution.py:18
  17.1 22.5 %collective-permute-start.2 = (bf16[2,128,256]{1,2,0:T(8,128)(2,1)S(1)}, bf16[2,128,256]{1,2,0:T(8,128)(2,1)S(1)}, u32[]{:S(2)}, u32[]{:S(2)}) collective-permute-start(bf16[2,128,256]{1,2,0:T(8,128)(2,1)S(1)} %copy.90), channel_id=1, source_target_pairs={{0,24},{4,28},{8,32},{12,36},{16,40},{20,44},{24,48},{28,52},{32,5... | collective-permute-start | bytes 393224 | tf_op jit(solution)/shard_map/ppermute | solution.py:18
  21.7 20.4 %collective-permute-start.3 = (bf16[2,128,256]{1,2,0:T(8,128)(2,1)S(1)}, bf16[2,128,256]{1,2,0:T(8,128)(2,1)S(1)}, u32[]{:S(2)}, u32[]{:S(2)}) collective-permute-start(bf16[2,128,256]{1,2,0:T(8,128)(2,1)S(1)} %copy.90), channel_id=1, source_target_pairs={{0,20},{4,24},{8,28},{12,32},{16,36},{20,40},{24,44},{28,48},{32,5... | collective-permute-start | bytes 393224 | tf_op jit(solution)/shard_map/ppermute | solution.py:18
  25.1 19.8 %collective-permute-start.4 = (bf16[2,128,256]{1,2,0:T(8,128)(2,1)S(1)}, bf16[2,128,256]{1,2,0:T(8,128)(2,1)S(1)}, u32[]{:S(2)}, u32[]{:S(2)}) collective-permute-start(bf16[2,128,256]{1,2,0:T(8,128)(2,1)S(1)} %copy.90), channel_id=1, source_target_pairs={{0,16},{4,20},{8,24},{12,28},{16,32},{20,36},{24,40},{28,44},{32,4... | collective-permute-start | bytes 393224 | tf_op jit(solution)/shard_map/ppermute | solution.py:18
  29.6 321.1 %all-reduce.3.cloned.1.call-start = ((), (), s32[]{:S(2)}) async-start(), calls=%async_computation.1 | async-start | bytes 22020096
  31.3 16.4 %collective-permute-start.5 = (bf16[2,128,256]{1,2,0:T(8,128)(2,1)S(1)}, bf16[2,128,256]{1,2,0:T(8,128)(2,1)S(1)}, u32[]{:S(2)}, u32[]{:S(2)}) collective-permute-start(bf16[2,128,256]{1,2,0:T(8,128)(2,1)S(1)} %copy.90), channel_id=1, source_target_pairs={{0,12},{4,16},{8,20},{12,24},{16,28},{20,32},{24,36},{28,40},{32,4... | collective-permute-start | bytes 393224 | tf_op jit(solution)/shard_map/ppermute | solution.py:18
  37.0 15.1 %collective-permute-start.6 = (bf16[2,128,256]{1,2,0:T(8,128)(2,1)S(1)}, bf16[2,128,256]{1,2,0:T(8,128)(2,1)S(1)}, u32[]{:S(2)}, u32[]{:S(2)}) collective-permute-start(bf16[2,128,256]{1,2,0:T(8,128)(2,1)S(1)} %copy.90), channel_id=1, source_target_pairs={{0,8},{4,12},{8,16},{12,20},{16,24},{20,28},{24,32},{28,36},{32,40... | collective-permute-start | bytes 393224 | tf_op jit(solution)/shard_map/ppermute | solution.py:18
  39.6 16.3 %collective-permute-start.7 = (bf16[2,128,256]{1,2,0:T(8,128)(2,1)S(1)}, bf16[2,128,256]{1,2,0:T(8,128)(2,1)S(1)}, u32[]{:S(2)}, u32[]{:S(2)}) collective-permute-start(bf16[2,128,256]{1,2,0:T(8,128)(2,1)S(1)} %copy.90), channel_id=1, source_target_pairs={{0,4},{4,8},{8,12},{12,16},{16,20},{20,24},{24,28},{28,32},{32,36}... | collective-permute-start | bytes 393224 | tf_op jit(solution)/shard_map/ppermute | solution.py:18
  42.2 16.6 %collective-permute-start.8 = (bf16[2,128,256]{1,2,0:T(8,128)(2,1)S(1)}, bf16[2,128,256]{1,2,0:T(8,128)(2,1)S(1)}, u32[]{:S(2)}, u32[]{:S(2)}) collective-permute-start(bf16[2,128,256]{1,2,0:T(8,128)(2,1)S(1)} %copy.101), channel_id=1, source_target_pairs={{0,32},{4,36},{8,40},{12,44},{16,48},{20,52},{24,56},{28,60},{32,6... | collective-permute-start | bytes 393224 | tf_op jit(solution)/shard_map/ppermute | solution.py:18
  44.9 18.4 %collective-permute-start.9 = (bf16[2,128,256]{1,2,0:T(8,128)(2,1)S(1)}, bf16[2,128,256]{1,2,0:T(8,128)(2,1)S(1)}, u32[]{:S(2)}, u32[]{:S(2)}) collective-permute-start(bf16[2,128,256]{1,2,0:T(8,128)(2,1)S(1)} %copy.101), channel_id=1, source_target_pairs={{0,28},{4,32},{8,36},{12,40},{16,44},{20,48},{24,52},{28,56},{32,6... | collective-permute-start | bytes 393224 | tf_op jit(solution)/shard_map/ppermute | solution.py:18
  47.7 18.2 %collective-permute-start.10 = (bf16[2,128,256]{1,2,0:T(8,128)(2,1)S(1)}, bf16[2,128,256]{1,2,0:T(8,128)(2,1)S(1)}, u32[]{:S(2)}, u32[]{:S(2)}) collective-permute-start(bf16[2,128,256]{1,2,0:T(8,128)(2,1)S(1)} %copy.101), channel_id=1, source_target_pairs={{0,24},{4,28},{8,32},{12,36},{16,40},{20,44},{24,48},{28,52},{32,5... | collective-permute-start | bytes 393224 | tf_op jit(solution)/shard_map/ppermute | solution.py:18
  52.1 17.8 %collective-permute-start.11 = (bf16[2,128,256]{1,2,0:T(8,128)(2,1)S(1)}, bf16[2,128,256]{1,2,0:T(8,128)(2,1)S(1)}, u32[]{:S(2)}, u32[]{:S(2)}) collective-permute-start(bf16[2,128,256]{1,2,0:T(8,128)(2,1)S(1)} %copy.101), channel_id=1, source_target_pairs={{0,20},{4,24},{8,28},{12,32},{16,36},{20,40},{24,44},{28,48},{32,5... | collective-permute-start | bytes 393224 | tf_op jit(solution)/shard_map/ppermute | solution.py:18
  56.0 14.6 %collective-permute-start.12 = (bf16[2,128,256]{1,2,0:T(8,128)(2,1)S(1)}, bf16[2,128,256]{1,2,0:T(8,128)(2,1)S(1)}, u32[]{:S(2)}, u32[]{:S(2)}) collective-permute-start(bf16[2,128,256]{1,2,0:T(8,128)(2,1)S(1)} %copy.101), channel_id=1, source_target_pairs={{0,16},{4,20},{8,24},{12,28},{16,32},{20,36},{24,40},{28,44},{32,4... | collective-permute-start | bytes 393224 | tf_op jit(solution)/shard_map/ppermute | solution.py:18
  58.8 19.1 %copy-start.3 = (bf16[2,1152,256]{1,2,0:T(8,128)(2,1)}, bf16[2,1152,256]{1,2,0:T(8,128)(2,1)S(1)}, u32[]{:S(2)}) copy-start(bf16[2,1152,256]{1,2,0:T(8,128)(2,1)S(1)} %constant_dynamic-update-slice_fusion) | copy-start | bytes 3538948
  58.8 12.5 %collective-permute-start.13 = (bf16[2,128,256]{1,2,0:T(8,128)(2,1)S(1)}, bf16[2,128,256]{1,2,0:T(8,128)(2,1)S(1)}, u32[]{:S(2)}, u32[]{:S(2)}) collective-permute-start(bf16[2,128,256]{1,2,0:T(8,128)(2,1)S(1)} %copy.101), channel_id=1, source_target_pairs={{0,12},{4,16},{8,20},{12,24},{16,28},{20,32},{24,36},{28,40},{32,4... | collective-permute-start | bytes 393224 | tf_op jit(solution)/shard_map/ppermute | solution.py:18
  63.3 8.6 %collective-permute-start.14 = (bf16[2,128,256]{1,2,0:T(8,128)(2,1)S(1)}, bf16[2,128,256]{1,2,0:T(8,128)(2,1)S(1)}, u32[]{:S(2)}, u32[]{:S(2)}) collective-permute-start(bf16[2,128,256]{1,2,0:T(8,128)(2,1)S(1)} %copy.101), channel_id=1, source_target_pairs={{0,8},{4,12},{8,16},{12,20},{16,24},{20,28},{24,32},{28,36},{32,40... | collective-permute-start | bytes 393224 | tf_op jit(solution)/shard_map/ppermute | solution.py:18
  65.9 6.7 %collective-permute-start.15 = (bf16[2,128,256]{1,2,0:T(8,128)(2,1)S(1)}, bf16[2,128,256]{1,2,0:T(8,128)(2,1)S(1)}, u32[]{:S(2)}, u32[]{:S(2)}) collective-permute-start(bf16[2,128,256]{1,2,0:T(8,128)(2,1)S(1)} %copy.101), channel_id=1, source_target_pairs={{0,4},{4,8},{8,12},{12,16},{16,20},{20,24},{24,28},{28,32},{32,36}... | collective-permute-start | bytes 393224 | tf_op jit(solution)/shard_map/ppermute | solution.py:18
  86.0 2.1 copy-start.2
  95.3 0.7 copy-start.12
  101.2 1.4 copy-start
  105.6 17.2 %collective-permute-start.23 = (f32[2,128,256]{2,1,0:T(8,128)}, f32[2,128,256]{2,1,0:T(8,128)}, u32[]{:S(2)}, u32[]{:S(2)}) collective-permute-start(f32[2,128,256]{2,1,0:T(8,128)} %copy.163), channel_id=1, source_target_pairs={{32,0},{36,4},{40,8},{44,12},{48,16},{52,20},{56,24},{60,28},{64,3... | collective-permute-start | bytes 786440 | tf_op jit(solution)/shard_map/ppermute | solution.py:18
  108.7 22.4 %collective-permute-start.22 = (f32[2,128,256]{2,1,0:T(8,128)}, f32[2,128,256]{2,1,0:T(8,128)}, u32[]{:S(2)}, u32[]{:S(2)}) collective-permute-start(f32[2,128,256]{2,1,0:T(8,128)} %copy.162), channel_id=1, source_target_pairs={{28,0},{32,4},{36,8},{40,12},{44,16},{48,20},{52,24},{56,28},{60,3... | collective-permute-start | bytes 786440 | tf_op jit(solution)/shard_map/ppermute | solution.py:18
  111.9 20.4 %collective-permute-start.21 = (f32[2,128,256]{2,1,0:T(8,128)}, f32[2,128,256]{2,1,0:T(8,128)}, u32[]{:S(2)}, u32[]{:S(2)}) collective-permute-start(f32[2,128,256]{2,1,0:T(8,128)} %copy.161), channel_id=1, source_target_pairs={{24,0},{28,4},{32,8},{36,12},{40,16},{44,20},{48,24},{52,28},{56,3... | collective-permute-start | bytes 786440 | tf_op jit(solution)/shard_map/ppermute | solution.py:18
  115.0 24.0 %collective-permute-start.20 = (f32[2,128,256]{2,1,0:T(8,128)}, f32[2,128,256]{2,1,0:T(8,128)}, u32[]{:S(2)}, u32[]{:S(2)}) collective-permute-start(f32[2,128,256]{2,1,0:T(8,128)} %copy.160), channel_id=1, source_target_pairs={{20,0},{24,4},{28,8},{32,12},{36,16},{40,20},{44,24},{48,28},{52,3... | collective-permute-start | bytes 786440 | tf_op jit(solution)/shard_map/ppermute | solution.py:18
  118.1 25.1 %collective-permute-start.19 = (f32[2,128,256]{2,1,0:T(8,128)}, f32[2,128,256]{2,1,0:T(8,128)}, u32[]{:S(2)}, u32[]{:S(2)}) collective-permute-start(f32[2,128,256]{2,1,0:T(8,128)} %copy.159), channel_id=1, source_target_pairs={{16,0},{20,4},{24,8},{28,12},{32,16},{36,20},{40,24},{44,28},{48,3... | collective-permute-start | bytes 786440 | tf_op jit(solution)/shard_map/ppermute | solution.py:18
  122.8 23.4 %collective-permute-start.18 = (f32[2,128,256]{2,1,0:T(8,128)}, f32[2,128,256]{2,1,0:T(8,128)}, u32[]{:S(2)}, u32[]{:S(2)}) collective-permute-start(f32[2,128,256]{2,1,0:T(8,128)} %copy.158), channel_id=1, source_target_pairs={{12,0},{16,4},{20,8},{24,12},{28,16},{32,20},{36,24},{40,28},{44,3... | collective-permute-start | bytes 786440 | tf_op jit(solution)/shard_map/ppermute | solution.py:18
  124.1 23.4 %copy-start.1 = (bf16[2,2,2,128,1152]{3,4,2,1,0:T(8,128)(2,1)S(1)}, bf16[2,2,2,128,1152]{3,4,2,1,0:T(8,128)(2,1)}, u32[]{:S(2)}) copy-start(bf16[2,2,2,128,1152]{3,4,2,1,0:T(8,128)(2,1)} %copy-done) | copy-start | bytes 7077892
  125.5 22.0 %copy-start.4 = (bf16[2,1152,256]{1,2,0:T(8,128)(2,1)S(1)}, bf16[2,1152,256]{1,2,0:T(8,128)(2,1)}, u32[]{:S(2)}) copy-start(bf16[2,1152,256]{1,2,0:T(8,128)(2,1)} %copy-done.3) | copy-start | bytes 3538948
  131.0 22.6 %collective-permute-start.17 = (f32[2,128,256]{2,1,0:T(8,128)}, f32[2,128,256]{2,1,0:T(8,128)}, u32[]{:S(2)}, u32[]{:S(2)}) collective-permute-start(f32[2,128,256]{2,1,0:T(8,128)} %copy.157), channel_id=1, source_target_pairs={{8,0},{12,4},{16,8},{20,12},{24,16},{28,20},{32,24},{36,28},{40,32... | collective-permute-start | bytes 786440 | tf_op jit(solution)/shard_map/ppermute | solution.py:18
  132.3 25.3 %collective-permute-start.16 = (f32[2,128,256]{2,1,0:T(8,128)}, f32[2,128,256]{2,1,0:T(8,128)}, u32[]{:S(2)}, u32[]{:S(2)}) collective-permute-start(f32[2,128,256]{2,1,0:T(8,128)} %copy.156), channel_id=1, source_target_pairs={{4,0},{8,4},{12,8},{16,12},{20,16},{24,20},{28,24},{32,28},{36,32}... | collective-permute-start | bytes 786440 | tf_op jit(solution)/shard_map/ppermute | solution.py:18
  139.0 38.6 %collective-permute-start.31 = (f32[2,128,256]{2,1,0:T(8,128)}, f32[2,128,256]{2,1,0:T(8,128)}, u32[]{:S(2)}, u32[]{:S(2)}) collective-permute-start(f32[2,128,256]{2,1,0:T(8,128)} %copy.172), channel_id=1, source_target_pairs={{32,0},{36,4},{40,8},{44,12},{48,16},{52,20},{56,24},{60,28},{64,3... | collective-permute-start | bytes 786440 | tf_op jit(solution)/shard_map/ppermute | solution.py:18
  143.2 52.0 %collective-permute-start.30 = (f32[2,128,256]{2,1,0:T(8,128)}, f32[2,128,256]{2,1,0:T(8,128)}, u32[]{:S(2)}, u32[]{:S(2)}) collective-permute-start(f32[2,128,256]{2,1,0:T(8,128)} %copy.171), channel_id=1, source_target_pairs={{28,0},{32,4},{36,8},{40,12},{44,16},{48,20},{52,24},{56,28},{60,3... | collective-permute-start | bytes 786440 | tf_op jit(solution)/shard_map/ppermute | solution.py:18
  146.2 50.3 %collective-permute-start.29 = (f32[2,128,256]{2,1,0:T(8,128)}, f32[2,128,256]{2,1,0:T(8,128)}, u32[]{:S(2)}, u32[]{:S(2)}) collective-permute-start(f32[2,128,256]{2,1,0:T(8,128)} %copy.170), channel_id=1, source_target_pairs={{24,0},{28,4},{32,8},{36,12},{40,16},{44,20},{48,24},{52,28},{56,3... | collective-permute-start | bytes 786440 | tf_op jit(solution)/shard_map/ppermute | solution.py:18
  148.8 4.1 %copy-start.9 = (f32[2,128,256]{1,2,0:T(8,128)S(1)}, f32[2,128,256]{1,2,0:T(8,128)}, u32[]{:S(2)}) copy-start(f32[2,128,256]{1,2,0:T(8,128)} %get-tuple-element.20) | copy-start | bytes 786436
  148.8 4.3 %copy-start.8 = (f32[2,128,256]{1,2,0:T(8,128)S(1)}, f32[2,128,256]{1,2,0:T(8,128)}, u32[]{:S(2)}) copy-start(f32[2,128,256]{1,2,0:T(8,128)} %get-tuple-element.21) | copy-start | bytes 786436
  148.8 4.4 %copy-start.7 = (f32[2,128,256]{1,2,0:T(8,128)S(1)}, f32[2,128,256]{1,2,0:T(8,128)}, u32[]{:S(2)}) copy-start(f32[2,128,256]{1,2,0:T(8,128)} %get-tuple-element.22) | copy-start | bytes 786436
  150.6 2.7 copy-start.6
  151.8 1.7 copy-start.5
  153.6 47.1 %collective-permute-start.28 = (f32[2,128,256]{2,1,0:T(8,128)S(1)}, f32[2,128,256]{2,1,0:T(8,128)S(1)}, u32[]{:S(2)}, u32[]{:S(2)}) collective-permute-start(f32[2,128,256]{2,1,0:T(8,128)S(1)} %copy.169), channel_id=1, source_target_pairs={{20,0},{24,4},{28,8},{32,12},{36,16},{40,20},{44,24},{48,28},{52,3... | collective-permute-start | bytes 786440 | tf_op jit(solution)/shard_map/ppermute | solution.py:18
  157.6 43.1 %collective-permute-start.27 = (f32[2,128,256]{2,1,0:T(8,128)S(1)}, f32[2,128,256]{2,1,0:T(8,128)S(1)}, u32[]{:S(2)}, u32[]{:S(2)}) collective-permute-start(f32[2,128,256]{2,1,0:T(8,128)S(1)} %copy.168), channel_id=1, source_target_pairs={{16,0},{20,4},{24,8},{28,12},{32,16},{36,20},{40,24},{44,28},{48,3... | collective-permute-start | bytes 786440 | tf_op jit(solution)/shard_map/ppermute | solution.py:18
  177.5 23.2 %collective-permute-start.26 = (f32[2,128,256]{2,1,0:T(8,128)S(1)}, f32[2,128,256]{2,1,0:T(8,128)S(1)}, u32[]{:S(2)}, u32[]{:S(2)}) collective-permute-start(f32[2,128,256]{2,1,0:T(8,128)S(1)} %copy.167), channel_id=1, source_target_pairs={{12,0},{16,4},{20,8},{24,12},{28,16},{32,20},{36,24},{40,28},{44,3... | collective-permute-start | bytes 786440 | tf_op jit(solution)/shard_map/ppermute | solution.py:18
  195.2 11.1 %collective-permute-start.25 = (f32[2,128,256]{2,1,0:T(8,128)S(1)}, f32[2,128,256]{2,1,0:T(8,128)S(1)}, u32[]{:S(2)}, u32[]{:S(2)}) collective-permute-start(f32[2,128,256]{2,1,0:T(8,128)S(1)} %copy.166), channel_id=1, source_target_pairs={{8,0},{12,4},{16,8},{20,12},{24,16},{28,20},{32,24},{36,28},{40,32... | collective-permute-start | bytes 786440 | tf_op jit(solution)/shard_map/ppermute | solution.py:18
  196.5 14.6 %collective-permute-start.24 = (f32[2,128,256]{2,1,0:T(8,128)S(1)}, f32[2,128,256]{2,1,0:T(8,128)S(1)}, u32[]{:S(2)}, u32[]{:S(2)}) collective-permute-start(f32[2,128,256]{2,1,0:T(8,128)S(1)} %copy.165), channel_id=1, source_target_pairs={{4,0},{8,4},{12,8},{16,12},{20,16},{24,20},{28,24},{32,28},{36,32}... | collective-permute-start | bytes 786440 | tf_op jit(solution)/shard_map/ppermute | solution.py:18
Sparse Core Ops, SparseCore 0:
  29.8 36.8 all-gather.1
  95.5 255.2 all-reduce.2
where the time goes:
time: 362 us; the launch traced here: 360 us
  waiting for transfers between devices  195 us (54%)
  starting transfers between devices  79.3 us (22%)
  local copies, waits for them, and re-layouts  36.3 us (10%)
  matrix products  24.9 us (7%)
  between operations  15.5 us (4%)
  other arithmetic  8.32 us (2%)
    unnamed x3, waiting for transfers between devices  138 us
    ppermute x32, starting transfers between devices, from_behind(): return lax.ppermute(block, axis, route)  79.3 us
    ppermute x32, waiting for transfers between devices, from_behind(): return lax.ppermute(block, axis, route)  57.5 us
    unnamed x66, local copies, waits for them, and re-layouts  32.6 us
  transfers between devices with their start and end apart: 34, of which 9 were waited for; matrix products, arithmetic and copies ran while one was open for 14% of the time, Pallas kernels for 0%

commit v1 on v0

v1 whole, which is shorter than its diff:
```python
import jax
import jax.numpy as jnp
from jax import lax
from jax.experimental import pallas as pl
from jax.experimental.pallas import tpu as pltpu
from jax.sharding import PartitionSpec as P

HEAD_SIZE = 128
WIN = 1024
CORES = 2
CHIPS_Y = 4
CHIPS_Z = 8
TP = 4
HALO_CHIPS = 4
LOG2_E = 1.4426950408889634

score_scale = 168.0 ** (-0.5)

NT = (((1,), (1,)), ((), ()))
TN = (((0,), (0,)), ((), ()))
NN = (((1,), (0,)), ((), ()))


def dot(a, b, dims=NN):
    return lax.dot_general(a, b, dims, preferred_element_type=jnp.float32)


def ctx_shift(block, move):
    count = CORES * CHIPS_Y * CHIPS_Z
    return lax.ppermute(block, "ctx", [(i, move(i)) for i in range(count)])


def to_sibling(block):
    return ctx_shift(block, lambda i: i ^ 1)


def chips_ahead(block, distance):
    count = CORES * CHIPS_Y * CHIPS_Z
    return ctx_shift(block, lambda i: (i + CORES * distance) % count)


def y_ahead(block, distance):
    def move(i):
        core, y, z = i % CORES, i // CORES % CHIPS_Y, i // (CORES * CHIPS_Y)
        return (z * CHIPS_Y + (y + distance) % CHIPS_Y) * CORES + core

    return ctx_shift(block, move)


def z_exchange(blocks):
    lanes = CORES * CHIPS_Y
    groups = [[z * lanes + lane for z in range(CHIPS_Z)] for lane in range(lanes)]
    return lax.all_to_all(blocks, "ctx", 0, 0, axis_index_groups=groups, tiled=True)


def tp_ahead(block, distance):
    return lax.ppermute(block, "tp", [(i, (i + distance) % TP) for i in range(TP)])


def query_positions(core, chip_pos, rows):
    lane = lax.broadcasted_iota(jnp.int32, (1, 2 * rows), 1)
    other = lane >= rows
    first = jnp.where(other, (1 - core) * rows - rows, core * rows)
    return chip_pos + first + lane


def forward_kernel(scalars, mine, recv, kv0, kv1, kv2, kv3, kv4, doc_mine, doc_recv, attn, weights):
    core, chip_pos = scalars[0], scalars[3]
    rows = mine.shape[1]
    query_pos = query_positions(core, chip_pos, rows)
    doc = jnp.concatenate([doc_mine[0], doc_recv[0]], axis=1)
    lowest = jnp.maximum(doc, query_pos - (WIN - 1))
    index = lax.broadcasted_iota(jnp.int32, (2 * rows, 2 * rows), 0)
    offset = index + jnp.where(index >= rows, (1 - core) * rows - rows, core * rows)
    for h in range(2):
        cols = slice(h * HEAD_SIZE, (h + 1) * HEAD_SIZE)
        q = jnp.concatenate([mine[0, :, cols], recv[0, :, cols]], axis=0)
        scores = []
        for d, kv in enumerate((kv0, kv1, kv2, kv3, kv4)):
            s = dot(kv[0, :, :HEAD_SIZE], q, NT) * (score_scale * LOG2_E)
            key_pos = offset + (chip_pos - 2 * rows * d)
            visible = key_pos >= lowest
            if d == 0:
                visible = visible & (key_pos <= query_pos)
            scores.append(jnp.where(visible, s, -1e30))
        top = scores[0]
        for s in scores[1:]:
            top = jnp.maximum(top, s)
        top = jnp.max(top, axis=0, keepdims=True)
        expo = [jnp.exp2(s - top) for s in scores]
        total = expo[0]
        for e in expo[1:]:
            total = total + e
        inverse = 1.0 / jnp.sum(total, axis=0, keepdims=True)
        acc = None
        for d, kv in enumerate((kv0, kv1, kv2, kv3, kv4)):
            w = (expo[d] * inverse).astype(jnp.bfloat16)
            weights[0, h, 2 * rows * d : 2 * rows * (d + 1), :] = w
            part = dot(kv[0, :, HEAD_SIZE:], w, TN)
            acc = part if acc is None else acc + part
        attn[0, :, cols] = acc.T.astype(jnp.bfloat16)


def projection_kernel(
    scalars, r0, r1, r2a, r2b, r3, t0, t1, t2a, t2b, t3, attn, o_weight,
    d_attn, w0, w1, w2, w3, acc, attn_rows, partial,
):
    step = pl.program_id(0)
    tp, y = scalars[1], scalars[2]
    piece = r0.shape[1]
    out_rows = w0.shape[1]

    def place(core_block, rel, seq):
        here = 4 * piece * core_block + piece * ((tp + rel) % TP)
        return seq, pl.ds(pl.multiple_of(here, piece), piece)

    slots = [(b, s, q) for b in range(2) for s in range(TP) for q in range(2)]

    @pl.when(step == 0)
    def _():
        for n, slot in enumerate(slots):
            seq, here = place(*slot)
            attn_rows[n * piece : (n + 1) * piece, :] = attn[seq, here, :]

    parts = []
    for ref in (r0, r1, r2a, r2b, r3, t0, t1, t2a, t2b, t3):
        for seq in range(ref.shape[0]):
            parts.append(ref[seq])
    rows = jnp.concatenate(parts, axis=0)
    product = dot(rows, o_weight[...])

    @pl.when(step == 0)
    def _():
        acc[...] = product

    @pl.when(step > 0)
    def _():
        acc[...] = acc[...] + product

    partial[...] = dot(rows, attn_rows[...], TN)
    for k, out in enumerate((w0, w1, w2, w3)):
        target = (y + k) % CHIPS_Y
        for z in range(out.shape[0]):
            start = pl.multiple_of((CHIPS_Y * z + target) * out_rows, 8)
            out[z] = partial[pl.ds(start, out_rows), :].astype(jnp.bfloat16)

    @pl.when(step == pl.num_programs(0) - 1)
    def _():
        for n, slot in enumerate(slots):
            seq, here = place(*slot)
            d_attn[seq, here, :] = acc[n * piece : (n + 1) * piece, :].astype(jnp.bfloat16)


def backward_kernel(
    mine, recv, kv0, kv1, kv2, kv3, kv4, weights, attn, d_attn,
    dq_mine, dq_other, g0, g1, g2, g3, g4,
):
    rows = mine.shape[1]
    heads = []
    for h in range(2):
        cols = slice(h * HEAD_SIZE, (h + 1) * HEAD_SIZE)
        q = jnp.concatenate([mine[0, :, cols], recv[0, :, cols]], axis=0)
        da = d_attn[0, :, cols]
        product = da.astype(jnp.float32) * attn[0, :, cols].astype(jnp.float32)
        delta = jnp.sum(product.T, axis=0, keepdims=True)
        heads.append((q, da, delta))
    dq = [None, None]
    for d, (kv, grad) in enumerate(zip((kv0, kv1, kv2, kv3, kv4), (g0, g1, g2, g3, g4))):
        keys = kv[0, :, :HEAD_SIZE]
        values = kv[0, :, HEAD_SIZE:]
        dk = dv = None
        for h, (q, da, delta) in enumerate(heads):
            w = weights[0, h, 2 * rows * d : 2 * rows * (d + 1), :]
            dp = dot(values, da, NT)
            ds = (w.astype(jnp.float32) * (dp - delta)).astype(jnp.bfloat16)
            v_part = dot(w, da)
            k_part = dot(ds, q)
            q_part = dot(keys, ds, TN)
            dv = v_part if dv is None else dv + v_part
            dk = k_part if dk is None else dk + k_part
            dq[h] = q_part if dq[h] is None else dq[h] + q_part
        grad[0, :, :HEAD_SIZE] = (dk * score_scale).astype(grad.dtype)
        grad[0, :, HEAD_SIZE:] = dv.astype(grad.dtype)
    for h in range(2):
        cols = slice(h * HEAD_SIZE, (h + 1) * HEAD_SIZE)
        full = (dq[h].T * score_scale).astype(jnp.bfloat16)
        dq_mine[0, :, cols] = full[:rows]
        dq_other[0, :, cols] = full[rows:]


def by_seq(shape):
    return pl.BlockSpec((1,) + shape[1:], lambda s, *_: (s,) + (0,) * (len(shape) - 1))


def forward(scalars, mine, recv, kvs, doc_mine, doc_recv):
    seqs, rows, width = mine.shape
    keys = 2 * rows * len(kvs)
    outs = (
        jax.ShapeDtypeStruct((seqs, 2 * rows, width // 2), jnp.bfloat16),
        jax.ShapeDtypeStruct((seqs, 2, keys, 2 * rows), jnp.bfloat16),
    )
    query_spec = pl.BlockSpec((1, rows, width // 2), lambda s, *_: (s, 0, 0))
    return pl.pallas_call(
        forward_kernel,
        out_shape=outs,
        grid_spec=pltpu.PrefetchScalarGridSpec(
            num_scalar_prefetch=1,
            grid=(seqs,),
            in_specs=[query_spec, query_spec]
            + [by_seq(kv.shape) for kv in kvs]
            + [by_seq(doc_mine.shape), by_seq(doc_recv.shape)],
            out_specs=[by_seq(o.shape) for o in outs],
        ),
        compiler_params=pltpu.CompilerParams(vmem_limit_bytes=48 << 20),
        name="attention_forward",
    )(scalars, mine, recv, *kvs, doc_mine, doc_recv)


def projection(scalars, pieces, attn, o_weight):
    seqs, chip_rows, width = attn.shape
    features = o_weight.shape[0]
    steps = 2
    block = features // steps
    out_rows = features // (CHIPS_Y * CHIPS_Z)
    slab = jax.ShapeDtypeStruct((CHIPS_Z, out_rows, width), jnp.bfloat16)
    slab_spec = pl.BlockSpec((CHIPS_Z // steps, out_rows, width), lambda i, *_: (i, 0, 0))
    whole = pl.BlockSpec(attn.shape, lambda i, *_: (0, 0, 0))
    return pl.pallas_call(
        projection_kernel,
        out_shape=(jax.ShapeDtypeStruct(attn.shape, jnp.bfloat16),) + (slab,) * CHIPS_Y,
        grid_spec=pltpu.PrefetchScalarGridSpec(
            num_scalar_prefetch=1,
            grid=(steps,),
            in_specs=[pl.BlockSpec(p.shape[:2] + (block,), lambda i, *_: (0, 0, i)) for p in pieces]
            + [whole, pl.BlockSpec((block, width), lambda i, scalars: (i, scalars[0]))],
            out_specs=[whole] + [slab_spec] * CHIPS_Y,
            scratch_shapes=[
                pltpu.VMEM((seqs * chip_rows, width), jnp.float32),
                pltpu.VMEM((seqs * chip_rows, width), jnp.bfloat16),
                pltpu.VMEM((block, width), jnp.float32),
            ],
        ),
        compiler_params=pltpu.CompilerParams(vmem_limit_bytes=56 << 20),
        name="projection_grads",
    )(scalars, *pieces, attn, o_weight)


def backward(mine, recv, kvs, weights, attn, d_attn):
    seqs, rows, width = mine.shape
    half = jax.ShapeDtypeStruct((seqs, rows, width // 2), jnp.bfloat16)
    outs = (half, half) + tuple(
        jax.ShapeDtypeStruct(kv.shape, jnp.float32 if d == 0 else jnp.bfloat16)
        for d, kv in enumerate(kvs)
    )
    query_spec = pl.BlockSpec((1, rows, width // 2), lambda s, *_: (s, 0, 0))
    return pl.pallas_call(
        backward_kernel,
        out_shape=outs,
        grid=(seqs,),
        in_specs=[query_spec, query_spec]
        + [by_seq(a.shape) for a in (*kvs, weights, attn, d_attn)],
        out_specs=[by_seq(o.shape) for o in outs],
        compiler_params=pltpu.CompilerParams(vmem_limit_bytes=48 << 20),
        name="attention_backward",
    )(mine, recv, *kvs, weights, attn, d_attn)


def local(query, key_states, value_state_rows, d_out, o_weight, doc_start):
    seq_count, shard_rows, query_width = query.shape
    ctx = lax.axis_index("ctx")
    tp = lax.axis_index("tp")
    core = ctx % CORES
    y = ctx // CORES % CHIPS_Y
    chip_pos = ctx // CORES * (CORES * shard_rows)
    scalars = jnp.stack([core, tp, y, chip_pos]).astype(jnp.int32)
    first = core == 0

    def halves(a):
        w = a.shape[-1] // 2
        return a[..., :w], a[..., w:]

    def head_share(core_zero):
        parts = [
            jnp.where(core_zero, *halves(a)) for a in (query, key_states, value_state_rows)
        ]
        return jnp.concatenate(parts, axis=-1)

    mine = head_share(first)
    recv = to_sibling(head_share(~first))
    doc_mine = doc_start[:, None, :]
    doc_recv = to_sibling(doc_mine)

    r0 = d_out
    r3 = tp_ahead(r0, 1)
    r1 = tp_ahead(r0, -1)
    r2a = tp_ahead(r3[:1], 1)
    r2b = tp_ahead(r1[1:], -1)
    pieces = [r0, r1, r2a, r2b, r3]
    pieces = pieces + [to_sibling(p) for p in pieces]

    kv_width = 2 * HEAD_SIZE
    kv0 = jnp.concatenate([mine[..., -kv_width:], recv[..., -kv_width:]], axis=1)
    kvs = [kv0] + [chips_ahead(kv0, d) for d in range(1, HALO_CHIPS + 1)]

    attn, weights = forward(scalars, mine, recv, kvs, doc_mine, doc_recv)
    d_attn, w0, *w_sent = projection(scalars, pieces, attn, o_weight)
    w_arrived = [y_ahead(w, k + 1) for k, w in enumerate(w_sent)]
    dq_mine, dq_other, g0, *g_sent = backward(mine, recv, kvs, weights, attn, d_attn)
    g_arrived = [chips_ahead(g, -d - 1) for d, g in enumerate(g_sent)]
    dq_recv = to_sibling(dq_other)

    w_sum = w0.astype(jnp.float32)
    for w in w_arrived:
        w_sum = w_sum + w.astype(jnp.float32)
    w_all = z_exchange(w_sum.astype(jnp.bfloat16))
    w_rows = jnp.sum(w_all.astype(jnp.float32), axis=0)
    half_rows = w_rows.shape[0] // 2
    w_top, w_bottom = w_rows[:half_rows], w_rows[half_rows:]
    w_mine = jnp.where(first, w_top, w_bottom)
    w_recv = to_sibling(jnp.where(first, w_bottom, w_top))

    grads = g0
    for g in g_arrived:
        grads = grads + g.astype(jnp.float32)
    grads = grads.astype(jnp.bfloat16)
    g_mine = grads[:, :shard_rows]
    g_recv = to_sibling(grads[:, shard_rows:])

    def by_core(own, other):
        return jnp.concatenate(
            [jnp.where(first, own, other), jnp.where(first, other, own)], axis=-1
        )

    return (
        by_core(dq_mine, dq_recv),
        by_core(g_mine[..., :HEAD_SIZE], g_recv[..., :HEAD_SIZE]),
        by_core(g_mine[..., HEAD_SIZE:], g_recv[..., HEAD_SIZE:]),
        by_core(w_mine, w_recv),
    )


def solution(mesh):
    return jax.shard_map(
        local,
        mesh=mesh,
        in_specs=(
            P(None, "ctx", "tp"),
            P(None, "ctx", "tp"),
            P(None, "ctx", "tp"),
            P(None, ("ctx", "tp"), None),
            P(None, "tp"),
            P(None, "ctx"),
        ),
        out_specs=(
            P(None, "ctx", "tp"),
            P(None, "ctx", "tp"),
            P(None, "ctx", "tp"),
            P("ctx", "tp"),
        ),
        check_vma=False,
    )
```

time: 362 us -> 141 us (0.39)
  waiting for transfers between devices: 195 us -> 50.4 us
  local copies, waits for them, and re-layouts: 36.3 us -> 3.21 us
  matrix products: 24.9 us -> 0 us
  starting transfers between devices: 79.3 us -> 56.3 us
  Pallas kernels: 0 us -> 20.9 us
  between operations: 15.5 us -> 0.83 us
    unnamed x3 -> x0, waiting for transfers between devices: 138 us -> none
    unnamed x66 -> x18, local copies, waits for them, and re-layouts: 32.6 us -> 3.15 us
    ppermute x32 -> x25, starting transfers between devices: 79.3 us -> 52.8 us  [the longest x21 46 us: ctx_shift(): return lax.ppermute(block, 'ctx', [(i, move(i)) for i in range(count)])]
    ppermute x32 -> x25, waiting for transfers between devices: 57.5 us -> 33.3 us  [the longest x21 23.4 us: ctx_shift(): return lax.ppermute(block, 'ctx', [(i, move(i)) for i in range(count)])]
    dot_general x8 -> x0, matrix products: 21.1 us -> none  [the longest x2 7.21 us: local(): jnp.dot(columns.T, attn[seq_id], preferred_element_type=jnp.float32)]
    pallas_call x0 -> x3, Pallas kernels: none -> 20.9 us  [the longest x1 11.6 us: projection(): pl.pallas_call(projection_kernel, out_shape=(jax.ShapeDtypeStruct(attn.sh...]
    all_to_all x0 -> x1, waiting for transfers between devices: none -> 17.1 us  [z_exchange(): lax.all_to_all(blocks, 'ctx', 0, 0, axis_index_groups=groups, tiled=True)]
    convert_element_type x3 -> x2, other arithmetic: 7.13 us -> 2.37 us  [the longest x1 1.19 us: local(): w_all = z_exchange(w_sum.astype(jnp.bfloat16))]
  transfers between devices with their start and end apart: 34 -> 26, of which waited for: 9 -> 14; matrix products, arithmetic and copies ran while one was open for 14% -> 5% of each run, Pallas kernels for 0% -> 7%
where the time goes in v1:
time: 141 us; the launch traced here: 139 us
  starting transfers between devices  56.3 us (40%)
  waiting for transfers between devices  50.4 us (36%)
  Pallas kernels  20.9 us (15%)
  other arithmetic  7.39 us (5%)
  local copies, waits for them, and re-layouts  3.21 us (2%)
    ppermute x21, starting transfers between devices, ctx_shift(): return lax.ppermute(block, 'ctx', [(i, move(i)) for i in range(count)])  46 us
    ppermute x21, waiting for transfers between devices, ctx_shift(): return lax.ppermute(block, 'ctx', [(i, move(i)) for i in range(count)])  23.4 us
    all_to_all x1, waiting for transfers between devices, z_exchange(): lax.all_to_all(blocks, 'ctx', 0, 0, axis_index_groups=groups, tiled=True)  17.1 us
    pallas_call x1, Pallas kernels, projection(): pl.pallas_call(projection_kernel, out_shape=(jax.ShapeDtypeStruct(attn.sh...  11.6 us
    ppermute x4, waiting for transfers between devices, tp_ahead(): lax.ppermute(block, 'tp', [(i, (i + distance) % TP) for i in range(TP)])  9.97 us
    ppermute x4, starting transfers between devices, tp_ahead(): lax.ppermute(block, 'tp', [(i, (i + distance) % TP) for i in range(TP)])  6.82 us
    pallas_call x1, Pallas kernels, backward(): pl.pallas_call(backward_kernel, out_shape=outs, grid=(seqs,), in_specs=[q...  5.17 us
    pallas_call x1, Pallas kernels, forward(): pl.pallas_call(forward_kernel, out_shape=outs, grid_spec=pltpu.PrefetchSc...  4.2 us
  transfers between devices with their start and end apart: 26, of which 14 were waited for; matrix products, arithmetic and copies ran while one was open for 5% of the time, Pallas kernels for 7%

profile of v1, /device:TPU:1, one launch (start us, length us, event | category | flops | bytes accessed | tf_op | source)
XLA Modules:
  0.0 139.2 jit_solution(686643319246586936)
XLA Ops:
  0.6 3.4 %collective-permute-start.6 = (bf16[2,32,5376]{2,1,0:T(8,128)(2,1)}, bf16[2,32,5376]{2,1,0:T(8,128)(2,1)S(1)}, u32[]{:S(2)}, u32[]{:S(2)}) collective-permute-start(bf16[2,32,5376]{2,1,0:T(8,128)(2,1)} %r0.1), channel_id=1, source_target_pairs={{0,3},{1,0},{2,1},{3,2},{4,7},{5,4},{6,5},{7,6},{8,11},{9,8},{10,9... | collective-permute-start | bytes 2064392 | tf_op jit(solution)/shard_map/ppermute | solution.py:57
  4.0 1.0 broadcast_select_fusion
  5.0 1.0 broadcast_select_fusion.4
  6.0 2.0 %collective-permute-start = (bf16[2,128,512]{2,1,0:T(8,128)(2,1)S(1)}, bf16[2,128,512]{2,1,0:T(8,128)(2,1)S(1)}, u32[]{:S(2)}, u32[]{:S(2)}) collective-permute-start(bf16[2,128,512]{2,1,0:T(8,128)(2,1)S(1)} %pad_maximum_fusion.1), channel_id=1, source_target_pairs={{0,4},{4,0},{8,12},{12,8},{16,20},{20,16},{24,28},{28,24},{32,36},... | collective-permute-start | bytes 786440 | tf_op jit(solution)/shard_map/ppermute | solution.py:30
  8.1 1.2 collective-permute-done.recv
  9.6 2.6 %collective-permute-start.2 = (bf16[2,256,256]{2,1,0:T(8,128)(2,1)S(1)}, bf16[2,256,256]{2,1,0:T(8,128)(2,1)S(1)}, u32[]{:S(2)}, u32[]{:S(2)}) collective-permute-start(bf16[2,256,256]{2,1,0:T(8,128)(2,1)S(1)} %pad_maximum_fusion.2.kv0), channel_id=1, source_target_pairs={{0,16},{4,20},{8,24},{12,28},{16,32},{20,36},{24,40},{28,44},{32,4... | collective-permute-start | bytes 786440 | tf_op jit(solution)/shard_map/ppermute | solution.py:30
  12.3 2.4 %collective-permute-start.3 = (bf16[2,256,256]{2,1,0:T(8,128)(2,1)S(1)}, bf16[2,256,256]{2,1,0:T(8,128)(2,1)S(1)}, u32[]{:S(2)}, u32[]{:S(2)}) collective-permute-start(bf16[2,256,256]{2,1,0:T(8,128)(2,1)S(1)} %pad_maximum_fusion.2.kv0), channel_id=1, source_target_pairs={{0,24},{4,28},{8,32},{12,36},{16,40},{20,44},{24,48},{28,52},{32,5... | collective-permute-start | bytes 786440 | tf_op jit(solution)/shard_map/ppermute | solution.py:30
  14.7 3.8 %collective-permute-done.6.r1 = bf16[2,32,5376]{2,1,0:T(8,128)(2,1)S(1)} collective-permute-done((bf16[2,32,5376]{2,1,0:T(8,128)(2,1)}, bf16[2,32,5376]{2,1,0:T(8,128)(2,1)S(1)}, u32[]{:S(2)}, u32[]{:S(2)}) %collective-permute-start.6) | collective-permute-done | bytes 688160 | tf_op jit(solution)/shard_map/ppermute | solution.py:57
  18.4 1.6 %collective-permute-start.4 = (bf16[2,256,256]{2,1,0:T(8,128)(2,1)S(1)}, bf16[2,256,256]{2,1,0:T(8,128)(2,1)S(1)}, u32[]{:S(2)}, u32[]{:S(2)}) collective-permute-start(bf16[2,256,256]{2,1,0:T(8,128)(2,1)S(1)} %pad_maximum_fusion.2.kv0), channel_id=1, source_target_pairs={{0,32},{4,36},{8,40},{12,44},{16,48},{20,52},{24,56},{28,60},{32,6... | collective-permute-start | bytes 786440 | tf_op jit(solution)/shard_map/ppermute | solution.py:30
  20.1 1.3 collective-permute-done.7.r3
  21.4 1.9 %collective-permute-start.5 = (s32[2,1,128]{2,1,0:T(1,128)S(1)}, s32[2,1,128]{2,1,0:T(1,128)S(1)}, u32[]{:S(2)}, u32[]{:S(2)}) collective-permute-start(s32[2,1,128]{2,1,0:T(1,128)S(1)} %bitcast.5), channel_id=1, source_target_pairs={{0,4},{4,0},{8,12},{12,8},{16,20},{20,16},{24,28},{28,24},{32,36},... | collective-permute-start | bytes 3080 | tf_op jit(solution)/shard_map/ppermute | solution.py:30
  23.4 0.8 collective-permute-done.5.doc_recv
  24.4 1.7 %collective-permute-done.1.kv1 = bf16[2,256,256]{2,1,0:T(8,128)(2,1)S(1)} collective-permute-done((bf16[2,256,256]{2,1,0:T(8,128)(2,1)S(1)}, bf16[2,256,256]{2,1,0:T(8,128)(2,1)S(1)}, u32[]{:S(2)}, u32[]{:S(2)}) %collective-permute-start.1) | collective-permute-done | bytes 262176 | tf_op jit(solution)/shard_map/ppermute | solution.py:30
  26.1 0.5 collective-permute-start.8
  26.6 1.2 collective-permute-done.2.kv2
  27.8 1.5 %collective-permute-start.11 = (bf16[2,32,5376]{2,1,0:T(8,128)(2,1)S(1)}, bf16[2,32,5376]{2,1,0:T(8,128)(2,1)}, u32[]{:S(2)}, u32[]{:S(2)}) collective-permute-start(bf16[2,32,5376]{2,1,0:T(8,128)(2,1)S(1)} %collective-permute-done.6.r1), channel_id=1, source_target_pairs={{0,4},{4,0},{8,12},{12,8},{16,20},{20,16},{24,28},{28,24},{32,36},... | collective-permute-start | bytes 2064392 | tf_op jit(solution)/shard_map/ppermute | solution.py:30
  29.3 3.0 %collective-permute-start.9 = (bf16[1,32,5376]{2,1,0:T(8,128)(2,1)S(1)}, bf16[1,32,5376]{2,1,0:T(8,128)(2,1)}, u32[]{:S(2)}, u32[]{:S(2)}) collective-permute-start(bf16[1,32,5376]{2,1,0:T(8,128)(2,1)S(1)} %slice.77), channel_id=1, source_target_pairs={{0,3},{1,0},{2,1},{3,2},{4,7},{5,4},{6,5},{7,6},{8,11},{9,8},{10,9... | collective-permute-start | bytes 1032200 | tf_op jit(solution)/shard_map/ppermute | solution.py:57
  32.5 3.4 %collective-permute-done.8.r2a = bf16[1,32,5376]{2,1,0:T(8,128)(2,1)} collective-permute-done((bf16[1,32,5376]{2,1,0:T(8,128)(2,1)S(1)}, bf16[1,32,5376]{2,1,0:T(8,128)(2,1)}, u32[]{:S(2)}, u32[]{:S(2)}) %collective-permute-start.8) | collective-permute-done | bytes 344096 | tf_op jit(solution)/shard_map/ppermute | solution.py:57
  35.9 2.3 %collective-permute-start.12 = (bf16[1,32,5376]{2,1,0:T(8,128)(2,1)}, bf16[1,32,5376]{2,1,0:T(8,128)(2,1)}, u32[]{:S(2)}, u32[]{:S(2)}) collective-permute-start(bf16[1,32,5376]{2,1,0:T(8,128)(2,1)} %collective-permute-done.8.r2a), channel_id=1, source_target_pairs={{0,4},{4,0},{8,12},{12,8},{16,20},{20,16},{24,28},{28,24},{32,36},... | collective-permute-start | bytes 1032200 | tf_op jit(solution)/shard_map/ppermute | solution.py:30
  38.2 1.5 %collective-permute-done.9.r2b = bf16[1,32,5376]{2,1,0:T(8,128)(2,1)} collective-permute-done((bf16[1,32,5376]{2,1,0:T(8,128)(2,1)S(1)}, bf16[1,32,5376]{2,1,0:T(8,128)(2,1)}, u32[]{:S(2)}, u32[]{:S(2)}) %collective-permute-start.9) | collective-permute-done | bytes 344096 | tf_op jit(solution)/shard_map/ppermute | solution.py:57
  39.7 0.8 collective-permute-start.13
  40.6 4.2 %attention_forward.1 = (bf16[2,256,256]{2,1,0:T(8,128)(2,1)S(1)}, bf16[2,2,1280,256]{3,2,1,0:T(8,128)(2,1)S(1)}) custom-call(s32[4]{0:T(128)S(1)} %pad_add_fusion.scalars, bf16[2,128,512]{2,1,0:T(8,128)(2,1)S(1)} %pad_maximum_fusion.mine, bf16[2,128,512]{2,1,0:T(8,128)(2,1)S(1)} %collective-permute-done.recv, ...), custom_call_target="tpu_custom_call" | custom-call | tf_op jit(solution)/shard_map/attention_forward/pallas_call | solution.py:203
  44.8 1.5 %copy-done = bf16[2,2,1280,256]{3,2,1,0:T(8,128)(2,1)} copy-done((bf16[2,2,1280,256]{3,2,1,0:T(8,128)(2,1)}, bf16[2,2,1280,256]{3,2,1,0:T(8,128)(2,1)S(1)}, u32[]{:S(2)}) %copy-start) | copy-done | bytes 2621464
  46.3 0.7 copy-done.1
  47.1 11.6 %projection_grads.1 = (bf16[2,256,256]{2,1,0:T(8,128)(2,1)}, bf16[8,168,256]{2,1,0:T(8,128)(2,1)}, bf16[8,168,256]{2,1,0:T(8,128)(2,1)}, bf16[8,168,256]{2,1,0:T(8,128)(2,1)}, bf16[8,168,256]{2,1,0:T(8,128)(2,1)}) custom-call(s32[4]{0:T(128)} %copy-done.4, bf16[2,32,5376]{2,1,0:T(8,128)(2,1)} %r0.1, bf16[2,32,5376]{2,1,0:T(8,128)(2,1)} %copy-done.6, ...), custom_call_target="tpu_custom_call" | custom-call | tf_op jit(solution)/shard_map/projection_grads/pallas_call | solution.py:228
  58.6 5.7 %collective-permute-start.23 = (bf16[8,168,256]{2,1,0:T(8,128)(2,1)}, bf16[8,168,256]{2,1,0:T(8,128)(2,1)S(1)}, u32[]{:S(2)}, u32[]{:S(2)}) collective-permute-start(bf16[8,168,256]{2,1,0:T(8,128)(2,1)} %get-tuple-element.31), channel_id=1, source_target_pairs={{0,24},{4,28},{8,0},{12,4},{16,8},{20,12},{24,16},{28,20},{32,56},... | collective-permute-start | bytes 2064392 | tf_op jit(solution)/shard_map/ppermute | solution.py:30
  64.3 5.2 %collective-permute-start.22 = (bf16[8,168,256]{2,1,0:T(8,128)(2,1)}, bf16[8,168,256]{2,1,0:T(8,128)(2,1)S(1)}, u32[]{:S(2)}, u32[]{:S(2)}) collective-permute-start(bf16[8,168,256]{2,1,0:T(8,128)(2,1)} %get-tuple-element.30), channel_id=1, source_target_pairs={{0,16},{4,20},{8,24},{12,28},{16,0},{20,4},{24,8},{28,12},{32,48},... | collective-permute-start | bytes 2064392 | tf_op jit(solution)/shard_map/ppermute | solution.py:30
  69.5 0.8 collective-permute-start.21
  70.3 0.9 copy-done.3
  71.2 5.2 %attention_backward.1 = (bf16[2,128,256]{2,1,0:T(8,128)(2,1)S(1)}, bf16[2,128,256]{2,1,0:T(8,128)(2,1)S(1)}, f32[2,256,256]{2,1,0:T(8,128)S(1)}, bf16[2,256,256]...) custom-call(bf16[2,128,512]{2,1,0:T(8,128)(2,1)S(1)} %pad_maximum_fu, ...), custom_call_target="tpu_custom_call" | custom-call | tf_op jit(solution)/shard_map/attention_backward/pallas_call | solution.py:256
  76.4 1.1 collective-permute-start.19
  77.5 0.4 collective-permute-start.18
  78.0 4.0 %collective-permute-done.23 = bf16[8,168,256]{2,1,0:T(8,128)(2,1)S(1)} collective-permute-done((bf16[8,168,256]{2,1,0:T(8,128)(2,1)}, bf16[8,168,256]{2,1,0:T(8,128)(2,1)S(1)}, u32[]{:S(2)}, u32[]{:S(2)}) %collective-permute-start.23) | collective-permute-done | bytes 688160 | tf_op jit(solution)/shard_map/ppermute | solution.py:30
  82.0 5.5 %collective-permute-start.17 = (bf16[2,256,256]{2,1,0:T(8,128)(2,1)S(1)}, bf16[2,256,256]{2,1,0:T(8,128)(2,1)}, u32[]{:S(2)}, u32[]{:S(2)}) collective-permute-start(bf16[2,256,256]{2,1,0:T(8,128)(2,1)S(1)} %get-tuple-element.25), channel_id=1, source_target_pairs={{0,240},{4,244},{8,248},{12,252},{16,0},{20,4},{24,8},{28,12},{32,... | collective-permute-start | bytes 786440 | tf_op jit(solution)/shard_map/ppermute | solution.py:30
  87.5 3.7 %collective-permute-done.22 = bf16[8,168,256]{2,1,0:T(8,128)(2,1)S(1)} collective-permute-done((bf16[8,168,256]{2,1,0:T(8,128)(2,1)}, bf16[8,168,256]{2,1,0:T(8,128)(2,1)S(1)}, u32[]{:S(2)}, u32[]{:S(2)}) %collective-permute-start.22) | collective-permute-done | bytes 688160 | tf_op jit(solution)/shard_map/ppermute | solution.py:30
  91.2 9.5 %collective-permute-start.16 = (bf16[2,256,256]{2,1,0:T(8,128)(2,1)S(1)}, bf16[2,256,256]{2,1,0:T(8,128)(2,1)}, u32[]{:S(2)}, u32[]{:S(2)}) collective-permute-start(bf16[2,256,256]{2,1,0:T(8,128)(2,1)S(1)} %get-tuple-element.24), channel_id=1, source_target_pairs={{0,248},{4,252},{8,0},{12,4},{16,8},{20,12},{24,16},{28,20},{32,24... | collective-permute-start | bytes 786440 | tf_op jit(solution)/shard_map/ppermute | solution.py:30
  100.7 10.0 %collective-permute-done.21 = bf16[8,168,256]{2,1,0:T(8,128)(2,1)S(1)} collective-permute-done((bf16[8,168,256]{2,1,0:T(8,128)(2,1)}, bf16[8,168,256]{2,1,0:T(8,128)(2,1)S(1)}, u32[]{:S(2)}, u32[]{:S(2)}) %collective-permute-start.21) | collective-permute-done | bytes 688160 | tf_op jit(solution)/shard_map/ppermute | solution.py:30
  110.7 1.2 add_convert_fusion
  111.9 3.5 %all-to-all-start = ((bf16[8,168,256]{2,1,0:T(8,128)(2,1)}), bf16[8,168,256]{2,1,0:T(8,128)(2,1)S(1)}, u32[]{:S(2)}, u32[]{:S(2)}) async-start(bf16[8,168,256]{2,1,0:T(8,128)(2,1)} %add_convert_fusion), calls=%async_computation | async-start | bytes 1376256 | tf_op jit(solution)/shard_map/all_to_all | solution.py:53
  115.4 0.9 collective-permute-start.15
  116.4 1.2 add_convert_fusion.1
  117.7 0.7 pad_maximum_fusion.3
  118.5 0.6 collective-permute-done.20
  119.1 0.7 pad_maximum_fusion.5
  119.7 17.1 %all-to-all-done = bf16[8,168,256]{2,1,0:T(8,128)(2,1)S(1)} async-done(((bf16[8,168,256]{2,1,0:T(8,128)(2,1)}), bf16[8,168,256]{2,1,0:T(8,128)(2,1)S(1)}, u32[]{:S(2)}, u32[]{:S(2)}) %all-to-all-start) | async-done | bytes 688160 | tf_op jit(solution)/shard_map/all_to_all | solution.py:53
  136.9 0.6 collective-permute-start.24
  137.5 0.7 pad_maximum_fusion.6
  138.5 0.7 pad_maximum_fusion.4
  (46 shorter events, 1.8 us)
Async XLA Ops:
  0.6 20.8 %copy-start.5 = (s32[2,128]{1,0:T(2,128)S(1)}, s32[2,128]{1,0:T(2,128)}, u32[]{:S(2)}) copy-start(s32[2,128]{1,0:T(2,128)} %param.11) | copy-start | bytes 3076
  0.6 17.8 %collective-permute-start.6 = (bf16[2,32,5376]{2,1,0:T(8,128)(2,1)}, bf16[2,32,5376]{2,1,0:T(8,128)(2,1)S(1)}, u32[]{:S(2)}, u32[]{:S(2)}) collective-permute-start(bf16[2,32,5376]{2,1,0:T(8,128)(2,1)} %r0.1), channel_id=1, source_target_pairs={{0,3},{1,0},{2,1},{3,2},{4,7},{5,4},{6,5},{7,6},{8,11},{9,8},{10,9... | collective-permute-start | bytes 2064392 | tf_op jit(solution)/shard_map/ppermute | solution.py:57
  4.0 17.4 %collective-permute-start.7 = (bf16[2,32,5376]{2,1,0:T(8,128)(2,1)}, bf16[2,32,5376]{2,1,0:T(8,128)(2,1)S(1)}, u32[]{:S(2)}, u32[]{:S(2)}) collective-permute-start(bf16[2,32,5376]{2,1,0:T(8,128)(2,1)} %r0.1), channel_id=1, source_target_pairs={{0,1},{1,2},{2,3},{3,0},{4,5},{5,6},{6,7},{7,4},{8,9},{9,10},{10,1... | collective-permute-start | bytes 2064392 | tf_op jit(solution)/shard_map/ppermute | solution.py:57
  6.0 3.2 %collective-permute-start = (bf16[2,128,512]{2,1,0:T(8,128)(2,1)S(1)}, bf16[2,128,512]{2,1,0:T(8,128)(2,1)S(1)}, u32[]{:S(2)}, u32[]{:S(2)}) collective-permute-start(bf16[2,128,512]{2,1,0:T(8,128)(2,1)S(1)} %pad_maximum_fusion.1), channel_id=1, source_target_pairs={{0,4},{4,0},{8,12},{12,8},{16,20},{20,16},{24,28},{28,24},{32,36},... | collective-permute-start | bytes 786440 | tf_op jit(solution)/shard_map/ppermute | solution.py:30
  9.3 16.9 %collective-permute-start.1 = (bf16[2,256,256]{2,1,0:T(8,128)(2,1)S(1)}, bf16[2,256,256]{2,1,0:T(8,128)(2,1)S(1)}, u32[]{:S(2)}, u32[]{:S(2)}) collective-permute-start(bf16[2,256,256]{2,1,0:T(8,128)(2,1)S(1)} %pad_maximum_fusion.2.kv0), channel_id=1, source_target_pairs={{0,8},{4,12},{8,16},{12,20},{16,24},{20,28},{24,32},{28,36},{32,40... | collective-permute-start | bytes 786440 | tf_op jit(solution)/shard_map/ppermute | solution.py:30
  9.6 18.1 %collective-permute-start.2 = (bf16[2,256,256]{2,1,0:T(8,128)(2,1)S(1)}, bf16[2,256,256]{2,1,0:T(8,128)(2,1)S(1)}, u32[]{:S(2)}, u32[]{:S(2)}) collective-permute-start(bf16[2,256,256]{2,1,0:T(8,128)(2,1)S(1)} %pad_maximum_fusion.2.kv0), channel_id=1, source_target_pairs={{0,16},{4,20},{8,24},{12,28},{16,32},{20,36},{24,40},{28,44},{32,4... | collective-permute-start | bytes 786440 | tf_op jit(solution)/shard_map/ppermute | solution.py:30
  12.3 17.0 %collective-permute-start.3 = (bf16[2,256,256]{2,1,0:T(8,128)(2,1)S(1)}, bf16[2,256,256]{2,1,0:T(8,128)(2,1)S(1)}, u32[]{:S(2)}, u32[]{:S(2)}) collective-permute-start(bf16[2,256,256]{2,1,0:T(8,128)(2,1)S(1)} %pad_maximum_fusion.2.kv0), channel_id=1, source_target_pairs={{0,24},{4,28},{8,32},{12,36},{16,40},{20,44},{24,48},{28,52},{32,5... | collective-permute-start | bytes 786440 | tf_op jit(solution)/shard_map/ppermute | solution.py:30
  18.4 26.4 %copy-start.6 = (bf16[2,32,5376]{2,1,0:T(8,128)(2,1)}, bf16[2,32,5376]{2,1,0:T(8,128)(2,1)S(1)}, u32[]{:S(2)}) copy-start(bf16[2,32,5376]{2,1,0:T(8,128)(2,1)S(1)} %collective-permute-done.6.r1) | copy-start | bytes 2064388
  18.4 13.8 %collective-permute-start.4 = (bf16[2,256,256]{2,1,0:T(8,128)(2,1)S(1)}, bf16[2,256,256]{2,1,0:T(8,128)(2,1)S(1)}, u32[]{:S(2)}, u32[]{:S(2)}) collective-permute-start(bf16[2,256,256]{2,1,0:T(8,128)(2,1)S(1)} %pad_maximum_fusion.2.kv0), channel_id=1, source_target_pairs={{0,32},{4,36},{8,40},{12,44},{16,48},{20,52},{24,56},{28,60},{32,6... | collective-permute-start | bytes 786440 | tf_op jit(solution)/shard_map/ppermute | solution.py:30
  21.4 23.4 %copy-start.7 = (bf16[2,32,5376]{2,1,0:T(8,128)(2,1)}, bf16[2,32,5376]{2,1,0:T(8,128)(2,1)S(1)}, u32[]{:S(2)}) copy-start(bf16[2,32,5376]{2,1,0:T(8,128)(2,1)S(1)} %collective-permute-done.7.r3) | copy-start | bytes 2064388
  21.4 2.7 %collective-permute-start.5 = (s32[2,1,128]{2,1,0:T(1,128)S(1)}, s32[2,1,128]{2,1,0:T(1,128)S(1)}, u32[]{:S(2)}, u32[]{:S(2)}) collective-permute-start(s32[2,1,128]{2,1,0:T(1,128)S(1)} %bitcast.5), channel_id=1, source_target_pairs={{0,4},{4,0},{8,12},{12,8},{16,20},{20,16},{24,28},{28,24},{32,36},... | collective-permute-start | bytes 3080 | tf_op jit(solution)/shard_map/ppermute | solution.py:30
  24.1 22.9 %collective-permute-start.10 = (bf16[2,32,5376]{2,1,0:T(8,128)(2,1)}, bf16[2,32,5376]{2,1,0:T(8,128)(2,1)}, u32[]{:S(2)}, u32[]{:S(2)}) collective-permute-start(bf16[2,32,5376]{2,1,0:T(8,128)(2,1)} %r0.1), channel_id=1, source_target_pairs={{0,4},{4,0},{8,12},{12,8},{16,20},{20,16},{24,28},{28,24},{32,36},... | collective-permute-start | bytes 2064392 | tf_op jit(solution)/shard_map/ppermute | solution.py:30
  26.1 9.7 %collective-permute-start.8 = (bf16[1,32,5376]{2,1,0:T(8,128)(2,1)S(1)}, bf16[1,32,5376]{2,1,0:T(8,128)(2,1)}, u32[]{:S(2)}, u32[]{:S(2)}) collective-permute-start(bf16[1,32,5376]{2,1,0:T(8,128)(2,1)S(1)} %slice.76), channel_id=1, source_target_pairs={{0,1},{1,2},{2,3},{3,0},{4,5},{5,6},{6,7},{7,4},{8,9},{9,10},{10,1... | collective-permute-start | bytes 1032200 | tf_op jit(solution)/shard_map/ppermute | solution.py:57
  27.8 19.3 %collective-permute-start.11 = (bf16[2,32,5376]{2,1,0:T(8,128)(2,1)S(1)}, bf16[2,32,5376]{2,1,0:T(8,128)(2,1)}, u32[]{:S(2)}, u32[]{:S(2)}) collective-permute-start(bf16[2,32,5376]{2,1,0:T(8,128)(2,1)S(1)} %collective-permute-done.6.r1), channel_id=1, source_target_pairs={{0,4},{4,0},{8,12},{12,8},{16,20},{20,16},{24,28},{28,24},{32,36},... | collective-permute-start | bytes 2064392 | tf_op jit(solution)/shard_map/ppermute | solution.py:30
  29.3 10.4 %collective-permute-start.9 = (bf16[1,32,5376]{2,1,0:T(8,128)(2,1)S(1)}, bf16[1,32,5376]{2,1,0:T(8,128)(2,1)}, u32[]{:S(2)}, u32[]{:S(2)}) collective-permute-start(bf16[1,32,5376]{2,1,0:T(8,128)(2,1)S(1)} %slice.77), channel_id=1, source_target_pairs={{0,3},{1,0},{2,1},{3,2},{4,7},{5,4},{6,5},{7,6},{8,11},{9,8},{10,9... | collective-permute-start | bytes 1032200 | tf_op jit(solution)/shard_map/ppermute | solution.py:57
  32.2 14.8 %collective-permute-start.14 = (bf16[2,32,5376]{2,1,0:T(8,128)(2,1)S(1)}, bf16[2,32,5376]{2,1,0:T(8,128)(2,1)}, u32[]{:S(2)}, u32[]{:S(2)}) collective-permute-start(bf16[2,32,5376]{2,1,0:T(8,128)(2,1)S(1)} %collective-permute-done.7.r3), channel_id=1, source_target_pairs={{0,4},{4,0},{8,12},{12,8},{16,20},{20,16},{24,28},{28,24},{32,36},... | collective-permute-start | bytes 2064392 | tf_op jit(solution)/shard_map/ppermute | solution.py:30
  35.9 11.1 %collective-permute-start.12 = (bf16[1,32,5376]{2,1,0:T(8,128)(2,1)}, bf16[1,32,5376]{2,1,0:T(8,128)(2,1)}, u32[]{:S(2)}, u32[]{:S(2)}) collective-permute-start(bf16[1,32,5376]{2,1,0:T(8,128)(2,1)} %collective-permute-done.8.r2a), channel_id=1, source_target_pairs={{0,4},{4,0},{8,12},{12,8},{16,20},{20,16},{24,28},{28,24},{32,36},... | collective-permute-start | bytes 1032200 | tf_op jit(solution)/shard_map/ppermute | solution.py:30
  39.7 7.3 %collective-permute-start.13 = (bf16[1,32,5376]{2,1,0:T(8,128)(2,1)}, bf16[1,32,5376]{2,1,0:T(8,128)(2,1)}, u32[]{:S(2)}, u32[]{:S(2)}) collective-permute-start(bf16[1,32,5376]{2,1,0:T(8,128)(2,1)} %collective-permute-done.9.r2b), channel_id=1, source_target_pairs={{0,4},{4,0},{8,12},{12,8},{16,20},{20,16},{24,28},{28,24},{32,36},... | collective-permute-start | bytes 1032200 | tf_op jit(solution)/shard_map/ppermute | solution.py:30
  40.6 6.5 %copy-start.4 = (s32[4]{0:T(128)}, s32[4]{0:T(128)S(1)}, u32[]{:S(2)}) copy-start(s32[4]{0:T(128)S(1)} %pad_add_fusion.scalars) | copy-start | bytes 52
  44.8 1.5 %copy-start = (bf16[2,2,1280,256]{3,2,1,0:T(8,128)(2,1)}, bf16[2,2,1280,256]{3,2,1,0:T(8,128)(2,1)S(1)}, u32[]{:S(2)}) copy-start(bf16[2,2,1280,256]{3,2,1,0:T(8,128)(2,1)S(1)} %get-tuple-element.18.weights) | copy-start | bytes 7864324
  46.3 0.7 copy-start.1
  47.0 23.2 %copy-start.2 = (bf16[2,256,256]{2,1,0:T(8,128)(2,1)S(1)}, bf16[2,256,256]{2,1,0:T(8,128)(2,1)}, u32[]{:S(2)}) copy-start(bf16[2,256,256]{2,1,0:T(8,128)(2,1)} %copy-done.1) | copy-start | bytes 786436
  58.6 23.3 %collective-permute-start.23 = (bf16[8,168,256]{2,1,0:T(8,128)(2,1)}, bf16[8,168,256]{2,1,0:T(8,128)(2,1)S(1)}, u32[]{:S(2)}, u32[]{:S(2)}) collective-permute-start(bf16[8,168,256]{2,1,0:T(8,128)(2,1)} %get-tuple-element.31), channel_id=1, source_target_pairs={{0,24},{4,28},{8,0},{12,4},{16,8},{20,12},{24,16},{28,20},{32,56},... | collective-permute-start | bytes 2064392 | tf_op jit(solution)/shard_map/ppermute | solution.py:30
  64.3 26.9 %collective-permute-start.22 = (bf16[8,168,256]{2,1,0:T(8,128)(2,1)}, bf16[8,168,256]{2,1,0:T(8,128)(2,1)S(1)}, u32[]{:S(2)}, u32[]{:S(2)}) collective-permute-start(bf16[8,168,256]{2,1,0:T(8,128)(2,1)} %get-tuple-element.30), channel_id=1, source_target_pairs={{0,16},{4,20},{8,24},{12,28},{16,0},{20,4},{24,8},{28,12},{32,48},... | collective-permute-start | bytes 2064392 | tf_op jit(solution)/shard_map/ppermute | solution.py:30
  69.5 41.2 %collective-permute-start.21 = (bf16[8,168,256]{2,1,0:T(8,128)(2,1)}, bf16[8,168,256]{2,1,0:T(8,128)(2,1)S(1)}, u32[]{:S(2)}, u32[]{:S(2)}) collective-permute-start(bf16[8,168,256]{2,1,0:T(8,128)(2,1)} %get-tuple-element.29), channel_id=1, source_target_pairs={{0,8},{4,12},{8,16},{12,20},{16,24},{20,28},{24,0},{28,4},{32,40},... | collective-permute-start | bytes 2064392 | tf_op jit(solution)/shard_map/ppermute | solution.py:30
  70.3 1.0 copy-start.3
  71.2 39.5 %copy-start.8 = (bf16[8,168,256]{2,1,0:T(8,128)(2,1)S(1)}, bf16[8,168,256]{2,1,0:T(8,128)(2,1)}, u32[]{:S(2)}) copy-start(bf16[8,168,256]{2,1,0:T(8,128)(2,1)} %get-tuple-element.28) | copy-start | bytes 2064388
  76.4 40.0 %collective-permute-start.19 = (bf16[2,256,256]{2,1,0:T(8,128)(2,1)S(1)}, bf16[2,256,256]{2,1,0:T(8,128)(2,1)S(1)}, u32[]{:S(2)}, u32[]{:S(2)}) collective-permute-start(bf16[2,256,256]{2,1,0:T(8,128)(2,1)S(1)} %get-tuple-element.27), channel_id=1, source_target_pairs={{0,224},{4,228},{8,232},{12,236},{16,240},{20,244},{24,248},{28,25... | collective-permute-start | bytes 786440 | tf_op jit(solution)/shard_map/ppermute | solution.py:30
  77.5 38.8 %collective-permute-start.18 = (bf16[2,256,256]{2,1,0:T(8,128)(2,1)S(1)}, bf16[2,256,256]{2,1,0:T(8,128)(2,1)S(1)}, u32[]{:S(2)}, u32[]{:S(2)}) collective-permute-start(bf16[2,256,256]{2,1,0:T(8,128)(2,1)S(1)} %get-tuple-element.26), channel_id=1, source_target_pairs={{0,232},{4,236},{8,240},{12,244},{16,248},{20,252},{24,0},{28,4},{... | collective-permute-start | bytes 786440 | tf_op jit(solution)/shard_map/ppermute | solution.py:30
  82.0 34.4 %collective-permute-start.17 = (bf16[2,256,256]{2,1,0:T(8,128)(2,1)S(1)}, bf16[2,256,256]{2,1,0:T(8,128)(2,1)}, u32[]{:S(2)}, u32[]{:S(2)}) collective-permute-start(bf16[2,256,256]{2,1,0:T(8,128)(2,1)S(1)} %get-tuple-element.25), channel_id=1, source_target_pairs={{0,240},{4,244},{8,248},{12,252},{16,0},{20,4},{24,8},{28,12},{32,... | collective-permute-start | bytes 786440 | tf_op jit(solution)/shard_map/ppermute | solution.py:30
  91.2 25.2 %collective-permute-start.16 = (bf16[2,256,256]{2,1,0:T(8,128)(2,1)S(1)}, bf16[2,256,256]{2,1,0:T(8,128)(2,1)}, u32[]{:S(2)}, u32[]{:S(2)}) collective-permute-start(bf16[2,256,256]{2,1,0:T(8,128)(2,1)S(1)} %get-tuple-element.24), channel_id=1, source_target_pairs={{0,248},{4,252},{8,0},{12,4},{16,8},{20,12},{24,16},{28,20},{32,24... | collective-permute-start | bytes 786440 | tf_op jit(solution)/shard_map/ppermute | solution.py:30
  111.9 24.9 %all-to-all-start = ((bf16[8,168,256]{2,1,0:T(8,128)(2,1)}), bf16[8,168,256]{2,1,0:T(8,128)(2,1)S(1)}, u32[]{:S(2)}, u32[]{:S(2)}) async-start(bf16[8,168,256]{2,1,0:T(8,128)(2,1)} %add_convert_fusion), calls=%async_computation | async-start | bytes 1376256 | tf_op jit(solution)/shard_map/all_to_all | solution.py:53
  115.4 2.3 %collective-permute-start.15 = (bf16[2,128,256]{2,1,0:T(8,128)(2,1)S(1)}, bf16[2,128,256]{2,1,0:T(8,128)(2,1)S(1)}, u32[]{:S(2)}, u32[]{:S(2)}) collective-permute-start(bf16[2,128,256]{2,1,0:T(8,128)(2,1)S(1)} %get-tuple-element.22), channel_id=1, source_target_pairs={{0,4},{4,0},{8,12},{12,8},{16,20},{20,16},{24,28},{28,24},{32,36},... | collective-permute-start | bytes 393224 | tf_op jit(solution)/shard_map/ppermute | solution.py:30
  117.6 1.4 %collective-permute-start.20 = (bf16[2,128,256]{2,1,0:T(8,128)(2,1)S(1)}, bf16[2,128,256]{2,1,0:T(8,128)(2,1)S(1)}, u32[]{:S(2)}, u32[]{:S(2)}) collective-permute-start(bf16[2,128,256]{2,1,0:T(8,128)(2,1)S(1)} %slice.79), channel_id=1, source_target_pairs={{0,4},{4,0},{8,12},{12,8},{16,20},{20,16},{24,28},{28,24},{32,36},... | collective-permute-start | bytes 393224 | tf_op jit(solution)/shard_map/ppermute | solution.py:30
  136.9 1.5 %collective-permute-start.24 = (f32[84,256]{1,0:T(8,128)S(1)}, f32[84,256]{1,0:T(8,128)S(1)}, u32[]{:S(2)}, u32[]{:S(2)}) collective-permute-start(f32[84,256]{1,0:T(8,128)S(1)} %slice_select_fusion), channel_id=1, source_target_pairs={{0,4},{4,0},{8,12},{12,8},{16,20},{20,16},{24,28},{28,24},{32,36},... | collective-permute-start | bytes 258056 | tf_op jit(solution)/shard_map/ppermute | solution.py:30

commit v2 on v1

--- a/solution.py
+++ b/solution.py
@@ -39,12 +39,29 @@
     return ctx_shift(block, lambda i: (i + CORES * distance) % count)
 
 
-def y_ahead(block, distance):
+def y_pair(y):
+    return y ^ 1
+
+
+def y_mirror(y):
+    return CHIPS_Y - 1 - y
+
+
+def y_route(block, target):
     def move(i):
         core, y, z = i % CORES, i // CORES % CHIPS_Y, i // (CORES * CHIPS_Y)
-        return (z * CHIPS_Y + (y + distance) % CHIPS_Y) * CORES + core
+        return (z * CHIPS_Y + target(y)) * CORES + core
 
     return ctx_shift(block, move)
+
+
+def y_exchange(blocks):
+    groups = [
+        [(z * CHIPS_Y + y) * CORES + core for y in range(CHIPS_Y)]
+        for z in range(CHIPS_Z)
+        for core in range(CORES)
+    ]
+    return lax.all_to_all(blocks, "ctx", 0, 0, axis_index_groups=groups, tiled=True)
 
 
 def z_exchange(blocks):
@@ -101,61 +118,99 @@
         attn[0, :, cols] = acc.T.astype(jnp.bfloat16)
 
 
-def projection_kernel(
-    scalars, r0, r1, r2a, r2b, r3, t0, t1, t2a, t2b, t3, attn, o_weight,
-    d_attn, w0, w1, w2, w3, acc, attn_rows, partial,
+def early_kernel(scalars, *refs):
+    *pieces, o_weight, d_attn, rows_t, acc = refs
+    step = pl.program_id(0)
+    parts = [ref[seq] for ref in pieces for seq in range(ref.shape[0])]
+    rows = jnp.concatenate(parts, axis=0)
+    product = dot(rows, o_weight[...])
+
+    @pl.when(step == 0)
+    def _():
+        acc[...] = product
+
+    @pl.when(step > 0)
+    def _():
+        acc[...] = acc[...] + product
+
+    rows_t[...] = rows.T
+
+    @pl.when(step == pl.num_programs(0) - 1)
+    def _():
+        d_attn[...] = acc[...].astype(jnp.bfloat16)
+
+
+def place(tp, piece, core_block, rel, seq):
+    here = TP * piece * core_block + piece * ((tp + rel) % TP)
+    return seq, pl.ds(pl.multiple_of(here, piece), piece)
+
+
+OWN_SLOTS = [(b, 0, q) for b in range(2) for q in range(2)]
+NEAR_SLOTS = [(b, s, q) for b in range(2) for s in (1, 3) for q in range(2)]
+FAR_SLOTS = [(b, 2, q) for b in range(2) for q in range(2)]
+
+
+def late_kernel(
+    scalars, r2a, r2b, t2a, t2b, own_t, near_t, attn, own, near, o_weight,
+    d_attn, sent_a, kept_a, sent_b, kept_b, acc, attn_own, attn_near, attn_far, partial,
 ):
     step = pl.program_id(0)
     tp, y = scalars[1], scalars[2]
-    piece = r0.shape[1]
-    out_rows = w0.shape[1]
-
-    def place(core_block, rel, seq):
-        here = 4 * piece * core_block + piece * ((tp + rel) % TP)
-        return seq, pl.ds(pl.multiple_of(here, piece), piece)
-
-    slots = [(b, s, q) for b in range(2) for s in range(TP) for q in range(2)]
+    piece = r2a.shape[1]
+    out_rows = sent_a.shape[2]
 
     @pl.when(step == 0)
     def _():
-        for n, slot in enumerate(slots):
-            seq, here = place(*slot)
-            attn_rows[n * piece : (n + 1) * piece, :] = attn[seq, here, :]
-
-    parts = []
-    for ref in (r0, r1, r2a, r2b, r3, t0, t1, t2a, t2b, t3):
-        for seq in range(ref.shape[0]):
-            parts.append(ref[seq])
-    rows = jnp.concatenate(parts, axis=0)
+        for slots, kept in ((OWN_SLOTS, attn_own), (NEAR_SLOTS, attn_near), (FAR_SLOTS, attn_far)):
+            for n, slot in enumerate(slots):
+                seq, here = place(tp, piece, *slot)
+                kept[n * piece : (n + 1) * piece, :] = attn[seq, here, :]
+        for slots, done in ((OWN_SLOTS, own), (NEAR_SLOTS, near)):
+            for n, slot in enumerate(slots):
+                seq, here = place(tp, piece, *slot)
+                d_attn[seq, here, :] = done[n * piece : (n + 1) * piece, :]
+
+    rows = jnp.concatenate([r2a[0], r2b[0], t2a[0], t2b[0]], axis=0)
+    partial[...] = (
+        dot(own_t[...], attn_own[...])
+        + dot(near_t[...], attn_near[...])
+        + dot(rows.T, attn_far[...])
+    )
+
+    def emit(out, order):
+        for n, target in enumerate(order):
+            for z in range(out.shape[1]):
+                start = pl.multiple_of((CHIPS_Y * z + target) * out_rows, 8)
+                out[n, z] = partial[pl.ds(start, out_rows), :].astype(jnp.bfloat16)
+
+    pair = y + 1 - 2 * (y % 2)
+    mirror = CHIPS_Y - 1 - y
+    mirror_pair = mirror + 1 - 2 * (mirror % 2)
+
     product = dot(rows, o_weight[...])
 
     @pl.when(step == 0)
     def _():
+        emit(sent_a, (pair, CHIPS_Y - 1 - pair))
+        emit(kept_a, (y, mirror))
         acc[...] = product
 
-    @pl.when(step > 0)
+    @pl.when(step == 1)
     def _():
-        acc[...] = acc[...] + product
-
-    partial[...] = dot(rows, attn_rows[...], TN)
-    for k, out in enumerate((w0, w1, w2, w3)):
-        target = (y + k) % CHIPS_Y
-        for z in range(out.shape[0]):
-            start = pl.multiple_of((CHIPS_Y * z + target) * out_rows, 8)
-            out[z] = partial[pl.ds(start, out_rows), :].astype(jnp.bfloat16)
-
-    @pl.when(step == pl.num_programs(0) - 1)
-    def _():
-        for n, slot in enumerate(slots):
-            seq, here = place(*slot)
-            d_attn[seq, here, :] = acc[n * piece : (n + 1) * piece, :].astype(jnp.bfloat16)
+        emit(sent_b, (mirror, mirror_pair))
+        emit(kept_b, (y, pair))
+        total = (acc[...] + product).astype(jnp.bfloat16)
+        for n, slot in enumerate(FAR_SLOTS):
+            seq, here = place(tp, piece, *slot)
+            d_attn[seq, here, :] = total[n * piece : (n + 1) * piece, :]
 
 
 def backward_kernel(
-    mine, recv, kv0, kv1, kv2, kv3, kv4, weights, attn, d_attn,
-    dq_mine, dq_other, g0, g1, g2, g3, g4,
+    scalars, mine, recv, kv0, kv1, kv2, kv3, kv4, weights, attn, d_attn,
+    dq_mine, dq_other, g_own, g_sent,
 ):
     rows = mine.shape[1]
+    y = scalars[2]
     heads = []
     for h in range(2):
         cols = slice(h * HEAD_SIZE, (h + 1) * HEAD_SIZE)
@@ -165,7 +220,7 @@
         delta = jnp.sum(product.T, axis=0, keepdims=True)
         heads.append((q, da, delta))
     dq = [None, None]
-    for d, (kv, grad) in enumerate(zip((kv0, kv1, kv2, kv3, kv4), (g0, g1, g2, g3, g4))):
+    for d, kv in enumerate((kv0, kv1, kv2, kv3, kv4)):
         keys = kv[0, :, :HEAD_SIZE]
         values = kv[0, :, HEAD_SIZE:]
         dk = dv = None
@@ -179,8 +234,13 @@
             dv = v_part if dv is None else dv + v_part
             dk = k_part if dk is None else dk + k_part
             dq[h] = q_part if dq[h] is None else dq[h] + q_part
-        grad[0, :, :HEAD_SIZE] = (dk * score_scale).astype(grad.dtype)
-        grad[0, :, HEAD_SIZE:] = dv.astype(grad.dtype)
+        if d == 0:
+            g_own[0, :, :HEAD_SIZE] = dk * score_scale
+            g_own[0, :, HEAD_SIZE:] = dv
+        else:
+            column = (y + CHIPS_Y - d) % CHIPS_Y
+            g_sent[column, 0, :, :HEAD_SIZE] = (dk * score_scale).astype(jnp.bfloat16)
+            g_sent[column, 0, :, HEAD_SIZE:] = dv.astype(jnp.bfloat16)
     for h in range(2):
         cols = slice(h * HEAD_SIZE, (h + 1) * HEAD_SIZE)
         full = (dq[h].T * score_scale).astype(jnp.bfloat16)
@@ -211,58 +271,117 @@
             + [by_seq(doc_mine.shape), by_seq(doc_recv.shape)],
             out_specs=[by_seq(o.shape) for o in outs],
         ),
-        compiler_params=pltpu.CompilerParams(vmem_limit_bytes=48 << 20),
+        compiler_params=pltpu.CompilerParams(vmem_limit_bytes=20 << 20),
+        cost_estimate=pl.CostEstimate(
+            flops=4 * seqs * 2 * 2 * rows * keys * HEAD_SIZE,
+            transcendentals=seqs * 2 * 2 * rows * keys,
+            bytes_accessed=8 << 20,
+        ),
         name="attention_forward",
     )(scalars, mine, recv, *kvs, doc_mine, doc_recv)
 
 
-def projection(scalars, pieces, attn, o_weight):
-    seqs, chip_rows, width = attn.shape
-    features = o_weight.shape[0]
-    steps = 2
+def early_projection(scalars, pieces, o_weight):
+    rows = sum(p.shape[0] * p.shape[1] for p in pieces)
+    features, both = o_weight.shape
+    width = both // 2
+    steps = 7
     block = features // steps
-    out_rows = features // (CHIPS_Y * CHIPS_Z)
-    slab = jax.ShapeDtypeStruct((CHIPS_Z, out_rows, width), jnp.bfloat16)
-    slab_spec = pl.BlockSpec((CHIPS_Z // steps, out_rows, width), lambda i, *_: (i, 0, 0))
-    whole = pl.BlockSpec(attn.shape, lambda i, *_: (0, 0, 0))
+    outs = (
+        jax.ShapeDtypeStruct((rows, width), jnp.bfloat16),
+        jax.ShapeDtypeStruct((features, rows), jnp.bfloat16),
+    )
     return pl.pallas_call(
-        projection_kernel,
-        out_shape=(jax.ShapeDtypeStruct(attn.shape, jnp.bfloat16),) + (slab,) * CHIPS_Y,
+        early_kernel,
+        out_shape=outs,
         grid_spec=pltpu.PrefetchScalarGridSpec(
             num_scalar_prefetch=1,
             grid=(steps,),
             in_specs=[pl.BlockSpec(p.shape[:2] + (block,), lambda i, *_: (0, 0, i)) for p in pieces]
-            + [whole, pl.BlockSpec((block, width), lambda i, scalars: (i, scalars[0]))],
-            out_specs=[whole] + [slab_spec] * CHIPS_Y,
-            scratch_shapes=[
-                pltpu.VMEM((seqs * chip_rows, width), jnp.float32),
-                pltpu.VMEM((seqs * chip_rows, width), jnp.bfloat16),
+            + [pl.BlockSpec((block, width), lambda i, scalars: (i, scalars[0]))],
+            out_specs=[
+                pl.BlockSpec((rows, width), lambda i, *_: (0, 0)),
+                pl.BlockSpec((block, rows), lambda i, *_: (i, 0)),
+            ],
+            scratch_shapes=[pltpu.VMEM((rows, width), jnp.float32)],
+        ),
+        compiler_params=pltpu.CompilerParams(vmem_limit_bytes=16 << 20),
+        cost_estimate=pl.CostEstimate(
+            flops=20 * rows * features * width, transcendentals=0, bytes_accessed=12 << 20
+        ),
+        name="projection_early",
+    )(scalars, *pieces, o_weight)
+
+
+def late_projection(scalars, pieces, rows_t, attn, early, o_weight):
+    width = attn.shape[-1]
+    features = o_weight.shape[0]
+    late_rows = sum(p.shape[0] * p.shape[1] for p in pieces)
+    steps = 2
+    block = features // steps
+    out_rows = features // (CHIPS_Y * CHIPS_Z)
+    slab = jax.ShapeDtypeStruct((2, CHIPS_Z // 2, out_rows, width), jnp.bfloat16)
+
+    def whole(a):
+        return pl.BlockSpec(a.shape, lambda i, *_: (0,) * len(a.shape))
+
+    return pl.pallas_call(
+        late_kernel,
+        out_shape=(jax.ShapeDtypeStruct(attn.shape, jnp.bfloat16),) + (slab,) * 4,
+        grid_spec=pltpu.PrefetchScalarGridSpec(
+            num_scalar_prefetch=1,
+            grid=(steps,),
+            in_specs=[pl.BlockSpec(p.shape[:2] + (block,), lambda i, *_: (0, 0, i)) for p in pieces]
+            + [pl.BlockSpec((block, r.shape[1]), lambda i, *_: (i, 0)) for r in rows_t]
+            + [whole(attn)]
+            + [whole(e) for e in early]
+            + [pl.BlockSpec((block, width), lambda i, scalars: (i, scalars[0]))],
+            out_specs=[whole(attn)] + [whole(slab)] * 4,
+            scratch_shapes=[pltpu.VMEM((late_rows, width), jnp.float32)]
+            + [pltpu.VMEM((r.shape[1], width), jnp.bfloat16) for r in rows_t]
+            + [
+                pltpu.VMEM((late_rows, width), jnp.bfloat16),
                 pltpu.VMEM((block, width), jnp.float32),
             ],
         ),
-        compiler_params=pltpu.CompilerParams(vmem_limit_bytes=56 << 20),
-        name="projection_grads",
-    )(scalars, *pieces, attn, o_weight)
-
-
-def backward(mine, recv, kvs, weights, attn, d_attn):
+        compiler_params=pltpu.CompilerParams(vmem_limit_bytes=32 << 20),
+        cost_estimate=pl.CostEstimate(
+            flops=2 * 6 * late_rows * features * width, transcendentals=0, bytes_accessed=12 << 20
+        ),
+        name="projection_late",
+    )(scalars, *pieces, *rows_t, attn, *early, o_weight)
+
+
+def backward(scalars, mine, recv, kvs, weights, attn, d_attn):
     seqs, rows, width = mine.shape
     half = jax.ShapeDtypeStruct((seqs, rows, width // 2), jnp.bfloat16)
-    outs = (half, half) + tuple(
-        jax.ShapeDtypeStruct(kv.shape, jnp.float32 if d == 0 else jnp.bfloat16)
-        for d, kv in enumerate(kvs)
-    )
+    shape = kvs[0].shape
+    own = jax.ShapeDtypeStruct(shape, jnp.float32)
+    sent = jax.ShapeDtypeStruct((CHIPS_Y,) + shape, jnp.bfloat16)
     query_spec = pl.BlockSpec((1, rows, width // 2), lambda s, *_: (s, 0, 0))
     return pl.pallas_call(
         backward_kernel,
-        out_shape=outs,
-        grid=(seqs,),
-        in_specs=[query_spec, query_spec]
-        + [by_seq(a.shape) for a in (*kvs, weights, attn, d_attn)],
-        out_specs=[by_seq(o.shape) for o in outs],
-        compiler_params=pltpu.CompilerParams(vmem_limit_bytes=48 << 20),
+        out_shape=(half, half, own, sent),
+        grid_spec=pltpu.PrefetchScalarGridSpec(
+            num_scalar_prefetch=1,
+            grid=(seqs,),
+            in_specs=[query_spec, query_spec]
+            + [by_seq(a.shape) for a in (*kvs, weights, attn, d_attn)],
+            out_specs=[
+                by_seq(half.shape),
+                by_seq(half.shape),
+                by_seq(own.shape),
+                pl.BlockSpec((CHIPS_Y, 1) + shape[1:], lambda s, *_: (0, s, 0, 0)),
+            ],
+        ),
+        compiler_params=pltpu.CompilerParams(vmem_limit_bytes=20 << 20),
+        cost_estimate=pl.CostEstimate(
+            flops=10 * seqs * 2 * 2 * rows * 10 * rows * HEAD_SIZE,
+            transcendentals=0,
+            bytes_accessed=8 << 20,
+        ),
         name="attention_backward",
-    )(mine, recv, *kvs, weights, attn, d_attn)
+    )(scalars, mine, recv, *kvs, weights, attn, d_attn)
 
 
 def local(query, key_states, value_state_rows, d_out, o_weight, doc_start):
@@ -285,46 +404,80 @@
         ]
         return jnp.concatenate(parts, axis=-1)
 
+    r3 = tp_ahead(d_out, 1)
+    r1 = tp_ahead(d_out, -1)
     mine = head_share(first)
     recv = to_sibling(head_share(~first))
     doc_mine = doc_start[:, None, :]
     doc_recv = to_sibling(doc_mine)
-
-    r0 = d_out
-    r3 = tp_ahead(r0, 1)
-    r1 = tp_ahead(r0, -1)
+    t0 = to_sibling(d_out)
+    recv, doc_recv, t0 = lax.optimization_barrier((recv, doc_recv, t0))
+
+    kv_width = 2 * HEAD_SIZE
+    kv0 = jnp.concatenate([mine[..., -kv_width:], recv[..., -kv_width:]], axis=1)
+    kv1, kv2, kv3 = (chips_ahead(kv0, d) for d in (1, 2, 3))
+    own, own_t = early_projection(scalars, [d_out, t0], o_weight)
+
+    r1, r3, own = lax.optimization_barrier((r1, r3, own))
     r2a = tp_ahead(r3[:1], 1)
     r2b = tp_ahead(r1[1:], -1)
-    pieces = [r0, r1, r2a, r2b, r3]
-    pieces = pieces + [to_sibling(p) for p in pieces]
-
-    kv_width = 2 * HEAD_SIZE
-    kv0 = jnp.concatenate([mine[..., -kv_width:], recv[..., -kv_width:]], axis=1)
-    kvs = [kv0] + [chips_ahead(kv0, d) for d in range(1, HALO_CHIPS + 1)]
-
+    kv1, kv2, kv3, kv_again, r1, r3 = lax.optimization_barrier((kv1, kv2, kv3, kv0, r1, r3))
+    kv4 = chips_ahead(kv_again, 4)
+    t1, t3, kv4 = lax.optimization_barrier((to_sibling(r1), to_sibling(r3), kv4))
+    near, near_t = early_projection(scalars, [r1, r3, t1, t3], o_weight)
+    kv1, near, r2a, r2b = lax.optimization_barrier((kv1, near, r2a, r2b))
+    kvs = [kv0, kv1, kv2, kv3, kv4]
     attn, weights = forward(scalars, mine, recv, kvs, doc_mine, doc_recv)
-    d_attn, w0, *w_sent = projection(scalars, pieces, attn, o_weight)
-    w_arrived = [y_ahead(w, k + 1) for k, w in enumerate(w_sent)]
-    dq_mine, dq_other, g0, *g_sent = backward(mine, recv, kvs, weights, attn, d_attn)
-    g_arrived = [chips_ahead(g, -d - 1) for d, g in enumerate(g_sent)]
+    d_attn, sent_a, kept_a, sent_b, kept_b = late_projection(
+        scalars,
+        [r2a, r2b, to_sibling(r2a), to_sibling(r2b)],
+        [own_t, near_t],
+        attn,
+        [own, near],
+        o_weight,
+    )
+    got_a = y_route(sent_a, y_pair)
+    got_b = y_route(sent_b, y_mirror)
+    dq_mine, dq_other, g_own, g_sent = backward(scalars, mine, recv, kvs, weights, attn, d_attn)
     dq_recv = to_sibling(dq_other)
 
-    w_sum = w0.astype(jnp.float32)
-    for w in w_arrived:
-        w_sum = w_sum + w.astype(jnp.float32)
-    w_all = z_exchange(w_sum.astype(jnp.bfloat16))
+    def added(*blocks):
+        total = blocks[0].astype(jnp.float32)
+        for block in blocks[1:]:
+            total = total + block.astype(jnp.float32)
+        return total
+
+    next_a = added(kept_a[1], got_a[1]).astype(jnp.bfloat16)
+    next_b = added(kept_b[1], got_b[1]).astype(jnp.bfloat16)
+    next_a, next_b, g_sent = lax.optimization_barrier((next_a, next_b, g_sent))
+    last_a = y_route(next_a, y_mirror)
+    last_b = y_route(next_b, y_pair)
+    g_columns = y_exchange(g_sent)
+    w_sum = jnp.concatenate(
+        [
+            added(kept_a[0], got_a[0], last_a).astype(jnp.bfloat16),
+            added(kept_b[0], got_b[0], last_b).astype(jnp.bfloat16),
+        ],
+        axis=0,
+    )
+    w_all = z_exchange(w_sum)
+
+    g_before = jnp.zeros(g_own.shape, jnp.float32)
+    grads = g_own
+    for column in range(CHIPS_Y):
+        block = g_columns[column].astype(jnp.float32)
+        grads = grads + jnp.where(column > y, block, 0.0)
+        g_before = g_before + jnp.where(column > y, 0.0, block)
+    g_before = chips_ahead(g_before.astype(jnp.bfloat16), -HALO_CHIPS)
+    grads = (grads + g_before.astype(jnp.float32)).astype(jnp.bfloat16)
+    g_mine = grads[:, :shard_rows]
+    g_recv = to_sibling(grads[:, shard_rows:])
+
     w_rows = jnp.sum(w_all.astype(jnp.float32), axis=0)
     half_rows = w_rows.shape[0] // 2
     w_top, w_bottom = w_rows[:half_rows], w_rows[half_rows:]
     w_mine = jnp.where(first, w_top, w_bottom)
     w_recv = to_sibling(jnp.where(first, w_bottom, w_top))
-
-    grads = g0
-    for g in g_arrived:
-        grads = grads + g.astype(jnp.float32)
-    grads = grads.astype(jnp.bfloat16)
-    g_mine = grads[:, :shard_rows]
-    g_recv = to_sibling(grads[:, shard_rows:])
 
     def by_core(own, other):
         return jnp.concatenate(

time: 141 us -> 138 us (0.979); the launches traced: 139 us -> 138 us
  other arithmetic: 7.39 us -> 12 us
  starting transfers between devices: 56.3 us -> 51.8 us
  waiting for transfers between devices: 50.4 us -> 47.6 us
    ppermute x21 -> x19, waiting for transfers between devices: 23.4 us -> 35.5 us  [ctx_shift(): return lax.ppermute(block, 'ctx', [(i, move(i)) for i in range(count)])]
    ppermute x21 -> x19, starting transfers between devices: 46 us -> 38.4 us  [ctx_shift(): return lax.ppermute(block, 'ctx', [(i, move(i)) for i in range(count)])]
    all_to_all x1, waiting for transfers between devices: 17.1 us -> 9.58 us  [z_exchange(): lax.all_to_all(blocks, 'ctx', 0, 0, axis_index_groups=groups, tiled=True)]
    ppermute x4, waiting for transfers between devices: 9.97 us -> 2.53 us  [tp_ahead(): lax.ppermute(block, 'tp', [(i, (i + distance) % TP) for i in range(TP)])]
    all_to_all x0 -> x1, starting transfers between devices: none -> 4.8 us  [y_exchange(): lax.all_to_all(blocks, 'ctx', 0, 0, axis_index_groups=groups, tiled=True)]
    convert_element_type x2 -> x6, other arithmetic: 2.37 us -> 6.04 us  [the longest x1 1.94 us: local(): added(kept_b[0], got_b[0], last_b).astype(jnp.bfloat16)]
    ppermute x4, starting transfers between devices: 6.82 us -> 4.64 us  [tp_ahead(): lax.ppermute(block, 'tp', [(i, (i + distance) % TP) for i in range(TP)])]
    unnamed x18 -> x14, local copies, waits for them, and re-layouts: 3.15 us -> 4.53 us
  transfers between devices with their start and end apart: 26 -> 25, of which waited for: 14 -> 13; matrix products, arithmetic and copies ran while one was open for 5% -> 7% of each run, Pallas kernels for 7% -> 12%
where the time goes in v2:
time: 138 us
  starting transfers between devices  51.8 us (38%)
  waiting for transfers between devices  47.6 us (34%)
  Pallas kernels  21.1 us (15%)
  other arithmetic  12 us (9%)
  local copies, waits for them, and re-layouts  4.6 us (3%)
    ppermute x19, starting transfers between devices, ctx_shift(): return lax.ppermute(block, 'ctx', [(i, move(i)) for i in range(count)])  38.4 us
    ppermute x19, waiting for transfers between devices, ctx_shift(): return lax.ppermute(block, 'ctx', [(i, move(i)) for i in range(count)])  35.5 us
    all_to_all x1, waiting for transfers between devices, z_exchange(): lax.all_to_all(blocks, 'ctx', 0, 0, axis_index_groups=groups, tiled=True)  9.58 us
    pallas_call x2, Pallas kernels, early_projection(): pl.pallas_call(early_kernel, out_shape=outs, grid_spec=pltpu.PrefetchScal...  7.51 us
    pallas_call x1, Pallas kernels, backward(): pl.pallas_call(backward_kernel, out_shape=(half, half, own, sent), grid_s...  5.19 us
    all_to_all x1, starting transfers between devices, y_exchange(): lax.all_to_all(blocks, 'ctx', 0, 0, axis_index_groups=groups, tiled=True)  4.8 us
    ppermute x4, starting transfers between devices, tp_ahead(): lax.ppermute(block, 'tp', [(i, (i + distance) % TP) for i in range(TP)])  4.64 us
    unnamed x14, local copies, waits for them, and re-layouts  4.53 us
  transfers between devices with their start and end apart: 25, of which 13 were waited for; matrix products, arithmetic and copies ran while one was open for 7% of the time, Pallas kernels for 12%

profile of v2, /device:TPU:1, one launch (start us, length us, event | category | flops | bytes accessed | tf_op | source)
XLA Modules:
  0.0 137.9 jit_solution(1939894396908168350)
XLA Ops:
  0.6 3.3 %collective-permute-start.2 = (bf16[2,32,5376]{2,1,0:T(8,128)(2,1)}, bf16[2,32,5376]{2,1,0:T(8,128)(2,1)S(1)}, u32[]{:S(2)}, u32[]{:S(2)}) collective-permute-start(bf16[2,32,5376]{2,1,0:T(8,128)(2,1)} %refs_0_.1), channel_id=1, source_target_pairs={{0,4},{4,0},{8,12},{12,8},{16,20},{20,16},{24,28},{28,24},{32,36},... | collective-permute-start | bytes 2064392 | tf_op jit(solution)/shard_map/ppermute | solution.py:30
  4.0 1.0 broadcast_select_fusion
  4.9 1.0 broadcast_select_fusion.4
  6.1 0.8 collective-permute-start.6
  6.9 0.7 collective-permute-start.7
  7.6 1.0 collective-permute-start.1
  8.7 1.0 collective-permute-done.1.doc_recv
  10.0 2.6 %collective-permute-start.4 = (bf16[2,256,256]{2,1,0:T(8,128)(2,1)S(1)}, bf16[2,256,256]{2,1,0:T(8,128)(2,1)S(1)}, u32[]{:S(2)}, u32[]{:S(2)}) collective-permute-start(bf16[2,256,256]{2,1,0:T(8,128)(2,1)S(1)} %pad_maximum_fusion.3.kv0), channel_id=1, source_target_pairs={{0,16},{4,20},{8,24},{12,28},{16,32},{20,36},{24,40},{28,44},{32,4... | collective-permute-start | bytes 786440 | tf_op jit(solution)/shard_map/ppermute | solution.py:30
  12.7 2.4 %collective-permute-start.5 = (bf16[2,256,256]{2,1,0:T(8,128)(2,1)S(1)}, bf16[2,256,256]{2,1,0:T(8,128)(2,1)S(1)}, u32[]{:S(2)}, u32[]{:S(2)}) collective-permute-start(bf16[2,256,256]{2,1,0:T(8,128)(2,1)S(1)} %pad_maximum_fusion.3.kv0), channel_id=1, source_target_pairs={{0,24},{4,28},{8,32},{12,36},{16,40},{20,44},{24,48},{28,52},{32,5... | collective-permute-start | bytes 786440 | tf_op jit(solution)/shard_map/ppermute | solution.py:30
  15.1 2.6 %copy-done = bf16[5376,512]{1,0:T(8,128)(2,1)S(1)} copy-done((bf16[5376,512]{1,0:T(8,128)(2,1)S(1)}, bf16[5376,512]{1,0:T(8,128)(2,1)}, u32[]{:S(2)}) %copy-start) | copy-done | bytes 5505048
  17.6 1.1 copy-done.2
  18.7 3.3 %projection_early.2 = (bf16[128,256]{1,0:T(8,128)(2,1)S(1)}, bf16[5376,128]{1,0:T(8,128)(2,1)S(1)}) custom-call(s32[4]{0:T(128)S(1)} %pad_add_fusion.scalars, bf16[2,32,5376]{2,1,0:T(8,128)(2,1)S(1)} %copy-done.2, bf16[2,32,5376]{2,1,0:T(8,128)(2,1)S(1)} %collective-permute-done.2.refs_1_, bf16[5376,512]{1,0:T(8,128)(2,1)S(1)} %copy-done), custom_call_target="tpu_custom_call" | custom-call | flops 3523215360 | bytes 12582912 | tf_op jit(solution)/shard_map/projection_early/pallas_call | solution.py:294
  22.0 0.9 collective-permute-done.6.refs_0_
  22.9 1.6 %collective-permute-done.7.refs_1_ = bf16[2,32,5376]{2,1,0:T(8,128)(2,1)S(1)} collective-permute-done((bf16[2,32,5376]{2,1,0:T(8,128)(2,1)}, bf16[2,32,5376]{2,1,0:T(8,128)(2,1)S(1)}, u32[]{:S(2)}, u32[]{:S(2)}) %collective-permute-start.7) | collective-permute-done | bytes 688160 | tf_op jit(solution)/shard_map/ppermute | solution.py:74
  24.6 2.1 %collective-permute-done.3.kv1 = bf16[2,256,256]{2,1,0:T(8,128)(2,1)S(1)} collective-permute-done((bf16[2,256,256]{2,1,0:T(8,128)(2,1)S(1)}, bf16[2,256,256]{2,1,0:T(8,128)(2,1)S(1)}, u32[]{:S(2)}, u32[]{:S(2)}) %collective-permute-start.3) | collective-permute-done | bytes 262176 | tf_op jit(solution)/shard_map/ppermute | solution.py:30
  26.6 1.6 %collective-permute-done.4.kv2 = bf16[2,256,256]{2,1,0:T(8,128)(2,1)S(1)} collective-permute-done((bf16[2,256,256]{2,1,0:T(8,128)(2,1)S(1)}, bf16[2,256,256]{2,1,0:T(8,128)(2,1)S(1)}, u32[]{:S(2)}, u32[]{:S(2)}) %collective-permute-start.4) | collective-permute-done | bytes 262176 | tf_op jit(solution)/shard_map/ppermute | solution.py:30
  28.2 1.4 %collective-permute-start.8 = (bf16[2,32,5376]{2,1,0:T(8,128)(2,1)S(1)}, bf16[2,32,5376]{2,1,0:T(8,128)(2,1)S(1)}, u32[]{:S(2)}, u32[]{:S(2)}) collective-permute-start(bf16[2,32,5376]{2,1,0:T(8,128)(2,1)S(1)} %collective-permute-done.6.refs_0_), channel_id=1, source_target_pairs={{0,4},{4,0},{8,12},{12,8},{16,20},{20,16},{24,28},{28,24},{32,36},... | collective-permute-start | bytes 2064392 | tf_op jit(solution)/shard_map/ppermute | solution.py:30
  30.3 2.6 %collective-permute-start.12 = (bf16[1,32,5376]{2,1,0:T(8,128)(2,1)S(1)}, bf16[1,32,5376]{2,1,0:T(8,128)(2,1)S(1)}, u32[]{:S(2)}, u32[]{:S(2)}) collective-permute-start(bf16[1,32,5376]{2,1,0:T(8,128)(2,1)S(1)} %slice.103), channel_id=1, source_target_pairs={{0,3},{1,0},{2,1},{3,2},{4,7},{5,4},{6,5},{7,6},{8,11},{9,8},{10,9... | collective-permute-start | bytes 1032200 | tf_op jit(solution)/shard_map/ppermute | solution.py:74
  32.8 5.4 %collective-permute-done.10.kv4 = bf16[2,256,256]{2,1,0:T(8,128)(2,1)S(1)} collective-permute-done((bf16[2,256,256]{2,1,0:T(8,128)(2,1)S(1)}, bf16[2,256,256]{2,1,0:T(8,128)(2,1)S(1)}, u32[]{:S(2)}, u32[]{:S(2)}) %collective-permute-start.10) | collective-permute-done | bytes 262176 | tf_op jit(solution)/shard_map/ppermute | solution.py:30
  38.2 4.2 %projection_early.3 = (bf16[256,256]{1,0:T(8,128)(2,1)S(1)}, bf16[5376,256]{1,0:T(8,128)(2,1)S(1)}) custom-call(s32[4]{0:T(128)S(1)} %pad_add_fusion.scalars, bf16[2,32,5376]{2,1,0:T(8,128)(2,1)S(1)} %collective-permute-done.6.refs_0_, bf16[2,32,5376]{2,1,0:T(8,128)(2,1)S(1)} %collective-permute-done.7.refs_1_, ...), custom_call_target="tpu_custom_call" | custom-call | flops 7046430720 | bytes 12582912 | tf_op jit(solution)/shard_map/projection_early/pallas_call | solution.py:294
  42.5 1.4 %collective-permute-start.13 = (bf16[1,32,5376]{2,1,0:T(8,128)(2,1)S(1)}, bf16[1,32,5376]{2,1,0:T(8,128)(2,1)S(1)}, u32[]{:S(2)}, u32[]{:S(2)}) collective-permute-start(bf16[1,32,5376]{2,1,0:T(8,128)(2,1)S(1)} %collective-permute-done.11.r2a), channel_id=1, source_target_pairs={{0,4},{4,0},{8,12},{12,8},{16,20},{20,16},{24,28},{28,24},{32,36},... | collective-permute-start | bytes 1032200 | tf_op jit(solution)/shard_map/ppermute | solution.py:30
  44.2 4.3 %attention_forward.1 = (bf16[2,256,256]{2,1,0:T(8,128)(2,1)S(1)}, bf16[2,2,1280,256]{3,2,1,0:T(8,128)(2,1)S(1)}) custom-call(s32[4]{0:T(128)S(1)} %pad_add_fusion.scalars, bf16[2,128,512]{2,1,0:T(8,128)(2,1)S(1)} %pad_maximum_fusion.1.mine, bf16[2,128,512]{2,1,0:T(8,128)(2,1)S(1)} %collective-permute-done.recv, ...), custom_call_target="tpu_custom_call" | custom-call | flops 671088640 | bytes 8388608 | tf_op jit(solution)/shard_map/attention_forward/pallas_call | solution.py:263
  48.6 4.1 %projection_late.1 = (bf16[2,256,256]{2,1,0:T(8,128)(2,1)S(1)}, bf16[2,4,168,256]{3,2,1,0:T(8,128)(2,1)S(1)}, bf16[2,4,168,256]{3,2,1,0:T(8,128)(2,1)S(1)}, bf16...) custom-call(s32[4]{0:T(128)S(1)} %pad_add_fusion.scalars, ...), custom_call_target="tpu_custom_call" | custom-call | flops 2113929216 | bytes 12582912 | tf_op jit(solution)/shard_map/projection_late/pallas_call | solution.py:328
  52.7 7.6 %collective-permute-start.16 = (bf16[2,4,168,256]{3,2,1,0:T(8,128)(2,1)S(1)}, bf16[2,4,168,256]{3,2,1,0:T(8,128)(2,1)S(1)}, u32[]{:S(2)}, u32[]{:S(2)}) collective-permute-start(bf16[2,4,168,256]{3,2,1,0:T(8,128)(2,1)S(1)} %get-tuple-element.71), channel_id=1, source_target_pairs={{0,8},{4,12},{8,0},{12,4},{16,24},{20,28},{24,16},{28,20},{32,40},... | collective-permute-start | bytes 2064392 | tf_op jit(solution)/shard_map/ppermute | solution.py:30
  60.3 4.5 %collective-permute-start.17 = (bf16[2,4,168,256]{3,2,1,0:T(8,128)(2,1)S(1)}, bf16[2,4,168,256]{3,2,1,0:T(8,128)(2,1)S(1)}, u32[]{:S(2)}, u32[]{:S(2)}) collective-permute-start(bf16[2,4,168,256]{3,2,1,0:T(8,128)(2,1)S(1)} %get-tuple-element.73), channel_id=1, source_target_pairs={{0,24},{4,28},{8,16},{12,20},{16,8},{20,12},{24,0},{28,4},{32,56},... | collective-permute-start | bytes 2064392 | tf_op jit(solution)/shard_map/ppermute | solution.py:30
  64.8 5.2 %attention_backward.1 = (bf16[2,128,256]{2,1,0:T(8,128)(2,1)S(1)}, bf16[2,128,256]{2,1,0:T(8,128)(2,1)S(1)}, f32[2,256,256]{2,1,0:T(8,128)S(1)}, bf16[4,2,256,256]{3,2,1,0:T(8,128)(2,1)}) custom-call(s32[4]{0:T(128)S(1)} %pad_add_fusion.scalars, bf16[2,128,512]{2,1,0:T(8,128)(2,1)S(1)} %pad_maximum_fusion.1.mine, ...), custom_call_target="tpu_custom_call" | custom-call | flops 1677721600 | bytes 8388608 | tf_op jit(solution)/shard_map/attention_backward/pallas_call | solution.py:362
  70.0 6.0 %collective-permute-done.16 = bf16[2,4,168,256]{3,2,1,0:T(8,128)(2,1)S(1)} collective-permute-done((bf16[2,4,168,256]{3,2,1,0:T(8,128)(2,1)S(1)}, bf16[2,4,168,256]{3,2,1,0:T(8,128)(2,1)S(1)}, u32[]{:S(2)}, u32[]{:S(2)}) %collective-permute-start.16) | collective-permute-done | bytes 688160 | tf_op jit(solution)/shard_map/ppermute | solution.py:30
  76.0 0.9 fusion.16
  76.9 3.3 %collective-permute-done.17 = bf16[2,4,168,256]{3,2,1,0:T(8,128)(2,1)S(1)} collective-permute-done((bf16[2,4,168,256]{3,2,1,0:T(8,128)(2,1)S(1)}, bf16[2,4,168,256]{3,2,1,0:T(8,128)(2,1)S(1)}, u32[]{:S(2)}, u32[]{:S(2)}) %collective-permute-start.17) | collective-permute-done | bytes 688160 | tf_op jit(solution)/shard_map/ppermute | solution.py:30
  80.1 0.9 copy-done.6
  81.0 0.8 fusion.17
  81.8 4.8 %all-to-all-start = ((bf16[4,2,256,256]{3,2,1,0:T(8,128)(2,1)}), bf16[4,2,256,256]{3,2,1,0:T(8,128)(2,1)S(1)}, u32[]{:S(2)}, u32[]{:S(2)}) async-start(bf16[4,2,256,256]{3,2,1,0:T(8,128)(2,1)} %get-tuple-element.75), calls=%async_computation | async-start | bytes 2097152 | tf_op jit(solution)/shard_map/all_to_all | solution.py:64
  86.6 2.7 %collective-permute-start.20 = (bf16[4,168,256]{2,1,0:T(8,128)(2,1)}, bf16[4,168,256]{2,1,0:T(8,128)(2,1)}, u32[]{:S(2)}, u32[]{:S(2)}) collective-permute-start(bf16[4,168,256]{2,1,0:T(8,128)(2,1)} %fusion.16), channel_id=1, source_target_pairs={{0,24},{4,28},{8,16},{12,20},{16,8},{20,12},{24,0},{28,4},{32,56},... | collective-permute-start | bytes 1032200 | tf_op jit(solution)/shard_map/ppermute | solution.py:30
  89.3 1.3 collective-permute-done.21
  90.7 1.9 %fusion = bf16[4,168,256]{2,1,0:T(8,128)(2,1)} fusion(bf16[4,168,256]{2,1,0:T(8,128)(2,1)} %collective-permute-done.21, bf16[2,4,168,256]{3,2,1,0:T(8,128)(2,1)} %copy-done.6, bf16[2,4,168,256]{3,2,1,0:T(8,128)(2,1)S(1)} %get-tuple-element.72), kind=kLoop, calls=%fused_computation.3 | loop fusion | flops 1032192 | bytes 1376256 | tf_op jit(solution)/shard_map/convert_element_type | solution.py:459
  92.6 14.4 %collective-permute-done.20 = bf16[4,168,256]{2,1,0:T(8,128)(2,1)} collective-permute-done((bf16[4,168,256]{2,1,0:T(8,128)(2,1)}, bf16[4,168,256]{2,1,0:T(8,128)(2,1)}, u32[]{:S(2)}, u32[]{:S(2)}) %collective-permute-start.20) | collective-permute-done | bytes 344096 | tf_op jit(solution)/shard_map/ppermute | solution.py:30
  107.0 1.2 fusion.1
  108.3 0.9 fusion.18
  109.2 0.9 pad_maximum_fusion
  110.1 4.0 %all-to-all-start.1 = ((bf16[8,168,256]{2,1,0:T(8,128)(2,1)}), bf16[8,168,256]{2,1,0:T(8,128)(2,1)S(1)}, u32[]{:S(2)}, u32[]{:S(2)}) async-start(bf16[8,168,256]{2,1,0:T(8,128)(2,1)} %pad_maximum_fusion), calls=%async_computation.1 | async-start | bytes 1376256 | tf_op jit(solution)/shard_map/all_to_all | solution.py:70
  114.0 3.4 %collective-permute-start.15 = (bf16[2,128,256]{2,1,0:T(8,128)(2,1)S(1)}, bf16[2,128,256]{2,1,0:T(8,128)(2,1)S(1)}, u32[]{:S(2)}, u32[]{:S(2)}) collective-permute-start(bf16[2,128,256]{2,1,0:T(8,128)(2,1)S(1)} %get-tuple-element.68), channel_id=1, source_target_pairs={{0,4},{4,0},{8,12},{12,8},{16,20},{20,16},{24,28},{28,24},{32,36},... | collective-permute-start | bytes 393224 | tf_op jit(solution)/shard_map/ppermute | solution.py:30
  117.7 3.4 %collective-permute-start.19 = (bf16[2,128,256]{2,1,0:T(8,128)(2,1)S(1)}, bf16[2,128,256]{2,1,0:T(8,128)(2,1)S(1)}, u32[]{:S(2)}, u32[]{:S(2)}) collective-permute-start(bf16[2,128,256]{2,1,0:T(8,128)(2,1)S(1)} %slice.130), channel_id=1, source_target_pairs={{0,4},{4,0},{8,12},{12,8},{16,20},{20,16},{24,28},{28,24},{32,36},... | collective-permute-start | bytes 393224 | tf_op jit(solution)/shard_map/ppermute | solution.py:30
  121.1 0.7 pad_maximum_fusion.4
  122.1 0.7 pad_maximum_fusion.6
  122.8 9.6 %all-to-all-done.1 = bf16[8,168,256]{2,1,0:T(8,128)(2,1)S(1)} async-done(((bf16[8,168,256]{2,1,0:T(8,128)(2,1)}), bf16[8,168,256]{2,1,0:T(8,128)(2,1)S(1)}, u32[]{:S(2)}, u32[]{:S(2)}) %all-to-all-start.1) | async-done | bytes 688160 | tf_op jit(solution)/shard_map/all_to_all | solution.py:70
  132.5 3.8 %collective-permute-start.22 = (f32[84,256]{1,0:T(8,128)S(1)}, f32[84,256]{1,0:T(8,128)S(1)}, u32[]{:S(2)}, u32[]{:S(2)}) collective-permute-start(f32[84,256]{1,0:T(8,128)S(1)} %slice_select_fusion), channel_id=1, source_target_pairs={{0,4},{4,0},{8,12},{12,8},{16,20},{20,16},{24,28},{28,24},{32,36},... | collective-permute-start | bytes 258056 | tf_op jit(solution)/shard_map/ppermute | solution.py:30
  136.2 0.7 pad_maximum_fusion.7
  137.2 0.7 pad_maximum_fusion.5
  (47 shorter events, 2.5 us)
Async XLA Ops:
  0.6 9.0 %collective-permute-start.2 = (bf16[2,32,5376]{2,1,0:T(8,128)(2,1)}, bf16[2,32,5376]{2,1,0:T(8,128)(2,1)S(1)}, u32[]{:S(2)}, u32[]{:S(2)}) collective-permute-start(bf16[2,32,5376]{2,1,0:T(8,128)(2,1)} %refs_0_.1), channel_id=1, source_target_pairs={{0,4},{4,0},{8,12},{12,8},{16,20},{20,16},{24,28},{28,24},{32,36},... | collective-permute-start | bytes 2064392 | tf_op jit(solution)/shard_map/ppermute | solution.py:30
  5.9 3.7 %collective-permute-start = (bf16[2,128,512]{2,1,0:T(8,128)(2,1)S(1)}, bf16[2,128,512]{2,1,0:T(8,128)(2,1)S(1)}, u32[]{:S(2)}, u32[]{:S(2)}) collective-permute-start(bf16[2,128,512]{2,1,0:T(8,128)(2,1)S(1)} %pad_maximum_fusion.2), channel_id=1, source_target_pairs={{0,4},{4,0},{8,12},{12,8},{16,20},{20,16},{24,28},{28,24},{32,36},... | collective-permute-start | bytes 786440 | tf_op jit(solution)/shard_map/ppermute | solution.py:30
  6.1 16.9 %collective-permute-start.6 = (bf16[2,32,5376]{2,1,0:T(8,128)(2,1)}, bf16[2,32,5376]{2,1,0:T(8,128)(2,1)S(1)}, u32[]{:S(2)}, u32[]{:S(2)}) collective-permute-start(bf16[2,32,5376]{2,1,0:T(8,128)(2,1)} %refs_0_.1), channel_id=1, source_target_pairs={{0,3},{1,0},{2,1},{3,2},{4,7},{5,4},{6,5},{7,6},{8,11},{9,8},{10,9... | collective-permute-start | bytes 2064392 | tf_op jit(solution)/shard_map/ppermute | solution.py:74
  6.9 17.7 %collective-permute-start.7 = (bf16[2,32,5376]{2,1,0:T(8,128)(2,1)}, bf16[2,32,5376]{2,1,0:T(8,128)(2,1)S(1)}, u32[]{:S(2)}, u32[]{:S(2)}) collective-permute-start(bf16[2,32,5376]{2,1,0:T(8,128)(2,1)} %refs_0_.1), channel_id=1, source_target_pairs={{0,1},{1,2},{2,3},{3,0},{4,5},{5,6},{6,7},{7,4},{8,9},{9,10},{10,1... | collective-permute-start | bytes 2064392 | tf_op jit(solution)/shard_map/ppermute | solution.py:74
  7.6 2.0 %collective-permute-start.1 = (s32[2,1,128]{2,1,0:T(1,128)}, s32[2,1,128]{2,1,0:T(1,128)S(1)}, u32[]{:S(2)}, u32[]{:S(2)}) collective-permute-start(s32[2,1,128]{2,1,0:T(1,128)} %bitcast.45), channel_id=1, source_target_pairs={{0,4},{4,0},{8,12},{12,8},{16,20},{20,16},{24,28},{28,24},{32,36},... | collective-permute-start | bytes 3080 | tf_op jit(solution)/shard_map/ppermute | solution.py:30
  9.7 17.0 %collective-permute-start.3 = (bf16[2,256,256]{2,1,0:T(8,128)(2,1)S(1)}, bf16[2,256,256]{2,1,0:T(8,128)(2,1)S(1)}, u32[]{:S(2)}, u32[]{:S(2)}) collective-permute-start(bf16[2,256,256]{2,1,0:T(8,128)(2,1)S(1)} %pad_maximum_fusion.3.kv0), channel_id=1, source_target_pairs={{0,8},{4,12},{8,16},{12,20},{16,24},{20,28},{24,32},{28,36},{32,40... | collective-permute-start | bytes 786440 | tf_op jit(solution)/shard_map/ppermute | solution.py:30
  10.0 18.2 %collective-permute-start.4 = (bf16[2,256,256]{2,1,0:T(8,128)(2,1)S(1)}, bf16[2,256,256]{2,1,0:T(8,128)(2,1)S(1)}, u32[]{:S(2)}, u32[]{:S(2)}) collective-permute-start(bf16[2,256,256]{2,1,0:T(8,128)(2,1)S(1)} %pad_maximum_fusion.3.kv0), channel_id=1, source_target_pairs={{0,16},{4,20},{8,24},{12,28},{16,32},{20,36},{24,40},{28,44},{32,4... | collective-permute-start | bytes 786440 | tf_op jit(solution)/shard_map/ppermute | solution.py:30
  12.7 15.5 %collective-permute-start.5 = (bf16[2,256,256]{2,1,0:T(8,128)(2,1)S(1)}, bf16[2,256,256]{2,1,0:T(8,128)(2,1)S(1)}, u32[]{:S(2)}, u32[]{:S(2)}) collective-permute-start(bf16[2,256,256]{2,1,0:T(8,128)(2,1)S(1)} %pad_maximum_fusion.3.kv0), channel_id=1, source_target_pairs={{0,24},{4,28},{8,32},{12,36},{16,40},{20,44},{24,48},{28,52},{32,5... | collective-permute-start | bytes 786440 | tf_op jit(solution)/shard_map/ppermute | solution.py:30
  15.1 2.6 %copy-start = (bf16[5376,512]{1,0:T(8,128)(2,1)S(1)}, bf16[5376,512]{1,0:T(8,128)(2,1)}, u32[]{:S(2)}) copy-start(bf16[5376,512]{1,0:T(8,128)(2,1)} %o_weight.1) | copy-start | bytes 16515076
  17.6 1.1 copy-start.2
  18.7 19.5 %copy-start.1 = (bf16[5376,512]{1,0:T(8,128)(2,1)S(1)}, bf16[5376,512]{1,0:T(8,128)(2,1)}, u32[]{:S(2)}) copy-start(bf16[5376,512]{1,0:T(8,128)(2,1)} %o_weight.1) | copy-start | bytes 16515076
  28.2 10.0 %collective-permute-start.8 = (bf16[2,32,5376]{2,1,0:T(8,128)(2,1)S(1)}, bf16[2,32,5376]{2,1,0:T(8,128)(2,1)S(1)}, u32[]{:S(2)}, u32[]{:S(2)}) collective-permute-start(bf16[2,32,5376]{2,1,0:T(8,128)(2,1)S(1)} %collective-permute-done.6.refs_0_), channel_id=1, source_target_pairs={{0,4},{4,0},{8,12},{12,8},{16,20},{20,16},{24,28},{28,24},{32,36},... | collective-permute-start | bytes 2064392 | tf_op jit(solution)/shard_map/ppermute | solution.py:30
  29.6 8.6 %collective-permute-start.9 = (bf16[2,32,5376]{2,1,0:T(8,128)(2,1)S(1)}, bf16[2,32,5376]{2,1,0:T(8,128)(2,1)S(1)}, u32[]{:S(2)}, u32[]{:S(2)}) collective-permute-start(bf16[2,32,5376]{2,1,0:T(8,128)(2,1)S(1)} %collective-permute-done.7.refs_1_), channel_id=1, source_target_pairs={{0,4},{4,0},{8,12},{12,8},{16,20},{20,16},{24,28},{28,24},{32,36},... | collective-permute-start | bytes 2064392 | tf_op jit(solution)/shard_map/ppermute | solution.py:30
  29.6 8.6 %collective-permute-start.10 = (bf16[2,256,256]{2,1,0:T(8,128)(2,1)S(1)}, bf16[2,256,256]{2,1,0:T(8,128)(2,1)S(1)}, u32[]{:S(2)}, u32[]{:S(2)}) collective-permute-start(bf16[2,256,256]{2,1,0:T(8,128)(2,1)S(1)} %pad_maximum_fusion.3.kv0), channel_id=1, source_target_pairs={{0,32},{4,36},{8,40},{12,44},{16,48},{20,52},{24,56},{28,60},{32,6... | collective-permute-start | bytes 786440 | tf_op jit(solution)/shard_map/ppermute | solution.py:30
  29.7 14.5 %copy-start.3 = (s32[2,128]{1,0:T(2,128)S(1)}, s32[2,128]{1,0:T(2,128)}, u32[]{:S(2)}) copy-start(s32[2,128]{1,0:T(2,128)} %param.11) | copy-start | bytes 3076
  29.7 12.7 %collective-permute-start.11 = (bf16[1,32,5376]{2,1,0:T(8,128)(2,1)S(1)}, bf16[1,32,5376]{2,1,0:T(8,128)(2,1)S(1)}, u32[]{:S(2)}, u32[]{:S(2)}) collective-permute-start(bf16[1,32,5376]{2,1,0:T(8,128)(2,1)S(1)} %slice.102), channel_id=1, source_target_pairs={{0,1},{1,2},{2,3},{3,0},{4,5},{5,6},{6,7},{7,4},{8,9},{9,10},{10,1... | collective-permute-start | bytes 1032200 | tf_op jit(solution)/shard_map/ppermute | solution.py:74
  30.3 12.2 %collective-permute-start.12 = (bf16[1,32,5376]{2,1,0:T(8,128)(2,1)S(1)}, bf16[1,32,5376]{2,1,0:T(8,128)(2,1)S(1)}, u32[]{:S(2)}, u32[]{:S(2)}) collective-permute-start(bf16[1,32,5376]{2,1,0:T(8,128)(2,1)S(1)} %slice.103), channel_id=1, source_target_pairs={{0,3},{1,0},{2,1},{3,2},{4,7},{5,4},{6,5},{7,6},{8,11},{9,8},{10,9... | collective-permute-start | bytes 1032200 | tf_op jit(solution)/shard_map/ppermute | solution.py:74
  42.5 6.1 %collective-permute-start.13 = (bf16[1,32,5376]{2,1,0:T(8,128)(2,1)S(1)}, bf16[1,32,5376]{2,1,0:T(8,128)(2,1)S(1)}, u32[]{:S(2)}, u32[]{:S(2)}) collective-permute-start(bf16[1,32,5376]{2,1,0:T(8,128)(2,1)S(1)} %collective-permute-done.11.r2a), channel_id=1, source_target_pairs={{0,4},{4,0},{8,12},{12,8},{16,20},{20,16},{24,28},{28,24},{32,36},... | collective-permute-start | bytes 1032200 | tf_op jit(solution)/shard_map/ppermute | solution.py:30
  43.9 4.6 %collective-permute-start.14 = (bf16[1,32,5376]{2,1,0:T(8,128)(2,1)S(1)}, bf16[1,32,5376]{2,1,0:T(8,128)(2,1)S(1)}, u32[]{:S(2)}, u32[]{:S(2)}) collective-permute-start(bf16[1,32,5376]{2,1,0:T(8,128)(2,1)S(1)} %collective-permute-done.12.r2b), channel_id=1, source_target_pairs={{0,4},{4,0},{8,12},{12,8},{16,20},{20,16},{24,28},{28,24},{32,36},... | collective-permute-start | bytes 1032200 | tf_op jit(solution)/shard_map/ppermute | solution.py:30
  52.7 23.3 %collective-permute-start.16 = (bf16[2,4,168,256]{3,2,1,0:T(8,128)(2,1)S(1)}, bf16[2,4,168,256]{3,2,1,0:T(8,128)(2,1)S(1)}, u32[]{:S(2)}, u32[]{:S(2)}) collective-permute-start(bf16[2,4,168,256]{3,2,1,0:T(8,128)(2,1)S(1)} %get-tuple-element.71), channel_id=1, source_target_pairs={{0,8},{4,12},{8,0},{12,4},{16,24},{20,28},{24,16},{28,20},{32,40},... | collective-permute-start | bytes 2064392 | tf_op jit(solution)/shard_map/ppermute | solution.py:30
  60.3 19.8 %collective-permute-start.17 = (bf16[2,4,168,256]{3,2,1,0:T(8,128)(2,1)S(1)}, bf16[2,4,168,256]{3,2,1,0:T(8,128)(2,1)S(1)}, u32[]{:S(2)}, u32[]{:S(2)}) collective-permute-start(bf16[2,4,168,256]{3,2,1,0:T(8,128)(2,1)S(1)} %get-tuple-element.73), channel_id=1, source_target_pairs={{0,24},{4,28},{8,16},{12,20},{16,8},{20,12},{24,0},{28,4},{32,56},... | collective-permute-start | bytes 2064392 | tf_op jit(solution)/shard_map/ppermute | solution.py:30
  76.0 4.2 %copy-start.5 = (bf16[2,4,168,256]{3,2,1,0:T(8,128)(2,1)}, bf16[2,4,168,256]{3,2,1,0:T(8,128)(2,1)S(1)}, u32[]{:S(2)}) copy-start(bf16[2,4,168,256]{3,2,1,0:T(8,128)(2,1)S(1)} %collective-permute-done.16) | copy-start | bytes 2064388
  80.1 0.9 copy-start.6
  81.8 8.8 %collective-permute-start.21 = (bf16[4,168,256]{2,1,0:T(8,128)(2,1)}, bf16[4,168,256]{2,1,0:T(8,128)(2,1)}, u32[]{:S(2)}, u32[]{:S(2)}) collective-permute-start(bf16[4,168,256]{2,1,0:T(8,128)(2,1)} %fusion.17), channel_id=1, source_target_pairs={{0,8},{4,12},{8,0},{12,4},{16,24},{20,28},{24,16},{28,20},{32,40},... | collective-permute-start | bytes 1032200 | tf_op jit(solution)/shard_map/ppermute | solution.py:30
  81.8 26.4 %all-to-all-start = ((bf16[4,2,256,256]{3,2,1,0:T(8,128)(2,1)}), bf16[4,2,256,256]{3,2,1,0:T(8,128)(2,1)S(1)}, u32[]{:S(2)}, u32[]{:S(2)}) async-start(bf16[4,2,256,256]{3,2,1,0:T(8,128)(2,1)} %get-tuple-element.75), calls=%async_computation | async-start | bytes 2097152 | tf_op jit(solution)/shard_map/all_to_all | solution.py:64
  86.6 20.4 %collective-permute-start.20 = (bf16[4,168,256]{2,1,0:T(8,128)(2,1)}, bf16[4,168,256]{2,1,0:T(8,128)(2,1)}, u32[]{:S(2)}, u32[]{:S(2)}) collective-permute-start(bf16[4,168,256]{2,1,0:T(8,128)(2,1)} %fusion.16), channel_id=1, source_target_pairs={{0,24},{4,28},{8,16},{12,20},{16,8},{20,12},{24,0},{28,4},{32,56},... | collective-permute-start | bytes 1032200 | tf_op jit(solution)/shard_map/ppermute | solution.py:30
  92.6 16.6 %copy-start.4 = (bf16[4,168,256]{2,1,0:T(8,128)(2,1)S(1)}, bf16[4,168,256]{2,1,0:T(8,128)(2,1)}, u32[]{:S(2)}) copy-start(bf16[4,168,256]{2,1,0:T(8,128)(2,1)} %fusion) | copy-start | bytes 1032196
  109.2 8.3 %collective-permute-start.18 = (bf16[2,256,256]{2,1,0:T(8,128)(2,1)}, bf16[2,256,256]{2,1,0:T(8,128)(2,1)S(1)}, u32[]{:S(2)}, u32[]{:S(2)}) collective-permute-start(bf16[2,256,256]{2,1,0:T(8,128)(2,1)} %fusion.18), channel_id=1, source_target_pairs={{0,224},{4,228},{8,232},{12,236},{16,240},{20,244},{24,248},{28,25... | collective-permute-start | bytes 786440 | tf_op jit(solution)/shard_map/ppermute | solution.py:30
  110.1 22.3 %all-to-all-start.1 = ((bf16[8,168,256]{2,1,0:T(8,128)(2,1)}), bf16[8,168,256]{2,1,0:T(8,128)(2,1)S(1)}, u32[]{:S(2)}, u32[]{:S(2)}) async-start(bf16[8,168,256]{2,1,0:T(8,128)(2,1)} %pad_maximum_fusion), calls=%async_computation.1 | async-start | bytes 1376256 | tf_op jit(solution)/shard_map/all_to_all | solution.py:70
  114.0 7.1 %collective-permute-start.15 = (bf16[2,128,256]{2,1,0:T(8,128)(2,1)S(1)}, bf16[2,128,256]{2,1,0:T(8,128)(2,1)S(1)}, u32[]{:S(2)}, u32[]{:S(2)}) collective-permute-start(bf16[2,128,256]{2,1,0:T(8,128)(2,1)S(1)} %get-tuple-element.68), channel_id=1, source_target_pairs={{0,4},{4,0},{8,12},{12,8},{16,20},{20,16},{24,28},{28,24},{32,36},... | collective-permute-start | bytes 393224 | tf_op jit(solution)/shard_map/ppermute | solution.py:30
  117.7 4.4 %collective-permute-start.19 = (bf16[2,128,256]{2,1,0:T(8,128)(2,1)S(1)}, bf16[2,128,256]{2,1,0:T(8,128)(2,1)S(1)}, u32[]{:S(2)}, u32[]{:S(2)}) collective-permute-start(bf16[2,128,256]{2,1,0:T(8,128)(2,1)S(1)} %slice.130), channel_id=1, source_target_pairs={{0,4},{4,0},{8,12},{12,8},{16,20},{20,16},{24,28},{28,24},{32,36},... | collective-permute-start | bytes 393224 | tf_op jit(solution)/shard_map/ppermute | solution.py:30
  132.5 4.7 %collective-permute-start.22 = (f32[84,256]{1,0:T(8,128)S(1)}, f32[84,256]{1,0:T(8,128)S(1)}, u32[]{:S(2)}, u32[]{:S(2)}) collective-permute-start(f32[84,256]{1,0:T(8,128)S(1)} %slice_select_fusion), channel_id=1, source_target_pairs={{0,4},{4,0},{8,12},{12,8},{16,20},{20,16},{24,28},{28,24},{32,36},... | collective-permute-start | bytes 258056 | tf_op jit(solution)/shard_map/ppermute | solution.py:30

commit v3 on v2

--- a/solution.py
+++ b/solution.py
@@ -11,7 +11,6 @@
 CHIPS_Y = 4
 CHIPS_Z = 8
 TP = 4
-HALO_CHIPS = 4
 LOG2_E = 1.4426950408889634
 
 score_scale = 168.0 ** (-0.5)
@@ -34,11 +33,6 @@
     return ctx_shift(block, lambda i: i ^ 1)
 
 
-def chips_ahead(block, distance):
-    count = CORES * CHIPS_Y * CHIPS_Z
-    return ctx_shift(block, lambda i: (i + CORES * distance) % count)
-
-
 def y_pair(y):
     return y ^ 1
 
@@ -47,12 +41,13 @@
     return CHIPS_Y - 1 - y
 
 
-def y_route(block, target):
-    def move(i):
+def y_route(block, target, inner=False):
+    route = []
+    for i in range(CORES * CHIPS_Y * CHIPS_Z):
         core, y, z = i % CORES, i // CORES % CHIPS_Y, i // (CORES * CHIPS_Y)
-        return (z * CHIPS_Y + target(y)) * CORES + core
-
-    return ctx_shift(block, move)
+        if not inner or 0 < y < CHIPS_Y - 1:
+            route.append((i, (z * CHIPS_Y + target(y)) * CORES + core))
+    return lax.ppermute(block, "ctx", route)
 
 
 def y_exchange(blocks):
@@ -65,9 +60,21 @@
 
 
 def z_exchange(blocks):
-    lanes = CORES * CHIPS_Y
-    groups = [[z * lanes + lane for z in range(CHIPS_Z)] for lane in range(lanes)]
+    groups = [
+        [(z * CHIPS_Y + y) * CORES + core for z in range(CHIPS_Z) for core in range(CORES)]
+        for y in range(CHIPS_Y)
+    ]
     return lax.all_to_all(blocks, "ctx", 0, 0, axis_index_groups=groups, tiled=True)
+
+
+def y_ahead(block, distance):
+    return y_route(block, lambda y: (y + distance) % CHIPS_Y)
+
+
+def z_ahead(block, distance, other_core=False):
+    count = CORES * CHIPS_Y * CHIPS_Z
+    step = CORES * CHIPS_Y * distance
+    return ctx_shift(block, lambda i: (i + step) % count ^ int(other_core))
 
 
 def tp_ahead(block, distance):
@@ -206,11 +213,10 @@
 
 
 def backward_kernel(
-    scalars, mine, recv, kv0, kv1, kv2, kv3, kv4, weights, attn, d_attn,
-    dq_mine, dq_other, g_own, g_sent,
+    mine, recv, kv0, kv1, kv2, kv3, kv4, weights, attn, d_attn,
+    dq_mine, dq_other, g_own, g1, g2, g3, g4,
 ):
     rows = mine.shape[1]
-    y = scalars[2]
     heads = []
     for h in range(2):
         cols = slice(h * HEAD_SIZE, (h + 1) * HEAD_SIZE)
@@ -220,12 +226,13 @@
         delta = jnp.sum(product.T, axis=0, keepdims=True)
         heads.append((q, da, delta))
     dq = [None, None]
-    for d, kv in enumerate((kv0, kv1, kv2, kv3, kv4)):
+    grads = (g_own, g1, g2, g3, g4)
+    for kv_index, (kv, grad) in enumerate(zip((kv0, kv1, kv2, kv3, kv4), grads)):
         keys = kv[0, :, :HEAD_SIZE]
         values = kv[0, :, HEAD_SIZE:]
         dk = dv = None
         for h, (q, da, delta) in enumerate(heads):
-            w = weights[0, h, 2 * rows * d : 2 * rows * (d + 1), :]
+            w = weights[0, h, 2 * rows * kv_index : 2 * rows * (kv_index + 1), :]
             dp = dot(values, da, NT)
             ds = (w.astype(jnp.float32) * (dp - delta)).astype(jnp.bfloat16)
             v_part = dot(w, da)
@@ -234,18 +241,62 @@
             dv = v_part if dv is None else dv + v_part
             dk = k_part if dk is None else dk + k_part
             dq[h] = q_part if dq[h] is None else dq[h] + q_part
-        if d == 0:
-            g_own[0, :, :HEAD_SIZE] = dk * score_scale
-            g_own[0, :, HEAD_SIZE:] = dv
-        else:
-            column = (y + CHIPS_Y - d) % CHIPS_Y
-            g_sent[column, 0, :, :HEAD_SIZE] = (dk * score_scale).astype(jnp.bfloat16)
-            g_sent[column, 0, :, HEAD_SIZE:] = dv.astype(jnp.bfloat16)
+        grad[0, :, :HEAD_SIZE] = (dk * score_scale).astype(grad.dtype)
+        grad[0, :, HEAD_SIZE:] = dv.astype(grad.dtype)
     for h in range(2):
         cols = slice(h * HEAD_SIZE, (h + 1) * HEAD_SIZE)
         full = (dq[h].T * score_scale).astype(jnp.bfloat16)
         dq_mine[0, :, cols] = full[:rows]
         dq_other[0, :, cols] = full[rows:]
+
+
+def merge_kernel(kept_a, got_a, last_a, kept_b, got_b, last_b, out):
+    half = kept_a.shape[1]
+    rows = out.shape[1]
+    for part, (kept, got, last) in enumerate(((kept_a, got_a, last_a), (kept_b, got_b, last_b))):
+        for z in range(half):
+            total = (
+                kept[0, z].astype(jnp.float32)
+                + got[0, z].astype(jnp.float32)
+                + last[z].astype(jnp.float32)
+            )
+            for core in range(CORES):
+                slot = CORES * (half * part + z) + core
+                out[slot] = total[core * rows : (core + 1) * rows].astype(jnp.bfloat16)
+
+
+def finish_kernel(blocks, out):
+    width = blocks.shape[2]
+    for core in range(CORES):
+        total = blocks[core].astype(jnp.float32)
+        for z in range(1, CHIPS_Z):
+            total = total + blocks[CORES * z + core].astype(jnp.float32)
+        out[:, core * width : (core + 1) * width] = total
+
+
+def merge(kept_a, got_a, last_a, kept_b, got_b, last_b):
+    _, half, rows, width = kept_a.shape
+    front = pl.BlockSpec((1, half, rows, width), lambda i: (0, 0, 0, 0))
+    flat = pl.BlockSpec((half, rows, width), lambda i: (0, 0, 0))
+    shape = (CORES * 2 * half, rows // CORES, width)
+    return pl.pallas_call(
+        merge_kernel,
+        out_shape=jax.ShapeDtypeStruct(shape, jnp.bfloat16),
+        grid=(1,),
+        in_specs=[front, front, flat] * 2,
+        out_specs=pl.BlockSpec(shape, lambda i: (0, 0, 0)),
+        compiler_params=pltpu.CompilerParams(vmem_limit_bytes=16 << 20),
+        name="projection_merge",
+    )(kept_a, got_a, last_a, kept_b, got_b, last_b)
+
+
+def finish(blocks):
+    count, rows, width = blocks.shape
+    return pl.pallas_call(
+        finish_kernel,
+        out_shape=jax.ShapeDtypeStruct((rows, CORES * width), jnp.float32),
+        name="projection_finish",
+    )(blocks)
 
 
 def by_seq(shape):
@@ -352,28 +403,21 @@
     )(scalars, *pieces, *rows_t, attn, *early, o_weight)
 
 
-def backward(scalars, mine, recv, kvs, weights, attn, d_attn):
+def backward(mine, recv, kvs, weights, attn, d_attn):
     seqs, rows, width = mine.shape
     half = jax.ShapeDtypeStruct((seqs, rows, width // 2), jnp.bfloat16)
     shape = kvs[0].shape
     own = jax.ShapeDtypeStruct(shape, jnp.float32)
-    sent = jax.ShapeDtypeStruct((CHIPS_Y,) + shape, jnp.bfloat16)
+    sent = jax.ShapeDtypeStruct(shape, jnp.bfloat16)
+    outs = (half, half, own) + (sent,) * (len(kvs) - 1)
     query_spec = pl.BlockSpec((1, rows, width // 2), lambda s, *_: (s, 0, 0))
     return pl.pallas_call(
         backward_kernel,
-        out_shape=(half, half, own, sent),
-        grid_spec=pltpu.PrefetchScalarGridSpec(
-            num_scalar_prefetch=1,
-            grid=(seqs,),
-            in_specs=[query_spec, query_spec]
-            + [by_seq(a.shape) for a in (*kvs, weights, attn, d_attn)],
-            out_specs=[
-                by_seq(half.shape),
-                by_seq(half.shape),
-                by_seq(own.shape),
-                pl.BlockSpec((CHIPS_Y, 1) + shape[1:], lambda s, *_: (0, s, 0, 0)),
-            ],
-        ),
+        out_shape=outs,
+        grid=(seqs,),
+        in_specs=[query_spec, query_spec]
+        + [by_seq(a.shape) for a in (*kvs, weights, attn, d_attn)],
+        out_specs=[by_seq(o.shape) for o in outs],
         compiler_params=pltpu.CompilerParams(vmem_limit_bytes=20 << 20),
         cost_estimate=pl.CostEstimate(
             flops=10 * seqs * 2 * 2 * rows * 10 * rows * HEAD_SIZE,
@@ -381,7 +425,7 @@
             bytes_accessed=8 << 20,
         ),
         name="attention_backward",
-    )(scalars, mine, recv, *kvs, weights, attn, d_attn)
+    )(mine, recv, *kvs, weights, attn, d_attn)
 
 
 def local(query, key_states, value_state_rows, d_out, o_weight, doc_start):
@@ -404,28 +448,41 @@
         ]
         return jnp.concatenate(parts, axis=-1)
 
-    r3 = tp_ahead(d_out, 1)
-    r1 = tp_ahead(d_out, -1)
+    kv_width = 2 * HEAD_SIZE
+    first_seq, second_seq = d_out[:1], d_out[1:]
+    r3a = tp_ahead(first_seq, 1)
+    r1b = tp_ahead(second_seq, -1)
     mine = head_share(first)
-    recv = to_sibling(head_share(~first))
-    doc_mine = doc_start[:, None, :]
+    shared = head_share(~first)
+    z_same = z_ahead(mine[..., -kv_width:], 1)
+    z_other = z_ahead(shared[..., -kv_width:], 1, other_core=True)
+    recv = to_sibling(shared)
+    z_same, z_other, recv, r3a, r1b, first_seq, second_seq, doc_mine, rows = (
+        lax.optimization_barrier(
+            (z_same, z_other, recv, r3a, r1b, first_seq, second_seq, doc_start[:, None, :], d_out)
+        )
+    )
+    r3b = tp_ahead(second_seq, 1)
+    r1a = tp_ahead(first_seq, -1)
     doc_recv = to_sibling(doc_mine)
-    t0 = to_sibling(d_out)
-    recv, doc_recv, t0 = lax.optimization_barrier((recv, doc_recv, t0))
-
-    kv_width = 2 * HEAD_SIZE
+    t0 = to_sibling(rows)
     kv0 = jnp.concatenate([mine[..., -kv_width:], recv[..., -kv_width:]], axis=1)
-    kv1, kv2, kv3 = (chips_ahead(kv0, d) for d in (1, 2, 3))
+    kv4 = jnp.concatenate([z_same, z_other], axis=1)
+    kv1, kv3 = (y_ahead(jnp.where(y + d < CHIPS_Y, kv0, kv4), d) for d in (1, CHIPS_Y - 1))
     own, own_t = early_projection(scalars, [d_out, t0], o_weight)
 
-    r1, r3, own = lax.optimization_barrier((r1, r3, own))
-    r2a = tp_ahead(r3[:1], 1)
-    r2b = tp_ahead(r1[1:], -1)
-    kv1, kv2, kv3, kv_again, r1, r3 = lax.optimization_barrier((kv1, kv2, kv3, kv0, r1, r3))
-    kv4 = chips_ahead(kv_again, 4)
-    t1, t3, kv4 = lax.optimization_barrier((to_sibling(r1), to_sibling(r3), kv4))
-    near, near_t = early_projection(scalars, [r1, r3, t1, t3], o_weight)
-    kv1, near, r2a, r2b = lax.optimization_barrier((kv1, near, r2a, r2b))
+    near_rows = [r1a, r1b, r3a, r3b]
+    *near_rows, kv1, kv3, own, doc_recv = lax.optimization_barrier(
+        (*near_rows, kv1, kv3, own, doc_recv)
+    )
+    low = y_route(kv3, lambda y: y - 1, inner=True)
+    high = y_route(kv1, lambda y: y + 1, inner=True)
+    r2a = tp_ahead(near_rows[2], 1)
+    r2b = tp_ahead(near_rows[1], -1)
+    near_rows = near_rows + [to_sibling(r) for r in near_rows]
+    kv2 = jnp.where(y < CHIPS_Y // 2, low, high)
+    near, near_t = early_projection(scalars, near_rows, o_weight)
+    near, r2a, r2b = lax.optimization_barrier((near, r2a, r2b))
     kvs = [kv0, kv1, kv2, kv3, kv4]
     attn, weights = forward(scalars, mine, recv, kvs, doc_mine, doc_recv)
     d_attn, sent_a, kept_a, sent_b, kept_b = late_projection(
@@ -438,7 +495,10 @@
     )
     got_a = y_route(sent_a, y_pair)
     got_b = y_route(sent_b, y_mirror)
-    dq_mine, dq_other, g_own, g_sent = backward(scalars, mine, recv, kvs, weights, attn, d_attn)
+    dq_mine, dq_other, g_own, *g_sent, g_before = backward(
+        mine, recv, kvs, weights, attn, d_attn
+    )
+    got_a, got_b, g_own = lax.optimization_barrier((got_a, got_b, g_own))
     dq_recv = to_sibling(dq_other)
 
     def added(*blocks):
@@ -449,35 +509,25 @@
 
     next_a = added(kept_a[1], got_a[1]).astype(jnp.bfloat16)
     next_b = added(kept_b[1], got_b[1]).astype(jnp.bfloat16)
-    next_a, next_b, g_sent = lax.optimization_barrier((next_a, next_b, g_sent))
     last_a = y_route(next_a, y_mirror)
     last_b = y_route(next_b, y_pair)
-    g_columns = y_exchange(g_sent)
-    w_sum = jnp.concatenate(
-        [
-            added(kept_a[0], got_a[0], last_a).astype(jnp.bfloat16),
-            added(kept_b[0], got_b[0], last_b).astype(jnp.bfloat16),
-        ],
-        axis=0,
-    )
+    w_sum = merge(kept_a, got_a, last_a, kept_b, got_b, last_b)
+    w_sum, g_sent = lax.optimization_barrier((w_sum, g_sent))
     w_all = z_exchange(w_sum)
 
-    g_before = jnp.zeros(g_own.shape, jnp.float32)
     grads = g_own
-    for column in range(CHIPS_Y):
-        block = g_columns[column].astype(jnp.float32)
-        grads = grads + jnp.where(column > y, block, 0.0)
-        g_before = g_before + jnp.where(column > y, 0.0, block)
-    g_before = chips_ahead(g_before.astype(jnp.bfloat16), -HALO_CHIPS)
-    grads = (grads + g_before.astype(jnp.float32)).astype(jnp.bfloat16)
-    g_mine = grads[:, :shard_rows]
-    g_recv = to_sibling(grads[:, shard_rows:])
-
-    w_rows = jnp.sum(w_all.astype(jnp.float32), axis=0)
-    half_rows = w_rows.shape[0] // 2
-    w_top, w_bottom = w_rows[:half_rows], w_rows[half_rows:]
-    w_mine = jnp.where(first, w_top, w_bottom)
-    w_recv = to_sibling(jnp.where(first, w_bottom, w_top))
+    g_before = g_before.astype(jnp.float32)
+    for d, sent in enumerate(g_sent, 1):
+        block = y_ahead(sent, -d).astype(jnp.float32)
+        here = y + d < CHIPS_Y
+        grads = grads + jnp.where(here, block, 0.0)
+        g_before = g_before + jnp.where(here, 0.0, block)
+    g_before = g_before.astype(jnp.bfloat16)
+    z_same = z_ahead(g_before[:, :shard_rows], -1)
+    z_other = z_ahead(g_before[:, shard_rows:], -1, other_core=True)
+    sibling = to_sibling(grads[:, shard_rows:].astype(jnp.bfloat16))
+    g_mine = added(grads[:, :shard_rows], z_same).astype(jnp.bfloat16)
+    g_recv = added(sibling, z_other).astype(jnp.bfloat16)
 
     def by_core(own, other):
         return jnp.concatenate(
@@ -488,7 +538,7 @@
         by_core(dq_mine, dq_recv),
         by_core(g_mine[..., :HEAD_SIZE], g_recv[..., :HEAD_SIZE]),
         by_core(g_mine[..., HEAD_SIZE:], g_recv[..., HEAD_SIZE:]),
-        by_core(w_mine, w_recv),
+        finish(w_all),
     )
 
 

time: 138 us -> 142 us (1.029)
  local copies, waits for them, and re-layouts: 4.6 us -> 13.9 us
  starting transfers between devices: 51.8 us -> 44.4 us
  Pallas kernels: 21.1 us -> 27 us
  other arithmetic: 12 us -> 8.07 us
    ppermute x0 -> x11, waiting for transfers between devices: none -> 25 us  [y_route(): return lax.ppermute(block, 'ctx', route)]
    ppermute x19 -> x15, starting transfers between devices: 38.4 us -> 18.2 us  [ctx_shift(): return lax.ppermute(block, 'ctx', [(i, move(i)) for i in range(count)])]
    ppermute x19 -> x15, waiting for transfers between devices: 35.5 us -> 21.8 us  [ctx_shift(): return lax.ppermute(block, 'ctx', [(i, move(i)) for i in range(count)])]
    ppermute x0 -> x11, starting transfers between devices: none -> 12.7 us  [y_route(): return lax.ppermute(block, 'ctx', route)]
    all_to_all x1, waiting for transfers between devices: 9.58 us -> 0.01 us  [z_exchange(): lax.all_to_all(blocks, 'ctx', 0, 0, axis_index_groups=groups, tiled=True)]
    unnamed x14 -> x53, local copies, waits for them, and re-layouts: 4.53 us -> 12.7 us
    all_to_all x1 -> x0, starting transfers between devices: 4.8 us -> none  [y_exchange(): lax.all_to_all(blocks, 'ctx', 0, 0, axis_index_groups=groups, tiled=True)]
    convert_element_type x4 -> x2, other arithmetic: 4.3 us -> 0.06 us  [the longest x1 0.03 us: local(): g_recv = added(sibling, z_other).astype(jnp.bfloat16)]
  transfers between devices with their start and end apart: 25 -> 33, of which waited for: 13 -> 9; matrix products, arithmetic and copies ran while one was open for 7% -> 5% of each run, Pallas kernels for 12% -> 13%
where the time goes in v3:
time: 142 us; the launch traced here: 141 us
  waiting for transfers between devices  46.9 us (33%)
  starting transfers between devices  44.4 us (31%)
  Pallas kernels  27 us (19%)
  local copies, waits for them, and re-layouts  13.9 us (10%)
  other arithmetic  8.07 us (6%)
    ppermute x11, waiting for transfers between devices, y_route(): return lax.ppermute(block, 'ctx', route)  25 us
    ppermute x15, waiting for transfers between devices, ctx_shift(): return lax.ppermute(block, 'ctx', [(i, move(i)) for i in range(count)])  21.8 us
    ppermute x15, starting transfers between devices, ctx_shift(): return lax.ppermute(block, 'ctx', [(i, move(i)) for i in range(count)])  18.2 us
    unnamed x53, local copies, waits for them, and re-layouts  12.7 us
    ppermute x11, starting transfers between devices, y_route(): return lax.ppermute(block, 'ctx', route)  12.7 us
    pallas_call x2, Pallas kernels, early_projection(): pl.pallas_call(early_kernel, out_shape=outs, grid_spec=pltpu.PrefetchScal...  9.03 us
    ppermute x6, starting transfers between devices, tp_ahead(): lax.ppermute(block, 'tp', [(i, (i + distance) % TP) for i in range(TP)])  6.79 us
    all_to_all x1, starting transfers between devices, z_exchange(): lax.all_to_all(blocks, 'ctx', 0, 0, axis_index_groups=groups, tiled=True)  6.76 us
  transfers between devices with their start and end apart: 33, of which 9 were waited for; matrix products, arithmetic and copies ran while one was open for 5% of the time, Pallas kernels for 13%

profile of v3, /device:TPU:1, one launch (start us, length us, event | category | flops | bytes accessed | tf_op | source)
XLA Modules:
  0.0 141.3 jit_solution(1589235648375161588)
XLA Ops:
  0.7 1.7 %broadcast_select_fusion.3 = (bf16[2,128,256]{2,1,0:T(8,128)(2,1)S(1)}, bf16[2,128,256]{2,1,0:T(8,128)(2,1)}) fusion(pred[]{:T(512)S(6)} %not.3, bf16[2,128,512]{2,1,0:T(8,128)(2,1)} %param.6, pred[]{:T(512)S(6)} %eq.6), kind=kLoop, calls=%fused_computation.32 | loop fusion | flops 131072 | bytes 524290 | tf_op jit(solution)/shard_map/jit(_where)/select_n | solution.py:447
  2.4 1.0 broadcast_select_fusion.7
  3.4 3.3 %collective-permute-start.2 = (bf16[2,128,512]{2,1,0:T(8,128)(2,1)S(1)}, bf16[2,128,512]{2,1,0:T(8,128)(2,1)S(1)}, u32[]{:S(2)}, u32[]{:S(2)}) collective-permute-start(bf16[2,128,512]{2,1,0:T(8,128)(2,1)S(1)} %pad_maximum_fusion.1), channel_id=1, source_target_pairs={{0,4},{4,0},{8,12},{12,8},{16,20},{20,16},{24,28},{28,24},{32,36},... | collective-permute-start | bytes 786440 | tf_op jit(solution)/shard_map/ppermute | solution.py:29
  6.7 1.1 fusion.10
  7.9 2.7 %collective-permute-start.4 = (bf16[1,32,5376]{2,1,0:T(8,128)(2,1)S(1)}, bf16[1,32,5376]{2,1,0:T(8,128)(2,1)}, u32[]{:S(2)}, u32[]{:S(2)}) collective-permute-start(bf16[1,32,5376]{2,1,0:T(8,128)(2,1)S(1)} %get-tuple-element.53), channel_id=1, source_target_pairs={{0,3},{1,0},{2,1},{3,2},{4,7},{5,4},{6,5},{7,6},{8,11},{9,8},{10,9... | collective-permute-start | bytes 1032200 | tf_op jit(solution)/shard_map/ppermute | solution.py:81
  10.7 2.3 %collective-permute-start.1 = (bf16[2,128,256]{2,1,0:T(8,128)(2,1)S(1)}, bf16[2,128,256]{2,1,0:T(8,128)(2,1)S(1)}, u32[]{:S(2)}, u32[]{:S(2)}) collective-permute-start(bf16[2,128,256]{2,1,0:T(8,128)(2,1)S(1)} %pad_maximum_fusion.5), channel_id=1, source_target_pairs={{0,36},{4,32},{8,44},{12,40},{16,52},{20,48},{24,60},{28,56},{32,6... | collective-permute-start | bytes 393224 | tf_op jit(solution)/shard_map/ppermute | solution.py:29
  13.1 4.9 %collective-permute-done = bf16[2,128,256]{2,1,0:T(8,128)(2,1)S(1)} collective-permute-done((bf16[2,128,256]{2,1,0:T(8,128)(2,1)S(1)}, bf16[2,128,256]{2,1,0:T(8,128)(2,1)S(1)}, u32[]{:S(2)}, u32[]{:S(2)}) %collective-permute-start) | collective-permute-done | bytes 131104 | tf_op jit(solution)/shard_map/ppermute | solution.py:29
  18.0 3.1 %collective-permute-done.1 = bf16[2,128,256]{2,1,0:T(8,128)(2,1)S(1)} collective-permute-done((bf16[2,128,256]{2,1,0:T(8,128)(2,1)S(1)}, bf16[2,128,256]{2,1,0:T(8,128)(2,1)S(1)}, u32[]{:S(2)}, u32[]{:S(2)}) %collective-permute-start.1) | collective-permute-done | bytes 131104 | tf_op jit(solution)/shard_map/ppermute | solution.py:29
  21.4 1.3 collective-permute-start.5
  23.0 0.8 broadcast_select_fusion.1
  23.8 1.3 collective-permute-start.7
  25.1 1.4 %collective-permute-start.8 = (bf16[2,256,256]{2,1,0:T(8,128)(2,1)S(1)}, bf16[2,256,256]{2,1,0:T(8,128)(2,1)}, u32[]{:S(2)}, u32[]{:S(2)}) collective-permute-start(bf16[2,256,256]{2,1,0:T(8,128)(2,1)S(1)} %get-tuple-element.98), channel_id=1, source_target_pairs={{0,24},{4,28},{8,0},{12,4},{16,8},{20,12},{24,16},{28,20},{32,56},... | collective-permute-start | bytes 786440 | tf_op jit(solution)/shard_map/ppermute | solution.py:50
  26.5 1.5 %collective-permute-start.10 = (s32[2,1,128]{2,1,0:T(1,128)S(1)}, s32[2,1,128]{2,1,0:T(1,128)S(1)}, u32[]{:S(2)}, u32[]{:S(2)}) collective-permute-start(s32[2,1,128]{2,1,0:T(1,128)S(1)} %bitcast.9), channel_id=1, source_target_pairs={{0,4},{4,0},{8,12},{12,8},{16,20},{20,16},{24,28},{28,24},{32,36},... | collective-permute-start | bytes 3080 | tf_op jit(solution)/shard_map/ppermute | solution.py:29
  28.0 2.6 %copy-done = bf16[5376,512]{1,0:T(8,128)(2,1)S(1)} copy-done((bf16[5376,512]{1,0:T(8,128)(2,1)S(1)}, bf16[5376,512]{1,0:T(8,128)(2,1)}, u32[]{:S(2)}) %copy-start) | copy-done | bytes 5505048
  30.6 3.3 %projection_early.2 = (bf16[128,256]{1,0:T(8,128)(2,1)S(1)}, bf16[5376,128]{1,0:T(8,128)(2,1)S(1)}) custom-call(s32[4]{0:T(128)S(1)} %pad_add_fusion.scalars, bf16[2,32,5376]{2,1,0:T(8,128)(2,1)S(1)} %copy-done.5, bf16[2,32,5376]{2,1,0:T(8,128)(2,1)S(1)} %collective-permute-done.9.refs_1_, bf16[5376,512]{1,0:T(8,128)(2,1)S(1)} %copy-done), custom_call_target="tpu_custom_call" | custom-call | flops 3523215360 | bytes 12582912 | tf_op jit(solution)/shard_map/projection_early/pallas_call | solution.py:345
  33.9 1.1 copy-done.3
  36.9 2.5 %collective-permute-start.18 = (bf16[1,32,5376]{2,1,0:T(8,128)(2,1)}, bf16[1,32,5376]{2,1,0:T(8,128)(2,1)}, u32[]{:S(2)}, u32[]{:S(2)}) collective-permute-start(bf16[1,32,5376]{2,1,0:T(8,128)(2,1)} %collective-permute-done.4.refs_1_), channel_id=1, source_target_pairs={{0,3},{1,0},{2,1},{3,2},{4,7},{5,4},{6,5},{7,6},{8,11},{9,8},{10,9... | collective-permute-start | bytes 1032200 | tf_op jit(solution)/shard_map/ppermute | solution.py:81
  39.3 1.3 collective-permute-start.11
  40.6 1.4 collective-permute-start.12
  42.0 5.7 %projection_early.3 = (bf16[256,256]{1,0:T(8,128)(2,1)S(1)}, bf16[5376,256]{1,0:T(8,128)(2,1)S(1)}) custom-call(s32[4]{0:T(128)S(1)} %pad_add_fusion.scalars, bf16[1,32,5376]{2,1,0:T(8,128)(2,1)S(1)} %collective-permute-done.5.refs_0_, bf16[1,32,5376]{2,1,0:T(8,128)(2,1)} %collective-permute-done.4.refs_1_, ...), custom_call_target="tpu_custom_call" | custom-call | flops 7046430720 | bytes 12582912 | tf_op jit(solution)/shard_map/projection_early/pallas_call | solution.py:345
  48.4 0.7 pad_maximum_fusion.mine
  49.2 1.1 broadcast_select_fusion.kv2
  50.3 0.9 copy-done.6
  51.2 0.9 copy-done.8
  52.2 0.9 copy-done.11
  53.8 0.7 copy-done.17
  55.1 5.2 %attention_forward.1 = (bf16[2,256,256]{2,1,0:T(8,128)(2,1)S(1)}, bf16[2,2,1280,256]{3,2,1,0:T(8,128)(2,1)S(1)}) custom-call(s32[4]{0:T(128)S(1)} %copy-done.14, bf16[2,128,512]{2,1,0:T(8,128)(2,1)S(1)} %copy-done.6, bf16[2,128,512]{2,1,0:T(8,128)(2,1)S(1)} %copy-done.11, bf16[2,256,256]{2,1,0:T(8,128)(2,1)S(1)} %copy-done.8, ...), custom_call_target="tpu_custom_call" | custom-call | flops 671088640 | bytes 8388608 | tf_op jit(solution)/shard_map/attention_forward/pallas_call | solution.py:314
  60.3 2.6 %copy-done.2 = bf16[5376,512]{1,0:T(8,128)(2,1)S(1)} copy-done((bf16[5376,512]{1,0:T(8,128)(2,1)S(1)}, bf16[5376,512]{1,0:T(8,128)(2,1)}, u32[]{:S(2)}) %copy-start.2) | copy-done | bytes 5505048
  63.6 4.9 %projection_late.1 = (bf16[2,256,256]{2,1,0:T(8,128)(2,1)S(1)}, bf16[2,4,168,256]{3,2,1,0:T(8,128)(2,1)S(1)}, bf16[2,4,168,256]{3,2,1,0:T(8,128)(2,1)S(1)}, bf16...) custom-call(s32[4]{0:T(128)S(1)} %copy-done.15, bf16[1,32,5376]{2,1,0:T(8,128)(2,1)S(1)} %collective-permute-done.17.r2a, ...), custom_call_target="tpu_custom_call" | custom-call | flops 2113929216 | bytes 12582912 | tf_op jit(solution)/shard_map/projection_late/pallas_call | solution.py:379
  68.4 4.9 %collective-permute-start.22 = (bf16[2,4,168,256]{3,2,1,0:T(8,128)(2,1)S(1)}, bf16[2,4,168,256]{3,2,1,0:T(8,128)(2,1)S(1)}, u32[]{:S(2)}, u32[]{:S(2)}) collective-permute-start(bf16[2,4,168,256]{3,2,1,0:T(8,128)(2,1)S(1)} %get-tuple-element.78), channel_id=1, source_target_pairs={{0,8},{4,12},{8,0},{12,4},{16,24},{20,28},{24,16},{28,20},{32,40},... | collective-permute-start | bytes 2064392 | tf_op jit(solution)/shard_map/ppermute | solution.py:50
  73.3 4.8 %attention_backward.1 = (bf16[2,128,256]{2,1,0:T(8,128)(2,1)S(1)}, bf16[2,128,256]{2,1,0:T(8,128)(2,1)S(1)}, f32[2,256,256]{2,1,0:T(8,128)S(1)}, bf16[2,256,256]...) custom-call(bf16[2,128,512]{2,1,0:T(8,128)(2,1)S(1)} %copy-done.7, ...), custom_call_target="tpu_custom_call" | custom-call | flops 1677721600 | bytes 8388608 | tf_op jit(solution)/shard_map/attention_backward/pallas_call | solution.py:414
  78.1 10.6 %collective-permute-done.22.got_a = bf16[2,4,168,256]{3,2,1,0:T(8,128)(2,1)S(1)} collective-permute-done((bf16[2,4,168,256]{3,2,1,0:T(8,128)(2,1)S(1)}, bf16[2,4,168,256]{3,2,1,0:T(8,128)(2,1)S(1)}, u32[]{:S(2)}, u32[]{:S(2)}) %collective-permute-start.22) | collective-permute-done | bytes 688160 | tf_op jit(solution)/shard_map/ppermute | solution.py:50
  88.8 2.0 %collective-permute-done.23.got_b = bf16[2,4,168,256]{3,2,1,0:T(8,128)(2,1)S(1)} collective-permute-done((bf16[2,4,168,256]{3,2,1,0:T(8,128)(2,1)S(1)}, bf16[2,4,168,256]{3,2,1,0:T(8,128)(2,1)S(1)}, u32[]{:S(2)}, u32[]{:S(2)}) %collective-permute-start.23) | collective-permute-done | bytes 688160 | tf_op jit(solution)/shard_map/ppermute | solution.py:50
  91.2 9.0 %collective-permute-done.24.last_a = bf16[4,168,256]{2,1,0:T(8,128)(2,1)S(1)} collective-permute-done((bf16[4,168,256]{2,1,0:T(8,128)(2,1)S(1)}, bf16[4,168,256]{2,1,0:T(8,128)(2,1)S(1)}, u32[]{:S(2)}, u32[]{:S(2)}) %collective-permute-start.24) | collective-permute-done | bytes 344096 | tf_op jit(solution)/shard_map/ppermute | solution.py:50
  100.1 1.2 projection_merge.1
  101.3 1.4 collective-permute-start.26
  102.7 0.9 collective-permute-start.28
  103.6 3.3 %collective-permute-start.21 = (bf16[2,128,256]{2,1,0:T(8,128)(2,1)S(1)}, bf16[2,128,256]{2,1,0:T(8,128)(2,1)S(1)}, u32[]{:S(2)}, u32[]{:S(2)}) collective-permute-start(bf16[2,128,256]{2,1,0:T(8,128)(2,1)S(1)} %get-tuple-element.77), channel_id=1, source_target_pairs={{0,4},{4,0},{8,12},{12,8},{16,20},{20,16},{24,28},{28,24},{32,36},... | collective-permute-start | bytes 393224 | tf_op jit(solution)/shard_map/ppermute | solution.py:29
  106.9 6.8 %all-to-all-start = ((bf16[16,84,256]{2,1,0:T(8,128)(2,1)}), bf16[16,84,256]{2,1,0:T(8,128)(2,1)S(1)}, u32[]{:S(2)}, u32[]{:S(2)}) async-start(bf16[16,84,256]{2,1,0:T(8,128)(2,1)} %projection_merge.1), calls=%async_computation | async-start | bytes 1441792 | tf_op jit(solution)/shard_map/all_to_all | solution.py:67
  113.7 3.4 %collective-permute-done.28 = bf16[2,256,256]{2,1,0:T(8,128)(2,1)S(1)} collective-permute-done((bf16[2,256,256]{2,1,0:T(8,128)(2,1)S(1)}, bf16[2,256,256]{2,1,0:T(8,128)(2,1)S(1)}, u32[]{:S(2)}, u32[]{:S(2)}) %collective-permute-start.28) | collective-permute-done | bytes 262176 | tf_op jit(solution)/shard_map/ppermute | solution.py:50
  117.4 4.8 %collective-permute-start.31 = (bf16[2,128,256]{2,1,0:T(8,128)(2,1)S(1)}, bf16[2,128,256]{2,1,0:T(8,128)(2,1)S(1)}, u32[]{:S(2)}, u32[]{:S(2)}) collective-permute-start(bf16[2,128,256]{2,1,0:T(8,128)(2,1)S(1)} %get-tuple-element.105), channel_id=1, source_target_pairs={{0,228},{4,224},{8,236},{12,232},{16,244},{20,240},{24,252},{28,24... | collective-permute-start | bytes 393224 | tf_op jit(solution)/shard_map/ppermute | solution.py:29
  122.4 0.7 pad_maximum_fusion.3
  123.1 0.8 collective-permute-start.29
  123.9 11.1 %collective-permute-done.31 = bf16[2,128,256]{2,1,0:T(8,128)(2,1)S(1)} collective-permute-done((bf16[2,128,256]{2,1,0:T(8,128)(2,1)S(1)}, bf16[2,128,256]{2,1,0:T(8,128)(2,1)S(1)}, u32[]{:S(2)}, u32[]{:S(2)}) %collective-permute-start.31) | collective-permute-done | bytes 131104 | tf_op jit(solution)/shard_map/ppermute | solution.py:29
  135.0 2.1 %collective-permute-done.29 = bf16[2,128,256]{2,1,0:T(8,128)(2,1)S(1)} collective-permute-done((bf16[2,128,256]{2,1,0:T(8,128)(2,1)S(1)}, bf16[2,128,256]{2,1,0:T(8,128)(2,1)S(1)}, u32[]{:S(2)}, u32[]{:S(2)}) %collective-permute-start.29) | collective-permute-done | bytes 131104 | tf_op jit(solution)/shard_map/ppermute | solution.py:29
  137.2 0.7 pad_maximum_fusion.6
  138.5 0.9 copy-done.20
  139.4 1.9 %projection_finish.1 = f32[84,512]{1,0:T(8,128)} custom-call(bf16[16,84,256]{2,1,0:T(8,128)(2,1)} %copy-done.20), custom_call_target="tpu_custom_call" | custom-call | tf_op jit(solution)/shard_map/projection_finish/pallas_call | solution.py:295
  (102 shorter events, 6.6 us)
Async XLA Ops:
  0.6 20.5 %copy-start.5 = (bf16[2,32,5376]{2,1,0:T(8,128)(2,1)S(1)}, bf16[2,32,5376]{2,1,0:T(8,128)(2,1)}, u32[]{:S(2)}) copy-start(bf16[2,32,5376]{2,1,0:T(8,128)(2,1)} %refs_0_.1) | copy-start | bytes 2064388
  0.7 25.9 %copy-start.16 = (s32[2,128]{1,0:T(2,128)S(1)}, s32[2,128]{1,0:T(2,128)}, u32[]{:S(2)}) copy-start(s32[2,128]{1,0:T(2,128)} %param.11) | copy-start | bytes 3076
  3.3 30.6 %copy-start.21 = (bf16[2,128,128]{2,1,0:T(8,128)(2,1)}, bf16[2,128,128]{2,1,0:T(8,128)(2,1)S(1)}, u32[]{:S(2)}) copy-start(bf16[2,128,128]{2,1,0:T(8,128)(2,1)S(1)} %get-tuple-element.114) | copy-start | bytes 196612
  3.3 30.6 %copy-start.23 = (bf16[2,128,128]{2,1,0:T(8,128)(2,1)}, bf16[2,128,128]{2,1,0:T(8,128)(2,1)S(1)}, u32[]{:S(2)}) copy-start(bf16[2,128,128]{2,1,0:T(8,128)(2,1)S(1)} %get-tuple-element.115) | copy-start | bytes 196612
  3.4 17.7 %collective-permute-start.2 = (bf16[2,128,512]{2,1,0:T(8,128)(2,1)S(1)}, bf16[2,128,512]{2,1,0:T(8,128)(2,1)S(1)}, u32[]{:S(2)}, u32[]{:S(2)}) collective-permute-start(bf16[2,128,512]{2,1,0:T(8,128)(2,1)S(1)} %pad_maximum_fusion.1), channel_id=1, source_target_pairs={{0,4},{4,0},{8,12},{12,8},{16,20},{20,16},{24,28},{28,24},{32,36},... | collective-permute-start | bytes 786440 | tf_op jit(solution)/shard_map/ppermute | solution.py:29
  7.9 13.3 %collective-permute-start.3 = (bf16[1,32,5376]{2,1,0:T(8,128)(2,1)S(1)}, bf16[1,32,5376]{2,1,0:T(8,128)(2,1)}, u32[]{:S(2)}, u32[]{:S(2)}) collective-permute-start(bf16[1,32,5376]{2,1,0:T(8,128)(2,1)S(1)} %get-tuple-element.50), channel_id=1, source_target_pairs={{0,1},{1,2},{2,3},{3,0},{4,5},{5,6},{6,7},{7,4},{8,9},{9,10},{10,1... | collective-permute-start | bytes 1032200 | tf_op jit(solution)/shard_map/ppermute | solution.py:81
  7.9 13.2 %collective-permute-start.4 = (bf16[1,32,5376]{2,1,0:T(8,128)(2,1)S(1)}, bf16[1,32,5376]{2,1,0:T(8,128)(2,1)}, u32[]{:S(2)}, u32[]{:S(2)}) collective-permute-start(bf16[1,32,5376]{2,1,0:T(8,128)(2,1)S(1)} %get-tuple-element.53), channel_id=1, source_target_pairs={{0,3},{1,0},{2,1},{3,2},{4,7},{5,4},{6,5},{7,6},{8,11},{9,8},{10,9... | collective-permute-start | bytes 1032200 | tf_op jit(solution)/shard_map/ppermute | solution.py:81
  10.6 7.4 %collective-permute-start = (bf16[2,128,256]{2,1,0:T(8,128)(2,1)S(1)}, bf16[2,128,256]{2,1,0:T(8,128)(2,1)S(1)}, u32[]{:S(2)}, u32[]{:S(2)}) collective-permute-start(bf16[2,128,256]{2,1,0:T(8,128)(2,1)S(1)} %pad_maximum_fusion.4), channel_id=1, source_target_pairs={{0,32},{4,36},{8,40},{12,44},{16,48},{20,52},{24,56},{28,60},{32,6... | collective-permute-start | bytes 393224 | tf_op jit(solution)/shard_map/ppermute | solution.py:29
  10.7 10.4 %collective-permute-start.1 = (bf16[2,128,256]{2,1,0:T(8,128)(2,1)S(1)}, bf16[2,128,256]{2,1,0:T(8,128)(2,1)S(1)}, u32[]{:S(2)}, u32[]{:S(2)}) collective-permute-start(bf16[2,128,256]{2,1,0:T(8,128)(2,1)S(1)} %pad_maximum_fusion.5), channel_id=1, source_target_pairs={{0,36},{4,32},{8,44},{12,40},{16,52},{20,48},{24,60},{28,56},{32,6... | collective-permute-start | bytes 393224 | tf_op jit(solution)/shard_map/ppermute | solution.py:29
  21.1 12.8 %copy-start.10 = (bf16[2,128,512]{2,1,0:T(8,128)(2,1)}, bf16[2,128,512]{2,1,0:T(8,128)(2,1)S(1)}, u32[]{:S(2)}) copy-start(bf16[2,128,512]{2,1,0:T(8,128)(2,1)S(1)} %collective-permute-done.2.recv) | copy-start | bytes 786436
  21.1 5.4 %collective-permute-start.9 = (bf16[2,32,5376]{2,1,0:T(8,128)(2,1)S(1)}, bf16[2,32,5376]{2,1,0:T(8,128)(2,1)S(1)}, u32[]{:S(2)}, u32[]{:S(2)}) collective-permute-start(bf16[2,32,5376]{2,1,0:T(8,128)(2,1)S(1)} %copy-done.5), channel_id=1, source_target_pairs={{0,4},{4,0},{8,12},{12,8},{16,20},{20,16},{24,28},{28,24},{32,36},... | collective-permute-start | bytes 2064392 | tf_op jit(solution)/shard_map/ppermute | solution.py:29
  21.4 20.7 %copy-start.13 = (s32[4]{0:T(128)}, s32[4]{0:T(128)S(1)}, u32[]{:S(2)}) copy-start(s32[4]{0:T(128)S(1)} %pad_add_fusion.scalars) | copy-start | bytes 52
  21.4 13.7 %collective-permute-start.5 = (bf16[1,32,5376]{2,1,0:T(8,128)(2,1)S(1)}, bf16[1,32,5376]{2,1,0:T(8,128)(2,1)S(1)}, u32[]{:S(2)}, u32[]{:S(2)}) collective-permute-start(bf16[1,32,5376]{2,1,0:T(8,128)(2,1)S(1)} %get-tuple-element.50), channel_id=1, source_target_pairs={{0,3},{1,0},{2,1},{3,2},{4,7},{5,4},{6,5},{7,6},{8,11},{9,8},{10,9... | collective-permute-start | bytes 1032200 | tf_op jit(solution)/shard_map/ppermute | solution.py:81
  22.7 12.4 %collective-permute-start.6 = (bf16[1,32,5376]{2,1,0:T(8,128)(2,1)S(1)}, bf16[1,32,5376]{2,1,0:T(8,128)(2,1)S(1)}, u32[]{:S(2)}, u32[]{:S(2)}) collective-permute-start(bf16[1,32,5376]{2,1,0:T(8,128)(2,1)S(1)} %get-tuple-element.53), channel_id=1, source_target_pairs={{0,1},{1,2},{2,3},{3,0},{4,5},{5,6},{6,7},{7,4},{8,9},{9,10},{10,1... | collective-permute-start | bytes 1032200 | tf_op jit(solution)/shard_map/ppermute | solution.py:81
  23.8 11.3 %collective-permute-start.7 = (bf16[2,256,256]{2,1,0:T(8,128)(2,1)S(1)}, bf16[2,256,256]{2,1,0:T(8,128)(2,1)}, u32[]{:S(2)}, u32[]{:S(2)}) collective-permute-start(bf16[2,256,256]{2,1,0:T(8,128)(2,1)S(1)} %get-tuple-element.99), channel_id=1, source_target_pairs={{0,8},{4,12},{8,16},{12,20},{16,24},{20,28},{24,0},{28,4},{32,40},... | collective-permute-start | bytes 786440 | tf_op jit(solution)/shard_map/ppermute | solution.py:50
  25.1 10.0 %collective-permute-start.8 = (bf16[2,256,256]{2,1,0:T(8,128)(2,1)S(1)}, bf16[2,256,256]{2,1,0:T(8,128)(2,1)}, u32[]{:S(2)}, u32[]{:S(2)}) collective-permute-start(bf16[2,256,256]{2,1,0:T(8,128)(2,1)S(1)} %get-tuple-element.98), channel_id=1, source_target_pairs={{0,24},{4,28},{8,0},{12,4},{16,8},{20,12},{24,16},{28,20},{32,56},... | collective-permute-start | bytes 786440 | tf_op jit(solution)/shard_map/ppermute | solution.py:50
  26.5 8.5 %collective-permute-start.10 = (s32[2,1,128]{2,1,0:T(1,128)S(1)}, s32[2,1,128]{2,1,0:T(1,128)S(1)}, u32[]{:S(2)}, u32[]{:S(2)}) collective-permute-start(s32[2,1,128]{2,1,0:T(1,128)S(1)} %bitcast.9), channel_id=1, source_target_pairs={{0,4},{4,0},{8,12},{12,8},{16,20},{20,16},{24,28},{28,24},{32,36},... | collective-permute-start | bytes 3080 | tf_op jit(solution)/shard_map/ppermute | solution.py:29
  30.6 11.4 %copy-start.1 = (bf16[5376,512]{1,0:T(8,128)(2,1)S(1)}, bf16[5376,512]{1,0:T(8,128)(2,1)}, u32[]{:S(2)}) copy-start(bf16[5376,512]{1,0:T(8,128)(2,1)} %o_weight.1) | copy-start | bytes 16515076
  35.0 12.7 %copy-start.18 = (s32[2,1,128]{2,1,0:T(1,128)}, s32[2,1,128]{2,1,0:T(1,128)S(1)}, u32[]{:S(2)}) copy-start(s32[2,1,128]{2,1,0:T(1,128)S(1)} %collective-permute-done.10.doc_recv) | copy-start | bytes 3076
  35.1 13.3 %copy-start.22 = (bf16[2,128,128]{2,1,0:T(8,128)(2,1)S(1)}, bf16[2,128,128]{2,1,0:T(8,128)(2,1)}, u32[]{:S(2)}) copy-start(bf16[2,128,128]{2,1,0:T(8,128)(2,1)} %copy-done.21) | copy-start | bytes 196612
  35.1 13.3 %copy-start.24 = (bf16[2,128,128]{2,1,0:T(8,128)(2,1)S(1)}, bf16[2,128,128]{2,1,0:T(8,128)(2,1)}, u32[]{:S(2)}) copy-start(bf16[2,128,128]{2,1,0:T(8,128)(2,1)} %copy-done.23) | copy-start | bytes 196612
  35.1 13.3 %copy-start.25 = (bf16[2,128,256]{2,1,0:T(8,128)(2,1)S(1)}, bf16[2,128,256]{2,1,0:T(8,128)(2,1)}, u32[]{:S(2)}) copy-start(bf16[2,128,256]{2,1,0:T(8,128)(2,1)} %get-tuple-element.110) | copy-start | bytes 393220
  35.1 1.7 %collective-permute-start.13 = (bf16[1,32,5376]{2,1,0:T(8,128)(2,1)S(1)}, bf16[1,32,5376]{2,1,0:T(8,128)(2,1)S(1)}, u32[]{:S(2)}, u32[]{:S(2)}) collective-permute-start(bf16[1,32,5376]{2,1,0:T(8,128)(2,1)S(1)} %collective-permute-done.5.refs_0_), channel_id=1, source_target_pairs={{0,4},{4,0},{8,12},{12,8},{16,20},{20,16},{24,28},{28,24},{32,36},... | collective-permute-start | bytes 1032200 | tf_op jit(solution)/shard_map/ppermute | solution.py:29
  35.2 4.1 %collective-permute-start.14 = (bf16[1,32,5376]{2,1,0:T(8,128)(2,1)}, bf16[1,32,5376]{2,1,0:T(8,128)(2,1)S(1)}, u32[]{:S(2)}, u32[]{:S(2)}) collective-permute-start(bf16[1,32,5376]{2,1,0:T(8,128)(2,1)} %collective-permute-done.4.refs_1_), channel_id=1, source_target_pairs={{0,4},{4,0},{8,12},{12,8},{16,20},{20,16},{24,28},{28,24},{32,36},... | collective-permute-start | bytes 1032200 | tf_op jit(solution)/shard_map/ppermute | solution.py:29
  35.7 4.9 %collective-permute-start.15 = (bf16[1,32,5376]{2,1,0:T(8,128)(2,1)}, bf16[1,32,5376]{2,1,0:T(8,128)(2,1)S(1)}, u32[]{:S(2)}, u32[]{:S(2)}) collective-permute-start(bf16[1,32,5376]{2,1,0:T(8,128)(2,1)} %collective-permute-done.3.refs_2_), channel_id=1, source_target_pairs={{0,4},{4,0},{8,12},{12,8},{16,20},{20,16},{24,28},{28,24},{32,36},... | collective-permute-start | bytes 1032200 | tf_op jit(solution)/shard_map/ppermute | solution.py:29
  35.8 6.2 %collective-permute-start.16 = (bf16[1,32,5376]{2,1,0:T(8,128)(2,1)S(1)}, bf16[1,32,5376]{2,1,0:T(8,128)(2,1)S(1)}, u32[]{:S(2)}, u32[]{:S(2)}) collective-permute-start(bf16[1,32,5376]{2,1,0:T(8,128)(2,1)S(1)} %collective-permute-done.6.refs_3_), channel_id=1, source_target_pairs={{0,4},{4,0},{8,12},{12,8},{16,20},{20,16},{24,28},{28,24},{32,36},... | collective-permute-start | bytes 1032200 | tf_op jit(solution)/shard_map/ppermute | solution.py:29
  36.2 11.6 %collective-permute-start.17 = (bf16[1,32,5376]{2,1,0:T(8,128)(2,1)}, bf16[1,32,5376]{2,1,0:T(8,128)(2,1)S(1)}, u32[]{:S(2)}, u32[]{:S(2)}) collective-permute-start(bf16[1,32,5376]{2,1,0:T(8,128)(2,1)} %collective-permute-done.3.refs_2_), channel_id=1, source_target_pairs={{0,1},{1,2},{2,3},{3,0},{4,5},{5,6},{6,7},{7,4},{8,9},{9,10},{10,1... | collective-permute-start | bytes 1032200 | tf_op jit(solution)/shard_map/ppermute | solution.py:81
  36.9 10.9 %collective-permute-start.18 = (bf16[1,32,5376]{2,1,0:T(8,128)(2,1)}, bf16[1,32,5376]{2,1,0:T(8,128)(2,1)}, u32[]{:S(2)}, u32[]{:S(2)}) collective-permute-start(bf16[1,32,5376]{2,1,0:T(8,128)(2,1)} %collective-permute-done.4.refs_1_), channel_id=1, source_target_pairs={{0,3},{1,0},{2,1},{3,2},{4,7},{5,4},{6,5},{7,6},{8,11},{9,8},{10,9... | collective-permute-start | bytes 1032200 | tf_op jit(solution)/shard_map/ppermute | solution.py:81
  39.3 9.8 %collective-permute-start.11 = (bf16[2,256,256]{2,1,0:T(8,128)(2,1)}, bf16[2,256,256]{2,1,0:T(8,128)(2,1)}, u32[]{:S(2)}, u32[]{:S(2)}) collective-permute-start(bf16[2,256,256]{2,1,0:T(8,128)(2,1)} %collective-permute-done.8.kv3), channel_id=1, source_target_pairs={{8,0},{12,4},{16,8},{20,12},{40,32},{44,36},{48,40},{52,44},{72,64... | collective-permute-start | bytes 786440 | tf_op jit(solution)/shard_map/ppermute | solution.py:50
  40.6 8.5 %collective-permute-start.12 = (bf16[2,256,256]{2,1,0:T(8,128)(2,1)}, bf16[2,256,256]{2,1,0:T(8,128)(2,1)}, u32[]{:S(2)}, u32[]{:S(2)}) collective-permute-start(bf16[2,256,256]{2,1,0:T(8,128)(2,1)} %collective-permute-done.7.kv1), channel_id=1, source_target_pairs={{8,16},{12,20},{16,24},{20,28},{40,48},{44,52},{48,56},{52,60},{72... | collective-permute-start | bytes 786440 | tf_op jit(solution)/shard_map/ppermute | solution.py:50
  47.8 12.5 %collective-permute-start.19 = (bf16[1,32,5376]{2,1,0:T(8,128)(2,1)S(1)}, bf16[1,32,5376]{2,1,0:T(8,128)(2,1)}, u32[]{:S(2)}, u32[]{:S(2)}) collective-permute-start(bf16[1,32,5376]{2,1,0:T(8,128)(2,1)S(1)} %collective-permute-done.17.r2a), channel_id=1, source_target_pairs={{0,4},{4,0},{8,12},{12,8},{16,20},{20,16},{24,28},{28,24},{32,36},... | collective-permute-start | bytes 1032200 | tf_op jit(solution)/shard_map/ppermute | solution.py:29
  48.3 12.0 %collective-permute-start.20 = (bf16[1,32,5376]{2,1,0:T(8,128)(2,1)}, bf16[1,32,5376]{2,1,0:T(8,128)(2,1)}, u32[]{:S(2)}, u32[]{:S(2)}) collective-permute-start(bf16[1,32,5376]{2,1,0:T(8,128)(2,1)} %collective-permute-done.18.r2b), channel_id=1, source_target_pairs={{0,4},{4,0},{8,12},{12,8},{16,20},{20,16},{24,28},{28,24},{32,36},... | collective-permute-start | bytes 1032200 | tf_op jit(solution)/shard_map/ppermute | solution.py:29
  49.2 11.2 %copy-start.4 = (bf16[5376,128]{1,0:T(8,128)(2,1)S(1)}, bf16[5376,128]{1,0:T(8,128)(2,1)}, u32[]{:S(2)}) copy-start(bf16[5376,128]{1,0:T(8,128)(2,1)} %copy-done.3) | copy-start | bytes 4128772
  63.6 9.8 %copy-start.7 = (bf16[2,128,512]{2,1,0:T(8,128)(2,1)S(1)}, bf16[2,128,512]{2,1,0:T(8,128)(2,1)}, u32[]{:S(2)}) copy-start(bf16[2,128,512]{2,1,0:T(8,128)(2,1)} %pad_maximum_fusion.mine) | copy-start | bytes 786436
  63.6 9.8 %copy-start.9 = (bf16[2,256,256]{2,1,0:T(8,128)(2,1)S(1)}, bf16[2,256,256]{2,1,0:T(8,128)(2,1)}, u32[]{:S(2)}) copy-start(bf16[2,256,256]{2,1,0:T(8,128)(2,1)} %get-tuple-element.108.kv0) | copy-start | bytes 786436
  63.6 9.8 %copy-start.12 = (bf16[2,128,512]{2,1,0:T(8,128)(2,1)S(1)}, bf16[2,128,512]{2,1,0:T(8,128)(2,1)}, u32[]{:S(2)}) copy-start(bf16[2,128,512]{2,1,0:T(8,128)(2,1)} %copy-done.10) | copy-start | bytes 786436
  68.4 20.3 %collective-permute-start.22 = (bf16[2,4,168,256]{3,2,1,0:T(8,128)(2,1)S(1)}, bf16[2,4,168,256]{3,2,1,0:T(8,128)(2,1)S(1)}, u32[]{:S(2)}, u32[]{:S(2)}) collective-permute-start(bf16[2,4,168,256]{3,2,1,0:T(8,128)(2,1)S(1)} %get-tuple-element.78), channel_id=1, source_target_pairs={{0,8},{4,12},{8,0},{12,4},{16,24},{20,28},{24,16},{28,20},{32,40},... | collective-permute-start | bytes 2064392 | tf_op jit(solution)/shard_map/ppermute | solution.py:50
  73.3 17.5 %collective-permute-start.23 = (bf16[2,4,168,256]{3,2,1,0:T(8,128)(2,1)S(1)}, bf16[2,4,168,256]{3,2,1,0:T(8,128)(2,1)S(1)}, u32[]{:S(2)}, u32[]{:S(2)}) collective-permute-start(bf16[2,4,168,256]{3,2,1,0:T(8,128)(2,1)S(1)} %get-tuple-element.79), channel_id=1, source_target_pairs={{0,24},{4,28},{8,16},{12,20},{16,8},{20,12},{24,0},{28,4},{32,56},... | collective-permute-start | bytes 2064392 | tf_op jit(solution)/shard_map/ppermute | solution.py:50
  90.9 9.3 %collective-permute-start.24 = (bf16[4,168,256]{2,1,0:T(8,128)(2,1)S(1)}, bf16[4,168,256]{2,1,0:T(8,128)(2,1)S(1)}, u32[]{:S(2)}, u32[]{:S(2)}) collective-permute-start(bf16[4,168,256]{2,1,0:T(8,128)(2,1)S(1)} %fusion.7), channel_id=1, source_target_pairs={{0,24},{4,28},{8,16},{12,20},{16,8},{20,12},{24,0},{28,4},{32,56},... | collective-permute-start | bytes 1032200 | tf_op jit(solution)/shard_map/ppermute | solution.py:50
  91.1 9.1 %collective-permute-start.25 = (bf16[4,168,256]{2,1,0:T(8,128)(2,1)S(1)}, bf16[4,168,256]{2,1,0:T(8,128)(2,1)S(1)}, u32[]{:S(2)}, u32[]{:S(2)}) collective-permute-start(bf16[4,168,256]{2,1,0:T(8,128)(2,1)S(1)} %fusion.8), channel_id=1, source_target_pairs={{0,8},{4,12},{8,0},{12,4},{16,24},{20,28},{24,16},{28,20},{32,40},... | collective-permute-start | bytes 1032200 | tf_op jit(solution)/shard_map/ppermute | solution.py:50
  101.3 12.3 %collective-permute-start.26 = (bf16[2,256,256]{2,1,0:T(8,128)(2,1)S(1)}, bf16[2,256,256]{2,1,0:T(8,128)(2,1)S(1)}, u32[]{:S(2)}, u32[]{:S(2)}) collective-permute-start(bf16[2,256,256]{2,1,0:T(8,128)(2,1)S(1)} %get-tuple-element.89), channel_id=1, source_target_pairs={{0,24},{4,28},{8,0},{12,4},{16,8},{20,12},{24,16},{28,20},{32,56},... | collective-permute-start | bytes 786440 | tf_op jit(solution)/shard_map/ppermute | solution.py:50
  102.7 11.0 %collective-permute-start.27 = (bf16[2,256,256]{2,1,0:T(8,128)(2,1)S(1)}, bf16[2,256,256]{2,1,0:T(8,128)(2,1)S(1)}, u32[]{:S(2)}, u32[]{:S(2)}) collective-permute-start(bf16[2,256,256]{2,1,0:T(8,128)(2,1)S(1)} %get-tuple-element.90), channel_id=1, source_target_pairs={{0,16},{4,20},{8,24},{12,28},{16,0},{20,4},{24,8},{28,12},{32,48},... | collective-permute-start | bytes 786440 | tf_op jit(solution)/shard_map/ppermute | solution.py:50
  102.7 14.4 %collective-permute-start.28 = (bf16[2,256,256]{2,1,0:T(8,128)(2,1)S(1)}, bf16[2,256,256]{2,1,0:T(8,128)(2,1)S(1)}, u32[]{:S(2)}, u32[]{:S(2)}) collective-permute-start(bf16[2,256,256]{2,1,0:T(8,128)(2,1)S(1)} %get-tuple-element.91), channel_id=1, source_target_pairs={{0,8},{4,12},{8,16},{12,20},{16,24},{20,28},{24,0},{28,4},{32,40},... | collective-permute-start | bytes 786440 | tf_op jit(solution)/shard_map/ppermute | solution.py:50
  103.6 18.8 %collective-permute-start.21 = (bf16[2,128,256]{2,1,0:T(8,128)(2,1)S(1)}, bf16[2,128,256]{2,1,0:T(8,128)(2,1)S(1)}, u32[]{:S(2)}, u32[]{:S(2)}) collective-permute-start(bf16[2,128,256]{2,1,0:T(8,128)(2,1)S(1)} %get-tuple-element.77), channel_id=1, source_target_pairs={{0,4},{4,0},{8,12},{12,8},{16,20},{20,16},{24,28},{28,24},{32,36},... | collective-permute-start | bytes 393224 | tf_op jit(solution)/shard_map/ppermute | solution.py:29
  106.9 31.6 %all-to-all-start = ((bf16[16,84,256]{2,1,0:T(8,128)(2,1)}), bf16[16,84,256]{2,1,0:T(8,128)(2,1)S(1)}, u32[]{:S(2)}, u32[]{:S(2)}) async-start(bf16[16,84,256]{2,1,0:T(8,128)(2,1)} %projection_merge.1), calls=%async_computation | async-start | bytes 1441792 | tf_op jit(solution)/shard_map/all_to_all | solution.py:67
  117.4 17.6 %collective-permute-start.31 = (bf16[2,128,256]{2,1,0:T(8,128)(2,1)S(1)}, bf16[2,128,256]{2,1,0:T(8,128)(2,1)S(1)}, u32[]{:S(2)}, u32[]{:S(2)}) collective-permute-start(bf16[2,128,256]{2,1,0:T(8,128)(2,1)S(1)} %get-tuple-element.105), channel_id=1, source_target_pairs={{0,228},{4,224},{8,236},{12,232},{16,244},{20,240},{24,252},{28,24... | collective-permute-start | bytes 393224 | tf_op jit(solution)/shard_map/ppermute | solution.py:29
  122.2 12.7 %collective-permute-start.30 = (bf16[2,128,256]{2,1,0:T(8,128)(2,1)S(1)}, bf16[2,128,256]{2,1,0:T(8,128)(2,1)S(1)}, u32[]{:S(2)}, u32[]{:S(2)}) collective-permute-start(bf16[2,128,256]{2,1,0:T(8,128)(2,1)S(1)} %slice.132), channel_id=1, source_target_pairs={{0,4},{4,0},{8,12},{12,8},{16,20},{20,16},{24,28},{28,24},{32,36},... | collective-permute-start | bytes 393224 | tf_op jit(solution)/shard_map/ppermute | solution.py:29
  123.1 14.0 %collective-permute-start.29 = (bf16[2,128,256]{2,1,0:T(8,128)(2,1)S(1)}, bf16[2,128,256]{2,1,0:T(8,128)(2,1)S(1)}, u32[]{:S(2)}, u32[]{:S(2)}) collective-permute-start(bf16[2,128,256]{2,1,0:T(8,128)(2,1)S(1)} %get-tuple-element.104), channel_id=1, source_target_pairs={{0,224},{4,228},{8,232},{12,236},{16,240},{20,244},{24,248},{28,25... | collective-permute-start | bytes 393224 | tf_op jit(solution)/shard_map/ppermute | solution.py:29
  (11 other events, 12.6 us)

commit v4 on v3

--- a/solution.py
+++ b/solution.py
@@ -88,8 +88,16 @@
     return chip_pos + first + lane
 
 
-def forward_kernel(scalars, mine, recv, kv0, kv1, kv2, kv3, kv4, doc_mine, doc_recv, attn, weights):
-    core, chip_pos = scalars[0], scalars[3]
+def key_values(y, kv0, kv1, low, high, kv3, kv4):
+    kv2 = jnp.where(y < CHIPS_Y // 2, low[0], high[0])
+    return kv0[0], kv1[0], kv2, kv3[0], kv4[0]
+
+
+def forward_kernel(
+    scalars, mine, recv, kv0, kv1, low, high, kv3, kv4, doc_mine, doc_recv, attn, weights
+):
+    core, y, chip_pos = scalars[0], scalars[2], scalars[3]
+    kvs = key_values(y, kv0, kv1, low, high, kv3, kv4)
     rows = mine.shape[1]
     query_pos = query_positions(core, chip_pos, rows)
     doc = jnp.concatenate([doc_mine[0], doc_recv[0]], axis=1)
@@ -100,8 +108,8 @@
         cols = slice(h * HEAD_SIZE, (h + 1) * HEAD_SIZE)
         q = jnp.concatenate([mine[0, :, cols], recv[0, :, cols]], axis=0)
         scores = []
-        for d, kv in enumerate((kv0, kv1, kv2, kv3, kv4)):
-            s = dot(kv[0, :, :HEAD_SIZE], q, NT) * (score_scale * LOG2_E)
+        for d, kv in enumerate(kvs):
+            s = dot(kv[:, :HEAD_SIZE], q, NT) * (score_scale * LOG2_E)
             key_pos = offset + (chip_pos - 2 * rows * d)
             visible = key_pos >= lowest
             if d == 0:
@@ -117,10 +125,10 @@
             total = total + e
         inverse = 1.0 / jnp.sum(total, axis=0, keepdims=True)
         acc = None
-        for d, kv in enumerate((kv0, kv1, kv2, kv3, kv4)):
+        for d, kv in enumerate(kvs):
             w = (expo[d] * inverse).astype(jnp.bfloat16)
             weights[0, h, 2 * rows * d : 2 * rows * (d + 1), :] = w
-            part = dot(kv[0, :, HEAD_SIZE:], w, TN)
+            part = dot(kv[:, HEAD_SIZE:], w, TN)
             acc = part if acc is None else acc + part
         attn[0, :, cols] = acc.T.astype(jnp.bfloat16)
 
@@ -213,10 +221,11 @@
 
 
 def backward_kernel(
-    mine, recv, kv0, kv1, kv2, kv3, kv4, weights, attn, d_attn,
+    scalars, mine, recv, kv0, kv1, low, high, kv3, kv4, weights, attn, d_attn,
     dq_mine, dq_other, g_own, g1, g2, g3, g4,
 ):
     rows = mine.shape[1]
+    kvs = key_values(scalars[2], kv0, kv1, low, high, kv3, kv4)
     heads = []
     for h in range(2):
         cols = slice(h * HEAD_SIZE, (h + 1) * HEAD_SIZE)
@@ -227,9 +236,9 @@
         heads.append((q, da, delta))
     dq = [None, None]
     grads = (g_own, g1, g2, g3, g4)
-    for kv_index, (kv, grad) in enumerate(zip((kv0, kv1, kv2, kv3, kv4), grads)):
-        keys = kv[0, :, :HEAD_SIZE]
-        values = kv[0, :, HEAD_SIZE:]
+    for kv_index, (kv, grad) in enumerate(zip(kvs, grads)):
+        keys = kv[:, :HEAD_SIZE]
+        values = kv[:, HEAD_SIZE:]
         dk = dv = None
         for h, (q, da, delta) in enumerate(heads):
             w = weights[0, h, 2 * rows * kv_index : 2 * rows * (kv_index + 1), :]
@@ -295,29 +304,73 @@
     return pl.pallas_call(
         finish_kernel,
         out_shape=jax.ShapeDtypeStruct((rows, CORES * width), jnp.float32),
+        compiler_params=pltpu.CompilerParams(vmem_limit_bytes=16 << 20),
         name="projection_finish",
     )(blocks)
 
 
+def split_kernel(
+    scalars, q_own, q_other, k_own, k_other, v_own, v_other,
+    q_mine, sent, kv_mine, kv_sent,
+):
+    width = q_other.shape[2]
+    q_mine[...] = q_own[...]
+    sent[:, :, :width] = q_other[...]
+    sent[:, :, width : width + HEAD_SIZE] = k_other[...]
+    sent[:, :, width + HEAD_SIZE :] = v_other[...]
+    kv_mine[:, :, :HEAD_SIZE] = k_own[...]
+    kv_mine[:, :, HEAD_SIZE:] = v_own[...]
+    kv_sent[:, :, :HEAD_SIZE] = k_other[...]
+    kv_sent[:, :, HEAD_SIZE:] = v_other[...]
+
+
+def split_heads(scalars, query, keys, values):
+    seqs, rows, width = query.shape
+    out = jax.ShapeDtypeStruct((seqs, rows, width // 2), jnp.bfloat16)
+    whole = jax.ShapeDtypeStruct(query.shape, jnp.bfloat16)
+    outs = (out, whole, out, out)
+
+    def half(a):
+        shape = a.shape[:2] + (a.shape[2] // 2,)
+        return [
+            pl.BlockSpec(shape, lambda i, scalars: (0, 0, scalars[0])),
+            pl.BlockSpec(shape, lambda i, scalars: (0, 0, 1 - scalars[0])),
+        ]
+
+    return pl.pallas_call(
+        split_kernel,
+        out_shape=outs,
+        grid_spec=pltpu.PrefetchScalarGridSpec(
+            num_scalar_prefetch=1,
+            grid=(1,),
+            in_specs=half(query) + half(keys) + half(values),
+            out_specs=[pl.BlockSpec(o.shape, lambda i, *_: (0, 0, 0)) for o in outs],
+        ),
+        compiler_params=pltpu.CompilerParams(vmem_limit_bytes=16 << 20),
+        name="split_heads",
+    )(scalars, query, query, keys, keys, values, values)
+
+
 def by_seq(shape):
     return pl.BlockSpec((1,) + shape[1:], lambda s, *_: (s,) + (0,) * (len(shape) - 1))
 
 
 def forward(scalars, mine, recv, kvs, doc_mine, doc_recv):
     seqs, rows, width = mine.shape
-    keys = 2 * rows * len(kvs)
+    keys = 2 * rows * (len(kvs) - 1)
     outs = (
-        jax.ShapeDtypeStruct((seqs, 2 * rows, width // 2), jnp.bfloat16),
+        jax.ShapeDtypeStruct((seqs, 2 * rows, width), jnp.bfloat16),
         jax.ShapeDtypeStruct((seqs, 2, keys, 2 * rows), jnp.bfloat16),
     )
-    query_spec = pl.BlockSpec((1, rows, width // 2), lambda s, *_: (s, 0, 0))
+    query_spec = by_seq(mine.shape)
+    recv_spec = pl.BlockSpec((1, rows, width), lambda s, *_: (s, 0, 0))
     return pl.pallas_call(
         forward_kernel,
         out_shape=outs,
         grid_spec=pltpu.PrefetchScalarGridSpec(
             num_scalar_prefetch=1,
             grid=(seqs,),
-            in_specs=[query_spec, query_spec]
+            in_specs=[query_spec, recv_spec]
             + [by_seq(kv.shape) for kv in kvs]
             + [by_seq(doc_mine.shape), by_seq(doc_recv.shape)],
             out_specs=[by_seq(o.shape) for o in outs],
@@ -403,21 +456,25 @@
     )(scalars, *pieces, *rows_t, attn, *early, o_weight)
 
 
-def backward(mine, recv, kvs, weights, attn, d_attn):
+def backward(scalars, mine, recv, kvs, weights, attn, d_attn):
     seqs, rows, width = mine.shape
-    half = jax.ShapeDtypeStruct((seqs, rows, width // 2), jnp.bfloat16)
+    half = jax.ShapeDtypeStruct((seqs, rows, width), jnp.bfloat16)
     shape = kvs[0].shape
     own = jax.ShapeDtypeStruct(shape, jnp.float32)
     sent = jax.ShapeDtypeStruct(shape, jnp.bfloat16)
-    outs = (half, half, own) + (sent,) * (len(kvs) - 1)
-    query_spec = pl.BlockSpec((1, rows, width // 2), lambda s, *_: (s, 0, 0))
+    outs = (half, half, own) + (sent,) * CHIPS_Y
+    query_spec = by_seq(mine.shape)
+    recv_spec = pl.BlockSpec((1, rows, width), lambda s, *_: (s, 0, 0))
     return pl.pallas_call(
         backward_kernel,
         out_shape=outs,
-        grid=(seqs,),
-        in_specs=[query_spec, query_spec]
-        + [by_seq(a.shape) for a in (*kvs, weights, attn, d_attn)],
-        out_specs=[by_seq(o.shape) for o in outs],
+        grid_spec=pltpu.PrefetchScalarGridSpec(
+            num_scalar_prefetch=1,
+            grid=(seqs,),
+            in_specs=[query_spec, recv_spec]
+            + [by_seq(a.shape) for a in (*kvs, weights, attn, d_attn)],
+            out_specs=[by_seq(o.shape) for o in outs],
+        ),
         compiler_params=pltpu.CompilerParams(vmem_limit_bytes=20 << 20),
         cost_estimate=pl.CostEstimate(
             flops=10 * seqs * 2 * 2 * rows * 10 * rows * HEAD_SIZE,
@@ -425,7 +482,7 @@
             bytes_accessed=8 << 20,
         ),
         name="attention_backward",
-    )(mine, recv, *kvs, weights, attn, d_attn)
+    )(scalars, mine, recv, *kvs, weights, attn, d_attn)
 
 
 def local(query, key_states, value_state_rows, d_out, o_weight, doc_start):
@@ -437,54 +494,51 @@
     chip_pos = ctx // CORES * (CORES * shard_rows)
     scalars = jnp.stack([core, tp, y, chip_pos]).astype(jnp.int32)
     first = core == 0
-
-    def halves(a):
-        w = a.shape[-1] // 2
-        return a[..., :w], a[..., w:]
-
-    def head_share(core_zero):
-        parts = [
-            jnp.where(core_zero, *halves(a)) for a in (query, key_states, value_state_rows)
-        ]
-        return jnp.concatenate(parts, axis=-1)
-
-    kv_width = 2 * HEAD_SIZE
+    early_y = [y + d < CHIPS_Y for d in range(1, CHIPS_Y)]
+    q_mine, sent, kv_mine, kv_sent = split_heads(scalars, query, key_states, value_state_rows)
+
     first_seq, second_seq = d_out[:1], d_out[1:]
     r3a = tp_ahead(first_seq, 1)
     r1b = tp_ahead(second_seq, -1)
-    mine = head_share(first)
-    shared = head_share(~first)
-    z_same = z_ahead(mine[..., -kv_width:], 1)
-    z_other = z_ahead(shared[..., -kv_width:], 1, other_core=True)
-    recv = to_sibling(shared)
-    z_same, z_other, recv, r3a, r1b, first_seq, second_seq, doc_mine, rows = (
-        lax.optimization_barrier(
-            (z_same, z_other, recv, r3a, r1b, first_seq, second_seq, doc_start[:, None, :], d_out)
+    doc_mine = doc_start[:, None, :]
+    doc_recv = to_sibling(doc_mine)
+    z_same = z_ahead(kv_mine, 1)
+    z_other = z_ahead(kv_sent, 1, other_core=True)
+    recv = to_sibling(sent)
+    (
+        z_same, z_other, recv, r3a, r1b, first_seq, second_seq, rows, doc_recv,
+        scalars, first, *early_y,
+    ) = lax.optimization_barrier(
+        (
+            z_same, z_other, recv, r3a, r1b, first_seq, second_seq, d_out, doc_recv,
+            scalars, first, *early_y,
         )
     )
     r3b = tp_ahead(second_seq, 1)
     r1a = tp_ahead(first_seq, -1)
-    doc_recv = to_sibling(doc_mine)
-    t0 = to_sibling(rows)
-    kv0 = jnp.concatenate([mine[..., -kv_width:], recv[..., -kv_width:]], axis=1)
+    kv0 = jnp.concatenate([kv_mine, recv[..., -2 * HEAD_SIZE :]], axis=1)
     kv4 = jnp.concatenate([z_same, z_other], axis=1)
-    kv1, kv3 = (y_ahead(jnp.where(y + d < CHIPS_Y, kv0, kv4), d) for d in (1, CHIPS_Y - 1))
+    kv_next = jnp.where(early_y[0], kv0, kv4)
+    kv_back = jnp.where(early_y[2], kv0, kv4)
+    kv_next, kv_back, t0, t1b, t3a = lax.optimization_barrier(
+        (kv_next, kv_back, to_sibling(rows), to_sibling(r1b), to_sibling(r3a))
+    )
+    kv1, kv3 = y_ahead(kv_next, 1), y_ahead(kv_back, 3)
     own, own_t = early_projection(scalars, [d_out, t0], o_weight)
 
     near_rows = [r1a, r1b, r3a, r3b]
-    *near_rows, kv1, kv3, own, doc_recv = lax.optimization_barrier(
-        (*near_rows, kv1, kv3, own, doc_recv)
-    )
+    *near_rows, kv1, kv3, own = lax.optimization_barrier((*near_rows, kv1, kv3, own))
     low = y_route(kv3, lambda y: y - 1, inner=True)
     high = y_route(kv1, lambda y: y + 1, inner=True)
     r2a = tp_ahead(near_rows[2], 1)
     r2b = tp_ahead(near_rows[1], -1)
-    near_rows = near_rows + [to_sibling(r) for r in near_rows]
-    kv2 = jnp.where(y < CHIPS_Y // 2, low, high)
+    r1a, r1b, r3a, r3b = near_rows
+    near_rows = [r1a, r1b, r3a, r3b, to_sibling(r1a), t1b, t3a, to_sibling(r3b)]
+    *near_rows, low, high = lax.optimization_barrier((*near_rows, low, high))
     near, near_t = early_projection(scalars, near_rows, o_weight)
     near, r2a, r2b = lax.optimization_barrier((near, r2a, r2b))
-    kvs = [kv0, kv1, kv2, kv3, kv4]
-    attn, weights = forward(scalars, mine, recv, kvs, doc_mine, doc_recv)
+    kvs = [kv0, kv1, low, high, kv3, kv4]
+    attn, weights = forward(scalars, q_mine, recv, kvs, doc_mine, doc_recv)
     d_attn, sent_a, kept_a, sent_b, kept_b = late_projection(
         scalars,
         [r2a, r2b, to_sibling(r2a), to_sibling(r2b)],
@@ -496,7 +550,7 @@
     got_a = y_route(sent_a, y_pair)
     got_b = y_route(sent_b, y_mirror)
     dq_mine, dq_other, g_own, *g_sent, g_before = backward(
-        mine, recv, kvs, weights, attn, d_attn
+        scalars, q_mine, recv, kvs, weights, attn, d_attn
     )
     got_a, got_b, g_own = lax.optimization_barrier((got_a, got_b, g_own))
     dq_recv = to_sibling(dq_other)
@@ -512,16 +566,14 @@
     last_a = y_route(next_a, y_mirror)
     last_b = y_route(next_b, y_pair)
     w_sum = merge(kept_a, got_a, last_a, kept_b, got_b, last_b)
-    w_sum, g_sent = lax.optimization_barrier((w_sum, g_sent))
     w_all = z_exchange(w_sum)
 
     grads = g_own
     g_before = g_before.astype(jnp.float32)
     for d, sent in enumerate(g_sent, 1):
         block = y_ahead(sent, -d).astype(jnp.float32)
-        here = y + d < CHIPS_Y
-        grads = grads + jnp.where(here, block, 0.0)
-        g_before = g_before + jnp.where(here, 0.0, block)
+        grads = grads + jnp.where(early_y[d - 1], block, 0.0)
+        g_before = g_before + jnp.where(early_y[d - 1], 0.0, block)
     g_before = g_before.astype(jnp.bfloat16)
     z_same = z_ahead(g_before[:, :shard_rows], -1)
     z_other = z_ahead(g_before[:, shard_rows:], -1, other_core=True)

time: 142 us -> 138 us (0.972)
  starting transfers between devices: 44.4 us -> 54.4 us
  local copies, waits for them, and re-layouts: 13.9 us -> 6.59 us
  other arithmetic: 8.07 us -> 2.23 us
  Pallas kernels: 27 us -> 22.9 us
  waiting for transfers between devices: 46.9 us -> 50.7 us
    ppermute x11, starting transfers between devices: 12.7 us -> 21.6 us  [y_route(): return lax.ppermute(block, 'ctx', route)]
    unnamed x53 -> x15, local copies, waits for them, and re-layouts: 12.7 us -> 5.34 us
    ppermute x15, waiting for transfers between devices: 21.8 us -> 28.5 us  [ctx_shift(): return lax.ppermute(block, 'ctx', [(i, move(i)) for i in range(count)])]
    select_n x4 -> x1, other arithmetic: 4.57 us -> 0.12 us  [local(): kv_back = jnp.where(early_y[2], kv0, kv4)]
    ppermute x11, waiting for transfers between devices: 25 us -> 22.2 us  [y_route(): return lax.ppermute(block, 'ctx', route)]
    ppermute x6, starting transfers between devices: 6.79 us -> 9.38 us  [tp_ahead(): lax.ppermute(block, 'tp', [(i, (i + distance) % TP) for i in range(TP)])]
    ppermute x15, starting transfers between devices: 18.2 us -> 16 us  [ctx_shift(): return lax.ppermute(block, 'ctx', [(i, move(i)) for i in range(count)])]
    pallas_call x2, Pallas kernels: 9.03 us -> 7.6 us  [early_projection(): pl.pallas_call(early_kernel, out_shape=outs, grid_spec=pltpu.PrefetchScal...]
  transfers between devices with their start and end apart: 33 -> 33, of which waited for: 9 -> 14; matrix products, arithmetic and copies ran while one was open for 5% -> 2% of each run, Pallas kernels for 13% -> 13%
where the time goes in v4:
time: 138 us
  starting transfers between devices  54.4 us (39%)
  waiting for transfers between devices  50.7 us (37%)
  Pallas kernels  22.9 us (17%)
  local copies, waits for them, and re-layouts  6.59 us (5%)
  other arithmetic  2.23 us (2%)
    ppermute x15, waiting for transfers between devices, ctx_shift(): return lax.ppermute(block, 'ctx', [(i, move(i)) for i in range(count)])  28.5 us
    ppermute x11, waiting for transfers between devices, y_route(): return lax.ppermute(block, 'ctx', route)  22.2 us
    ppermute x11, starting transfers between devices, y_route(): return lax.ppermute(block, 'ctx', route)  21.6 us
    ppermute x15, starting transfers between devices, ctx_shift(): return lax.ppermute(block, 'ctx', [(i, move(i)) for i in range(count)])  16 us
    ppermute x6, starting transfers between devices, tp_ahead(): lax.ppermute(block, 'tp', [(i, (i + distance) % TP) for i in range(TP)])  9.38 us
    pallas_call x2, Pallas kernels, early_projection(): pl.pallas_call(early_kernel, out_shape=outs, grid_spec=pltpu.PrefetchScal...  7.6 us
    all_to_all x1, starting transfers between devices, z_exchange(): lax.all_to_all(blocks, 'ctx', 0, 0, axis_index_groups=groups, tiled=True)  7.39 us
    unnamed x15, local copies, waits for them, and re-layouts  5.34 us
  transfers between devices with their start and end apart: 33, of which 14 were waited for; matrix products, arithmetic and copies ran while one was open for 2% of the time, Pallas kernels for 13%

profile of v4, /device:TPU:1, one launch (start us, length us, event | category | flops | bytes accessed | tf_op | source)
XLA Modules:
  0.0 137.6 jit_solution(12091538281965205792)
XLA Ops:
  0.6 1.2 fusion.10
  1.8 3.4 %collective-permute-start.4 = (bf16[1,32,5376]{2,1,0:T(8,128)(2,1)S(1)}, bf16[1,32,5376]{2,1,0:T(8,128)(2,1)S(1)}, u32[]{:S(2)}, u32[]{:S(2)}) collective-permute-start(bf16[1,32,5376]{2,1,0:T(8,128)(2,1)S(1)} %get-tuple-element.78), channel_id=1, source_target_pairs={{0,3},{1,0},{2,1},{3,2},{4,7},{5,4},{6,5},{7,6},{8,11},{9,8},{10,9... | collective-permute-start | bytes 1032200 | tf_op jit(solution)/shard_map/ppermute | solution.py:81
  5.3 0.9 copy-done.2
  6.3 0.9 copy-done.4
  7.2 0.9 copy-done.5
  8.1 0.7 split_heads.1
  8.7 2.0 %collective-permute-start.2 = (bf16[2,128,512]{2,1,0:T(8,128)(2,1)S(1)}, bf16[2,128,512]{2,1,0:T(8,128)(2,1)S(1)}, u32[]{:S(2)}, u32[]{:S(2)}) collective-permute-start(bf16[2,128,512]{2,1,0:T(8,128)(2,1)S(1)} %get-tuple-element.70), channel_id=1, source_target_pairs={{0,4},{4,0},{8,12},{12,8},{16,20},{20,16},{24,28},{28,24},{32,36},... | collective-permute-start | bytes 786440 | tf_op jit(solution)/shard_map/ppermute | solution.py:29
  10.9 0.9 collective-permute-start.1
  12.2 1.3 collective-permute-start
  13.5 6.3 %collective-permute-done.1 = bf16[2,128,256]{2,1,0:T(8,128)(2,1)S(1)} collective-permute-done((bf16[2,128,256]{2,1,0:T(8,128)(2,1)S(1)}, bf16[2,128,256]{2,1,0:T(8,128)(2,1)S(1)}, u32[]{:S(2)}, u32[]{:S(2)}) %collective-permute-start.1) | collective-permute-done | bytes 131104 | tf_op jit(solution)/shard_map/ppermute | solution.py:29
  19.7 2.0 %collective-permute-done = bf16[2,128,256]{2,1,0:T(8,128)(2,1)S(1)} collective-permute-done((bf16[2,128,256]{2,1,0:T(8,128)(2,1)S(1)}, bf16[2,128,256]{2,1,0:T(8,128)(2,1)S(1)}, u32[]{:S(2)}, u32[]{:S(2)}) %collective-permute-start) | collective-permute-done | bytes 131104 | tf_op jit(solution)/shard_map/ppermute | solution.py:29
  21.8 1.0 collective-permute-start.8
  22.8 3.0 %collective-permute-start.6 = (bf16[1,32,5376]{2,1,0:T(8,128)(2,1)S(1)}, bf16[1,32,5376]{2,1,0:T(8,128)(2,1)S(1)}, u32[]{:S(2)}, u32[]{:S(2)}) collective-permute-start(bf16[1,32,5376]{2,1,0:T(8,128)(2,1)S(1)} %get-tuple-element.75), channel_id=1, source_target_pairs={{0,3},{1,0},{2,1},{3,2},{4,7},{5,4},{6,5},{7,6},{8,11},{9,8},{10,9... | collective-permute-start | bytes 1032200 | tf_op jit(solution)/shard_map/ppermute | solution.py:81
  26.5 1.0 collective-permute-done.9.refs_5_
  28.0 1.3 collective-permute-start.11
  29.3 1.4 %collective-permute-start.12 = (bf16[2,256,256]{2,1,0:T(8,128)(2,1)S(1)}, bf16[2,256,256]{2,1,0:T(8,128)(2,1)S(1)}, u32[]{:S(2)}, u32[]{:S(2)}) collective-permute-start(bf16[2,256,256]{2,1,0:T(8,128)(2,1)S(1)} %get-tuple-element.85), channel_id=1, source_target_pairs={{0,24},{4,28},{8,0},{12,4},{16,8},{20,12},{24,16},{28,20},{32,56},... | collective-permute-start | bytes 786440 | tf_op jit(solution)/shard_map/ppermute | solution.py:50
  30.8 2.6 %copy-done = bf16[5376,512]{1,0:T(8,128)(2,1)S(1)} copy-done((bf16[5376,512]{1,0:T(8,128)(2,1)S(1)}, bf16[5376,512]{1,0:T(8,128)(2,1)}, u32[]{:S(2)}) %copy-start) | copy-done | bytes 5505048
  33.3 3.3 %projection_early.2 = (bf16[128,256]{1,0:T(8,128)(2,1)S(1)}, bf16[5376,128]{1,0:T(8,128)(2,1)S(1)}) custom-call(s32[4]{0:T(128)S(1)} %pad_add_fusion.scalars, bf16[2,32,5376]{2,1,0:T(8,128)(2,1)S(1)} %copy-done.3, bf16[2,32,5376]{2,1,0:T(8,128)(2,1)S(1)} %collective-permute-done.8.refs_1_, bf16[5376,512]{1,0:T(8,128)(2,1)S(1)} %copy-done), custom_call_target="tpu_custom_call" | custom-call | flops 3523215360 | bytes 12582912 | tf_op jit(solution)/shard_map/projection_early/pallas_call | solution.py:398
  37.0 1.1 collective-permute-start.13
  38.1 0.7 collective-permute-start.16
  38.8 1.3 collective-permute-start.15
  40.1 3.0 %collective-permute-start.18 = (bf16[1,32,5376]{2,1,0:T(8,128)(2,1)S(1)}, bf16[1,32,5376]{2,1,0:T(8,128)(2,1)S(1)}, u32[]{:S(2)}, u32[]{:S(2)}) collective-permute-start(bf16[1,32,5376]{2,1,0:T(8,128)(2,1)S(1)} %collective-permute-done.4.refs_1_), channel_id=1, source_target_pairs={{0,3},{1,0},{2,1},{3,2},{4,7},{5,4},{6,5},{7,6},{8,11},{9,8},{10,9... | collective-permute-start | bytes 1032200 | tf_op jit(solution)/shard_map/ppermute | solution.py:81
  43.0 7.0 %collective-permute-done.15.low = bf16[2,256,256]{2,1,0:T(8,128)(2,1)S(1)} collective-permute-done((bf16[2,256,256]{2,1,0:T(8,128)(2,1)S(1)}, bf16[2,256,256]{2,1,0:T(8,128)(2,1)S(1)}, u32[]{:S(2)}, u32[]{:S(2)}) %collective-permute-start.15) | collective-permute-done | bytes 262176 | tf_op jit(solution)/shard_map/ppermute | solution.py:50
  50.1 4.3 %projection_early.3 = (bf16[256,256]{1,0:T(8,128)(2,1)S(1)}, bf16[5376,256]{1,0:T(8,128)(2,1)S(1)}) custom-call(s32[4]{0:T(128)S(1)} %pad_add_fusion.scalars, bf16[1,32,5376]{2,1,0:T(8,128)(2,1)S(1)} %collective-permute-done.6.refs_0_, bf16[1,32,5376]{2,1,0:T(8,128)(2,1)S(1)} %collective-permute-done.4.refs_1_, ...), custom_call_target="tpu_custom_call" | custom-call | flops 7046430720 | bytes 12582912 | tf_op jit(solution)/shard_map/projection_early/pallas_call | solution.py:398
  54.4 1.4 %collective-permute-start.19 = (bf16[1,32,5376]{2,1,0:T(8,128)(2,1)S(1)}, bf16[1,32,5376]{2,1,0:T(8,128)(2,1)S(1)}, u32[]{:S(2)}, u32[]{:S(2)}) collective-permute-start(bf16[1,32,5376]{2,1,0:T(8,128)(2,1)S(1)} %collective-permute-done.17.r2a), channel_id=1, source_target_pairs={{0,4},{4,0},{8,12},{12,8},{16,20},{20,16},{24,28},{28,24},{32,36},... | collective-permute-start | bytes 1032200 | tf_op jit(solution)/shard_map/ppermute | solution.py:29
  56.0 4.2 %attention_forward.1 = (bf16[2,256,256]{2,1,0:T(8,128)(2,1)S(1)}, bf16[2,2,1280,256]{3,2,1,0:T(8,128)(2,1)S(1)}) custom-call(s32[4]{0:T(128)S(1)} %pad_add_fusion.scalars, bf16[2,128,256]{2,1,0:T(8,128)(2,1)S(1)} %get-tuple-element.73.mine, bf16[2,128,512]{2,1,0:T(8,128)(2,1)S(1)} %collective-permute-done.2.recv, ...), custom_call_target="tpu_custom_call" | custom-call | flops 671088640 | bytes 8388608 | tf_op jit(solution)/shard_map/attention_forward/pallas_call | solution.py:367
  60.2 4.1 %projection_late.1 = (bf16[2,256,256]{2,1,0:T(8,128)(2,1)S(1)}, bf16[2,4,168,256]{3,2,1,0:T(8,128)(2,1)S(1)}, bf16[2,4,168,256]{3,2,1,0:T(8,128)(2,1)S(1)}, bf16...) custom-call(s32[4]{0:T(128)S(1)} %pad_add_fusion.scalars, ...), custom_call_target="tpu_custom_call" | custom-call | flops 2113929216 | bytes 12582912 | tf_op jit(solution)/shard_map/projection_late/pallas_call | solution.py:432
  64.3 3.4 %collective-permute-start.22 = (bf16[2,4,168,256]{3,2,1,0:T(8,128)(2,1)S(1)}, bf16[2,4,168,256]{3,2,1,0:T(8,128)(2,1)S(1)}, u32[]{:S(2)}, u32[]{:S(2)}) collective-permute-start(bf16[2,4,168,256]{3,2,1,0:T(8,128)(2,1)S(1)} %get-tuple-element.119), channel_id=1, source_target_pairs={{0,8},{4,12},{8,0},{12,4},{16,24},{20,28},{24,16},{28,20},{32,40},... | collective-permute-start | bytes 2064392 | tf_op jit(solution)/shard_map/ppermute | solution.py:50
  67.8 2.8 %collective-permute-start.23 = (bf16[2,4,168,256]{3,2,1,0:T(8,128)(2,1)S(1)}, bf16[2,4,168,256]{3,2,1,0:T(8,128)(2,1)S(1)}, u32[]{:S(2)}, u32[]{:S(2)}) collective-permute-start(bf16[2,4,168,256]{3,2,1,0:T(8,128)(2,1)S(1)} %get-tuple-element.120), channel_id=1, source_target_pairs={{0,24},{4,28},{8,16},{12,20},{16,8},{20,12},{24,0},{28,4},{32,56},... | collective-permute-start | bytes 2064392 | tf_op jit(solution)/shard_map/ppermute | solution.py:50
  70.6 4.3 %attention_backward.1 = (bf16[2,128,256]{2,1,0:T(8,128)(2,1)S(1)}, bf16[2,128,256]{2,1,0:T(8,128)(2,1)S(1)}, f32[2,256,256]{2,1,0:T(8,128)S(1)}, bf16[2,256,256]...) custom-call(s32[4]{0:T(128)S(1)} %pad_add_fusion.scalars, ...), custom_call_target="tpu_custom_call" | custom-call | flops 1677721600 | bytes 8388608 | tf_op jit(solution)/shard_map/attention_backward/pallas_call | solution.py:468
  75.0 2.4 %collective-permute-start.25 = (bf16[2,256,256]{2,1,0:T(8,128)(2,1)S(1)}, bf16[2,256,256]{2,1,0:T(8,128)(2,1)S(1)}, u32[]{:S(2)}, u32[]{:S(2)}) collective-permute-start(bf16[2,256,256]{2,1,0:T(8,128)(2,1)S(1)} %get-tuple-element.125), channel_id=1, source_target_pairs={{0,16},{4,20},{8,24},{12,28},{16,0},{20,4},{24,8},{28,12},{32,48},... | collective-permute-start | bytes 786440 | tf_op jit(solution)/shard_map/ppermute | solution.py:50
  77.4 5.7 %collective-permute-done.22.got_a = bf16[2,4,168,256]{3,2,1,0:T(8,128)(2,1)S(1)} collective-permute-done((bf16[2,4,168,256]{3,2,1,0:T(8,128)(2,1)S(1)}, bf16[2,4,168,256]{3,2,1,0:T(8,128)(2,1)S(1)}, u32[]{:S(2)}, u32[]{:S(2)}) %collective-permute-start.22) | collective-permute-done | bytes 688160 | tf_op jit(solution)/shard_map/ppermute | solution.py:50
  83.1 2.3 %collective-permute-done.23.got_b = bf16[2,4,168,256]{3,2,1,0:T(8,128)(2,1)S(1)} collective-permute-done((bf16[2,4,168,256]{3,2,1,0:T(8,128)(2,1)S(1)}, bf16[2,4,168,256]{3,2,1,0:T(8,128)(2,1)S(1)}, u32[]{:S(2)}, u32[]{:S(2)}) %collective-permute-start.23) | collective-permute-done | bytes 688160 | tf_op jit(solution)/shard_map/ppermute | solution.py:50
  85.5 4.9 %collective-permute-start.31 = (bf16[4,168,256]{2,1,0:T(8,128)(2,1)S(1)}, bf16[4,168,256]{2,1,0:T(8,128)(2,1)S(1)}, u32[]{:S(2)}, u32[]{:S(2)}) collective-permute-start(bf16[4,168,256]{2,1,0:T(8,128)(2,1)S(1)} %fusion.8), channel_id=1, source_target_pairs={{0,8},{4,12},{8,0},{12,4},{16,24},{20,28},{24,16},{28,20},{32,40},... | collective-permute-start | bytes 1032200 | tf_op jit(solution)/shard_map/ppermute | solution.py:50
  90.5 3.4 %collective-permute-start.30 = (bf16[4,168,256]{2,1,0:T(8,128)(2,1)S(1)}, bf16[4,168,256]{2,1,0:T(8,128)(2,1)S(1)}, u32[]{:S(2)}, u32[]{:S(2)}) collective-permute-start(bf16[4,168,256]{2,1,0:T(8,128)(2,1)S(1)} %fusion.7), channel_id=1, source_target_pairs={{0,24},{4,28},{8,16},{12,20},{16,8},{20,12},{24,0},{28,4},{32,56},... | collective-permute-start | bytes 1032200 | tf_op jit(solution)/shard_map/ppermute | solution.py:50
  93.9 1.8 %collective-permute-done.24 = bf16[2,256,256]{2,1,0:T(8,128)(2,1)S(1)} collective-permute-done((bf16[2,256,256]{2,1,0:T(8,128)(2,1)S(1)}, bf16[2,256,256]{2,1,0:T(8,128)(2,1)S(1)}, u32[]{:S(2)}, u32[]{:S(2)}) %collective-permute-start.24) | collective-permute-done | bytes 262176 | tf_op jit(solution)/shard_map/ppermute | solution.py:50
  95.6 3.1 %collective-permute-start.21 = (bf16[2,128,256]{2,1,0:T(8,128)(2,1)S(1)}, bf16[2,128,256]{2,1,0:T(8,128)(2,1)S(1)}, u32[]{:S(2)}, u32[]{:S(2)}) collective-permute-start(bf16[2,128,256]{2,1,0:T(8,128)(2,1)S(1)} %get-tuple-element.118), channel_id=1, source_target_pairs={{0,4},{4,0},{8,12},{12,8},{16,20},{20,16},{24,28},{28,24},{32,36},... | collective-permute-start | bytes 393224 | tf_op jit(solution)/shard_map/ppermute | solution.py:29
  99.0 2.1 %collective-permute-done.31.last_b = bf16[4,168,256]{2,1,0:T(8,128)(2,1)S(1)} collective-permute-done((bf16[4,168,256]{2,1,0:T(8,128)(2,1)S(1)}, bf16[4,168,256]{2,1,0:T(8,128)(2,1)S(1)}, u32[]{:S(2)}, u32[]{:S(2)}) %collective-permute-start.31) | collective-permute-done | bytes 344096 | tf_op jit(solution)/shard_map/ppermute | solution.py:50
  101.1 2.9 %collective-permute-done.30.last_a = bf16[4,168,256]{2,1,0:T(8,128)(2,1)S(1)} collective-permute-done((bf16[4,168,256]{2,1,0:T(8,128)(2,1)S(1)}, bf16[4,168,256]{2,1,0:T(8,128)(2,1)S(1)}, u32[]{:S(2)}, u32[]{:S(2)}) %collective-permute-start.30) | collective-permute-done | bytes 344096 | tf_op jit(solution)/shard_map/ppermute | solution.py:50
  104.0 1.2 projection_merge.1
  105.2 7.4 %all-to-all-start = ((bf16[16,84,256]{2,1,0:T(8,128)(2,1)}), bf16[16,84,256]{2,1,0:T(8,128)(2,1)S(1)}, u32[]{:S(2)}, u32[]{:S(2)}) async-start(bf16[16,84,256]{2,1,0:T(8,128)(2,1)} %projection_merge.1), calls=%async_computation | async-start | bytes 1441792 | tf_op jit(solution)/shard_map/all_to_all | solution.py:67
  112.8 2.9 %collective-permute-start.29 = (bf16[2,128,256]{2,1,0:T(8,128)(2,1)S(1)}, bf16[2,128,256]{2,1,0:T(8,128)(2,1)S(1)}, u32[]{:S(2)}, u32[]{:S(2)}) collective-permute-start(bf16[2,128,256]{2,1,0:T(8,128)(2,1)S(1)} %get-tuple-element.143), channel_id=1, source_target_pairs={{0,228},{4,224},{8,236},{12,232},{16,244},{20,240},{24,252},{28,24... | collective-permute-start | bytes 393224 | tf_op jit(solution)/shard_map/ppermute | solution.py:29
  115.8 0.7 pad_maximum_fusion.1
  116.5 1.2 collective-permute-start.27
  117.7 16.2 %collective-permute-done.29 = bf16[2,128,256]{2,1,0:T(8,128)(2,1)S(1)} collective-permute-done((bf16[2,128,256]{2,1,0:T(8,128)(2,1)S(1)}, bf16[2,128,256]{2,1,0:T(8,128)(2,1)S(1)}, u32[]{:S(2)}, u32[]{:S(2)}) %collective-permute-start.29) | collective-permute-done | bytes 131104 | tf_op jit(solution)/shard_map/ppermute | solution.py:29
  133.9 2.1 %collective-permute-done.27 = bf16[2,128,256]{2,1,0:T(8,128)(2,1)S(1)} collective-permute-done((bf16[2,128,256]{2,1,0:T(8,128)(2,1)S(1)}, bf16[2,128,256]{2,1,0:T(8,128)(2,1)S(1)}, u32[]{:S(2)}, u32[]{:S(2)}) %collective-permute-start.27) | collective-permute-done | bytes 131104 | tf_op jit(solution)/shard_map/ppermute | solution.py:29
  136.1 0.7 pad_maximum_fusion.2
  136.9 0.8 projection_finish.1
  (57 shorter events, 3.1 us)
Async XLA Ops:
  0.6 30.1 %copy-start.3 = (bf16[2,32,5376]{2,1,0:T(8,128)(2,1)S(1)}, bf16[2,32,5376]{2,1,0:T(8,128)(2,1)}, u32[]{:S(2)}) copy-start(bf16[2,32,5376]{2,1,0:T(8,128)(2,1)} %refs_0_.1) | copy-start | bytes 2064388
  1.8 20.0 %collective-permute-start.4 = (bf16[1,32,5376]{2,1,0:T(8,128)(2,1)S(1)}, bf16[1,32,5376]{2,1,0:T(8,128)(2,1)S(1)}, u32[]{:S(2)}, u32[]{:S(2)}) collective-permute-start(bf16[1,32,5376]{2,1,0:T(8,128)(2,1)S(1)} %get-tuple-element.78), channel_id=1, source_target_pairs={{0,3},{1,0},{2,1},{3,2},{4,7},{5,4},{6,5},{7,6},{8,11},{9,8},{10,9... | collective-permute-start | bytes 1032200 | tf_op jit(solution)/shard_map/ppermute | solution.py:81
  5.2 16.6 %collective-permute-start.3 = (bf16[1,32,5376]{2,1,0:T(8,128)(2,1)S(1)}, bf16[1,32,5376]{2,1,0:T(8,128)(2,1)S(1)}, u32[]{:S(2)}, u32[]{:S(2)}) collective-permute-start(bf16[1,32,5376]{2,1,0:T(8,128)(2,1)S(1)} %get-tuple-element.75), channel_id=1, source_target_pairs={{0,1},{1,2},{2,3},{3,0},{4,5},{5,6},{6,7},{7,4},{8,9},{9,10},{10,1... | collective-permute-start | bytes 1032200 | tf_op jit(solution)/shard_map/ppermute | solution.py:81
  5.3 1.0 copy-start.2
  6.3 0.9 copy-start.4
  7.2 0.9 copy-start.5
  8.7 13.1 %collective-permute-start.2 = (bf16[2,128,512]{2,1,0:T(8,128)(2,1)S(1)}, bf16[2,128,512]{2,1,0:T(8,128)(2,1)S(1)}, u32[]{:S(2)}, u32[]{:S(2)}) collective-permute-start(bf16[2,128,512]{2,1,0:T(8,128)(2,1)S(1)} %get-tuple-element.70), channel_id=1, source_target_pairs={{0,4},{4,0},{8,12},{12,8},{16,20},{20,16},{24,28},{28,24},{32,36},... | collective-permute-start | bytes 786440 | tf_op jit(solution)/shard_map/ppermute | solution.py:29
  10.8 1.4 collective-permute-start.5
  10.9 8.9 %collective-permute-start.1 = (bf16[2,128,256]{2,1,0:T(8,128)(2,1)S(1)}, bf16[2,128,256]{2,1,0:T(8,128)(2,1)S(1)}, u32[]{:S(2)}, u32[]{:S(2)}) collective-permute-start(bf16[2,128,256]{2,1,0:T(8,128)(2,1)S(1)} %get-tuple-element.69), channel_id=1, source_target_pairs={{0,36},{4,32},{8,44},{12,40},{16,52},{20,48},{24,60},{28,56},{32,6... | collective-permute-start | bytes 393224 | tf_op jit(solution)/shard_map/ppermute | solution.py:29
  12.2 9.6 %collective-permute-start = (bf16[2,128,256]{2,1,0:T(8,128)(2,1)S(1)}, bf16[2,128,256]{2,1,0:T(8,128)(2,1)S(1)}, u32[]{:S(2)}, u32[]{:S(2)}) collective-permute-start(bf16[2,128,256]{2,1,0:T(8,128)(2,1)S(1)} %get-tuple-element.68), channel_id=1, source_target_pairs={{0,32},{4,36},{8,40},{12,44},{16,48},{20,52},{24,56},{28,60},{32,6... | collective-permute-start | bytes 393224 | tf_op jit(solution)/shard_map/ppermute | solution.py:29
  21.8 6.2 %collective-permute-start.8 = (bf16[2,32,5376]{2,1,0:T(8,128)(2,1)}, bf16[2,32,5376]{2,1,0:T(8,128)(2,1)S(1)}, u32[]{:S(2)}, u32[]{:S(2)}) collective-permute-start(bf16[2,32,5376]{2,1,0:T(8,128)(2,1)} %refs_0_.1), channel_id=1, source_target_pairs={{0,4},{4,0},{8,12},{12,8},{16,20},{20,16},{24,28},{28,24},{32,36},... | collective-permute-start | bytes 2064392 | tf_op jit(solution)/shard_map/ppermute | solution.py:29
  22.8 13.8 %collective-permute-start.6 = (bf16[1,32,5376]{2,1,0:T(8,128)(2,1)S(1)}, bf16[1,32,5376]{2,1,0:T(8,128)(2,1)S(1)}, u32[]{:S(2)}, u32[]{:S(2)}) collective-permute-start(bf16[1,32,5376]{2,1,0:T(8,128)(2,1)S(1)} %get-tuple-element.75), channel_id=1, source_target_pairs={{0,3},{1,0},{2,1},{3,2},{4,7},{5,4},{6,5},{7,6},{8,11},{9,8},{10,9... | collective-permute-start | bytes 1032200 | tf_op jit(solution)/shard_map/ppermute | solution.py:81
  25.9 10.8 %collective-permute-start.7 = (bf16[1,32,5376]{2,1,0:T(8,128)(2,1)S(1)}, bf16[1,32,5376]{2,1,0:T(8,128)(2,1)S(1)}, u32[]{:S(2)}, u32[]{:S(2)}) collective-permute-start(bf16[1,32,5376]{2,1,0:T(8,128)(2,1)S(1)} %get-tuple-element.78), channel_id=1, source_target_pairs={{0,1},{1,2},{2,3},{3,0},{4,5},{5,6},{6,7},{7,4},{8,9},{9,10},{10,1... | collective-permute-start | bytes 1032200 | tf_op jit(solution)/shard_map/ppermute | solution.py:81
  25.9 1.7 %collective-permute-start.9 = (bf16[1,32,5376]{2,1,0:T(8,128)(2,1)S(1)}, bf16[1,32,5376]{2,1,0:T(8,128)(2,1)S(1)}, u32[]{:S(2)}, u32[]{:S(2)}) collective-permute-start(bf16[1,32,5376]{2,1,0:T(8,128)(2,1)S(1)} %collective-permute-done.4.refs_1_), channel_id=1, source_target_pairs={{0,4},{4,0},{8,12},{12,8},{16,20},{20,16},{24,28},{28,24},{32,36},... | collective-permute-start | bytes 1032200 | tf_op jit(solution)/shard_map/ppermute | solution.py:29
  26.2 1.8 %collective-permute-start.10 = (bf16[1,32,5376]{2,1,0:T(8,128)(2,1)S(1)}, bf16[1,32,5376]{2,1,0:T(8,128)(2,1)S(1)}, u32[]{:S(2)}, u32[]{:S(2)}) collective-permute-start(bf16[1,32,5376]{2,1,0:T(8,128)(2,1)S(1)} %collective-permute-done.3.refs_2_), channel_id=1, source_target_pairs={{0,4},{4,0},{8,12},{12,8},{16,20},{20,16},{24,28},{28,24},{32,36},... | collective-permute-start | bytes 1032200 | tf_op jit(solution)/shard_map/ppermute | solution.py:29
  28.0 8.9 %collective-permute-start.11 = (bf16[2,256,256]{2,1,0:T(8,128)(2,1)S(1)}, bf16[2,256,256]{2,1,0:T(8,128)(2,1)S(1)}, u32[]{:S(2)}, u32[]{:S(2)}) collective-permute-start(bf16[2,256,256]{2,1,0:T(8,128)(2,1)S(1)} %get-tuple-element.84), channel_id=1, source_target_pairs={{0,8},{4,12},{8,16},{12,20},{16,24},{20,28},{24,0},{28,4},{32,40},... | collective-permute-start | bytes 786440 | tf_op jit(solution)/shard_map/ppermute | solution.py:50
  29.3 7.6 %collective-permute-start.12 = (bf16[2,256,256]{2,1,0:T(8,128)(2,1)S(1)}, bf16[2,256,256]{2,1,0:T(8,128)(2,1)S(1)}, u32[]{:S(2)}, u32[]{:S(2)}) collective-permute-start(bf16[2,256,256]{2,1,0:T(8,128)(2,1)S(1)} %get-tuple-element.85), channel_id=1, source_target_pairs={{0,24},{4,28},{8,0},{12,4},{16,8},{20,12},{24,16},{28,20},{32,56},... | collective-permute-start | bytes 786440 | tf_op jit(solution)/shard_map/ppermute | solution.py:50
  30.8 2.6 %copy-start = (bf16[5376,512]{1,0:T(8,128)(2,1)S(1)}, bf16[5376,512]{1,0:T(8,128)(2,1)}, u32[]{:S(2)}) copy-start(bf16[5376,512]{1,0:T(8,128)(2,1)} %o_weight.1) | copy-start | bytes 16515076
  33.3 16.8 %copy-start.1 = (bf16[5376,512]{1,0:T(8,128)(2,1)S(1)}, bf16[5376,512]{1,0:T(8,128)(2,1)}, u32[]{:S(2)}) copy-start(bf16[5376,512]{1,0:T(8,128)(2,1)} %o_weight.1) | copy-start | bytes 16515076
  37.0 19.0 %copy-start.6 = (s32[2,128]{1,0:T(2,128)S(1)}, s32[2,128]{1,0:T(2,128)}, u32[]{:S(2)}) copy-start(s32[2,128]{1,0:T(2,128)} %param.11) | copy-start | bytes 3076
  37.0 13.1 %collective-permute-start.13 = (bf16[1,32,5376]{2,1,0:T(8,128)(2,1)S(1)}, bf16[1,32,5376]{2,1,0:T(8,128)(2,1)S(1)}, u32[]{:S(2)}, u32[]{:S(2)}) collective-permute-start(bf16[1,32,5376]{2,1,0:T(8,128)(2,1)S(1)} %collective-permute-done.6.refs_0_), channel_id=1, source_target_pairs={{0,4},{4,0},{8,12},{12,8},{16,20},{20,16},{24,28},{28,24},{32,36},... | collective-permute-start | bytes 1032200 | tf_op jit(solution)/shard_map/ppermute | solution.py:29
  38.0 12.0 %collective-permute-start.14 = (bf16[1,32,5376]{2,1,0:T(8,128)(2,1)S(1)}, bf16[1,32,5376]{2,1,0:T(8,128)(2,1)S(1)}, u32[]{:S(2)}, u32[]{:S(2)}) collective-permute-start(bf16[1,32,5376]{2,1,0:T(8,128)(2,1)S(1)} %collective-permute-done.7.refs_3_), channel_id=1, source_target_pairs={{0,4},{4,0},{8,12},{12,8},{16,20},{20,16},{24,28},{28,24},{32,36},... | collective-permute-start | bytes 1032200 | tf_op jit(solution)/shard_map/ppermute | solution.py:29
  38.1 4.9 %collective-permute-start.16 = (bf16[2,256,256]{2,1,0:T(8,128)(2,1)S(1)}, bf16[2,256,256]{2,1,0:T(8,128)(2,1)S(1)}, u32[]{:S(2)}, u32[]{:S(2)}) collective-permute-start(bf16[2,256,256]{2,1,0:T(8,128)(2,1)S(1)} %collective-permute-done.11.kv1), channel_id=1, source_target_pairs={{8,16},{12,20},{16,24},{20,28},{40,48},{44,52},{48,56},{52,60},{72... | collective-permute-start | bytes 786440 | tf_op jit(solution)/shard_map/ppermute | solution.py:50
  38.8 11.3 %collective-permute-start.15 = (bf16[2,256,256]{2,1,0:T(8,128)(2,1)S(1)}, bf16[2,256,256]{2,1,0:T(8,128)(2,1)S(1)}, u32[]{:S(2)}, u32[]{:S(2)}) collective-permute-start(bf16[2,256,256]{2,1,0:T(8,128)(2,1)S(1)} %collective-permute-done.12.kv3), channel_id=1, source_target_pairs={{8,0},{12,4},{16,8},{20,12},{40,32},{44,36},{48,40},{52,44},{72,64... | collective-permute-start | bytes 786440 | tf_op jit(solution)/shard_map/ppermute | solution.py:50
  40.1 14.3 %collective-permute-start.18 = (bf16[1,32,5376]{2,1,0:T(8,128)(2,1)S(1)}, bf16[1,32,5376]{2,1,0:T(8,128)(2,1)S(1)}, u32[]{:S(2)}, u32[]{:S(2)}) collective-permute-start(bf16[1,32,5376]{2,1,0:T(8,128)(2,1)S(1)} %collective-permute-done.4.refs_1_), channel_id=1, source_target_pairs={{0,3},{1,0},{2,1},{3,2},{4,7},{5,4},{6,5},{7,6},{8,11},{9,8},{10,9... | collective-permute-start | bytes 1032200 | tf_op jit(solution)/shard_map/ppermute | solution.py:81
  43.0 11.4 %collective-permute-start.17 = (bf16[1,32,5376]{2,1,0:T(8,128)(2,1)S(1)}, bf16[1,32,5376]{2,1,0:T(8,128)(2,1)S(1)}, u32[]{:S(2)}, u32[]{:S(2)}) collective-permute-start(bf16[1,32,5376]{2,1,0:T(8,128)(2,1)S(1)} %collective-permute-done.3.refs_2_), channel_id=1, source_target_pairs={{0,1},{1,2},{2,3},{3,0},{4,5},{5,6},{6,7},{7,4},{8,9},{9,10},{10,1... | collective-permute-start | bytes 1032200 | tf_op jit(solution)/shard_map/ppermute | solution.py:81
  54.4 5.8 %collective-permute-start.19 = (bf16[1,32,5376]{2,1,0:T(8,128)(2,1)S(1)}, bf16[1,32,5376]{2,1,0:T(8,128)(2,1)S(1)}, u32[]{:S(2)}, u32[]{:S(2)}) collective-permute-start(bf16[1,32,5376]{2,1,0:T(8,128)(2,1)S(1)} %collective-permute-done.17.r2a), channel_id=1, source_target_pairs={{0,4},{4,0},{8,12},{12,8},{16,20},{20,16},{24,28},{28,24},{32,36},... | collective-permute-start | bytes 1032200 | tf_op jit(solution)/shard_map/ppermute | solution.py:29
  55.9 4.4 %collective-permute-start.20 = (bf16[1,32,5376]{2,1,0:T(8,128)(2,1)S(1)}, bf16[1,32,5376]{2,1,0:T(8,128)(2,1)S(1)}, u32[]{:S(2)}, u32[]{:S(2)}) collective-permute-start(bf16[1,32,5376]{2,1,0:T(8,128)(2,1)S(1)} %collective-permute-done.18.r2b), channel_id=1, source_target_pairs={{0,4},{4,0},{8,12},{12,8},{16,20},{20,16},{24,28},{28,24},{32,36},... | collective-permute-start | bytes 1032200 | tf_op jit(solution)/shard_map/ppermute | solution.py:29
  64.3 18.8 %collective-permute-start.22 = (bf16[2,4,168,256]{3,2,1,0:T(8,128)(2,1)S(1)}, bf16[2,4,168,256]{3,2,1,0:T(8,128)(2,1)S(1)}, u32[]{:S(2)}, u32[]{:S(2)}) collective-permute-start(bf16[2,4,168,256]{3,2,1,0:T(8,128)(2,1)S(1)} %get-tuple-element.119), channel_id=1, source_target_pairs={{0,8},{4,12},{8,0},{12,4},{16,24},{20,28},{24,16},{28,20},{32,40},... | collective-permute-start | bytes 2064392 | tf_op jit(solution)/shard_map/ppermute | solution.py:50
  67.8 17.7 %collective-permute-start.23 = (bf16[2,4,168,256]{3,2,1,0:T(8,128)(2,1)S(1)}, bf16[2,4,168,256]{3,2,1,0:T(8,128)(2,1)S(1)}, u32[]{:S(2)}, u32[]{:S(2)}) collective-permute-start(bf16[2,4,168,256]{3,2,1,0:T(8,128)(2,1)S(1)} %get-tuple-element.120), channel_id=1, source_target_pairs={{0,24},{4,28},{8,16},{12,20},{16,8},{20,12},{24,0},{28,4},{32,56},... | collective-permute-start | bytes 2064392 | tf_op jit(solution)/shard_map/ppermute | solution.py:50
  74.9 20.7 %collective-permute-start.24 = (bf16[2,256,256]{2,1,0:T(8,128)(2,1)S(1)}, bf16[2,256,256]{2,1,0:T(8,128)(2,1)S(1)}, u32[]{:S(2)}, u32[]{:S(2)}) collective-permute-start(bf16[2,256,256]{2,1,0:T(8,128)(2,1)S(1)} %get-tuple-element.123), channel_id=1, source_target_pairs={{0,24},{4,28},{8,0},{12,4},{16,8},{20,12},{24,16},{28,20},{32,56},... | collective-permute-start | bytes 786440 | tf_op jit(solution)/shard_map/ppermute | solution.py:50
  75.0 23.7 %collective-permute-start.25 = (bf16[2,256,256]{2,1,0:T(8,128)(2,1)S(1)}, bf16[2,256,256]{2,1,0:T(8,128)(2,1)S(1)}, u32[]{:S(2)}, u32[]{:S(2)}) collective-permute-start(bf16[2,256,256]{2,1,0:T(8,128)(2,1)S(1)} %get-tuple-element.125), channel_id=1, source_target_pairs={{0,16},{4,20},{8,24},{12,28},{16,0},{20,4},{24,8},{28,12},{32,48},... | collective-permute-start | bytes 786440 | tf_op jit(solution)/shard_map/ppermute | solution.py:50
  77.4 21.3 %collective-permute-start.26 = (bf16[2,256,256]{2,1,0:T(8,128)(2,1)S(1)}, bf16[2,256,256]{2,1,0:T(8,128)(2,1)S(1)}, u32[]{:S(2)}, u32[]{:S(2)}) collective-permute-start(bf16[2,256,256]{2,1,0:T(8,128)(2,1)S(1)} %get-tuple-element.126), channel_id=1, source_target_pairs={{0,8},{4,12},{8,16},{12,20},{16,24},{20,28},{24,0},{28,4},{32,40},... | collective-permute-start | bytes 786440 | tf_op jit(solution)/shard_map/ppermute | solution.py:50
  85.5 15.6 %collective-permute-start.31 = (bf16[4,168,256]{2,1,0:T(8,128)(2,1)S(1)}, bf16[4,168,256]{2,1,0:T(8,128)(2,1)S(1)}, u32[]{:S(2)}, u32[]{:S(2)}) collective-permute-start(bf16[4,168,256]{2,1,0:T(8,128)(2,1)S(1)} %fusion.8), channel_id=1, source_target_pairs={{0,8},{4,12},{8,0},{12,4},{16,24},{20,28},{24,16},{28,20},{32,40},... | collective-permute-start | bytes 1032200 | tf_op jit(solution)/shard_map/ppermute | solution.py:50
  90.5 13.6 %collective-permute-start.30 = (bf16[4,168,256]{2,1,0:T(8,128)(2,1)S(1)}, bf16[4,168,256]{2,1,0:T(8,128)(2,1)S(1)}, u32[]{:S(2)}, u32[]{:S(2)}) collective-permute-start(bf16[4,168,256]{2,1,0:T(8,128)(2,1)S(1)} %fusion.7), channel_id=1, source_target_pairs={{0,24},{4,28},{8,16},{12,20},{16,8},{20,12},{24,0},{28,4},{32,56},... | collective-permute-start | bytes 1032200 | tf_op jit(solution)/shard_map/ppermute | solution.py:50
  95.6 20.1 %collective-permute-start.21 = (bf16[2,128,256]{2,1,0:T(8,128)(2,1)S(1)}, bf16[2,128,256]{2,1,0:T(8,128)(2,1)S(1)}, u32[]{:S(2)}, u32[]{:S(2)}) collective-permute-start(bf16[2,128,256]{2,1,0:T(8,128)(2,1)S(1)} %get-tuple-element.118), channel_id=1, source_target_pairs={{0,4},{4,0},{8,12},{12,8},{16,20},{20,16},{24,28},{28,24},{32,36},... | collective-permute-start | bytes 393224 | tf_op jit(solution)/shard_map/ppermute | solution.py:29
  105.2 31.7 %all-to-all-start = ((bf16[16,84,256]{2,1,0:T(8,128)(2,1)}), bf16[16,84,256]{2,1,0:T(8,128)(2,1)S(1)}, u32[]{:S(2)}, u32[]{:S(2)}) async-start(bf16[16,84,256]{2,1,0:T(8,128)(2,1)} %projection_merge.1), calls=%async_computation | async-start | bytes 1441792 | tf_op jit(solution)/shard_map/all_to_all | solution.py:67
  112.6 5.0 %collective-permute-start.28 = (bf16[2,128,256]{2,1,0:T(8,128)(2,1)S(1)}, bf16[2,128,256]{2,1,0:T(8,128)(2,1)S(1)}, u32[]{:S(2)}, u32[]{:S(2)}) collective-permute-start(bf16[2,128,256]{2,1,0:T(8,128)(2,1)S(1)} %slice.85), channel_id=1, source_target_pairs={{0,4},{4,0},{8,12},{12,8},{16,20},{20,16},{24,28},{28,24},{32,36},... | collective-permute-start | bytes 393224 | tf_op jit(solution)/shard_map/ppermute | solution.py:29
  112.8 21.1 %collective-permute-start.29 = (bf16[2,128,256]{2,1,0:T(8,128)(2,1)S(1)}, bf16[2,128,256]{2,1,0:T(8,128)(2,1)S(1)}, u32[]{:S(2)}, u32[]{:S(2)}) collective-permute-start(bf16[2,128,256]{2,1,0:T(8,128)(2,1)S(1)} %get-tuple-element.143), channel_id=1, source_target_pairs={{0,228},{4,224},{8,236},{12,232},{16,244},{20,240},{24,252},{28,24... | collective-permute-start | bytes 393224 | tf_op jit(solution)/shard_map/ppermute | solution.py:29
  116.5 19.6 %collective-permute-start.27 = (bf16[2,128,256]{2,1,0:T(8,128)(2,1)S(1)}, bf16[2,128,256]{2,1,0:T(8,128)(2,1)S(1)}, u32[]{:S(2)}, u32[]{:S(2)}) collective-permute-start(bf16[2,128,256]{2,1,0:T(8,128)(2,1)S(1)} %get-tuple-element.142), channel_id=1, source_target_pairs={{0,224},{4,228},{8,232},{12,236},{16,240},{20,244},{24,248},{28,25... | collective-permute-start | bytes 393224 | tf_op jit(solution)/shard_map/ppermute | solution.py:29

commit v5 on v4

--- a/solution.py
+++ b/solution.py
@@ -41,22 +41,12 @@
     return CHIPS_Y - 1 - y
 
 
-def y_route(block, target, inner=False):
-    route = []
-    for i in range(CORES * CHIPS_Y * CHIPS_Z):
+def y_route(block, target):
+    def move(i):
         core, y, z = i % CORES, i // CORES % CHIPS_Y, i // (CORES * CHIPS_Y)
-        if not inner or 0 < y < CHIPS_Y - 1:
-            route.append((i, (z * CHIPS_Y + target(y)) * CORES + core))
-    return lax.ppermute(block, "ctx", route)
-
-
-def y_exchange(blocks):
-    groups = [
-        [(z * CHIPS_Y + y) * CORES + core for y in range(CHIPS_Y)]
-        for z in range(CHIPS_Z)
-        for core in range(CORES)
-    ]
-    return lax.all_to_all(blocks, "ctx", 0, 0, axis_index_groups=groups, tiled=True)
+        return (z * CHIPS_Y + target(y)) * CORES + core
+
+    return ctx_shift(block, move)
 
 
 def z_exchange(blocks):
@@ -67,14 +57,9 @@
     return lax.all_to_all(blocks, "ctx", 0, 0, axis_index_groups=groups, tiled=True)
 
 
-def y_ahead(block, distance):
-    return y_route(block, lambda y: (y + distance) % CHIPS_Y)
-
-
-def z_ahead(block, distance, other_core=False):
+def chips_ahead(block, distance):
     count = CORES * CHIPS_Y * CHIPS_Z
-    step = CORES * CHIPS_Y * distance
-    return ctx_shift(block, lambda i: (i + step) % count ^ int(other_core))
+    return ctx_shift(block, lambda i: (i + CORES * distance) % count)
 
 
 def tp_ahead(block, distance):
@@ -88,16 +73,11 @@
     return chip_pos + first + lane
 
 
-def key_values(y, kv0, kv1, low, high, kv3, kv4):
-    kv2 = jnp.where(y < CHIPS_Y // 2, low[0], high[0])
-    return kv0[0], kv1[0], kv2, kv3[0], kv4[0]
-
-
 def forward_kernel(
-    scalars, mine, recv, kv0, kv1, low, high, kv3, kv4, doc_mine, doc_recv, attn, weights
+    scalars, mine, recv, kv0, kv1, kv2, kv3, kv4, doc_mine, doc_recv, attn, weights
 ):
-    core, y, chip_pos = scalars[0], scalars[2], scalars[3]
-    kvs = key_values(y, kv0, kv1, low, high, kv3, kv4)
+    core, chip_pos = scalars[0], scalars[3]
+    kvs = [kv[0] for kv in (kv0, kv1, kv2, kv3, kv4)]
     rows = mine.shape[1]
     query_pos = query_positions(core, chip_pos, rows)
     doc = jnp.concatenate([doc_mine[0], doc_recv[0]], axis=1)
@@ -221,11 +201,11 @@
 
 
 def backward_kernel(
-    scalars, mine, recv, kv0, kv1, low, high, kv3, kv4, weights, attn, d_attn,
+    mine, recv, kv0, kv1, kv2, kv3, kv4, weights, attn, d_attn,
     dq_mine, dq_other, g_own, g1, g2, g3, g4,
 ):
     rows = mine.shape[1]
-    kvs = key_values(scalars[2], kv0, kv1, low, high, kv3, kv4)
+    kvs = [kv[0] for kv in (kv0, kv1, kv2, kv3, kv4)]
     heads = []
     for h in range(2):
         cols = slice(h * HEAD_SIZE, (h + 1) * HEAD_SIZE)
@@ -311,7 +291,7 @@
 
 def split_kernel(
     scalars, q_own, q_other, k_own, k_other, v_own, v_other,
-    q_mine, sent, kv_mine, kv_sent,
+    q_mine, sent, kv_mine,
 ):
     width = q_other.shape[2]
     q_mine[...] = q_own[...]
@@ -320,15 +300,13 @@
     sent[:, :, width + HEAD_SIZE :] = v_other[...]
     kv_mine[:, :, :HEAD_SIZE] = k_own[...]
     kv_mine[:, :, HEAD_SIZE:] = v_own[...]
-    kv_sent[:, :, :HEAD_SIZE] = k_other[...]
-    kv_sent[:, :, HEAD_SIZE:] = v_other[...]
 
 
 def split_heads(scalars, query, keys, values):
     seqs, rows, width = query.shape
     out = jax.ShapeDtypeStruct((seqs, rows, width // 2), jnp.bfloat16)
     whole = jax.ShapeDtypeStruct(query.shape, jnp.bfloat16)
-    outs = (out, whole, out, out)
+    outs = (out, whole, out)
 
     def half(a):
         shape = a.shape[:2] + (a.shape[2] // 2,)
@@ -357,7 +335,7 @@
 
 def forward(scalars, mine, recv, kvs, doc_mine, doc_recv):
     seqs, rows, width = mine.shape
-    keys = 2 * rows * (len(kvs) - 1)
+    keys = 2 * rows * len(kvs)
     outs = (
         jax.ShapeDtypeStruct((seqs, 2 * rows, width), jnp.bfloat16),
         jax.ShapeDtypeStruct((seqs, 2, keys, 2 * rows), jnp.bfloat16),
@@ -456,25 +434,22 @@
     )(scalars, *pieces, *rows_t, attn, *early, o_weight)
 
 
-def backward(scalars, mine, recv, kvs, weights, attn, d_attn):
+def backward(mine, recv, kvs, weights, attn, d_attn):
     seqs, rows, width = mine.shape
     half = jax.ShapeDtypeStruct((seqs, rows, width), jnp.bfloat16)
     shape = kvs[0].shape
     own = jax.ShapeDtypeStruct(shape, jnp.float32)
     sent = jax.ShapeDtypeStruct(shape, jnp.bfloat16)
-    outs = (half, half, own) + (sent,) * CHIPS_Y
+    outs = (half, half, own) + (sent,) * (len(kvs) - 1)
     query_spec = by_seq(mine.shape)
     recv_spec = pl.BlockSpec((1, rows, width), lambda s, *_: (s, 0, 0))
     return pl.pallas_call(
         backward_kernel,
         out_shape=outs,
-        grid_spec=pltpu.PrefetchScalarGridSpec(
-            num_scalar_prefetch=1,
-            grid=(seqs,),
-            in_specs=[query_spec, recv_spec]
-            + [by_seq(a.shape) for a in (*kvs, weights, attn, d_attn)],
-            out_specs=[by_seq(o.shape) for o in outs],
-        ),
+        grid=(seqs,),
+        in_specs=[query_spec, recv_spec]
+        + [by_seq(a.shape) for a in (*kvs, weights, attn, d_attn)],
+        out_specs=[by_seq(o.shape) for o in outs],
         compiler_params=pltpu.CompilerParams(vmem_limit_bytes=20 << 20),
         cost_estimate=pl.CostEstimate(
             flops=10 * seqs * 2 * 2 * rows * 10 * rows * HEAD_SIZE,
@@ -482,7 +457,7 @@
             bytes_accessed=8 << 20,
         ),
         name="attention_backward",
-    )(scalars, mine, recv, *kvs, weights, attn, d_attn)
+    )(mine, recv, *kvs, weights, attn, d_attn)
 
 
 def local(query, key_states, value_state_rows, d_out, o_weight, doc_start):
@@ -494,50 +469,32 @@
     chip_pos = ctx // CORES * (CORES * shard_rows)
     scalars = jnp.stack([core, tp, y, chip_pos]).astype(jnp.int32)
     first = core == 0
-    early_y = [y + d < CHIPS_Y for d in range(1, CHIPS_Y)]
-    q_mine, sent, kv_mine, kv_sent = split_heads(scalars, query, key_states, value_state_rows)
-
-    first_seq, second_seq = d_out[:1], d_out[1:]
-    r3a = tp_ahead(first_seq, 1)
-    r1b = tp_ahead(second_seq, -1)
+    q_mine, sent, kv_mine = split_heads(scalars, query, key_states, value_state_rows)
+
+    r3 = tp_ahead(d_out, 1)
+    r1 = tp_ahead(d_out, -1)
+    recv = to_sibling(sent)
     doc_mine = doc_start[:, None, :]
     doc_recv = to_sibling(doc_mine)
-    z_same = z_ahead(kv_mine, 1)
-    z_other = z_ahead(kv_sent, 1, other_core=True)
-    recv = to_sibling(sent)
-    (
-        z_same, z_other, recv, r3a, r1b, first_seq, second_seq, rows, doc_recv,
-        scalars, first, *early_y,
-    ) = lax.optimization_barrier(
-        (
-            z_same, z_other, recv, r3a, r1b, first_seq, second_seq, d_out, doc_recv,
-            scalars, first, *early_y,
-        )
-    )
-    r3b = tp_ahead(second_seq, 1)
-    r1a = tp_ahead(first_seq, -1)
+    t0 = to_sibling(d_out)
+    recv, doc_recv, t0, scalars, first = lax.optimization_barrier(
+        (recv, doc_recv, t0, scalars, first)
+    )
     kv0 = jnp.concatenate([kv_mine, recv[..., -2 * HEAD_SIZE :]], axis=1)
-    kv4 = jnp.concatenate([z_same, z_other], axis=1)
-    kv_next = jnp.where(early_y[0], kv0, kv4)
-    kv_back = jnp.where(early_y[2], kv0, kv4)
-    kv_next, kv_back, t0, t1b, t3a = lax.optimization_barrier(
-        (kv_next, kv_back, to_sibling(rows), to_sibling(r1b), to_sibling(r3a))
-    )
-    kv1, kv3 = y_ahead(kv_next, 1), y_ahead(kv_back, 3)
+    kv1, kv3, kv4 = (chips_ahead(kv0, d) for d in (1, 3, 4))
     own, own_t = early_projection(scalars, [d_out, t0], o_weight)
 
-    near_rows = [r1a, r1b, r3a, r3b]
-    *near_rows, kv1, kv3, own = lax.optimization_barrier((*near_rows, kv1, kv3, own))
-    low = y_route(kv3, lambda y: y - 1, inner=True)
-    high = y_route(kv1, lambda y: y + 1, inner=True)
-    r2a = tp_ahead(near_rows[2], 1)
-    r2b = tp_ahead(near_rows[1], -1)
-    r1a, r1b, r3a, r3b = near_rows
-    near_rows = [r1a, r1b, r3a, r3b, to_sibling(r1a), t1b, t3a, to_sibling(r3b)]
-    *near_rows, low, high = lax.optimization_barrier((*near_rows, low, high))
-    near, near_t = early_projection(scalars, near_rows, o_weight)
-    near, r2a, r2b = lax.optimization_barrier((near, r2a, r2b))
-    kvs = [kv0, kv1, low, high, kv3, kv4]
+    r1, r3, own, kv1, kv3, kv4, kv_again = lax.optimization_barrier(
+        (r1, r3, own, kv1, kv3, kv4, kv0)
+    )
+    kv2 = chips_ahead(kv_again, 2)
+    r2a = tp_ahead(r3[:1], 1)
+    r2b = tp_ahead(r1[1:], -1)
+    near, near_t = early_projection(
+        scalars, [r1, r3, to_sibling(r1), to_sibling(r3)], o_weight
+    )
+    near, r2a, r2b, kv2 = lax.optimization_barrier((near, r2a, r2b, kv2))
+    kvs = [kv0, kv1, kv2, kv3, kv4]
     attn, weights = forward(scalars, q_mine, recv, kvs, doc_mine, doc_recv)
     d_attn, sent_a, kept_a, sent_b, kept_b = late_projection(
         scalars,
@@ -549,10 +506,11 @@
     )
     got_a = y_route(sent_a, y_pair)
     got_b = y_route(sent_b, y_mirror)
-    dq_mine, dq_other, g_own, *g_sent, g_before = backward(
-        scalars, q_mine, recv, kvs, weights, attn, d_attn
-    )
-    got_a, got_b, g_own = lax.optimization_barrier((got_a, got_b, g_own))
+    dq_mine, dq_other, g_own, *g_sent = backward(
+        q_mine, recv, kvs, weights, attn, d_attn
+    )
+    *g_near, g_far = (chips_ahead(g, -d) for d, g in enumerate(g_sent, 1))
+    got_a, got_b, g_own, *g_near = lax.optimization_barrier((got_a, got_b, g_own, *g_near))
     dq_recv = to_sibling(dq_other)
 
     def added(*blocks):
@@ -565,21 +523,13 @@
     next_b = added(kept_b[1], got_b[1]).astype(jnp.bfloat16)
     last_a = y_route(next_a, y_mirror)
     last_b = y_route(next_b, y_pair)
+    last_a, last_b, g_far = lax.optimization_barrier((last_a, last_b, g_far))
     w_sum = merge(kept_a, got_a, last_a, kept_b, got_b, last_b)
     w_all = z_exchange(w_sum)
 
-    grads = g_own
-    g_before = g_before.astype(jnp.float32)
-    for d, sent in enumerate(g_sent, 1):
-        block = y_ahead(sent, -d).astype(jnp.float32)
-        grads = grads + jnp.where(early_y[d - 1], block, 0.0)
-        g_before = g_before + jnp.where(early_y[d - 1], 0.0, block)
-    g_before = g_before.astype(jnp.bfloat16)
-    z_same = z_ahead(g_before[:, :shard_rows], -1)
-    z_other = z_ahead(g_before[:, shard_rows:], -1, other_core=True)
-    sibling = to_sibling(grads[:, shard_rows:].astype(jnp.bfloat16))
-    g_mine = added(grads[:, :shard_rows], z_same).astype(jnp.bfloat16)
-    g_recv = added(sibling, z_other).astype(jnp.bfloat16)
+    grads = added(g_own, *g_near, g_far).astype(jnp.bfloat16)
+    g_mine = grads[:, :shard_rows]
+    g_recv = to_sibling(grads[:, shard_rows:])
 
     def by_core(own, other):
         return jnp.concatenate(

time: 138 us -> 131 us (0.949)
  starting transfers between devices: 54.4 us -> 34.7 us
  waiting for transfers between devices: 50.7 us -> 64.7 us
    ppermute x11 -> x0, waiting for transfers between devices: 22.2 us -> none  [y_route(): return lax.ppermute(block, 'ctx', route)]
    ppermute x11 -> x0, starting transfers between devices: 21.6 us -> none  [y_route(): return lax.ppermute(block, 'ctx', route)]
    all_to_all x1, waiting for transfers between devices: 0.01 us -> 18.5 us  [z_exchange(): lax.all_to_all(blocks, 'ctx', 0, 0, axis_index_groups=groups, tiled=True)]
    ppermute x15 -> x21, waiting for transfers between devices: 28.5 us -> 41.8 us  [ctx_shift(): return lax.ppermute(block, 'ctx', [(i, move(i)) for i in range(count)])]
    ppermute x15 -> x21, starting transfers between devices: 16 us -> 21.8 us  [ctx_shift(): return lax.ppermute(block, 'ctx', [(i, move(i)) for i in range(count)])]
    ppermute x6 -> x4, starting transfers between devices: 9.38 us -> 4.63 us  [tp_ahead(): lax.ppermute(block, 'tp', [(i, (i + distance) % TP) for i in range(TP)])]
    ppermute x6 -> x4, waiting for transfers between devices: 0.02 us -> 4.46 us  [tp_ahead(): lax.ppermute(block, 'tp', [(i, (i + distance) % TP) for i in range(TP)])]
    unnamed x15 -> x14, local copies, waits for them, and re-layouts: 5.34 us -> 6.43 us
  transfers between devices with their start and end apart: 33 -> 26, of which waited for: 14 -> 13; matrix products, arithmetic and copies ran while one was open for 2% -> 1% of each run, Pallas kernels for 13% -> 12%
where the time goes in v5:
time: 131 us
  waiting for transfers between devices  64.7 us (49%)
  starting transfers between devices  34.7 us (26%)
  Pallas kernels  22.3 us (17%)
  local copies, waits for them, and re-layouts  6.49 us (5%)
  other arithmetic  1.92 us (1%)
    ppermute x21, waiting for transfers between devices, ctx_shift(): return lax.ppermute(block, 'ctx', [(i, move(i)) for i in range(count)])  41.8 us
    ppermute x21, starting transfers between devices, ctx_shift(): return lax.ppermute(block, 'ctx', [(i, move(i)) for i in range(count)])  21.8 us
    all_to_all x1, waiting for transfers between devices, z_exchange(): lax.all_to_all(blocks, 'ctx', 0, 0, axis_index_groups=groups, tiled=True)  18.5 us
    all_to_all x1, starting transfers between devices, z_exchange(): lax.all_to_all(blocks, 'ctx', 0, 0, axis_index_groups=groups, tiled=True)  8.2 us
    pallas_call x2, Pallas kernels, early_projection(): pl.pallas_call(early_kernel, out_shape=outs, grid_spec=pltpu.PrefetchScal...  7.51 us
    unnamed x14, local copies, waits for them, and re-layouts  6.43 us
    ppermute x4, starting transfers between devices, tp_ahead(): lax.ppermute(block, 'tp', [(i, (i + distance) % TP) for i in range(TP)])  4.63 us
    ppermute x4, waiting for transfers between devices, tp_ahead(): lax.ppermute(block, 'tp', [(i, (i + distance) % TP) for i in range(TP)])  4.46 us
  transfers between devices with their start and end apart: 26, of which 13 were waited for; matrix products, arithmetic and copies ran while one was open for 1% of the time, Pallas kernels for 12%

profile of v5, /device:TPU:1, one launch (start us, length us, event | category | flops | bytes accessed | tf_op | source)
XLA Modules:
  0.0 130.9 jit_solution(11269228683973116093)
XLA Ops:
  0.6 3.3 %collective-permute-start.2 = (bf16[2,32,5376]{2,1,0:T(8,128)(2,1)}, bf16[2,32,5376]{2,1,0:T(8,128)(2,1)S(1)}, u32[]{:S(2)}, u32[]{:S(2)}) collective-permute-start(bf16[2,32,5376]{2,1,0:T(8,128)(2,1)} %refs_0_.1), channel_id=1, source_target_pairs={{0,4},{4,0},{8,12},{12,8},{16,20},{20,16},{24,28},{28,24},{32,36},... | collective-permute-start | bytes 2064392 | tf_op jit(solution)/shard_map/ppermute | solution.py:29
  4.0 0.9 copy-done.2
  5.0 0.9 copy-done.3
  5.9 0.9 copy-done.4
  6.8 0.7 split_heads.1
  7.6 0.8 collective-permute-start.3
  8.4 0.7 collective-permute-start.4
  9.1 1.0 collective-permute-start.1
  10.1 1.0 collective-permute-done.1.doc_recv
  11.2 0.7 collective-permute-start.7
  11.9 2.7 %collective-permute-start.6 = (bf16[2,256,256]{2,1,0:T(8,128)(2,1)S(1)}, bf16[2,256,256]{2,1,0:T(8,128)(2,1)S(1)}, u32[]{:S(2)}, u32[]{:S(2)}) collective-permute-start(bf16[2,256,256]{2,1,0:T(8,128)(2,1)S(1)} %pad_maximum_fusion.kv0), channel_id=1, source_target_pairs={{0,24},{4,28},{8,32},{12,36},{16,40},{20,44},{24,48},{28,52},{32,5... | collective-permute-start | bytes 786440 | tf_op jit(solution)/shard_map/ppermute | solution.py:29
  14.7 2.6 %copy-done = bf16[5376,512]{1,0:T(8,128)(2,1)S(1)} copy-done((bf16[5376,512]{1,0:T(8,128)(2,1)S(1)}, bf16[5376,512]{1,0:T(8,128)(2,1)}, u32[]{:S(2)}) %copy-start) | copy-done | bytes 5505048
  17.3 1.1 copy-done.5
  18.4 3.3 %projection_early.2 = (bf16[128,256]{1,0:T(8,128)(2,1)S(1)}, bf16[5376,128]{1,0:T(8,128)(2,1)S(1)}) custom-call(s32[4]{0:T(128)S(1)} %pad_add_fusion.scalars, bf16[2,32,5376]{2,1,0:T(8,128)(2,1)S(1)} %copy-done.5, bf16[2,32,5376]{2,1,0:T(8,128)(2,1)S(1)} %collective-permute-done.2.refs_1_, bf16[5376,512]{1,0:T(8,128)(2,1)S(1)} %copy-done), custom_call_target="tpu_custom_call" | custom-call | flops 3523215360 | bytes 12582912 | tf_op jit(solution)/shard_map/projection_early/pallas_call | solution.py:376
  21.7 2.8 %collective-permute-done.3.refs_0_ = bf16[2,32,5376]{2,1,0:T(8,128)(2,1)S(1)} collective-permute-done((bf16[2,32,5376]{2,1,0:T(8,128)(2,1)}, bf16[2,32,5376]{2,1,0:T(8,128)(2,1)S(1)}, u32[]{:S(2)}, u32[]{:S(2)}) %collective-permute-start.3) | collective-permute-done | bytes 688160 | tf_op jit(solution)/shard_map/ppermute | solution.py:66
  24.4 1.6 %collective-permute-done.4.refs_1_ = bf16[2,32,5376]{2,1,0:T(8,128)(2,1)S(1)} collective-permute-done((bf16[2,32,5376]{2,1,0:T(8,128)(2,1)}, bf16[2,32,5376]{2,1,0:T(8,128)(2,1)S(1)}, u32[]{:S(2)}, u32[]{:S(2)}) %collective-permute-start.4) | collective-permute-done | bytes 688160 | tf_op jit(solution)/shard_map/ppermute | solution.py:66
  26.1 2.8 %collective-permute-done.6.kv3 = bf16[2,256,256]{2,1,0:T(8,128)(2,1)S(1)} collective-permute-done((bf16[2,256,256]{2,1,0:T(8,128)(2,1)S(1)}, bf16[2,256,256]{2,1,0:T(8,128)(2,1)S(1)}, u32[]{:S(2)}, u32[]{:S(2)}) %collective-permute-start.6) | collective-permute-done | bytes 262176 | tf_op jit(solution)/shard_map/ppermute | solution.py:29
  28.9 7.1 %collective-permute-done.5.kv1 = bf16[2,256,256]{2,1,0:T(8,128)(2,1)S(1)} collective-permute-done((bf16[2,256,256]{2,1,0:T(8,128)(2,1)S(1)}, bf16[2,256,256]{2,1,0:T(8,128)(2,1)S(1)}, u32[]{:S(2)}, u32[]{:S(2)}) %collective-permute-start.5) | collective-permute-done | bytes 262176 | tf_op jit(solution)/shard_map/ppermute | solution.py:29
  35.9 0.8 collective-permute-start.8
  36.9 0.6 collective-permute-start.10
  37.5 2.6 %collective-permute-start.11 = (bf16[1,32,5376]{2,1,0:T(8,128)(2,1)S(1)}, bf16[1,32,5376]{2,1,0:T(8,128)(2,1)S(1)}, u32[]{:S(2)}, u32[]{:S(2)}) collective-permute-start(bf16[1,32,5376]{2,1,0:T(8,128)(2,1)S(1)} %slice.41), channel_id=1, source_target_pairs={{0,3},{1,0},{2,1},{3,2},{4,7},{5,4},{6,5},{7,6},{8,11},{9,8},{10,9... | collective-permute-start | bytes 1032200 | tf_op jit(solution)/shard_map/ppermute | solution.py:66
  40.1 4.2 %projection_early.3 = (bf16[256,256]{1,0:T(8,128)(2,1)S(1)}, bf16[5376,256]{1,0:T(8,128)(2,1)S(1)}) custom-call(s32[4]{0:T(128)S(1)} %pad_add_fusion.scalars, bf16[2,32,5376]{2,1,0:T(8,128)(2,1)S(1)} %collective-permute-done.3.refs_0_, bf16[2,32,5376]{2,1,0:T(8,128)(2,1)S(1)} %collective-permute-done.4.refs_1_, ...), custom_call_target="tpu_custom_call" | custom-call | flops 7046430720 | bytes 12582912 | tf_op jit(solution)/shard_map/projection_early/pallas_call | solution.py:376
  44.3 3.6 %collective-permute-done.12.kv2 = bf16[2,256,256]{2,1,0:T(8,128)(2,1)S(1)} collective-permute-done((bf16[2,256,256]{2,1,0:T(8,128)(2,1)S(1)}, bf16[2,256,256]{2,1,0:T(8,128)(2,1)S(1)}, u32[]{:S(2)}, u32[]{:S(2)}) %collective-permute-start.12) | collective-permute-done | bytes 262176 | tf_op jit(solution)/shard_map/ppermute | solution.py:29
  47.9 1.3 %collective-permute-start.13 = (bf16[1,32,5376]{2,1,0:T(8,128)(2,1)S(1)}, bf16[1,32,5376]{2,1,0:T(8,128)(2,1)S(1)}, u32[]{:S(2)}, u32[]{:S(2)}) collective-permute-start(bf16[1,32,5376]{2,1,0:T(8,128)(2,1)S(1)} %collective-permute-done.10.r2a), channel_id=1, source_target_pairs={{0,4},{4,0},{8,12},{12,8},{16,20},{20,16},{24,28},{28,24},{32,36},... | collective-permute-start | bytes 1032200 | tf_op jit(solution)/shard_map/ppermute | solution.py:29
  49.3 0.3 collective-permute-start.14
  49.5 4.2 %attention_forward.1 = (bf16[2,256,256]{2,1,0:T(8,128)(2,1)S(1)}, bf16[2,2,1280,256]{3,2,1,0:T(8,128)(2,1)S(1)}) custom-call(s32[4]{0:T(128)S(1)} %pad_add_fusion.scalars, bf16[2,128,256]{2,1,0:T(8,128)(2,1)S(1)} %get-tuple-element.52.mine, bf16[2,128,512]{2,1,0:T(8,128)(2,1)S(1)} %collective-permute-done.recv, ...), custom_call_target="tpu_custom_call" | custom-call | flops 671088640 | bytes 8388608 | tf_op jit(solution)/shard_map/attention_forward/pallas_call | solution.py:345
  53.8 4.1 %projection_late.1 = (bf16[2,256,256]{2,1,0:T(8,128)(2,1)S(1)}, bf16[2,4,168,256]{3,2,1,0:T(8,128)(2,1)S(1)}, bf16[2,4,168,256]{3,2,1,0:T(8,128)(2,1)S(1)}, bf16...) custom-call(s32[4]{0:T(128)S(1)} %pad_add_fusion.scalars, ...), custom_call_target="tpu_custom_call" | custom-call | flops 2113929216 | bytes 12582912 | tf_op jit(solution)/shard_map/projection_late/pallas_call | solution.py:410
  58.1 3.8 %attention_backward.1 = (bf16[2,128,256]{2,1,0:T(8,128)(2,1)S(1)}, bf16[2,128,256]{2,1,0:T(8,128)(2,1)S(1)}, f32[2,256,256]{2,1,0:T(8,128)S(1)}, bf16[2,256,256]...) custom-call(bf16[2,128,256]{2,1,0:T(8,128)(2,1)S(1)} %get-tuple-elem, ...), custom_call_target="tpu_custom_call" | custom-call | flops 1677721600 | bytes 8388608 | tf_op jit(solution)/shard_map/attention_backward/pallas_call | solution.py:446
  62.0 4.7 %collective-permute-start.18 = (bf16[2,256,256]{2,1,0:T(8,128)(2,1)S(1)}, bf16[2,256,256]{2,1,0:T(8,128)(2,1)S(1)}, u32[]{:S(2)}, u32[]{:S(2)}) collective-permute-start(bf16[2,256,256]{2,1,0:T(8,128)(2,1)S(1)} %get-tuple-element.81), channel_id=1, source_target_pairs={{0,248},{4,252},{8,0},{12,4},{16,8},{20,12},{24,16},{28,20},{32,24... | collective-permute-start | bytes 786440 | tf_op jit(solution)/shard_map/ppermute | solution.py:29
  66.6 1.3 collective-permute-start.19
  67.9 0.2 collective-permute-start.20
  68.1 18.0 %collective-permute-done.18 = bf16[2,256,256]{2,1,0:T(8,128)(2,1)S(1)} collective-permute-done((bf16[2,256,256]{2,1,0:T(8,128)(2,1)S(1)}, bf16[2,256,256]{2,1,0:T(8,128)(2,1)S(1)}, u32[]{:S(2)}, u32[]{:S(2)}) %collective-permute-start.18) | collective-permute-done | bytes 262176 | tf_op jit(solution)/shard_map/ppermute | solution.py:29
  86.1 1.3 collective-permute-done.20
  87.5 2.7 %collective-permute-start.22 = (bf16[4,168,256]{2,1,0:T(8,128)(2,1)S(1)}, bf16[4,168,256]{2,1,0:T(8,128)(2,1)S(1)}, u32[]{:S(2)}, u32[]{:S(2)}) collective-permute-start(bf16[4,168,256]{2,1,0:T(8,128)(2,1)S(1)} %fusion.1), channel_id=1, source_target_pairs={{0,8},{4,12},{8,0},{12,4},{16,24},{20,28},{24,16},{28,20},{32,40},... | collective-permute-start | bytes 1032200 | tf_op jit(solution)/shard_map/ppermute | solution.py:29
  90.4 1.6 %collective-permute-start.23 = (bf16[2,256,256]{2,1,0:T(8,128)(2,1)S(1)}, bf16[2,256,256]{2,1,0:T(8,128)(2,1)S(1)}, u32[]{:S(2)}, u32[]{:S(2)}) collective-permute-start(bf16[2,256,256]{2,1,0:T(8,128)(2,1)S(1)} %get-tuple-element.92), channel_id=1, source_target_pairs={{0,224},{4,228},{8,232},{12,236},{16,240},{20,244},{24,248},{28,25... | collective-permute-start | bytes 786440 | tf_op jit(solution)/shard_map/ppermute | solution.py:29
  92.0 4.6 %collective-permute-done.23 = bf16[2,256,256]{2,1,0:T(8,128)(2,1)S(1)} collective-permute-done((bf16[2,256,256]{2,1,0:T(8,128)(2,1)S(1)}, bf16[2,256,256]{2,1,0:T(8,128)(2,1)S(1)}, u32[]{:S(2)}, u32[]{:S(2)}) %collective-permute-start.23) | collective-permute-done | bytes 262176 | tf_op jit(solution)/shard_map/ppermute | solution.py:29
  96.6 0.6 collective-permute-done.22.last_b
  97.2 2.3 %collective-permute-done.21.last_a = bf16[4,168,256]{2,1,0:T(8,128)(2,1)S(1)} collective-permute-done((bf16[4,168,256]{2,1,0:T(8,128)(2,1)S(1)}, bf16[4,168,256]{2,1,0:T(8,128)(2,1)S(1)}, u32[]{:S(2)}, u32[]{:S(2)}) %collective-permute-start.21) | collective-permute-done | bytes 344096 | tf_op jit(solution)/shard_map/ppermute | solution.py:29
  99.5 1.2 projection_merge.1
  100.6 8.2 %all-to-all-start = ((bf16[16,84,256]{2,1,0:T(8,128)(2,1)}), bf16[16,84,256]{2,1,0:T(8,128)(2,1)S(1)}, u32[]{:S(2)}, u32[]{:S(2)}) async-start(bf16[16,84,256]{2,1,0:T(8,128)(2,1)} %projection_merge.1), calls=%async_computation | async-start | bytes 1441792 | tf_op jit(solution)/shard_map/all_to_all | solution.py:57
  108.8 0.2 collective-permute-start.15
  109.0 0.1 add_convert_fusion.2
  109.2 0.4 collective-permute-start.24
  109.6 0.6 collective-permute-done.15
  110.2 0.7 pad_maximum_fusion.1
  110.9 0.7 pad_maximum_fusion.2
  111.7 18.5 %all-to-all-done.blocks = bf16[16,84,256]{2,1,0:T(8,128)(2,1)S(1)} async-done(((bf16[16,84,256]{2,1,0:T(8,128)(2,1)}), bf16[16,84,256]{2,1,0:T(8,128)(2,1)S(1)}, u32[]{:S(2)}, u32[]{:S(2)}) %all-to-all-start) | async-done | bytes 688160 | tf_op jit(solution)/shard_map/all_to_all | solution.py:57
  130.1 0.8 projection_finish.1
  (39 shorter events, 1.1 us)
Async XLA Ops:
  0.6 10.5 %collective-permute-start.2 = (bf16[2,32,5376]{2,1,0:T(8,128)(2,1)}, bf16[2,32,5376]{2,1,0:T(8,128)(2,1)S(1)}, u32[]{:S(2)}, u32[]{:S(2)}) collective-permute-start(bf16[2,32,5376]{2,1,0:T(8,128)(2,1)} %refs_0_.1), channel_id=1, source_target_pairs={{0,4},{4,0},{8,12},{12,8},{16,20},{20,16},{24,28},{28,24},{32,36},... | collective-permute-start | bytes 2064392 | tf_op jit(solution)/shard_map/ppermute | solution.py:29
  4.0 1.0 copy-start.2
  5.0 0.9 copy-start.3
  5.9 0.9 copy-start.4
  7.5 3.7 %collective-permute-start = (bf16[2,128,512]{2,1,0:T(8,128)(2,1)S(1)}, bf16[2,128,512]{2,1,0:T(8,128)(2,1)S(1)}, u32[]{:S(2)}, u32[]{:S(2)}) collective-permute-start(bf16[2,128,512]{2,1,0:T(8,128)(2,1)S(1)} %get-tuple-element.50), channel_id=1, source_target_pairs={{0,4},{4,0},{8,12},{12,8},{16,20},{20,16},{24,28},{28,24},{32,36},... | collective-permute-start | bytes 786440 | tf_op jit(solution)/shard_map/ppermute | solution.py:29
  7.6 16.8 %collective-permute-start.3 = (bf16[2,32,5376]{2,1,0:T(8,128)(2,1)}, bf16[2,32,5376]{2,1,0:T(8,128)(2,1)S(1)}, u32[]{:S(2)}, u32[]{:S(2)}) collective-permute-start(bf16[2,32,5376]{2,1,0:T(8,128)(2,1)} %refs_0_.1), channel_id=1, source_target_pairs={{0,3},{1,0},{2,1},{3,2},{4,7},{5,4},{6,5},{7,6},{8,11},{9,8},{10,9... | collective-permute-start | bytes 2064392 | tf_op jit(solution)/shard_map/ppermute | solution.py:66
  8.4 17.7 %collective-permute-start.4 = (bf16[2,32,5376]{2,1,0:T(8,128)(2,1)}, bf16[2,32,5376]{2,1,0:T(8,128)(2,1)S(1)}, u32[]{:S(2)}, u32[]{:S(2)}) collective-permute-start(bf16[2,32,5376]{2,1,0:T(8,128)(2,1)} %refs_0_.1), channel_id=1, source_target_pairs={{0,1},{1,2},{2,3},{3,0},{4,5},{5,6},{6,7},{7,4},{8,9},{9,10},{10,1... | collective-permute-start | bytes 2064392 | tf_op jit(solution)/shard_map/ppermute | solution.py:66
  9.1 2.0 %collective-permute-start.1 = (s32[2,1,128]{2,1,0:T(1,128)}, s32[2,1,128]{2,1,0:T(1,128)S(1)}, u32[]{:S(2)}, u32[]{:S(2)}) collective-permute-start(s32[2,1,128]{2,1,0:T(1,128)} %bitcast.9), channel_id=1, source_target_pairs={{0,4},{4,0},{8,12},{12,8},{16,20},{20,16},{24,28},{28,24},{32,36},... | collective-permute-start | bytes 3080 | tf_op jit(solution)/shard_map/ppermute | solution.py:29
  11.2 14.9 %collective-permute-start.7 = (bf16[2,256,256]{2,1,0:T(8,128)(2,1)S(1)}, bf16[2,256,256]{2,1,0:T(8,128)(2,1)S(1)}, u32[]{:S(2)}, u32[]{:S(2)}) collective-permute-start(bf16[2,256,256]{2,1,0:T(8,128)(2,1)S(1)} %pad_maximum_fusion.kv0), channel_id=1, source_target_pairs={{0,32},{4,36},{8,40},{12,44},{16,48},{20,52},{24,56},{28,60},{32,6... | collective-permute-start | bytes 786440 | tf_op jit(solution)/shard_map/ppermute | solution.py:29
  11.9 17.0 %collective-permute-start.6 = (bf16[2,256,256]{2,1,0:T(8,128)(2,1)S(1)}, bf16[2,256,256]{2,1,0:T(8,128)(2,1)S(1)}, u32[]{:S(2)}, u32[]{:S(2)}) collective-permute-start(bf16[2,256,256]{2,1,0:T(8,128)(2,1)S(1)} %pad_maximum_fusion.kv0), channel_id=1, source_target_pairs={{0,24},{4,28},{8,32},{12,36},{16,40},{20,44},{24,48},{28,52},{32,5... | collective-permute-start | bytes 786440 | tf_op jit(solution)/shard_map/ppermute | solution.py:29
  14.6 21.3 %collective-permute-start.5 = (bf16[2,256,256]{2,1,0:T(8,128)(2,1)S(1)}, bf16[2,256,256]{2,1,0:T(8,128)(2,1)S(1)}, u32[]{:S(2)}, u32[]{:S(2)}) collective-permute-start(bf16[2,256,256]{2,1,0:T(8,128)(2,1)S(1)} %pad_maximum_fusion.kv0), channel_id=1, source_target_pairs={{0,8},{4,12},{8,16},{12,20},{16,24},{20,28},{24,32},{28,36},{32,40... | collective-permute-start | bytes 786440 | tf_op jit(solution)/shard_map/ppermute | solution.py:29
  14.7 2.6 %copy-start = (bf16[5376,512]{1,0:T(8,128)(2,1)S(1)}, bf16[5376,512]{1,0:T(8,128)(2,1)}, u32[]{:S(2)}) copy-start(bf16[5376,512]{1,0:T(8,128)(2,1)} %o_weight.1) | copy-start | bytes 16515076
  17.3 1.1 copy-start.5
  18.4 21.7 %copy-start.1 = (bf16[5376,512]{1,0:T(8,128)(2,1)S(1)}, bf16[5376,512]{1,0:T(8,128)(2,1)}, u32[]{:S(2)}) copy-start(bf16[5376,512]{1,0:T(8,128)(2,1)} %o_weight.1) | copy-start | bytes 16515076
  35.9 4.1 %collective-permute-start.8 = (bf16[2,32,5376]{2,1,0:T(8,128)(2,1)S(1)}, bf16[2,32,5376]{2,1,0:T(8,128)(2,1)S(1)}, u32[]{:S(2)}, u32[]{:S(2)}) collective-permute-start(bf16[2,32,5376]{2,1,0:T(8,128)(2,1)S(1)} %collective-permute-done.3.refs_0_), channel_id=1, source_target_pairs={{0,4},{4,0},{8,12},{12,8},{16,20},{20,16},{24,28},{28,24},{32,36},... | collective-permute-start | bytes 2064392 | tf_op jit(solution)/shard_map/ppermute | solution.py:29
  36.8 3.3 %collective-permute-start.9 = (bf16[2,32,5376]{2,1,0:T(8,128)(2,1)S(1)}, bf16[2,32,5376]{2,1,0:T(8,128)(2,1)S(1)}, u32[]{:S(2)}, u32[]{:S(2)}) collective-permute-start(bf16[2,32,5376]{2,1,0:T(8,128)(2,1)S(1)} %collective-permute-done.4.refs_1_), channel_id=1, source_target_pairs={{0,4},{4,0},{8,12},{12,8},{16,20},{20,16},{24,28},{28,24},{32,36},... | collective-permute-start | bytes 2064392 | tf_op jit(solution)/shard_map/ppermute | solution.py:29
  36.8 12.7 %copy-start.6 = (s32[2,128]{1,0:T(2,128)S(1)}, s32[2,128]{1,0:T(2,128)}, u32[]{:S(2)}) copy-start(s32[2,128]{1,0:T(2,128)} %param.11) | copy-start | bytes 3076
  36.8 11.1 %collective-permute-start.12 = (bf16[2,256,256]{2,1,0:T(8,128)(2,1)S(1)}, bf16[2,256,256]{2,1,0:T(8,128)(2,1)S(1)}, u32[]{:S(2)}, u32[]{:S(2)}) collective-permute-start(bf16[2,256,256]{2,1,0:T(8,128)(2,1)S(1)} %pad_maximum_fusion.kv0), channel_id=1, source_target_pairs={{0,16},{4,20},{8,24},{12,28},{16,32},{20,36},{24,40},{28,44},{32,4... | collective-permute-start | bytes 786440 | tf_op jit(solution)/shard_map/ppermute | solution.py:29
  36.9 11.0 %collective-permute-start.10 = (bf16[1,32,5376]{2,1,0:T(8,128)(2,1)S(1)}, bf16[1,32,5376]{2,1,0:T(8,128)(2,1)S(1)}, u32[]{:S(2)}, u32[]{:S(2)}) collective-permute-start(bf16[1,32,5376]{2,1,0:T(8,128)(2,1)S(1)} %slice.40), channel_id=1, source_target_pairs={{0,1},{1,2},{2,3},{3,0},{4,5},{5,6},{6,7},{7,4},{8,9},{9,10},{10,1... | collective-permute-start | bytes 1032200 | tf_op jit(solution)/shard_map/ppermute | solution.py:66
  37.5 10.5 %collective-permute-start.11 = (bf16[1,32,5376]{2,1,0:T(8,128)(2,1)S(1)}, bf16[1,32,5376]{2,1,0:T(8,128)(2,1)S(1)}, u32[]{:S(2)}, u32[]{:S(2)}) collective-permute-start(bf16[1,32,5376]{2,1,0:T(8,128)(2,1)S(1)} %slice.41), channel_id=1, source_target_pairs={{0,3},{1,0},{2,1},{3,2},{4,7},{5,4},{6,5},{7,6},{8,11},{9,8},{10,9... | collective-permute-start | bytes 1032200 | tf_op jit(solution)/shard_map/ppermute | solution.py:66
  47.9 5.8 %collective-permute-start.13 = (bf16[1,32,5376]{2,1,0:T(8,128)(2,1)S(1)}, bf16[1,32,5376]{2,1,0:T(8,128)(2,1)S(1)}, u32[]{:S(2)}, u32[]{:S(2)}) collective-permute-start(bf16[1,32,5376]{2,1,0:T(8,128)(2,1)S(1)} %collective-permute-done.10.r2a), channel_id=1, source_target_pairs={{0,4},{4,0},{8,12},{12,8},{16,20},{20,16},{24,28},{28,24},{32,36},... | collective-permute-start | bytes 1032200 | tf_op jit(solution)/shard_map/ppermute | solution.py:29
  49.3 4.5 %collective-permute-start.14 = (bf16[1,32,5376]{2,1,0:T(8,128)(2,1)S(1)}, bf16[1,32,5376]{2,1,0:T(8,128)(2,1)S(1)}, u32[]{:S(2)}, u32[]{:S(2)}) collective-permute-start(bf16[1,32,5376]{2,1,0:T(8,128)(2,1)S(1)} %collective-permute-done.11.r2b), channel_id=1, source_target_pairs={{0,4},{4,0},{8,12},{12,8},{16,20},{20,16},{24,28},{28,24},{32,36},... | collective-permute-start | bytes 1032200 | tf_op jit(solution)/shard_map/ppermute | solution.py:29
  57.9 29.4 %collective-permute-start.16 = (bf16[2,4,168,256]{3,2,1,0:T(8,128)(2,1)S(1)}, bf16[2,4,168,256]{3,2,1,0:T(8,128)(2,1)S(1)}, u32[]{:S(2)}, u32[]{:S(2)}) collective-permute-start(bf16[2,4,168,256]{3,2,1,0:T(8,128)(2,1)S(1)} %get-tuple-element.78), channel_id=1, source_target_pairs={{0,8},{4,12},{8,0},{12,4},{16,24},{20,28},{24,16},{28,20},{32,40},... | collective-permute-start | bytes 2064392 | tf_op jit(solution)/shard_map/ppermute | solution.py:29
  58.0 29.3 %collective-permute-start.17 = (bf16[2,4,168,256]{3,2,1,0:T(8,128)(2,1)S(1)}, bf16[2,4,168,256]{3,2,1,0:T(8,128)(2,1)S(1)}, u32[]{:S(2)}, u32[]{:S(2)}) collective-permute-start(bf16[2,4,168,256]{3,2,1,0:T(8,128)(2,1)S(1)} %get-tuple-element.79), channel_id=1, source_target_pairs={{0,24},{4,28},{8,16},{12,20},{16,8},{20,12},{24,0},{28,4},{32,56},... | collective-permute-start | bytes 2064392 | tf_op jit(solution)/shard_map/ppermute | solution.py:29
  62.0 24.1 %collective-permute-start.18 = (bf16[2,256,256]{2,1,0:T(8,128)(2,1)S(1)}, bf16[2,256,256]{2,1,0:T(8,128)(2,1)S(1)}, u32[]{:S(2)}, u32[]{:S(2)}) collective-permute-start(bf16[2,256,256]{2,1,0:T(8,128)(2,1)S(1)} %get-tuple-element.81), channel_id=1, source_target_pairs={{0,248},{4,252},{8,0},{12,4},{16,8},{20,12},{24,16},{28,20},{32,24... | collective-permute-start | bytes 786440 | tf_op jit(solution)/shard_map/ppermute | solution.py:29
  66.6 19.4 %collective-permute-start.19 = (bf16[2,256,256]{2,1,0:T(8,128)(2,1)S(1)}, bf16[2,256,256]{2,1,0:T(8,128)(2,1)S(1)}, u32[]{:S(2)}, u32[]{:S(2)}) collective-permute-start(bf16[2,256,256]{2,1,0:T(8,128)(2,1)S(1)} %get-tuple-element.82), channel_id=1, source_target_pairs={{0,240},{4,244},{8,248},{12,252},{16,0},{20,4},{24,8},{28,12},{32,... | collective-permute-start | bytes 786440 | tf_op jit(solution)/shard_map/ppermute | solution.py:29
  67.9 19.5 %collective-permute-start.20 = (bf16[2,256,256]{2,1,0:T(8,128)(2,1)S(1)}, bf16[2,256,256]{2,1,0:T(8,128)(2,1)S(1)}, u32[]{:S(2)}, u32[]{:S(2)}) collective-permute-start(bf16[2,256,256]{2,1,0:T(8,128)(2,1)S(1)} %get-tuple-element.83), channel_id=1, source_target_pairs={{0,232},{4,236},{8,240},{12,244},{16,248},{20,252},{24,0},{28,4},{... | collective-permute-start | bytes 786440 | tf_op jit(solution)/shard_map/ppermute | solution.py:29
  87.5 9.7 %collective-permute-start.22 = (bf16[4,168,256]{2,1,0:T(8,128)(2,1)S(1)}, bf16[4,168,256]{2,1,0:T(8,128)(2,1)S(1)}, u32[]{:S(2)}, u32[]{:S(2)}) collective-permute-start(bf16[4,168,256]{2,1,0:T(8,128)(2,1)S(1)} %fusion.1), channel_id=1, source_target_pairs={{0,8},{4,12},{8,0},{12,4},{16,24},{20,28},{24,16},{28,20},{32,40},... | collective-permute-start | bytes 1032200 | tf_op jit(solution)/shard_map/ppermute | solution.py:29
  90.3 9.2 %collective-permute-start.21 = (bf16[4,168,256]{2,1,0:T(8,128)(2,1)S(1)}, bf16[4,168,256]{2,1,0:T(8,128)(2,1)S(1)}, u32[]{:S(2)}, u32[]{:S(2)}) collective-permute-start(bf16[4,168,256]{2,1,0:T(8,128)(2,1)S(1)} %fusion), channel_id=1, source_target_pairs={{0,24},{4,28},{8,16},{12,20},{16,8},{20,12},{24,0},{28,4},{32,56},... | collective-permute-start | bytes 1032200 | tf_op jit(solution)/shard_map/ppermute | solution.py:29
  90.4 6.2 %collective-permute-start.23 = (bf16[2,256,256]{2,1,0:T(8,128)(2,1)S(1)}, bf16[2,256,256]{2,1,0:T(8,128)(2,1)S(1)}, u32[]{:S(2)}, u32[]{:S(2)}) collective-permute-start(bf16[2,256,256]{2,1,0:T(8,128)(2,1)S(1)} %get-tuple-element.92), channel_id=1, source_target_pairs={{0,224},{4,228},{8,232},{12,236},{16,240},{20,244},{24,248},{28,25... | collective-permute-start | bytes 786440 | tf_op jit(solution)/shard_map/ppermute | solution.py:29
  100.6 29.5 %all-to-all-start = ((bf16[16,84,256]{2,1,0:T(8,128)(2,1)}), bf16[16,84,256]{2,1,0:T(8,128)(2,1)S(1)}, u32[]{:S(2)}, u32[]{:S(2)}) async-start(bf16[16,84,256]{2,1,0:T(8,128)(2,1)} %projection_merge.1), calls=%async_computation | async-start | bytes 1441792 | tf_op jit(solution)/shard_map/all_to_all | solution.py:57
  108.8 1.3 %collective-permute-start.15 = (bf16[2,128,256]{2,1,0:T(8,128)(2,1)S(1)}, bf16[2,128,256]{2,1,0:T(8,128)(2,1)S(1)}, u32[]{:S(2)}, u32[]{:S(2)}) collective-permute-start(bf16[2,128,256]{2,1,0:T(8,128)(2,1)S(1)} %get-tuple-element.77), channel_id=1, source_target_pairs={{0,4},{4,0},{8,12},{12,8},{16,20},{20,16},{24,28},{28,24},{32,36},... | collective-permute-start | bytes 393224 | tf_op jit(solution)/shard_map/ppermute | solution.py:29
  109.2 1.7 %collective-permute-start.24 = (bf16[2,128,256]{2,1,0:T(8,128)(2,1)S(1)}, bf16[2,128,256]{2,1,0:T(8,128)(2,1)S(1)}, u32[]{:S(2)}, u32[]{:S(2)}) collective-permute-start(bf16[2,128,256]{2,1,0:T(8,128)(2,1)S(1)} %slice.52), channel_id=1, source_target_pairs={{0,4},{4,0},{8,12},{12,8},{16,20},{20,16},{24,28},{28,24},{32,36},... | collective-permute-start | bytes 393224 | tf_op jit(solution)/shard_map/ppermute | solution.py:29

commit v6 on v5

--- a/solution.py
+++ b/solution.py
@@ -509,9 +509,12 @@
     dq_mine, dq_other, g_own, *g_sent = backward(
         q_mine, recv, kvs, weights, attn, d_attn
     )
-    *g_near, g_far = (chips_ahead(g, -d) for d, g in enumerate(g_sent, 1))
-    got_a, got_b, g_own, *g_near = lax.optimization_barrier((got_a, got_b, g_own, *g_near))
+    *g_near, g_far = g_sent
+    g_far = chips_ahead(g_far, -4)
     dq_recv = to_sibling(dq_other)
+    got_a, got_b, g_own, g_far, dq_recv = lax.optimization_barrier(
+        (got_a, got_b, g_own, g_far, dq_recv)
+    )
 
     def added(*blocks):
         total = blocks[0].astype(jnp.float32)
@@ -523,9 +526,10 @@
     next_b = added(kept_b[1], got_b[1]).astype(jnp.bfloat16)
     last_a = y_route(next_a, y_mirror)
     last_b = y_route(next_b, y_pair)
-    last_a, last_b, g_far = lax.optimization_barrier((last_a, last_b, g_far))
     w_sum = merge(kept_a, got_a, last_a, kept_b, got_b, last_b)
+    w_sum, *g_near = lax.optimization_barrier((w_sum, *g_near))
     w_all = z_exchange(w_sum)
+    g_near = [chips_ahead(g, -d) for d, g in enumerate(g_near, 1)]
 
     grads = added(g_own, *g_near, g_far).astype(jnp.bfloat16)
     g_mine = grads[:, :shard_rows]

time: 131 us -> 140 us (1.069); the launches traced: 131 us -> 138 us
  waiting for transfers between devices: 64.7 us -> 69.3 us
  starting transfers between devices: 34.7 us -> 37 us
    ppermute x21, waiting for transfers between devices: 41.8 us -> 64.9 us  [ctx_shift(): return lax.ppermute(block, 'ctx', [(i, move(i)) for i in range(count)])]
    all_to_all x1, waiting for transfers between devices: 18.5 us -> 0.01 us  [z_exchange(): lax.all_to_all(blocks, 'ctx', 0, 0, axis_index_groups=groups, tiled=True)]
    ppermute x21, starting transfers between devices: 21.8 us -> 24.4 us  [ctx_shift(): return lax.ppermute(block, 'ctx', [(i, move(i)) for i in range(count)])]
  transfers between devices with their start and end apart: 26 -> 26, of which waited for: 13 -> 16; matrix products, arithmetic and copies ran while one was open for 1% -> 1% of each run, Pallas kernels for 12% -> 12%
where the time goes in v6:
time: 140 us; the launch traced here: 138 us
  waiting for transfers between devices  69.3 us (50%)
  starting transfers between devices  37 us (26%)
  Pallas kernels  22.3 us (16%)
  local copies, waits for them, and re-layouts  6.49 us (5%)
  other arithmetic  1.92 us (1%)
    ppermute x21, waiting for transfers between devices, ctx_shift(): return lax.ppermute(block, 'ctx', [(i, move(i)) for i in range(count)])  64.9 us
    ppermute x21, starting transfers between devices, ctx_shift(): return lax.ppermute(block, 'ctx', [(i, move(i)) for i in range(count)])  24.4 us
    all_to_all x1, starting transfers between devices, z_exchange(): lax.all_to_all(blocks, 'ctx', 0, 0, axis_index_groups=groups, tiled=True)  7.97 us
    pallas_call x2, Pallas kernels, early_projection(): pl.pallas_call(early_kernel, out_shape=outs, grid_spec=pltpu.PrefetchScal...  7.51 us
    unnamed x14, local copies, waits for them, and re-layouts  6.43 us
    ppermute x4, starting transfers between devices, tp_ahead(): lax.ppermute(block, 'tp', [(i, (i + distance) % TP) for i in range(TP)])  4.63 us
    ppermute x4, waiting for transfers between devices, tp_ahead(): lax.ppermute(block, 'tp', [(i, (i + distance) % TP) for i in range(TP)])  4.46 us
    pallas_call x1, Pallas kernels, forward(): pl.pallas_call(forward_kernel, out_shape=outs, grid_spec=pltpu.PrefetchSc...  4.24 us
  transfers between devices with their start and end apart: 26, of which 16 were waited for; matrix products, arithmetic and copies ran while one was open for 1% of the time, Pallas kernels for 12%

profile of v6, /device:TPU:1, one launch (start us, length us, event | category | flops | bytes accessed | tf_op | source)
XLA Modules:
  0.0 137.9 jit_solution(12021703524637594590)
XLA Ops:
  0.6 3.3 %collective-permute-start.2 = (bf16[2,32,5376]{2,1,0:T(8,128)(2,1)}, bf16[2,32,5376]{2,1,0:T(8,128)(2,1)S(1)}, u32[]{:S(2)}, u32[]{:S(2)}) collective-permute-start(bf16[2,32,5376]{2,1,0:T(8,128)(2,1)} %refs_0_.1), channel_id=1, source_target_pairs={{0,4},{4,0},{8,12},{12,8},{16,20},{20,16},{24,28},{28,24},{32,36},... | collective-permute-start | bytes 2064392 | tf_op jit(solution)/shard_map/ppermute | solution.py:29
  4.0 0.9 copy-done.2
  5.0 0.9 copy-done.3
  5.9 0.9 copy-done.4
  6.8 0.7 split_heads.1
  7.6 0.8 collective-permute-start.3
  8.4 0.7 collective-permute-start.4
  9.1 1.0 collective-permute-start.1
  10.1 1.0 collective-permute-done.1.doc_recv
  11.2 0.7 collective-permute-start.7
  11.9 2.7 %collective-permute-start.6 = (bf16[2,256,256]{2,1,0:T(8,128)(2,1)S(1)}, bf16[2,256,256]{2,1,0:T(8,128)(2,1)S(1)}, u32[]{:S(2)}, u32[]{:S(2)}) collective-permute-start(bf16[2,256,256]{2,1,0:T(8,128)(2,1)S(1)} %pad_maximum_fusion.kv0), channel_id=1, source_target_pairs={{0,24},{4,28},{8,32},{12,36},{16,40},{20,44},{24,48},{28,52},{32,5... | collective-permute-start | bytes 786440 | tf_op jit(solution)/shard_map/ppermute | solution.py:29
  14.7 2.6 %copy-done = bf16[5376,512]{1,0:T(8,128)(2,1)S(1)} copy-done((bf16[5376,512]{1,0:T(8,128)(2,1)S(1)}, bf16[5376,512]{1,0:T(8,128)(2,1)}, u32[]{:S(2)}) %copy-start) | copy-done | bytes 5505048
  17.3 1.1 copy-done.5
  18.4 3.3 %projection_early.2 = (bf16[128,256]{1,0:T(8,128)(2,1)S(1)}, bf16[5376,128]{1,0:T(8,128)(2,1)S(1)}) custom-call(s32[4]{0:T(128)S(1)} %pad_add_fusion.scalars, bf16[2,32,5376]{2,1,0:T(8,128)(2,1)S(1)} %copy-done.5, bf16[2,32,5376]{2,1,0:T(8,128)(2,1)S(1)} %collective-permute-done.2.refs_1_, bf16[5376,512]{1,0:T(8,128)(2,1)S(1)} %copy-done), custom_call_target="tpu_custom_call" | custom-call | flops 3523215360 | bytes 12582912 | tf_op jit(solution)/shard_map/projection_early/pallas_call | solution.py:376
  21.7 2.8 %collective-permute-done.3.refs_0_ = bf16[2,32,5376]{2,1,0:T(8,128)(2,1)S(1)} collective-permute-done((bf16[2,32,5376]{2,1,0:T(8,128)(2,1)}, bf16[2,32,5376]{2,1,0:T(8,128)(2,1)S(1)}, u32[]{:S(2)}, u32[]{:S(2)}) %collective-permute-start.3) | collective-permute-done | bytes 688160 | tf_op jit(solution)/shard_map/ppermute | solution.py:66
  24.4 1.6 %collective-permute-done.4.refs_1_ = bf16[2,32,5376]{2,1,0:T(8,128)(2,1)S(1)} collective-permute-done((bf16[2,32,5376]{2,1,0:T(8,128)(2,1)}, bf16[2,32,5376]{2,1,0:T(8,128)(2,1)S(1)}, u32[]{:S(2)}, u32[]{:S(2)}) %collective-permute-start.4) | collective-permute-done | bytes 688160 | tf_op jit(solution)/shard_map/ppermute | solution.py:66
  26.1 2.8 %collective-permute-done.6.kv3 = bf16[2,256,256]{2,1,0:T(8,128)(2,1)S(1)} collective-permute-done((bf16[2,256,256]{2,1,0:T(8,128)(2,1)S(1)}, bf16[2,256,256]{2,1,0:T(8,128)(2,1)S(1)}, u32[]{:S(2)}, u32[]{:S(2)}) %collective-permute-start.6) | collective-permute-done | bytes 262176 | tf_op jit(solution)/shard_map/ppermute | solution.py:29
  28.9 7.1 %collective-permute-done.5.kv1 = bf16[2,256,256]{2,1,0:T(8,128)(2,1)S(1)} collective-permute-done((bf16[2,256,256]{2,1,0:T(8,128)(2,1)S(1)}, bf16[2,256,256]{2,1,0:T(8,128)(2,1)S(1)}, u32[]{:S(2)}, u32[]{:S(2)}) %collective-permute-start.5) | collective-permute-done | bytes 262176 | tf_op jit(solution)/shard_map/ppermute | solution.py:29
  35.9 0.8 collective-permute-start.8
  36.9 0.6 collective-permute-start.10
  37.5 2.6 %collective-permute-start.11 = (bf16[1,32,5376]{2,1,0:T(8,128)(2,1)S(1)}, bf16[1,32,5376]{2,1,0:T(8,128)(2,1)S(1)}, u32[]{:S(2)}, u32[]{:S(2)}) collective-permute-start(bf16[1,32,5376]{2,1,0:T(8,128)(2,1)S(1)} %slice.41), channel_id=1, source_target_pairs={{0,3},{1,0},{2,1},{3,2},{4,7},{5,4},{6,5},{7,6},{8,11},{9,8},{10,9... | collective-permute-start | bytes 1032200 | tf_op jit(solution)/shard_map/ppermute | solution.py:66
  40.1 4.2 %projection_early.3 = (bf16[256,256]{1,0:T(8,128)(2,1)S(1)}, bf16[5376,256]{1,0:T(8,128)(2,1)S(1)}) custom-call(s32[4]{0:T(128)S(1)} %pad_add_fusion.scalars, bf16[2,32,5376]{2,1,0:T(8,128)(2,1)S(1)} %collective-permute-done.3.refs_0_, bf16[2,32,5376]{2,1,0:T(8,128)(2,1)S(1)} %collective-permute-done.4.refs_1_, ...), custom_call_target="tpu_custom_call" | custom-call | flops 7046430720 | bytes 12582912 | tf_op jit(solution)/shard_map/projection_early/pallas_call | solution.py:376
  44.3 3.6 %collective-permute-done.12.kv2 = bf16[2,256,256]{2,1,0:T(8,128)(2,1)S(1)} collective-permute-done((bf16[2,256,256]{2,1,0:T(8,128)(2,1)S(1)}, bf16[2,256,256]{2,1,0:T(8,128)(2,1)S(1)}, u32[]{:S(2)}, u32[]{:S(2)}) %collective-permute-start.12) | collective-permute-done | bytes 262176 | tf_op jit(solution)/shard_map/ppermute | solution.py:29
  47.9 1.3 collective-permute-start.13
  49.3 0.3 collective-permute-start.14
  49.5 4.2 %attention_forward.1 = (bf16[2,256,256]{2,1,0:T(8,128)(2,1)S(1)}, bf16[2,2,1280,256]{3,2,1,0:T(8,128)(2,1)S(1)}) custom-call(s32[4]{0:T(128)S(1)} %pad_add_fusion.scalars, bf16[2,128,256]{2,1,0:T(8,128)(2,1)S(1)} %get-tuple-element.52.mine, bf16[2,128,512]{2,1,0:T(8,128)(2,1)S(1)} %collective-permute-done.recv, ...), custom_call_target="tpu_custom_call" | custom-call | flops 671088640 | bytes 8388608 | tf_op jit(solution)/shard_map/attention_forward/pallas_call | solution.py:345
  53.8 4.1 %projection_late.1 = (bf16[2,256,256]{2,1,0:T(8,128)(2,1)S(1)}, bf16[2,4,168,256]{3,2,1,0:T(8,128)(2,1)S(1)}, bf16[2,4,168,256]{3,2,1,0:T(8,128)(2,1)S(1)}, bf16...) custom-call(s32[4]{0:T(128)S(1)} %pad_add_fusion.scalars, ...), custom_call_target="tpu_custom_call" | custom-call | flops 2113929216 | bytes 12582912 | tf_op jit(solution)/shard_map/projection_late/pallas_call | solution.py:410
  58.1 3.8 %attention_backward.1 = (bf16[2,128,256]{2,1,0:T(8,128)(2,1)S(1)}, bf16[2,128,256]{2,1,0:T(8,128)(2,1)S(1)}, f32[2,256,256]{2,1,0:T(8,128)S(1)}, bf16[2,256,256]...) custom-call(bf16[2,128,256]{2,1,0:T(8,128)(2,1)S(1)} %get-tuple-elem, ...), custom_call_target="tpu_custom_call" | custom-call | flops 1677721600 | bytes 8388608 | tf_op jit(solution)/shard_map/attention_backward/pallas_call | solution.py:446
  62.0 4.9 %collective-permute-start.17 = (bf16[2,256,256]{2,1,0:T(8,128)(2,1)S(1)}, bf16[2,256,256]{2,1,0:T(8,128)(2,1)S(1)}, u32[]{:S(2)}, u32[]{:S(2)}) collective-permute-start(bf16[2,256,256]{2,1,0:T(8,128)(2,1)S(1)} %get-tuple-element.80), channel_id=1, source_target_pairs={{0,224},{4,228},{8,232},{12,236},{16,240},{20,244},{24,248},{28,25... | collective-permute-start | bytes 786440 | tf_op jit(solution)/shard_map/ppermute | solution.py:29
  66.9 1.3 collective-permute-start.18
  68.2 1.0 collective-permute-done.18
  69.2 2.2 %collective-permute-done.17 = bf16[2,256,256]{2,1,0:T(8,128)(2,1)S(1)} collective-permute-done((bf16[2,256,256]{2,1,0:T(8,128)(2,1)S(1)}, bf16[2,256,256]{2,1,0:T(8,128)(2,1)S(1)}, u32[]{:S(2)}, u32[]{:S(2)}) %collective-permute-start.17) | collective-permute-done | bytes 262176 | tf_op jit(solution)/shard_map/ppermute | solution.py:29
  71.4 3.4 %collective-permute-done.15.got_a = bf16[2,4,168,256]{3,2,1,0:T(8,128)(2,1)S(1)} collective-permute-done((bf16[2,4,168,256]{3,2,1,0:T(8,128)(2,1)S(1)}, bf16[2,4,168,256]{3,2,1,0:T(8,128)(2,1)S(1)}, u32[]{:S(2)}, u32[]{:S(2)}) %collective-permute-start.15) | collective-permute-done | bytes 688160 | tf_op jit(solution)/shard_map/ppermute | solution.py:29
  74.8 1.3 collective-permute-done.16.got_b
  76.4 0.8 collective-permute-start.19
  77.2 7.6 %collective-permute-done.20.last_b = bf16[4,168,256]{2,1,0:T(8,128)(2,1)S(1)} collective-permute-done((bf16[4,168,256]{2,1,0:T(8,128)(2,1)S(1)}, bf16[4,168,256]{2,1,0:T(8,128)(2,1)S(1)}, u32[]{:S(2)}, u32[]{:S(2)}) %collective-permute-start.20) | collective-permute-done | bytes 344096 | tf_op jit(solution)/shard_map/ppermute | solution.py:29
  84.8 1.0 collective-permute-done.19.last_a
  85.8 1.2 projection_merge.1
  87.0 8.0 %all-to-all-start = ((bf16[16,84,256]{2,1,0:T(8,128)(2,1)}), bf16[16,84,256]{2,1,0:T(8,128)(2,1)S(1)}, u32[]{:S(2)}, u32[]{:S(2)}) async-start(bf16[16,84,256]{2,1,0:T(8,128)(2,1)} %projection_merge.1), calls=%async_computation | async-start | bytes 1441792 | tf_op jit(solution)/shard_map/all_to_all | solution.py:57
  94.9 4.2 %collective-permute-start.21 = (bf16[2,256,256]{2,1,0:T(8,128)(2,1)S(1)}, bf16[2,256,256]{2,1,0:T(8,128)(2,1)S(1)}, u32[]{:S(2)}, u32[]{:S(2)}) collective-permute-start(bf16[2,256,256]{2,1,0:T(8,128)(2,1)S(1)} %get-tuple-element.91), channel_id=1, source_target_pairs={{0,248},{4,252},{8,0},{12,4},{16,8},{20,12},{24,16},{28,20},{32,24... | collective-permute-start | bytes 786440 | tf_op jit(solution)/shard_map/ppermute | solution.py:29
  99.3 1.6 %collective-permute-start.23 = (bf16[2,256,256]{2,1,0:T(8,128)(2,1)S(1)}, bf16[2,256,256]{2,1,0:T(8,128)(2,1)S(1)}, u32[]{:S(2)}, u32[]{:S(2)}) collective-permute-start(bf16[2,256,256]{2,1,0:T(8,128)(2,1)S(1)} %get-tuple-element.93), channel_id=1, source_target_pairs={{0,232},{4,236},{8,240},{12,244},{16,248},{20,252},{24,0},{28,4},{... | collective-permute-start | bytes 786440 | tf_op jit(solution)/shard_map/ppermute | solution.py:29
  100.8 18.3 %collective-permute-done.21 = bf16[2,256,256]{2,1,0:T(8,128)(2,1)S(1)} collective-permute-done((bf16[2,256,256]{2,1,0:T(8,128)(2,1)S(1)}, bf16[2,256,256]{2,1,0:T(8,128)(2,1)S(1)}, u32[]{:S(2)}, u32[]{:S(2)}) %collective-permute-start.21) | collective-permute-done | bytes 262176 | tf_op jit(solution)/shard_map/ppermute | solution.py:29
  119.1 8.2 %collective-permute-done.22 = bf16[2,256,256]{2,1,0:T(8,128)(2,1)S(1)} collective-permute-done((bf16[2,256,256]{2,1,0:T(8,128)(2,1)S(1)}, bf16[2,256,256]{2,1,0:T(8,128)(2,1)S(1)}, u32[]{:S(2)}, u32[]{:S(2)}) %collective-permute-start.22) | collective-permute-done | bytes 262176 | tf_op jit(solution)/shard_map/ppermute | solution.py:29
  127.3 7.2 %collective-permute-done.23 = bf16[2,256,256]{2,1,0:T(8,128)(2,1)S(1)} collective-permute-done((bf16[2,256,256]{2,1,0:T(8,128)(2,1)S(1)}, bf16[2,256,256]{2,1,0:T(8,128)(2,1)S(1)}, u32[]{:S(2)}, u32[]{:S(2)}) %collective-permute-start.23) | collective-permute-done | bytes 262176 | tf_op jit(solution)/shard_map/ppermute | solution.py:29
  134.7 0.7 collective-permute-start.24
  135.4 0.7 pad_maximum_fusion.1
  136.4 0.7 pad_maximum_fusion.2
  137.1 0.8 projection_finish.1
  (39 shorter events, 1.6 us)
Async XLA Ops:
  0.6 10.5 %collective-permute-start.2 = (bf16[2,32,5376]{2,1,0:T(8,128)(2,1)}, bf16[2,32,5376]{2,1,0:T(8,128)(2,1)S(1)}, u32[]{:S(2)}, u32[]{:S(2)}) collective-permute-start(bf16[2,32,5376]{2,1,0:T(8,128)(2,1)} %refs_0_.1), channel_id=1, source_target_pairs={{0,4},{4,0},{8,12},{12,8},{16,20},{20,16},{24,28},{28,24},{32,36},... | collective-permute-start | bytes 2064392 | tf_op jit(solution)/shard_map/ppermute | solution.py:29
  4.0 1.0 copy-start.2
  5.0 0.9 copy-start.3
  5.9 0.9 copy-start.4
  7.5 3.7 %collective-permute-start = (bf16[2,128,512]{2,1,0:T(8,128)(2,1)S(1)}, bf16[2,128,512]{2,1,0:T(8,128)(2,1)S(1)}, u32[]{:S(2)}, u32[]{:S(2)}) collective-permute-start(bf16[2,128,512]{2,1,0:T(8,128)(2,1)S(1)} %get-tuple-element.50), channel_id=1, source_target_pairs={{0,4},{4,0},{8,12},{12,8},{16,20},{20,16},{24,28},{28,24},{32,36},... | collective-permute-start | bytes 786440 | tf_op jit(solution)/shard_map/ppermute | solution.py:29
  7.6 16.8 %collective-permute-start.3 = (bf16[2,32,5376]{2,1,0:T(8,128)(2,1)}, bf16[2,32,5376]{2,1,0:T(8,128)(2,1)S(1)}, u32[]{:S(2)}, u32[]{:S(2)}) collective-permute-start(bf16[2,32,5376]{2,1,0:T(8,128)(2,1)} %refs_0_.1), channel_id=1, source_target_pairs={{0,3},{1,0},{2,1},{3,2},{4,7},{5,4},{6,5},{7,6},{8,11},{9,8},{10,9... | collective-permute-start | bytes 2064392 | tf_op jit(solution)/shard_map/ppermute | solution.py:66
  8.4 17.7 %collective-permute-start.4 = (bf16[2,32,5376]{2,1,0:T(8,128)(2,1)}, bf16[2,32,5376]{2,1,0:T(8,128)(2,1)S(1)}, u32[]{:S(2)}, u32[]{:S(2)}) collective-permute-start(bf16[2,32,5376]{2,1,0:T(8,128)(2,1)} %refs_0_.1), channel_id=1, source_target_pairs={{0,1},{1,2},{2,3},{3,0},{4,5},{5,6},{6,7},{7,4},{8,9},{9,10},{10,1... | collective-permute-start | bytes 2064392 | tf_op jit(solution)/shard_map/ppermute | solution.py:66
  9.1 2.0 %collective-permute-start.1 = (s32[2,1,128]{2,1,0:T(1,128)}, s32[2,1,128]{2,1,0:T(1,128)S(1)}, u32[]{:S(2)}, u32[]{:S(2)}) collective-permute-start(s32[2,1,128]{2,1,0:T(1,128)} %bitcast.9), channel_id=1, source_target_pairs={{0,4},{4,0},{8,12},{12,8},{16,20},{20,16},{24,28},{28,24},{32,36},... | collective-permute-start | bytes 3080 | tf_op jit(solution)/shard_map/ppermute | solution.py:29
  11.2 14.9 %collective-permute-start.7 = (bf16[2,256,256]{2,1,0:T(8,128)(2,1)S(1)}, bf16[2,256,256]{2,1,0:T(8,128)(2,1)S(1)}, u32[]{:S(2)}, u32[]{:S(2)}) collective-permute-start(bf16[2,256,256]{2,1,0:T(8,128)(2,1)S(1)} %pad_maximum_fusion.kv0), channel_id=1, source_target_pairs={{0,32},{4,36},{8,40},{12,44},{16,48},{20,52},{24,56},{28,60},{32,6... | collective-permute-start | bytes 786440 | tf_op jit(solution)/shard_map/ppermute | solution.py:29
  11.9 17.0 %collective-permute-start.6 = (bf16[2,256,256]{2,1,0:T(8,128)(2,1)S(1)}, bf16[2,256,256]{2,1,0:T(8,128)(2,1)S(1)}, u32[]{:S(2)}, u32[]{:S(2)}) collective-permute-start(bf16[2,256,256]{2,1,0:T(8,128)(2,1)S(1)} %pad_maximum_fusion.kv0), channel_id=1, source_target_pairs={{0,24},{4,28},{8,32},{12,36},{16,40},{20,44},{24,48},{28,52},{32,5... | collective-permute-start | bytes 786440 | tf_op jit(solution)/shard_map/ppermute | solution.py:29
  14.6 21.3 %collective-permute-start.5 = (bf16[2,256,256]{2,1,0:T(8,128)(2,1)S(1)}, bf16[2,256,256]{2,1,0:T(8,128)(2,1)S(1)}, u32[]{:S(2)}, u32[]{:S(2)}) collective-permute-start(bf16[2,256,256]{2,1,0:T(8,128)(2,1)S(1)} %pad_maximum_fusion.kv0), channel_id=1, source_target_pairs={{0,8},{4,12},{8,16},{12,20},{16,24},{20,28},{24,32},{28,36},{32,40... | collective-permute-start | bytes 786440 | tf_op jit(solution)/shard_map/ppermute | solution.py:29
  14.7 2.6 %copy-start = (bf16[5376,512]{1,0:T(8,128)(2,1)S(1)}, bf16[5376,512]{1,0:T(8,128)(2,1)}, u32[]{:S(2)}) copy-start(bf16[5376,512]{1,0:T(8,128)(2,1)} %o_weight.1) | copy-start | bytes 16515076
  17.3 1.1 copy-start.5
  18.4 21.7 %copy-start.1 = (bf16[5376,512]{1,0:T(8,128)(2,1)S(1)}, bf16[5376,512]{1,0:T(8,128)(2,1)}, u32[]{:S(2)}) copy-start(bf16[5376,512]{1,0:T(8,128)(2,1)} %o_weight.1) | copy-start | bytes 16515076
  35.9 4.1 %collective-permute-start.8 = (bf16[2,32,5376]{2,1,0:T(8,128)(2,1)S(1)}, bf16[2,32,5376]{2,1,0:T(8,128)(2,1)S(1)}, u32[]{:S(2)}, u32[]{:S(2)}) collective-permute-start(bf16[2,32,5376]{2,1,0:T(8,128)(2,1)S(1)} %collective-permute-done.3.refs_0_), channel_id=1, source_target_pairs={{0,4},{4,0},{8,12},{12,8},{16,20},{20,16},{24,28},{28,24},{32,36},... | collective-permute-start | bytes 2064392 | tf_op jit(solution)/shard_map/ppermute | solution.py:29
  36.8 3.3 %collective-permute-start.9 = (bf16[2,32,5376]{2,1,0:T(8,128)(2,1)S(1)}, bf16[2,32,5376]{2,1,0:T(8,128)(2,1)S(1)}, u32[]{:S(2)}, u32[]{:S(2)}) collective-permute-start(bf16[2,32,5376]{2,1,0:T(8,128)(2,1)S(1)} %collective-permute-done.4.refs_1_), channel_id=1, source_target_pairs={{0,4},{4,0},{8,12},{12,8},{16,20},{20,16},{24,28},{28,24},{32,36},... | collective-permute-start | bytes 2064392 | tf_op jit(solution)/shard_map/ppermute | solution.py:29
  36.8 12.7 %copy-start.6 = (s32[2,128]{1,0:T(2,128)S(1)}, s32[2,128]{1,0:T(2,128)}, u32[]{:S(2)}) copy-start(s32[2,128]{1,0:T(2,128)} %param.11) | copy-start | bytes 3076
  36.8 11.1 %collective-permute-start.12 = (bf16[2,256,256]{2,1,0:T(8,128)(2,1)S(1)}, bf16[2,256,256]{2,1,0:T(8,128)(2,1)S(1)}, u32[]{:S(2)}, u32[]{:S(2)}) collective-permute-start(bf16[2,256,256]{2,1,0:T(8,128)(2,1)S(1)} %pad_maximum_fusion.kv0), channel_id=1, source_target_pairs={{0,16},{4,20},{8,24},{12,28},{16,32},{20,36},{24,40},{28,44},{32,4... | collective-permute-start | bytes 786440 | tf_op jit(solution)/shard_map/ppermute | solution.py:29
  36.9 11.0 %collective-permute-start.10 = (bf16[1,32,5376]{2,1,0:T(8,128)(2,1)S(1)}, bf16[1,32,5376]{2,1,0:T(8,128)(2,1)S(1)}, u32[]{:S(2)}, u32[]{:S(2)}) collective-permute-start(bf16[1,32,5376]{2,1,0:T(8,128)(2,1)S(1)} %slice.40), channel_id=1, source_target_pairs={{0,1},{1,2},{2,3},{3,0},{4,5},{5,6},{6,7},{7,4},{8,9},{9,10},{10,1... | collective-permute-start | bytes 1032200 | tf_op jit(solution)/shard_map/ppermute | solution.py:66
  37.5 10.5 %collective-permute-start.11 = (bf16[1,32,5376]{2,1,0:T(8,128)(2,1)S(1)}, bf16[1,32,5376]{2,1,0:T(8,128)(2,1)S(1)}, u32[]{:S(2)}, u32[]{:S(2)}) collective-permute-start(bf16[1,32,5376]{2,1,0:T(8,128)(2,1)S(1)} %slice.41), channel_id=1, source_target_pairs={{0,3},{1,0},{2,1},{3,2},{4,7},{5,4},{6,5},{7,6},{8,11},{9,8},{10,9... | collective-permute-start | bytes 1032200 | tf_op jit(solution)/shard_map/ppermute | solution.py:66
  47.9 5.8 %collective-permute-start.13 = (bf16[1,32,5376]{2,1,0:T(8,128)(2,1)S(1)}, bf16[1,32,5376]{2,1,0:T(8,128)(2,1)S(1)}, u32[]{:S(2)}, u32[]{:S(2)}) collective-permute-start(bf16[1,32,5376]{2,1,0:T(8,128)(2,1)S(1)} %collective-permute-done.10.r2a), channel_id=1, source_target_pairs={{0,4},{4,0},{8,12},{12,8},{16,20},{20,16},{24,28},{28,24},{32,36},... | collective-permute-start | bytes 1032200 | tf_op jit(solution)/shard_map/ppermute | solution.py:29
  49.3 4.5 %collective-permute-start.14 = (bf16[1,32,5376]{2,1,0:T(8,128)(2,1)S(1)}, bf16[1,32,5376]{2,1,0:T(8,128)(2,1)S(1)}, u32[]{:S(2)}, u32[]{:S(2)}) collective-permute-start(bf16[1,32,5376]{2,1,0:T(8,128)(2,1)S(1)} %collective-permute-done.11.r2b), channel_id=1, source_target_pairs={{0,4},{4,0},{8,12},{12,8},{16,20},{20,16},{24,28},{28,24},{32,36},... | collective-permute-start | bytes 1032200 | tf_op jit(solution)/shard_map/ppermute | solution.py:29
  57.9 16.9 %collective-permute-start.15 = (bf16[2,4,168,256]{3,2,1,0:T(8,128)(2,1)S(1)}, bf16[2,4,168,256]{3,2,1,0:T(8,128)(2,1)S(1)}, u32[]{:S(2)}, u32[]{:S(2)}) collective-permute-start(bf16[2,4,168,256]{3,2,1,0:T(8,128)(2,1)S(1)} %get-tuple-element.77), channel_id=1, source_target_pairs={{0,8},{4,12},{8,0},{12,4},{16,24},{20,28},{24,16},{28,20},{32,40},... | collective-permute-start | bytes 2064392 | tf_op jit(solution)/shard_map/ppermute | solution.py:29
  58.0 18.1 %collective-permute-start.16 = (bf16[2,4,168,256]{3,2,1,0:T(8,128)(2,1)S(1)}, bf16[2,4,168,256]{3,2,1,0:T(8,128)(2,1)S(1)}, u32[]{:S(2)}, u32[]{:S(2)}) collective-permute-start(bf16[2,4,168,256]{3,2,1,0:T(8,128)(2,1)S(1)} %get-tuple-element.78), channel_id=1, source_target_pairs={{0,24},{4,28},{8,16},{12,20},{16,8},{20,12},{24,0},{28,4},{32,56},... | collective-permute-start | bytes 2064392 | tf_op jit(solution)/shard_map/ppermute | solution.py:29
  62.0 9.5 %collective-permute-start.17 = (bf16[2,256,256]{2,1,0:T(8,128)(2,1)S(1)}, bf16[2,256,256]{2,1,0:T(8,128)(2,1)S(1)}, u32[]{:S(2)}, u32[]{:S(2)}) collective-permute-start(bf16[2,256,256]{2,1,0:T(8,128)(2,1)S(1)} %get-tuple-element.80), channel_id=1, source_target_pairs={{0,224},{4,228},{8,232},{12,236},{16,240},{20,244},{24,248},{28,25... | collective-permute-start | bytes 786440 | tf_op jit(solution)/shard_map/ppermute | solution.py:29
  66.9 2.3 %collective-permute-start.18 = (bf16[2,128,256]{2,1,0:T(8,128)(2,1)S(1)}, bf16[2,128,256]{2,1,0:T(8,128)(2,1)S(1)}, u32[]{:S(2)}, u32[]{:S(2)}) collective-permute-start(bf16[2,128,256]{2,1,0:T(8,128)(2,1)S(1)} %get-tuple-element.81), channel_id=1, source_target_pairs={{0,4},{4,0},{8,12},{12,8},{16,20},{20,16},{24,28},{28,24},{32,36},... | collective-permute-start | bytes 393224 | tf_op jit(solution)/shard_map/ppermute | solution.py:29
  76.2 8.6 %collective-permute-start.20 = (bf16[4,168,256]{2,1,0:T(8,128)(2,1)S(1)}, bf16[4,168,256]{2,1,0:T(8,128)(2,1)S(1)}, u32[]{:S(2)}, u32[]{:S(2)}) collective-permute-start(bf16[4,168,256]{2,1,0:T(8,128)(2,1)S(1)} %fusion.1), channel_id=1, source_target_pairs={{0,8},{4,12},{8,0},{12,4},{16,24},{20,28},{24,16},{28,20},{32,40},... | collective-permute-start | bytes 1032200 | tf_op jit(solution)/shard_map/ppermute | solution.py:29
  76.4 9.4 %collective-permute-start.19 = (bf16[4,168,256]{2,1,0:T(8,128)(2,1)S(1)}, bf16[4,168,256]{2,1,0:T(8,128)(2,1)S(1)}, u32[]{:S(2)}, u32[]{:S(2)}) collective-permute-start(bf16[4,168,256]{2,1,0:T(8,128)(2,1)S(1)} %fusion), channel_id=1, source_target_pairs={{0,24},{4,28},{8,16},{12,20},{16,8},{20,12},{24,0},{28,4},{32,56},... | collective-permute-start | bytes 1032200 | tf_op jit(solution)/shard_map/ppermute | solution.py:29
  87.0 50.1 %all-to-all-start = ((bf16[16,84,256]{2,1,0:T(8,128)(2,1)}), bf16[16,84,256]{2,1,0:T(8,128)(2,1)S(1)}, u32[]{:S(2)}, u32[]{:S(2)}) async-start(bf16[16,84,256]{2,1,0:T(8,128)(2,1)} %projection_merge.1), calls=%async_computation | async-start | bytes 1441792 | tf_op jit(solution)/shard_map/all_to_all | solution.py:57
  94.9 24.2 %collective-permute-start.21 = (bf16[2,256,256]{2,1,0:T(8,128)(2,1)S(1)}, bf16[2,256,256]{2,1,0:T(8,128)(2,1)S(1)}, u32[]{:S(2)}, u32[]{:S(2)}) collective-permute-start(bf16[2,256,256]{2,1,0:T(8,128)(2,1)S(1)} %get-tuple-element.91), channel_id=1, source_target_pairs={{0,248},{4,252},{8,0},{12,4},{16,8},{20,12},{24,16},{28,20},{32,24... | collective-permute-start | bytes 786440 | tf_op jit(solution)/shard_map/ppermute | solution.py:29
  99.1 28.1 %collective-permute-start.22 = (bf16[2,256,256]{2,1,0:T(8,128)(2,1)S(1)}, bf16[2,256,256]{2,1,0:T(8,128)(2,1)S(1)}, u32[]{:S(2)}, u32[]{:S(2)}) collective-permute-start(bf16[2,256,256]{2,1,0:T(8,128)(2,1)S(1)} %get-tuple-element.92), channel_id=1, source_target_pairs={{0,240},{4,244},{8,248},{12,252},{16,0},{20,4},{24,8},{28,12},{32,... | collective-permute-start | bytes 786440 | tf_op jit(solution)/shard_map/ppermute | solution.py:29
  99.3 35.2 %collective-permute-start.23 = (bf16[2,256,256]{2,1,0:T(8,128)(2,1)S(1)}, bf16[2,256,256]{2,1,0:T(8,128)(2,1)S(1)}, u32[]{:S(2)}, u32[]{:S(2)}) collective-permute-start(bf16[2,256,256]{2,1,0:T(8,128)(2,1)S(1)} %get-tuple-element.93), channel_id=1, source_target_pairs={{0,232},{4,236},{8,240},{12,244},{16,248},{20,252},{24,0},{28,4},{... | collective-permute-start | bytes 786440 | tf_op jit(solution)/shard_map/ppermute | solution.py:29
  134.7 1.7 %collective-permute-start.24 = (bf16[2,128,256]{2,1,0:T(8,128)(2,1)S(1)}, bf16[2,128,256]{2,1,0:T(8,128)(2,1)S(1)}, u32[]{:S(2)}, u32[]{:S(2)}) collective-permute-start(bf16[2,128,256]{2,1,0:T(8,128)(2,1)S(1)} %slice.52), channel_id=1, source_target_pairs={{0,4},{4,0},{8,12},{12,8},{16,20},{20,16},{24,28},{28,24},{32,36},... | collective-permute-start | bytes 393224 | tf_op jit(solution)/shard_map/ppermute | solution.py:29

commit v7 on v6

--- a/solution.py
+++ b/solution.py
@@ -509,11 +509,11 @@
     dq_mine, dq_other, g_own, *g_sent = backward(
         q_mine, recv, kvs, weights, attn, d_attn
     )
-    *g_near, g_far = g_sent
-    g_far = chips_ahead(g_far, -4)
+    g_near, g_far = g_sent[:2], g_sent[2:]
+    g_far = [chips_ahead(g, -d) for d, g in enumerate(g_far, 3)]
     dq_recv = to_sibling(dq_other)
-    got_a, got_b, g_own, g_far, dq_recv = lax.optimization_barrier(
-        (got_a, got_b, g_own, g_far, dq_recv)
+    got_a, got_b, g_own, dq_recv, *g_far = lax.optimization_barrier(
+        (got_a, got_b, g_own, dq_recv, *g_far)
     )
 
     def added(*blocks):
@@ -531,7 +531,7 @@
     w_all = z_exchange(w_sum)
     g_near = [chips_ahead(g, -d) for d, g in enumerate(g_near, 1)]
 
-    grads = added(g_own, *g_near, g_far).astype(jnp.bfloat16)
+    grads = added(g_own, *g_near, *g_far).astype(jnp.bfloat16)
     g_mine = grads[:, :shard_rows]
     g_recv = to_sibling(grads[:, shard_rows:])
 

time: 140 us -> 138 us (0.986)
  the two profiles are of different devices: /device:TPU:1 before, /device:TPU:23 now
where the time goes in v7:
time: 138 us; the launch traced here: 137 us
  waiting for transfers between devices  62.9 us (46%)
  starting transfers between devices  42.9 us (31%)
  Pallas kernels  22.2 us (16%)
  local copies, waits for them, and re-layouts  6.49 us (5%)
  other arithmetic  1.92 us (1%)
    ppermute x21, waiting for transfers between devices, ctx_shift(): return lax.ppermute(block, 'ctx', [(i, move(i)) for i in range(count)])  60.1 us
    ppermute x21, starting transfers between devices, ctx_shift(): return lax.ppermute(block, 'ctx', [(i, move(i)) for i in range(count)])  31.2 us
    all_to_all x1, starting transfers between devices, z_exchange(): lax.all_to_all(blocks, 'ctx', 0, 0, axis_index_groups=groups, tiled=True)  7.54 us
    pallas_call x2, Pallas kernels, early_projection(): pl.pallas_call(early_kernel, out_shape=outs, grid_spec=pltpu.PrefetchScal...  7.51 us
    unnamed x14, local copies, waits for them, and re-layouts  6.43 us
    pallas_call x1, Pallas kernels, forward(): pl.pallas_call(forward_kernel, out_shape=outs, grid_spec=pltpu.PrefetchSc...  4.23 us
    ppermute x4, starting transfers between devices, tp_ahead(): lax.ppermute(block, 'tp', [(i, (i + distance) % TP) for i in range(TP)])  4.18 us
    pallas_call x1, Pallas kernels, late_projection(): pl.pallas_call(late_kernel, out_shape=(jax.ShapeDtypeStruct(attn.shape, j...  4.12 us
  transfers between devices with their start and end apart: 26, of which 14 were waited for; matrix products, arithmetic and copies ran while one was open for 1% of the time, Pallas kernels for 12%

profile of v7, /device:TPU:23, one launch (start us, length us, event | category | flops | bytes accessed | tf_op | source)
XLA Modules:
  0.0 137.2 jit_solution(11880459275793055135)
XLA Ops:
  0.6 0.8 collective-permute-start.2
  1.5 0.9 copy-done.2
  2.4 0.9 copy-done.3
  3.3 0.9 copy-done.4
  4.2 0.7 split_heads.1
  5.0 0.6 collective-permute-start.3
  5.6 2.1 %collective-permute-start.4 = (bf16[2,32,5376]{2,1,0:T(8,128)(2,1)}, bf16[2,32,5376]{2,1,0:T(8,128)(2,1)S(1)}, u32[]{:S(2)}, u32[]{:S(2)}) collective-permute-start(bf16[2,32,5376]{2,1,0:T(8,128)(2,1)} %refs_0_.1), channel_id=1, source_target_pairs={{0,1},{1,2},{2,3},{3,0},{4,5},{5,6},{6,7},{7,4},{8,9},{9,10},{10,1... | collective-permute-start | bytes 2064392 | tf_op jit(solution)/shard_map/ppermute | solution.py:66
  7.7 1.0 collective-permute-start.1
  8.7 1.0 collective-permute-done.1.doc_recv
  9.8 1.7 %collective-permute-start.7 = (bf16[2,256,256]{2,1,0:T(8,128)(2,1)S(1)}, bf16[2,256,256]{2,1,0:T(8,128)(2,1)S(1)}, u32[]{:S(2)}, u32[]{:S(2)}) collective-permute-start(bf16[2,256,256]{2,1,0:T(8,128)(2,1)S(1)} %pad_maximum_fusion.kv0), channel_id=1, source_target_pairs={{0,32},{4,36},{8,40},{12,44},{16,48},{20,52},{24,56},{28,60},{32,6... | collective-permute-start | bytes 786440 | tf_op jit(solution)/shard_map/ppermute | solution.py:29
  11.5 1.5 %collective-permute-start.6 = (bf16[2,256,256]{2,1,0:T(8,128)(2,1)S(1)}, bf16[2,256,256]{2,1,0:T(8,128)(2,1)S(1)}, u32[]{:S(2)}, u32[]{:S(2)}) collective-permute-start(bf16[2,256,256]{2,1,0:T(8,128)(2,1)S(1)} %pad_maximum_fusion.kv0), channel_id=1, source_target_pairs={{0,24},{4,28},{8,32},{12,36},{16,40},{20,44},{24,48},{28,52},{32,5... | collective-permute-start | bytes 786440 | tf_op jit(solution)/shard_map/ppermute | solution.py:29
  13.0 1.3 collective-permute-start.5
  14.3 2.6 %copy-done = bf16[5376,512]{1,0:T(8,128)(2,1)S(1)} copy-done((bf16[5376,512]{1,0:T(8,128)(2,1)S(1)}, bf16[5376,512]{1,0:T(8,128)(2,1)}, u32[]{:S(2)}) %copy-start) | copy-done | bytes 5505048
  16.9 1.1 copy-done.5
  18.0 3.3 %projection_early.2 = (bf16[128,256]{1,0:T(8,128)(2,1)S(1)}, bf16[5376,128]{1,0:T(8,128)(2,1)S(1)}) custom-call(s32[4]{0:T(128)S(1)} %pad_add_fusion.scalars, bf16[2,32,5376]{2,1,0:T(8,128)(2,1)S(1)} %copy-done.5, bf16[2,32,5376]{2,1,0:T(8,128)(2,1)S(1)} %collective-permute-done.2.refs_1_, bf16[5376,512]{1,0:T(8,128)(2,1)S(1)} %copy-done), custom_call_target="tpu_custom_call" | custom-call | flops 3523215360 | bytes 12582912 | tf_op jit(solution)/shard_map/projection_early/pallas_call | solution.py:376
  21.3 1.8 %collective-permute-done.3.refs_0_ = bf16[2,32,5376]{2,1,0:T(8,128)(2,1)S(1)} collective-permute-done((bf16[2,32,5376]{2,1,0:T(8,128)(2,1)}, bf16[2,32,5376]{2,1,0:T(8,128)(2,1)S(1)}, u32[]{:S(2)}, u32[]{:S(2)}) %collective-permute-start.3) | collective-permute-done | bytes 688160 | tf_op jit(solution)/shard_map/ppermute | solution.py:66
  23.1 5.1 %collective-permute-done.6.kv3 = bf16[2,256,256]{2,1,0:T(8,128)(2,1)S(1)} collective-permute-done((bf16[2,256,256]{2,1,0:T(8,128)(2,1)S(1)}, bf16[2,256,256]{2,1,0:T(8,128)(2,1)S(1)}, u32[]{:S(2)}, u32[]{:S(2)}) %collective-permute-start.6) | collective-permute-done | bytes 262176 | tf_op jit(solution)/shard_map/ppermute | solution.py:29
  28.2 1.3 collective-permute-start.8
  29.6 4.3 %collective-permute-start.12 = (bf16[2,256,256]{2,1,0:T(8,128)(2,1)S(1)}, bf16[2,256,256]{2,1,0:T(8,128)(2,1)S(1)}, u32[]{:S(2)}, u32[]{:S(2)}) collective-permute-start(bf16[2,256,256]{2,1,0:T(8,128)(2,1)S(1)} %pad_maximum_fusion.kv0), channel_id=1, source_target_pairs={{0,16},{4,20},{8,24},{12,28},{16,32},{20,36},{24,40},{28,44},{32,4... | collective-permute-start | bytes 786440 | tf_op jit(solution)/shard_map/ppermute | solution.py:29
  33.9 1.5 %collective-permute-start.11 = (bf16[1,32,5376]{2,1,0:T(8,128)(2,1)S(1)}, bf16[1,32,5376]{2,1,0:T(8,128)(2,1)S(1)}, u32[]{:S(2)}, u32[]{:S(2)}) collective-permute-start(bf16[1,32,5376]{2,1,0:T(8,128)(2,1)S(1)} %slice.41), channel_id=1, source_target_pairs={{0,3},{1,0},{2,1},{3,2},{4,7},{5,4},{6,5},{7,6},{8,11},{9,8},{10,9... | collective-permute-start | bytes 1032200 | tf_op jit(solution)/shard_map/ppermute | solution.py:66
  35.3 4.2 %projection_early.3 = (bf16[256,256]{1,0:T(8,128)(2,1)S(1)}, bf16[5376,256]{1,0:T(8,128)(2,1)S(1)}) custom-call(s32[4]{0:T(128)S(1)} %pad_add_fusion.scalars, bf16[2,32,5376]{2,1,0:T(8,128)(2,1)S(1)} %collective-permute-done.3.refs_0_, bf16[2,32,5376]{2,1,0:T(8,128)(2,1)S(1)} %collective-permute-done.4.refs_1_, ...), custom_call_target="tpu_custom_call" | custom-call | flops 7046430720 | bytes 12582912 | tf_op jit(solution)/shard_map/projection_early/pallas_call | solution.py:376
  39.6 3.3 %collective-permute-done.12.kv2 = bf16[2,256,256]{2,1,0:T(8,128)(2,1)S(1)} collective-permute-done((bf16[2,256,256]{2,1,0:T(8,128)(2,1)S(1)}, bf16[2,256,256]{2,1,0:T(8,128)(2,1)S(1)}, u32[]{:S(2)}, u32[]{:S(2)}) %collective-permute-start.12) | collective-permute-done | bytes 262176 | tf_op jit(solution)/shard_map/ppermute | solution.py:29
  42.8 1.0 collective-permute-done.11.r2b
  43.9 1.7 %collective-permute-start.13 = (bf16[1,32,5376]{2,1,0:T(8,128)(2,1)S(1)}, bf16[1,32,5376]{2,1,0:T(8,128)(2,1)S(1)}, u32[]{:S(2)}, u32[]{:S(2)}) collective-permute-start(bf16[1,32,5376]{2,1,0:T(8,128)(2,1)S(1)} %collective-permute-done.10.r2a), channel_id=1, source_target_pairs={{0,4},{4,0},{8,12},{12,8},{16,20},{20,16},{24,28},{28,24},{32,36},... | collective-permute-start | bytes 1032200 | tf_op jit(solution)/shard_map/ppermute | solution.py:29
  45.5 4.2 %attention_forward.1 = (bf16[2,256,256]{2,1,0:T(8,128)(2,1)S(1)}, bf16[2,2,1280,256]{3,2,1,0:T(8,128)(2,1)S(1)}) custom-call(s32[4]{0:T(128)S(1)} %pad_add_fusion.scalars, bf16[2,128,256]{2,1,0:T(8,128)(2,1)S(1)} %get-tuple-element.52.mine, bf16[2,128,512]{2,1,0:T(8,128)(2,1)S(1)} %collective-permute-done.recv, ...), custom_call_target="tpu_custom_call" | custom-call | flops 671088640 | bytes 8388608 | tf_op jit(solution)/shard_map/attention_forward/pallas_call | solution.py:345
  49.8 4.1 %projection_late.1 = (bf16[2,256,256]{2,1,0:T(8,128)(2,1)S(1)}, bf16[2,4,168,256]{3,2,1,0:T(8,128)(2,1)S(1)}, bf16[2,4,168,256]{3,2,1,0:T(8,128)(2,1)S(1)}, bf16...) custom-call(s32[4]{0:T(128)S(1)} %pad_add_fusion.scalars, ...), custom_call_target="tpu_custom_call" | custom-call | flops 2113929216 | bytes 12582912 | tf_op jit(solution)/shard_map/projection_late/pallas_call | solution.py:410
  54.0 4.0 %collective-permute-start.16 = (bf16[2,4,168,256]{3,2,1,0:T(8,128)(2,1)S(1)}, bf16[2,4,168,256]{3,2,1,0:T(8,128)(2,1)S(1)}, u32[]{:S(2)}, u32[]{:S(2)}) collective-permute-start(bf16[2,4,168,256]{3,2,1,0:T(8,128)(2,1)S(1)} %get-tuple-element.78), channel_id=1, source_target_pairs={{0,24},{4,28},{8,16},{12,20},{16,8},{20,12},{24,0},{28,4},{32,56},... | collective-permute-start | bytes 2064392 | tf_op jit(solution)/shard_map/ppermute | solution.py:29
  58.0 3.8 %attention_backward.1 = (bf16[2,128,256]{2,1,0:T(8,128)(2,1)S(1)}, bf16[2,128,256]{2,1,0:T(8,128)(2,1)S(1)}, f32[2,256,256]{2,1,0:T(8,128)S(1)}, bf16[2,256,256]...) custom-call(bf16[2,128,256]{2,1,0:T(8,128)(2,1)S(1)} %get-tuple-elem, ...), custom_call_target="tpu_custom_call" | custom-call | flops 1677721600 | bytes 8388608 | tf_op jit(solution)/shard_map/attention_backward/pallas_call | solution.py:446
  61.8 2.5 %collective-permute-start.18 = (bf16[2,256,256]{2,1,0:T(8,128)(2,1)S(1)}, bf16[2,256,256]{2,1,0:T(8,128)(2,1)S(1)}, u32[]{:S(2)}, u32[]{:S(2)}) collective-permute-start(bf16[2,256,256]{2,1,0:T(8,128)(2,1)S(1)} %get-tuple-element.81), channel_id=1, source_target_pairs={{0,232},{4,236},{8,240},{12,244},{16,248},{20,252},{24,0},{28,4},{... | collective-permute-start | bytes 786440 | tf_op jit(solution)/shard_map/ppermute | solution.py:29
  64.3 0.3 collective-permute-start.19
  64.5 1.3 collective-permute-start.17
  65.8 1.0 collective-permute-done.17
  66.8 3.1 %collective-permute-done.18 = bf16[2,256,256]{2,1,0:T(8,128)(2,1)S(1)} collective-permute-done((bf16[2,256,256]{2,1,0:T(8,128)(2,1)S(1)}, bf16[2,256,256]{2,1,0:T(8,128)(2,1)S(1)}, u32[]{:S(2)}, u32[]{:S(2)}) %collective-permute-start.18) | collective-permute-done | bytes 262176 | tf_op jit(solution)/shard_map/ppermute | solution.py:29
  69.9 5.4 %collective-permute-done.19 = bf16[2,256,256]{2,1,0:T(8,128)(2,1)S(1)} collective-permute-done((bf16[2,256,256]{2,1,0:T(8,128)(2,1)S(1)}, bf16[2,256,256]{2,1,0:T(8,128)(2,1)S(1)}, u32[]{:S(2)}, u32[]{:S(2)}) %collective-permute-start.19) | collective-permute-done | bytes 262176 | tf_op jit(solution)/shard_map/ppermute | solution.py:29
  75.3 3.6 %collective-permute-done.16.got_b = bf16[2,4,168,256]{3,2,1,0:T(8,128)(2,1)S(1)} collective-permute-done((bf16[2,4,168,256]{3,2,1,0:T(8,128)(2,1)S(1)}, bf16[2,4,168,256]{3,2,1,0:T(8,128)(2,1)S(1)}, u32[]{:S(2)}, u32[]{:S(2)}) %collective-permute-start.16) | collective-permute-done | bytes 688160 | tf_op jit(solution)/shard_map/ppermute | solution.py:29
  79.2 2.9 %collective-permute-start.20 = (bf16[4,168,256]{2,1,0:T(8,128)(2,1)S(1)}, bf16[4,168,256]{2,1,0:T(8,128)(2,1)S(1)}, u32[]{:S(2)}, u32[]{:S(2)}) collective-permute-start(bf16[4,168,256]{2,1,0:T(8,128)(2,1)S(1)} %fusion), channel_id=1, source_target_pairs={{0,24},{4,28},{8,16},{12,20},{16,8},{20,12},{24,0},{28,4},{32,56},... | collective-permute-start | bytes 1032200 | tf_op jit(solution)/shard_map/ppermute | solution.py:29
  82.1 5.5 %collective-permute-done.21.last_b = bf16[4,168,256]{2,1,0:T(8,128)(2,1)S(1)} collective-permute-done((bf16[4,168,256]{2,1,0:T(8,128)(2,1)S(1)}, bf16[4,168,256]{2,1,0:T(8,128)(2,1)S(1)}, u32[]{:S(2)}, u32[]{:S(2)}) %collective-permute-start.21) | collective-permute-done | bytes 344096 | tf_op jit(solution)/shard_map/ppermute | solution.py:29
  87.6 1.5 %collective-permute-done.20.last_a = bf16[4,168,256]{2,1,0:T(8,128)(2,1)S(1)} collective-permute-done((bf16[4,168,256]{2,1,0:T(8,128)(2,1)S(1)}, bf16[4,168,256]{2,1,0:T(8,128)(2,1)S(1)}, u32[]{:S(2)}, u32[]{:S(2)}) %collective-permute-start.20) | collective-permute-done | bytes 344096 | tf_op jit(solution)/shard_map/ppermute | solution.py:29
  89.1 1.2 projection_merge.1
  90.3 7.5 %all-to-all-start = ((bf16[16,84,256]{2,1,0:T(8,128)(2,1)}), bf16[16,84,256]{2,1,0:T(8,128)(2,1)S(1)}, u32[]{:S(2)}, u32[]{:S(2)}) async-start(bf16[16,84,256]{2,1,0:T(8,128)(2,1)} %projection_merge.1), calls=%async_computation | async-start | bytes 1441792 | tf_op jit(solution)/shard_map/all_to_all | solution.py:57
  97.9 1.5 %collective-permute-start.22 = (bf16[2,256,256]{2,1,0:T(8,128)(2,1)S(1)}, bf16[2,256,256]{2,1,0:T(8,128)(2,1)S(1)}, u32[]{:S(2)}, u32[]{:S(2)}) collective-permute-start(bf16[2,256,256]{2,1,0:T(8,128)(2,1)S(1)} %get-tuple-element.91), channel_id=1, source_target_pairs={{0,248},{4,252},{8,0},{12,4},{16,8},{20,12},{24,16},{28,20},{32,24... | collective-permute-start | bytes 786440 | tf_op jit(solution)/shard_map/ppermute | solution.py:29
  99.3 4.0 %collective-permute-start.23 = (bf16[2,256,256]{2,1,0:T(8,128)(2,1)S(1)}, bf16[2,256,256]{2,1,0:T(8,128)(2,1)S(1)}, u32[]{:S(2)}, u32[]{:S(2)}) collective-permute-start(bf16[2,256,256]{2,1,0:T(8,128)(2,1)S(1)} %get-tuple-element.92), channel_id=1, source_target_pairs={{0,240},{4,244},{8,248},{12,252},{16,0},{20,4},{24,8},{28,12},{32,... | collective-permute-start | bytes 786440 | tf_op jit(solution)/shard_map/ppermute | solution.py:29
  103.3 2.2 %collective-permute-done.22 = bf16[2,256,256]{2,1,0:T(8,128)(2,1)S(1)} collective-permute-done((bf16[2,256,256]{2,1,0:T(8,128)(2,1)S(1)}, bf16[2,256,256]{2,1,0:T(8,128)(2,1)S(1)}, u32[]{:S(2)}, u32[]{:S(2)}) %collective-permute-start.22) | collective-permute-done | bytes 262176 | tf_op jit(solution)/shard_map/ppermute | solution.py:29
  105.6 28.0 %collective-permute-done.23 = bf16[2,256,256]{2,1,0:T(8,128)(2,1)S(1)} collective-permute-done((bf16[2,256,256]{2,1,0:T(8,128)(2,1)S(1)}, bf16[2,256,256]{2,1,0:T(8,128)(2,1)S(1)}, u32[]{:S(2)}, u32[]{:S(2)}) %collective-permute-start.23) | collective-permute-done | bytes 262176 | tf_op jit(solution)/shard_map/ppermute | solution.py:29
  133.7 1.0 collective-permute-start.24
  134.7 0.7 pad_maximum_fusion.1
  135.7 0.7 pad_maximum_fusion.2
  136.4 0.8 projection_finish.1
  (39 shorter events, 1.2 us)
Async XLA Ops:
  0.6 9.1 %collective-permute-start.2 = (bf16[2,32,5376]{2,1,0:T(8,128)(2,1)}, bf16[2,32,5376]{2,1,0:T(8,128)(2,1)S(1)}, u32[]{:S(2)}, u32[]{:S(2)}) collective-permute-start(bf16[2,32,5376]{2,1,0:T(8,128)(2,1)} %refs_0_.1), channel_id=1, source_target_pairs={{0,4},{4,0},{8,12},{12,8},{16,20},{20,16},{24,28},{28,24},{32,36},... | collective-permute-start | bytes 2064392 | tf_op jit(solution)/shard_map/ppermute | solution.py:29
  1.5 1.0 copy-start.2
  2.4 0.9 copy-start.3
  3.3 0.9 copy-start.4
  4.9 4.9 %collective-permute-start = (bf16[2,128,512]{2,1,0:T(8,128)(2,1)S(1)}, bf16[2,128,512]{2,1,0:T(8,128)(2,1)S(1)}, u32[]{:S(2)}, u32[]{:S(2)}) collective-permute-start(bf16[2,128,512]{2,1,0:T(8,128)(2,1)S(1)} %get-tuple-element.50), channel_id=1, source_target_pairs={{0,4},{4,0},{8,12},{12,8},{16,20},{20,16},{24,28},{28,24},{32,36},... | collective-permute-start | bytes 786440 | tf_op jit(solution)/shard_map/ppermute | solution.py:29
  5.0 18.0 %collective-permute-start.3 = (bf16[2,32,5376]{2,1,0:T(8,128)(2,1)}, bf16[2,32,5376]{2,1,0:T(8,128)(2,1)S(1)}, u32[]{:S(2)}, u32[]{:S(2)}) collective-permute-start(bf16[2,32,5376]{2,1,0:T(8,128)(2,1)} %refs_0_.1), channel_id=1, source_target_pairs={{0,3},{1,0},{2,1},{3,2},{4,7},{5,4},{6,5},{7,6},{8,11},{9,8},{10,9... | collective-permute-start | bytes 2064392 | tf_op jit(solution)/shard_map/ppermute | solution.py:66
  5.6 17.5 %collective-permute-start.4 = (bf16[2,32,5376]{2,1,0:T(8,128)(2,1)}, bf16[2,32,5376]{2,1,0:T(8,128)(2,1)S(1)}, u32[]{:S(2)}, u32[]{:S(2)}) collective-permute-start(bf16[2,32,5376]{2,1,0:T(8,128)(2,1)} %refs_0_.1), channel_id=1, source_target_pairs={{0,1},{1,2},{2,3},{3,0},{4,5},{5,6},{6,7},{7,4},{8,9},{9,10},{10,1... | collective-permute-start | bytes 2064392 | tf_op jit(solution)/shard_map/ppermute | solution.py:66
  7.7 2.0 %collective-permute-start.1 = (s32[2,1,128]{2,1,0:T(1,128)}, s32[2,1,128]{2,1,0:T(1,128)S(1)}, u32[]{:S(2)}, u32[]{:S(2)}) collective-permute-start(s32[2,1,128]{2,1,0:T(1,128)} %bitcast.9), channel_id=1, source_target_pairs={{0,4},{4,0},{8,12},{12,8},{16,20},{20,16},{24,28},{28,24},{32,36},... | collective-permute-start | bytes 3080 | tf_op jit(solution)/shard_map/ppermute | solution.py:29
  9.8 13.3 %collective-permute-start.7 = (bf16[2,256,256]{2,1,0:T(8,128)(2,1)S(1)}, bf16[2,256,256]{2,1,0:T(8,128)(2,1)S(1)}, u32[]{:S(2)}, u32[]{:S(2)}) collective-permute-start(bf16[2,256,256]{2,1,0:T(8,128)(2,1)S(1)} %pad_maximum_fusion.kv0), channel_id=1, source_target_pairs={{0,32},{4,36},{8,40},{12,44},{16,48},{20,52},{24,56},{28,60},{32,6... | collective-permute-start | bytes 786440 | tf_op jit(solution)/shard_map/ppermute | solution.py:29
  11.5 16.7 %collective-permute-start.6 = (bf16[2,256,256]{2,1,0:T(8,128)(2,1)S(1)}, bf16[2,256,256]{2,1,0:T(8,128)(2,1)S(1)}, u32[]{:S(2)}, u32[]{:S(2)}) collective-permute-start(bf16[2,256,256]{2,1,0:T(8,128)(2,1)S(1)} %pad_maximum_fusion.kv0), channel_id=1, source_target_pairs={{0,24},{4,28},{8,32},{12,36},{16,40},{20,44},{24,48},{28,52},{32,5... | collective-permute-start | bytes 786440 | tf_op jit(solution)/shard_map/ppermute | solution.py:29
  13.0 15.2 %collective-permute-start.5 = (bf16[2,256,256]{2,1,0:T(8,128)(2,1)S(1)}, bf16[2,256,256]{2,1,0:T(8,128)(2,1)S(1)}, u32[]{:S(2)}, u32[]{:S(2)}) collective-permute-start(bf16[2,256,256]{2,1,0:T(8,128)(2,1)S(1)} %pad_maximum_fusion.kv0), channel_id=1, source_target_pairs={{0,8},{4,12},{8,16},{12,20},{16,24},{20,28},{24,32},{28,36},{32,40... | collective-permute-start | bytes 786440 | tf_op jit(solution)/shard_map/ppermute | solution.py:29
  14.3 2.6 %copy-start = (bf16[5376,512]{1,0:T(8,128)(2,1)S(1)}, bf16[5376,512]{1,0:T(8,128)(2,1)}, u32[]{:S(2)}) copy-start(bf16[5376,512]{1,0:T(8,128)(2,1)} %o_weight.1) | copy-start | bytes 16515076
  16.9 1.1 copy-start.5
  18.0 17.3 %copy-start.1 = (bf16[5376,512]{1,0:T(8,128)(2,1)S(1)}, bf16[5376,512]{1,0:T(8,128)(2,1)}, u32[]{:S(2)}) copy-start(bf16[5376,512]{1,0:T(8,128)(2,1)} %o_weight.1) | copy-start | bytes 16515076
  28.2 7.1 %collective-permute-start.8 = (bf16[2,32,5376]{2,1,0:T(8,128)(2,1)S(1)}, bf16[2,32,5376]{2,1,0:T(8,128)(2,1)S(1)}, u32[]{:S(2)}, u32[]{:S(2)}) collective-permute-start(bf16[2,32,5376]{2,1,0:T(8,128)(2,1)S(1)} %collective-permute-done.3.refs_0_), channel_id=1, source_target_pairs={{0,4},{4,0},{8,12},{12,8},{16,20},{20,16},{24,28},{28,24},{32,36},... | collective-permute-start | bytes 2064392 | tf_op jit(solution)/shard_map/ppermute | solution.py:29
  29.5 5.8 %collective-permute-start.9 = (bf16[2,32,5376]{2,1,0:T(8,128)(2,1)S(1)}, bf16[2,32,5376]{2,1,0:T(8,128)(2,1)S(1)}, u32[]{:S(2)}, u32[]{:S(2)}) collective-permute-start(bf16[2,32,5376]{2,1,0:T(8,128)(2,1)S(1)} %collective-permute-done.4.refs_1_), channel_id=1, source_target_pairs={{0,4},{4,0},{8,12},{12,8},{16,20},{20,16},{24,28},{28,24},{32,36},... | collective-permute-start | bytes 2064392 | tf_op jit(solution)/shard_map/ppermute | solution.py:29
  29.5 16.0 %copy-start.6 = (s32[2,128]{1,0:T(2,128)S(1)}, s32[2,128]{1,0:T(2,128)}, u32[]{:S(2)}) copy-start(s32[2,128]{1,0:T(2,128)} %param.11) | copy-start | bytes 3076
  29.6 13.3 %collective-permute-start.12 = (bf16[2,256,256]{2,1,0:T(8,128)(2,1)S(1)}, bf16[2,256,256]{2,1,0:T(8,128)(2,1)S(1)}, u32[]{:S(2)}, u32[]{:S(2)}) collective-permute-start(bf16[2,256,256]{2,1,0:T(8,128)(2,1)S(1)} %pad_maximum_fusion.kv0), channel_id=1, source_target_pairs={{0,16},{4,20},{8,24},{12,28},{16,32},{20,36},{24,40},{28,44},{32,4... | collective-permute-start | bytes 786440 | tf_op jit(solution)/shard_map/ppermute | solution.py:29
  33.8 9.0 %collective-permute-start.10 = (bf16[1,32,5376]{2,1,0:T(8,128)(2,1)S(1)}, bf16[1,32,5376]{2,1,0:T(8,128)(2,1)S(1)}, u32[]{:S(2)}, u32[]{:S(2)}) collective-permute-start(bf16[1,32,5376]{2,1,0:T(8,128)(2,1)S(1)} %slice.40), channel_id=1, source_target_pairs={{0,1},{1,2},{2,3},{3,0},{4,5},{5,6},{6,7},{7,4},{8,9},{9,10},{10,1... | collective-permute-start | bytes 1032200 | tf_op jit(solution)/shard_map/ppermute | solution.py:66
  33.9 10.0 %collective-permute-start.11 = (bf16[1,32,5376]{2,1,0:T(8,128)(2,1)S(1)}, bf16[1,32,5376]{2,1,0:T(8,128)(2,1)S(1)}, u32[]{:S(2)}, u32[]{:S(2)}) collective-permute-start(bf16[1,32,5376]{2,1,0:T(8,128)(2,1)S(1)} %slice.41), channel_id=1, source_target_pairs={{0,3},{1,0},{2,1},{3,2},{4,7},{5,4},{6,5},{7,6},{8,11},{9,8},{10,9... | collective-permute-start | bytes 1032200 | tf_op jit(solution)/shard_map/ppermute | solution.py:66
  43.9 5.9 %collective-permute-start.13 = (bf16[1,32,5376]{2,1,0:T(8,128)(2,1)S(1)}, bf16[1,32,5376]{2,1,0:T(8,128)(2,1)S(1)}, u32[]{:S(2)}, u32[]{:S(2)}) collective-permute-start(bf16[1,32,5376]{2,1,0:T(8,128)(2,1)S(1)} %collective-permute-done.10.r2a), channel_id=1, source_target_pairs={{0,4},{4,0},{8,12},{12,8},{16,20},{20,16},{24,28},{28,24},{32,36},... | collective-permute-start | bytes 1032200 | tf_op jit(solution)/shard_map/ppermute | solution.py:29
  45.5 4.3 %collective-permute-start.14 = (bf16[1,32,5376]{2,1,0:T(8,128)(2,1)S(1)}, bf16[1,32,5376]{2,1,0:T(8,128)(2,1)S(1)}, u32[]{:S(2)}, u32[]{:S(2)}) collective-permute-start(bf16[1,32,5376]{2,1,0:T(8,128)(2,1)S(1)} %collective-permute-done.11.r2b), channel_id=1, source_target_pairs={{0,4},{4,0},{8,12},{12,8},{16,20},{20,16},{24,28},{28,24},{32,36},... | collective-permute-start | bytes 1032200 | tf_op jit(solution)/shard_map/ppermute | solution.py:29
  53.9 21.4 %collective-permute-start.15 = (bf16[2,4,168,256]{3,2,1,0:T(8,128)(2,1)S(1)}, bf16[2,4,168,256]{3,2,1,0:T(8,128)(2,1)S(1)}, u32[]{:S(2)}, u32[]{:S(2)}) collective-permute-start(bf16[2,4,168,256]{3,2,1,0:T(8,128)(2,1)S(1)} %get-tuple-element.77), channel_id=1, source_target_pairs={{0,8},{4,12},{8,0},{12,4},{16,24},{20,28},{24,16},{28,20},{32,40},... | collective-permute-start | bytes 2064392 | tf_op jit(solution)/shard_map/ppermute | solution.py:29
  54.0 24.9 %collective-permute-start.16 = (bf16[2,4,168,256]{3,2,1,0:T(8,128)(2,1)S(1)}, bf16[2,4,168,256]{3,2,1,0:T(8,128)(2,1)S(1)}, u32[]{:S(2)}, u32[]{:S(2)}) collective-permute-start(bf16[2,4,168,256]{3,2,1,0:T(8,128)(2,1)S(1)} %get-tuple-element.78), channel_id=1, source_target_pairs={{0,24},{4,28},{8,16},{12,20},{16,8},{20,12},{24,0},{28,4},{32,56},... | collective-permute-start | bytes 2064392 | tf_op jit(solution)/shard_map/ppermute | solution.py:29
  61.8 8.1 %collective-permute-start.18 = (bf16[2,256,256]{2,1,0:T(8,128)(2,1)S(1)}, bf16[2,256,256]{2,1,0:T(8,128)(2,1)S(1)}, u32[]{:S(2)}, u32[]{:S(2)}) collective-permute-start(bf16[2,256,256]{2,1,0:T(8,128)(2,1)S(1)} %get-tuple-element.81), channel_id=1, source_target_pairs={{0,232},{4,236},{8,240},{12,244},{16,248},{20,252},{24,0},{28,4},{... | collective-permute-start | bytes 786440 | tf_op jit(solution)/shard_map/ppermute | solution.py:29
  64.3 11.1 %collective-permute-start.19 = (bf16[2,256,256]{2,1,0:T(8,128)(2,1)S(1)}, bf16[2,256,256]{2,1,0:T(8,128)(2,1)S(1)}, u32[]{:S(2)}, u32[]{:S(2)}) collective-permute-start(bf16[2,256,256]{2,1,0:T(8,128)(2,1)S(1)} %get-tuple-element.82), channel_id=1, source_target_pairs={{0,224},{4,228},{8,232},{12,236},{16,240},{20,244},{24,248},{28,25... | collective-permute-start | bytes 786440 | tf_op jit(solution)/shard_map/ppermute | solution.py:29
  64.5 2.3 %collective-permute-start.17 = (bf16[2,128,256]{2,1,0:T(8,128)(2,1)S(1)}, bf16[2,128,256]{2,1,0:T(8,128)(2,1)S(1)}, u32[]{:S(2)}, u32[]{:S(2)}) collective-permute-start(bf16[2,128,256]{2,1,0:T(8,128)(2,1)S(1)} %get-tuple-element.80), channel_id=1, source_target_pairs={{0,4},{4,0},{8,12},{12,8},{16,20},{20,16},{24,28},{28,24},{32,36},... | collective-permute-start | bytes 393224 | tf_op jit(solution)/shard_map/ppermute | solution.py:29
  79.0 8.6 %collective-permute-start.21 = (bf16[4,168,256]{2,1,0:T(8,128)(2,1)S(1)}, bf16[4,168,256]{2,1,0:T(8,128)(2,1)S(1)}, u32[]{:S(2)}, u32[]{:S(2)}) collective-permute-start(bf16[4,168,256]{2,1,0:T(8,128)(2,1)S(1)} %fusion.1), channel_id=1, source_target_pairs={{0,8},{4,12},{8,0},{12,4},{16,24},{20,28},{24,16},{28,20},{32,40},... | collective-permute-start | bytes 1032200 | tf_op jit(solution)/shard_map/ppermute | solution.py:29
  79.2 9.9 %collective-permute-start.20 = (bf16[4,168,256]{2,1,0:T(8,128)(2,1)S(1)}, bf16[4,168,256]{2,1,0:T(8,128)(2,1)S(1)}, u32[]{:S(2)}, u32[]{:S(2)}) collective-permute-start(bf16[4,168,256]{2,1,0:T(8,128)(2,1)S(1)} %fusion), channel_id=1, source_target_pairs={{0,24},{4,28},{8,16},{12,20},{16,8},{20,12},{24,0},{28,4},{32,56},... | collective-permute-start | bytes 1032200 | tf_op jit(solution)/shard_map/ppermute | solution.py:29
  90.3 46.1 %all-to-all-start = ((bf16[16,84,256]{2,1,0:T(8,128)(2,1)}), bf16[16,84,256]{2,1,0:T(8,128)(2,1)S(1)}, u32[]{:S(2)}, u32[]{:S(2)}) async-start(bf16[16,84,256]{2,1,0:T(8,128)(2,1)} %projection_merge.1), calls=%async_computation | async-start | bytes 1441792 | tf_op jit(solution)/shard_map/all_to_all | solution.py:57
  97.9 7.7 %collective-permute-start.22 = (bf16[2,256,256]{2,1,0:T(8,128)(2,1)S(1)}, bf16[2,256,256]{2,1,0:T(8,128)(2,1)S(1)}, u32[]{:S(2)}, u32[]{:S(2)}) collective-permute-start(bf16[2,256,256]{2,1,0:T(8,128)(2,1)S(1)} %get-tuple-element.91), channel_id=1, source_target_pairs={{0,248},{4,252},{8,0},{12,4},{16,8},{20,12},{24,16},{28,20},{32,24... | collective-permute-start | bytes 786440 | tf_op jit(solution)/shard_map/ppermute | solution.py:29
  99.3 34.2 %collective-permute-start.23 = (bf16[2,256,256]{2,1,0:T(8,128)(2,1)S(1)}, bf16[2,256,256]{2,1,0:T(8,128)(2,1)S(1)}, u32[]{:S(2)}, u32[]{:S(2)}) collective-permute-start(bf16[2,256,256]{2,1,0:T(8,128)(2,1)S(1)} %get-tuple-element.92), channel_id=1, source_target_pairs={{0,240},{4,244},{8,248},{12,252},{16,0},{20,4},{24,8},{28,12},{32,... | collective-permute-start | bytes 786440 | tf_op jit(solution)/shard_map/ppermute | solution.py:29
  133.7 1.9 %collective-permute-start.24 = (bf16[2,128,256]{2,1,0:T(8,128)(2,1)S(1)}, bf16[2,128,256]{2,1,0:T(8,128)(2,1)S(1)}, u32[]{:S(2)}, u32[]{:S(2)}) collective-permute-start(bf16[2,128,256]{2,1,0:T(8,128)(2,1)S(1)} %slice.52), channel_id=1, source_target_pairs={{0,4},{4,0},{8,12},{12,8},{16,20},{20,16},{24,28},{28,24},{32,36},... | collective-permute-start | bytes 393224 | tf_op jit(solution)/shard_map/ppermute | solution.py:29

commit v8 on v5

--- a/solution.py
+++ b/solution.py
@@ -60,6 +60,10 @@
 def chips_ahead(block, distance):
     count = CORES * CHIPS_Y * CHIPS_Z
     return ctx_shift(block, lambda i: (i + CORES * distance) % count)
+
+
+def y_ahead(block, distance):
+    return y_route(block, lambda y: (y + distance) % CHIPS_Y)
 
 
 def tp_ahead(block, distance):
@@ -477,23 +481,25 @@
     doc_mine = doc_start[:, None, :]
     doc_recv = to_sibling(doc_mine)
     t0 = to_sibling(d_out)
-    recv, doc_recv, t0, scalars, first = lax.optimization_barrier(
-        (recv, doc_recv, t0, scalars, first)
+    recv, doc_recv, t0, scalars, first, one_row, two_rows = lax.optimization_barrier(
+        (recv, doc_recv, t0, scalars, first, y < 1, y < 2)
     )
     kv0 = jnp.concatenate([kv_mine, recv[..., -2 * HEAD_SIZE :]], axis=1)
-    kv1, kv3, kv4 = (chips_ahead(kv0, d) for d in (1, 3, 4))
+    kv4, kv1 = (chips_ahead(kv0, d) for d in (4, 1))
     own, own_t = early_projection(scalars, [d_out, t0], o_weight)
 
-    r1, r3, own, kv1, kv3, kv4, kv_again = lax.optimization_barrier(
-        (r1, r3, own, kv1, kv3, kv4, kv0)
-    )
-    kv2 = chips_ahead(kv_again, 2)
+    kv_two = jnp.where(two_rows, kv0, kv4)
+    kv_three = jnp.where(one_row, kv0, kv4)
+    r1, r3, own, kv1, kv_two, kv_three = lax.optimization_barrier(
+        (r1, r3, own, kv1, kv_two, kv_three)
+    )
+    kv2, kv3 = y_ahead(kv_two, 2), y_ahead(kv_three, 3)
     r2a = tp_ahead(r3[:1], 1)
     r2b = tp_ahead(r1[1:], -1)
     near, near_t = early_projection(
         scalars, [r1, r3, to_sibling(r1), to_sibling(r3)], o_weight
     )
-    near, r2a, r2b, kv2 = lax.optimization_barrier((near, r2a, r2b, kv2))
+    near, r2a, r2b, kv2, kv3 = lax.optimization_barrier((near, r2a, r2b, kv2, kv3))
     kvs = [kv0, kv1, kv2, kv3, kv4]
     attn, weights = forward(scalars, q_mine, recv, kvs, doc_mine, doc_recv)
     d_attn, sent_a, kept_a, sent_b, kept_b = late_projection(

time: 131 us -> 130 us (level)
  waiting for transfers between devices: 64.7 us -> 56.2 us
  starting transfers between devices: 34.7 us -> 41.9 us
    ppermute x21, waiting for transfers between devices: 41.8 us -> 31.9 us  [ctx_shift(): return lax.ppermute(block, 'ctx', [(i, move(i)) for i in range(count)])]
    ppermute x21, starting transfers between devices: 21.8 us -> 26.6 us  [ctx_shift(): return lax.ppermute(block, 'ctx', [(i, move(i)) for i in range(count)])]
    all_to_all x1, starting transfers between devices: 8.2 us -> 11.1 us  [z_exchange(): lax.all_to_all(blocks, 'ctx', 0, 0, axis_index_groups=groups, tiled=True)]
    ppermute x4, waiting for transfers between devices: 4.46 us -> 5.87 us  [tp_ahead(): lax.ppermute(block, 'tp', [(i, (i + distance) % TP) for i in range(TP)])]
  transfers between devices with their start and end apart: 26 -> 26, of which waited for: 13 -> 12; matrix products, arithmetic and copies ran while one was open for 1% -> 2% of each run, Pallas kernels for 12% -> 12%
where the time goes in v8:
time: 130 us
  waiting for transfers between devices  56.2 us (43%)
  starting transfers between devices  41.9 us (32%)
  Pallas kernels  22.2 us (17%)
  local copies, waits for them, and re-layouts  6.5 us (5%)
  other arithmetic  2.02 us (2%)
    ppermute x21, waiting for transfers between devices, ctx_shift(): return lax.ppermute(block, 'ctx', [(i, move(i)) for i in range(count)])  31.9 us
    ppermute x21, starting transfers between devices, ctx_shift(): return lax.ppermute(block, 'ctx', [(i, move(i)) for i in range(count)])  26.6 us
    all_to_all x1, waiting for transfers between devices, z_exchange(): lax.all_to_all(blocks, 'ctx', 0, 0, axis_index_groups=groups, tiled=True)  18.5 us
    all_to_all x1, starting transfers between devices, z_exchange(): lax.all_to_all(blocks, 'ctx', 0, 0, axis_index_groups=groups, tiled=True)  11.1 us
    pallas_call x2, Pallas kernels, early_projection(): pl.pallas_call(early_kernel, out_shape=outs, grid_spec=pltpu.PrefetchScal...  7.51 us
    unnamed x14, local copies, waits for them, and re-layouts  6.43 us
    ppermute x4, waiting for transfers between devices, tp_ahead(): lax.ppermute(block, 'tp', [(i, (i + distance) % TP) for i in range(TP)])  5.87 us
    pallas_call x1, Pallas kernels, forward(): pl.pallas_call(forward_kernel, out_shape=outs, grid_spec=pltpu.PrefetchSc...  4.23 us
  transfers between devices with their start and end apart: 26, of which 12 were waited for; matrix products, arithmetic and copies ran while one was open for 2% of the time, Pallas kernels for 12%

profile of v8, /device:TPU:1, one launch (start us, length us, event | category | flops | bytes accessed | tf_op | source)
XLA Modules:
  0.0 129.6 jit_solution(11786302923744574945)
XLA Ops:
  0.6 3.3 %collective-permute-start.2 = (bf16[2,32,5376]{2,1,0:T(8,128)(2,1)}, bf16[2,32,5376]{2,1,0:T(8,128)(2,1)S(1)}, u32[]{:S(2)}, u32[]{:S(2)}) collective-permute-start(bf16[2,32,5376]{2,1,0:T(8,128)(2,1)} %refs_0_.1), channel_id=1, source_target_pairs={{0,4},{4,0},{8,12},{12,8},{16,20},{20,16},{24,28},{28,24},{32,36},... | collective-permute-start | bytes 2064392 | tf_op jit(solution)/shard_map/ppermute | solution.py:29
  4.0 0.9 copy-done.2
  5.0 0.9 copy-done.3
  5.9 0.9 copy-done.4
  6.8 0.7 split_heads.1
  7.6 0.5 collective-permute-start.1
  8.1 0.8 collective-permute-start.3
  8.8 0.7 collective-permute-start.4
  9.6 1.0 collective-permute-start.6
  10.6 1.3 %collective-permute-start.5 = (bf16[2,256,256]{2,1,0:T(8,128)(2,1)S(1)}, bf16[2,256,256]{2,1,0:T(8,128)(2,1)S(1)}, u32[]{:S(2)}, u32[]{:S(2)}) collective-permute-start(bf16[2,256,256]{2,1,0:T(8,128)(2,1)S(1)} %pad_maximum_fusion.kv0), channel_id=1, source_target_pairs={{0,8},{4,12},{8,16},{12,20},{16,24},{20,28},{24,32},{28,36},{32,40... | collective-permute-start | bytes 786440 | tf_op jit(solution)/shard_map/ppermute | solution.py:29
  11.9 2.6 %copy-done = bf16[5376,512]{1,0:T(8,128)(2,1)S(1)} copy-done((bf16[5376,512]{1,0:T(8,128)(2,1)S(1)}, bf16[5376,512]{1,0:T(8,128)(2,1)}, u32[]{:S(2)}) %copy-start) | copy-done | bytes 5505048
  14.5 1.1 copy-done.5
  15.6 3.3 %projection_early.2 = (bf16[128,256]{1,0:T(8,128)(2,1)S(1)}, bf16[5376,128]{1,0:T(8,128)(2,1)S(1)}) custom-call(s32[4]{0:T(128)S(1)} %pad_add_fusion.scalars, bf16[2,32,5376]{2,1,0:T(8,128)(2,1)S(1)} %copy-done.5, bf16[2,32,5376]{2,1,0:T(8,128)(2,1)S(1)} %collective-permute-done.2.refs_1_, bf16[5376,512]{1,0:T(8,128)(2,1)S(1)} %copy-done), custom_call_target="tpu_custom_call" | custom-call | flops 3523215360 | bytes 12582912 | tf_op jit(solution)/shard_map/projection_early/pallas_call | solution.py:380
  18.9 2.1 %collective-permute-done.6.kv4 = bf16[2,256,256]{2,1,0:T(8,128)(2,1)S(1)} collective-permute-done((bf16[2,256,256]{2,1,0:T(8,128)(2,1)S(1)}, bf16[2,256,256]{2,1,0:T(8,128)(2,1)S(1)}, u32[]{:S(2)}, u32[]{:S(2)}) %collective-permute-start.6) | collective-permute-done | bytes 262176 | tf_op jit(solution)/shard_map/ppermute | solution.py:29
  21.0 4.2 %collective-permute-done.3.refs_0_ = bf16[2,32,5376]{2,1,0:T(8,128)(2,1)S(1)} collective-permute-done((bf16[2,32,5376]{2,1,0:T(8,128)(2,1)}, bf16[2,32,5376]{2,1,0:T(8,128)(2,1)S(1)}, u32[]{:S(2)}, u32[]{:S(2)}) %collective-permute-start.3) | collective-permute-done | bytes 688160 | tf_op jit(solution)/shard_map/ppermute | solution.py:70
  25.3 1.6 %collective-permute-done.4.refs_1_ = bf16[2,32,5376]{2,1,0:T(8,128)(2,1)S(1)} collective-permute-done((bf16[2,32,5376]{2,1,0:T(8,128)(2,1)}, bf16[2,32,5376]{2,1,0:T(8,128)(2,1)S(1)}, u32[]{:S(2)}, u32[]{:S(2)}) %collective-permute-start.4) | collective-permute-done | bytes 688160 | tf_op jit(solution)/shard_map/ppermute | solution.py:70
  26.9 2.1 %collective-permute-done.5.kv1 = bf16[2,256,256]{2,1,0:T(8,128)(2,1)S(1)} collective-permute-done((bf16[2,256,256]{2,1,0:T(8,128)(2,1)S(1)}, bf16[2,256,256]{2,1,0:T(8,128)(2,1)S(1)}, u32[]{:S(2)}, u32[]{:S(2)}) %collective-permute-start.5) | collective-permute-done | bytes 262176 | tf_op jit(solution)/shard_map/ppermute | solution.py:29
  29.0 0.9 collective-permute-start.7
  29.9 1.2 collective-permute-start.11
  31.2 0.8 collective-permute-start.12
  31.9 2.7 %collective-permute-start.10 = (bf16[1,32,5376]{2,1,0:T(8,128)(2,1)S(1)}, bf16[1,32,5376]{2,1,0:T(8,128)(2,1)S(1)}, u32[]{:S(2)}, u32[]{:S(2)}) collective-permute-start(bf16[1,32,5376]{2,1,0:T(8,128)(2,1)S(1)} %slice.41), channel_id=1, source_target_pairs={{0,3},{1,0},{2,1},{3,2},{4,7},{5,4},{6,5},{7,6},{8,11},{9,8},{10,9... | collective-permute-start | bytes 1032200 | tf_op jit(solution)/shard_map/ppermute | solution.py:70
  34.6 4.2 %projection_early.3 = (bf16[256,256]{1,0:T(8,128)(2,1)S(1)}, bf16[5376,256]{1,0:T(8,128)(2,1)S(1)}) custom-call(s32[4]{0:T(128)S(1)} %pad_add_fusion.scalars, bf16[2,32,5376]{2,1,0:T(8,128)(2,1)S(1)} %collective-permute-done.3.refs_0_, bf16[2,32,5376]{2,1,0:T(8,128)(2,1)S(1)} %collective-permute-done.4.refs_1_, ...), custom_call_target="tpu_custom_call" | custom-call | flops 7046430720 | bytes 12582912 | tf_op jit(solution)/shard_map/projection_early/pallas_call | solution.py:380
  38.9 4.2 %collective-permute-done.12.kv3 = bf16[2,256,256]{2,1,0:T(8,128)(2,1)S(1)} collective-permute-done((bf16[2,256,256]{2,1,0:T(8,128)(2,1)S(1)}, bf16[2,256,256]{2,1,0:T(8,128)(2,1)S(1)}, u32[]{:S(2)}, u32[]{:S(2)}) %collective-permute-start.12) | collective-permute-done | bytes 262176 | tf_op jit(solution)/shard_map/ppermute | solution.py:29
  43.1 1.4 %collective-permute-start.13 = (bf16[1,32,5376]{2,1,0:T(8,128)(2,1)S(1)}, bf16[1,32,5376]{2,1,0:T(8,128)(2,1)S(1)}, u32[]{:S(2)}, u32[]{:S(2)}) collective-permute-start(bf16[1,32,5376]{2,1,0:T(8,128)(2,1)S(1)} %collective-permute-done.9.r2a), channel_id=1, source_target_pairs={{0,4},{4,0},{8,12},{12,8},{16,20},{20,16},{24,28},{28,24},{32,36},... | collective-permute-start | bytes 1032200 | tf_op jit(solution)/shard_map/ppermute | solution.py:29
  44.5 0.3 collective-permute-start.14
  44.8 4.2 %attention_forward.1 = (bf16[2,256,256]{2,1,0:T(8,128)(2,1)S(1)}, bf16[2,2,1280,256]{3,2,1,0:T(8,128)(2,1)S(1)}) custom-call(s32[4]{0:T(128)S(1)} %pad_add_fusion.scalars, bf16[2,128,256]{2,1,0:T(8,128)(2,1)S(1)} %get-tuple-element.54.mine, bf16[2,128,512]{2,1,0:T(8,128)(2,1)S(1)} %collective-permute-done.recv, ...), custom_call_target="tpu_custom_call" | custom-call | flops 671088640 | bytes 8388608 | tf_op jit(solution)/shard_map/attention_forward/pallas_call | solution.py:349
  49.0 4.1 %projection_late.1 = (bf16[2,256,256]{2,1,0:T(8,128)(2,1)S(1)}, bf16[2,4,168,256]{3,2,1,0:T(8,128)(2,1)S(1)}, bf16[2,4,168,256]{3,2,1,0:T(8,128)(2,1)S(1)}, bf16...) custom-call(s32[4]{0:T(128)S(1)} %pad_add_fusion.scalars, ...), custom_call_target="tpu_custom_call" | custom-call | flops 2113929216 | bytes 12582912 | tf_op jit(solution)/shard_map/projection_late/pallas_call | solution.py:414
  53.2 1.0 collective-permute-start.16
  54.2 1.5 %collective-permute-start.17 = (bf16[2,4,168,256]{3,2,1,0:T(8,128)(2,1)S(1)}, bf16[2,4,168,256]{3,2,1,0:T(8,128)(2,1)S(1)}, u32[]{:S(2)}, u32[]{:S(2)}) collective-permute-start(bf16[2,4,168,256]{3,2,1,0:T(8,128)(2,1)S(1)} %get-tuple-element.83), channel_id=1, source_target_pairs={{0,24},{4,28},{8,16},{12,20},{16,8},{20,12},{24,0},{28,4},{32,56},... | collective-permute-start | bytes 2064392 | tf_op jit(solution)/shard_map/ppermute | solution.py:29
  55.7 3.8 %attention_backward.1 = (bf16[2,128,256]{2,1,0:T(8,128)(2,1)S(1)}, bf16[2,128,256]{2,1,0:T(8,128)(2,1)S(1)}, f32[2,256,256]{2,1,0:T(8,128)S(1)}, bf16[2,256,256]...) custom-call(bf16[2,128,256]{2,1,0:T(8,128)(2,1)S(1)} %get-tuple-elem, ...), custom_call_target="tpu_custom_call" | custom-call | flops 1677721600 | bytes 8388608 | tf_op jit(solution)/shard_map/attention_backward/pallas_call | solution.py:450
  59.5 6.5 %collective-permute-start.18 = (bf16[2,256,256]{2,1,0:T(8,128)(2,1)S(1)}, bf16[2,256,256]{2,1,0:T(8,128)(2,1)S(1)}, u32[]{:S(2)}, u32[]{:S(2)}) collective-permute-start(bf16[2,256,256]{2,1,0:T(8,128)(2,1)S(1)} %get-tuple-element.85), channel_id=1, source_target_pairs={{0,248},{4,252},{8,0},{12,4},{16,8},{20,12},{24,16},{28,20},{32,24... | collective-permute-start | bytes 786440 | tf_op jit(solution)/shard_map/ppermute | solution.py:29
  66.0 1.4 %collective-permute-start.19 = (bf16[2,256,256]{2,1,0:T(8,128)(2,1)S(1)}, bf16[2,256,256]{2,1,0:T(8,128)(2,1)S(1)}, u32[]{:S(2)}, u32[]{:S(2)}) collective-permute-start(bf16[2,256,256]{2,1,0:T(8,128)(2,1)S(1)} %get-tuple-element.86), channel_id=1, source_target_pairs={{0,240},{4,244},{8,248},{12,252},{16,0},{20,4},{24,8},{28,12},{32,... | collective-permute-start | bytes 786440 | tf_op jit(solution)/shard_map/ppermute | solution.py:29
  67.4 13.9 %collective-permute-done.18 = bf16[2,256,256]{2,1,0:T(8,128)(2,1)S(1)} collective-permute-done((bf16[2,256,256]{2,1,0:T(8,128)(2,1)S(1)}, bf16[2,256,256]{2,1,0:T(8,128)(2,1)S(1)}, u32[]{:S(2)}, u32[]{:S(2)}) %collective-permute-start.18) | collective-permute-done | bytes 262176 | tf_op jit(solution)/shard_map/ppermute | solution.py:29
  81.3 2.1 %collective-permute-done.19 = bf16[2,256,256]{2,1,0:T(8,128)(2,1)S(1)} collective-permute-done((bf16[2,256,256]{2,1,0:T(8,128)(2,1)S(1)}, bf16[2,256,256]{2,1,0:T(8,128)(2,1)S(1)}, u32[]{:S(2)}, u32[]{:S(2)}) %collective-permute-start.19) | collective-permute-done | bytes 262176 | tf_op jit(solution)/shard_map/ppermute | solution.py:29
  83.4 2.6 %collective-permute-done.20 = bf16[2,256,256]{2,1,0:T(8,128)(2,1)S(1)} collective-permute-done((bf16[2,256,256]{2,1,0:T(8,128)(2,1)S(1)}, bf16[2,256,256]{2,1,0:T(8,128)(2,1)S(1)}, u32[]{:S(2)}, u32[]{:S(2)}) %collective-permute-start.20) | collective-permute-done | bytes 262176 | tf_op jit(solution)/shard_map/ppermute | solution.py:29
  86.4 4.7 %collective-permute-start.23 = (bf16[2,256,256]{2,1,0:T(8,128)(2,1)S(1)}, bf16[2,256,256]{2,1,0:T(8,128)(2,1)S(1)}, u32[]{:S(2)}, u32[]{:S(2)}) collective-permute-start(bf16[2,256,256]{2,1,0:T(8,128)(2,1)S(1)} %get-tuple-element.96), channel_id=1, source_target_pairs={{0,224},{4,228},{8,232},{12,236},{16,240},{20,244},{24,248},{28,25... | collective-permute-start | bytes 786440 | tf_op jit(solution)/shard_map/ppermute | solution.py:29
  91.0 3.6 %collective-permute-done.23 = bf16[2,256,256]{2,1,0:T(8,128)(2,1)S(1)} collective-permute-done((bf16[2,256,256]{2,1,0:T(8,128)(2,1)S(1)}, bf16[2,256,256]{2,1,0:T(8,128)(2,1)S(1)}, u32[]{:S(2)}, u32[]{:S(2)}) %collective-permute-start.23) | collective-permute-done | bytes 262176 | tf_op jit(solution)/shard_map/ppermute | solution.py:29
  94.6 0.7 collective-permute-done.21.last_a
  95.3 1.2 projection_merge.1
  96.5 11.1 %all-to-all-start = ((bf16[16,84,256]{2,1,0:T(8,128)(2,1)}), bf16[16,84,256]{2,1,0:T(8,128)(2,1)S(1)}, u32[]{:S(2)}, u32[]{:S(2)}) async-start(bf16[16,84,256]{2,1,0:T(8,128)(2,1)} %projection_merge.1), calls=%async_computation | async-start | bytes 1441792 | tf_op jit(solution)/shard_map/all_to_all | solution.py:57
  107.5 0.2 collective-permute-start.15
  107.7 0.1 add_convert_fusion.2
  107.9 0.4 collective-permute-start.24
  108.3 0.6 collective-permute-done.15
  108.9 0.7 pad_maximum_fusion.1
  109.7 0.7 pad_maximum_fusion.2
  110.4 18.5 %all-to-all-done.blocks = bf16[16,84,256]{2,1,0:T(8,128)(2,1)S(1)} async-done(((bf16[16,84,256]{2,1,0:T(8,128)(2,1)}), bf16[16,84,256]{2,1,0:T(8,128)(2,1)S(1)}, u32[]{:S(2)}, u32[]{:S(2)}) %all-to-all-start) | async-done | bytes 688160 | tf_op jit(solution)/shard_map/all_to_all | solution.py:57
  128.9 0.8 projection_finish.1
  (40 shorter events, 0.9 us)
Async XLA Ops:
  0.6 8.9 %collective-permute-start.2 = (bf16[2,32,5376]{2,1,0:T(8,128)(2,1)}, bf16[2,32,5376]{2,1,0:T(8,128)(2,1)S(1)}, u32[]{:S(2)}, u32[]{:S(2)}) collective-permute-start(bf16[2,32,5376]{2,1,0:T(8,128)(2,1)} %refs_0_.1), channel_id=1, source_target_pairs={{0,4},{4,0},{8,12},{12,8},{16,20},{20,16},{24,28},{28,24},{32,36},... | collective-permute-start | bytes 2064392 | tf_op jit(solution)/shard_map/ppermute | solution.py:29
  4.0 1.0 copy-start.2
  5.0 0.9 copy-start.3
  5.9 0.9 copy-start.4
  7.5 2.1 %collective-permute-start = (bf16[2,128,512]{2,1,0:T(8,128)(2,1)S(1)}, bf16[2,128,512]{2,1,0:T(8,128)(2,1)S(1)}, u32[]{:S(2)}, u32[]{:S(2)}) collective-permute-start(bf16[2,128,512]{2,1,0:T(8,128)(2,1)S(1)} %get-tuple-element.52), channel_id=1, source_target_pairs={{0,4},{4,0},{8,12},{12,8},{16,20},{20,16},{24,28},{28,24},{32,36},... | collective-permute-start | bytes 786440 | tf_op jit(solution)/shard_map/ppermute | solution.py:29
  7.6 1.9 %collective-permute-start.1 = (s32[2,1,128]{2,1,0:T(1,128)}, s32[2,1,128]{2,1,0:T(1,128)S(1)}, u32[]{:S(2)}, u32[]{:S(2)}) collective-permute-start(s32[2,1,128]{2,1,0:T(1,128)} %bitcast.9), channel_id=1, source_target_pairs={{0,4},{4,0},{8,12},{12,8},{16,20},{20,16},{24,28},{28,24},{32,36},... | collective-permute-start | bytes 3080 | tf_op jit(solution)/shard_map/ppermute | solution.py:29
  8.1 17.2 %collective-permute-start.3 = (bf16[2,32,5376]{2,1,0:T(8,128)(2,1)}, bf16[2,32,5376]{2,1,0:T(8,128)(2,1)S(1)}, u32[]{:S(2)}, u32[]{:S(2)}) collective-permute-start(bf16[2,32,5376]{2,1,0:T(8,128)(2,1)} %refs_0_.1), channel_id=1, source_target_pairs={{0,3},{1,0},{2,1},{3,2},{4,7},{5,4},{6,5},{7,6},{8,11},{9,8},{10,9... | collective-permute-start | bytes 2064392 | tf_op jit(solution)/shard_map/ppermute | solution.py:70
  8.8 18.1 %collective-permute-start.4 = (bf16[2,32,5376]{2,1,0:T(8,128)(2,1)}, bf16[2,32,5376]{2,1,0:T(8,128)(2,1)S(1)}, u32[]{:S(2)}, u32[]{:S(2)}) collective-permute-start(bf16[2,32,5376]{2,1,0:T(8,128)(2,1)} %refs_0_.1), channel_id=1, source_target_pairs={{0,1},{1,2},{2,3},{3,0},{4,5},{5,6},{6,7},{7,4},{8,9},{9,10},{10,1... | collective-permute-start | bytes 2064392 | tf_op jit(solution)/shard_map/ppermute | solution.py:70
  9.6 11.3 %collective-permute-start.6 = (bf16[2,256,256]{2,1,0:T(8,128)(2,1)S(1)}, bf16[2,256,256]{2,1,0:T(8,128)(2,1)S(1)}, u32[]{:S(2)}, u32[]{:S(2)}) collective-permute-start(bf16[2,256,256]{2,1,0:T(8,128)(2,1)S(1)} %pad_maximum_fusion.kv0), channel_id=1, source_target_pairs={{0,32},{4,36},{8,40},{12,44},{16,48},{20,52},{24,56},{28,60},{32,6... | collective-permute-start | bytes 786440 | tf_op jit(solution)/shard_map/ppermute | solution.py:29
  10.6 18.4 %collective-permute-start.5 = (bf16[2,256,256]{2,1,0:T(8,128)(2,1)S(1)}, bf16[2,256,256]{2,1,0:T(8,128)(2,1)S(1)}, u32[]{:S(2)}, u32[]{:S(2)}) collective-permute-start(bf16[2,256,256]{2,1,0:T(8,128)(2,1)S(1)} %pad_maximum_fusion.kv0), channel_id=1, source_target_pairs={{0,8},{4,12},{8,16},{12,20},{16,24},{20,28},{24,32},{28,36},{32,40... | collective-permute-start | bytes 786440 | tf_op jit(solution)/shard_map/ppermute | solution.py:29
  11.9 2.6 %copy-start = (bf16[5376,512]{1,0:T(8,128)(2,1)S(1)}, bf16[5376,512]{1,0:T(8,128)(2,1)}, u32[]{:S(2)}) copy-start(bf16[5376,512]{1,0:T(8,128)(2,1)} %o_weight.1) | copy-start | bytes 16515076
  14.5 1.1 copy-start.5
  15.6 19.1 %copy-start.1 = (bf16[5376,512]{1,0:T(8,128)(2,1)S(1)}, bf16[5376,512]{1,0:T(8,128)(2,1)}, u32[]{:S(2)}) copy-start(bf16[5376,512]{1,0:T(8,128)(2,1)} %o_weight.1) | copy-start | bytes 16515076
  29.0 3.0 %collective-permute-start.7 = (bf16[2,32,5376]{2,1,0:T(8,128)(2,1)S(1)}, bf16[2,32,5376]{2,1,0:T(8,128)(2,1)S(1)}, u32[]{:S(2)}, u32[]{:S(2)}) collective-permute-start(bf16[2,32,5376]{2,1,0:T(8,128)(2,1)S(1)} %collective-permute-done.3.refs_0_), channel_id=1, source_target_pairs={{0,4},{4,0},{8,12},{12,8},{16,20},{20,16},{24,28},{28,24},{32,36},... | collective-permute-start | bytes 2064392 | tf_op jit(solution)/shard_map/ppermute | solution.py:29
  29.9 4.8 %collective-permute-start.8 = (bf16[2,32,5376]{2,1,0:T(8,128)(2,1)S(1)}, bf16[2,32,5376]{2,1,0:T(8,128)(2,1)S(1)}, u32[]{:S(2)}, u32[]{:S(2)}) collective-permute-start(bf16[2,32,5376]{2,1,0:T(8,128)(2,1)S(1)} %collective-permute-done.4.refs_1_), channel_id=1, source_target_pairs={{0,4},{4,0},{8,12},{12,8},{16,20},{20,16},{24,28},{28,24},{32,36},... | collective-permute-start | bytes 2064392 | tf_op jit(solution)/shard_map/ppermute | solution.py:29
  29.9 14.8 %copy-start.6 = (s32[2,128]{1,0:T(2,128)S(1)}, s32[2,128]{1,0:T(2,128)}, u32[]{:S(2)}) copy-start(s32[2,128]{1,0:T(2,128)} %param.11) | copy-start | bytes 3076
  29.9 9.0 %collective-permute-start.11 = (bf16[2,256,256]{2,1,0:T(8,128)(2,1)S(1)}, bf16[2,256,256]{2,1,0:T(8,128)(2,1)S(1)}, u32[]{:S(2)}, u32[]{:S(2)}) collective-permute-start(bf16[2,256,256]{2,1,0:T(8,128)(2,1)S(1)} %get-tuple-element.66), channel_id=1, source_target_pairs={{0,16},{4,20},{8,24},{12,28},{16,0},{20,4},{24,8},{28,12},{32,48},... | collective-permute-start | bytes 786440 | tf_op jit(solution)/shard_map/ppermute | solution.py:29
  31.2 12.0 %collective-permute-start.12 = (bf16[2,256,256]{2,1,0:T(8,128)(2,1)S(1)}, bf16[2,256,256]{2,1,0:T(8,128)(2,1)S(1)}, u32[]{:S(2)}, u32[]{:S(2)}) collective-permute-start(bf16[2,256,256]{2,1,0:T(8,128)(2,1)S(1)} %get-tuple-element.67), channel_id=1, source_target_pairs={{0,24},{4,28},{8,0},{12,4},{16,8},{20,12},{24,16},{28,20},{32,56},... | collective-permute-start | bytes 786440 | tf_op jit(solution)/shard_map/ppermute | solution.py:29
  31.9 11.2 %collective-permute-start.9 = (bf16[1,32,5376]{2,1,0:T(8,128)(2,1)S(1)}, bf16[1,32,5376]{2,1,0:T(8,128)(2,1)S(1)}, u32[]{:S(2)}, u32[]{:S(2)}) collective-permute-start(bf16[1,32,5376]{2,1,0:T(8,128)(2,1)S(1)} %slice.40), channel_id=1, source_target_pairs={{0,1},{1,2},{2,3},{3,0},{4,5},{5,6},{6,7},{7,4},{8,9},{9,10},{10,1... | collective-permute-start | bytes 1032200 | tf_op jit(solution)/shard_map/ppermute | solution.py:70
  31.9 11.2 %collective-permute-start.10 = (bf16[1,32,5376]{2,1,0:T(8,128)(2,1)S(1)}, bf16[1,32,5376]{2,1,0:T(8,128)(2,1)S(1)}, u32[]{:S(2)}, u32[]{:S(2)}) collective-permute-start(bf16[1,32,5376]{2,1,0:T(8,128)(2,1)S(1)} %slice.41), channel_id=1, source_target_pairs={{0,3},{1,0},{2,1},{3,2},{4,7},{5,4},{6,5},{7,6},{8,11},{9,8},{10,9... | collective-permute-start | bytes 1032200 | tf_op jit(solution)/shard_map/ppermute | solution.py:70
  43.1 5.9 %collective-permute-start.13 = (bf16[1,32,5376]{2,1,0:T(8,128)(2,1)S(1)}, bf16[1,32,5376]{2,1,0:T(8,128)(2,1)S(1)}, u32[]{:S(2)}, u32[]{:S(2)}) collective-permute-start(bf16[1,32,5376]{2,1,0:T(8,128)(2,1)S(1)} %collective-permute-done.9.r2a), channel_id=1, source_target_pairs={{0,4},{4,0},{8,12},{12,8},{16,20},{20,16},{24,28},{28,24},{32,36},... | collective-permute-start | bytes 1032200 | tf_op jit(solution)/shard_map/ppermute | solution.py:29
  44.5 4.5 %collective-permute-start.14 = (bf16[1,32,5376]{2,1,0:T(8,128)(2,1)S(1)}, bf16[1,32,5376]{2,1,0:T(8,128)(2,1)S(1)}, u32[]{:S(2)}, u32[]{:S(2)}) collective-permute-start(bf16[1,32,5376]{2,1,0:T(8,128)(2,1)S(1)} %collective-permute-done.10.r2b), channel_id=1, source_target_pairs={{0,4},{4,0},{8,12},{12,8},{16,20},{20,16},{24,28},{28,24},{32,36},... | collective-permute-start | bytes 1032200 | tf_op jit(solution)/shard_map/ppermute | solution.py:29
  53.2 32.9 %collective-permute-start.16 = (bf16[2,4,168,256]{3,2,1,0:T(8,128)(2,1)S(1)}, bf16[2,4,168,256]{3,2,1,0:T(8,128)(2,1)S(1)}, u32[]{:S(2)}, u32[]{:S(2)}) collective-permute-start(bf16[2,4,168,256]{3,2,1,0:T(8,128)(2,1)S(1)} %get-tuple-element.82), channel_id=1, source_target_pairs={{0,8},{4,12},{8,0},{12,4},{16,24},{20,28},{24,16},{28,20},{32,40},... | collective-permute-start | bytes 2064392 | tf_op jit(solution)/shard_map/ppermute | solution.py:29
  54.2 31.8 %collective-permute-start.17 = (bf16[2,4,168,256]{3,2,1,0:T(8,128)(2,1)S(1)}, bf16[2,4,168,256]{3,2,1,0:T(8,128)(2,1)S(1)}, u32[]{:S(2)}, u32[]{:S(2)}) collective-permute-start(bf16[2,4,168,256]{3,2,1,0:T(8,128)(2,1)S(1)} %get-tuple-element.83), channel_id=1, source_target_pairs={{0,24},{4,28},{8,16},{12,20},{16,8},{20,12},{24,0},{28,4},{32,56},... | collective-permute-start | bytes 2064392 | tf_op jit(solution)/shard_map/ppermute | solution.py:29
  59.5 21.8 %collective-permute-start.18 = (bf16[2,256,256]{2,1,0:T(8,128)(2,1)S(1)}, bf16[2,256,256]{2,1,0:T(8,128)(2,1)S(1)}, u32[]{:S(2)}, u32[]{:S(2)}) collective-permute-start(bf16[2,256,256]{2,1,0:T(8,128)(2,1)S(1)} %get-tuple-element.85), channel_id=1, source_target_pairs={{0,248},{4,252},{8,0},{12,4},{16,8},{20,12},{24,16},{28,20},{32,24... | collective-permute-start | bytes 786440 | tf_op jit(solution)/shard_map/ppermute | solution.py:29
  66.0 17.4 %collective-permute-start.19 = (bf16[2,256,256]{2,1,0:T(8,128)(2,1)S(1)}, bf16[2,256,256]{2,1,0:T(8,128)(2,1)S(1)}, u32[]{:S(2)}, u32[]{:S(2)}) collective-permute-start(bf16[2,256,256]{2,1,0:T(8,128)(2,1)S(1)} %get-tuple-element.86), channel_id=1, source_target_pairs={{0,240},{4,244},{8,248},{12,252},{16,0},{20,4},{24,8},{28,12},{32,... | collective-permute-start | bytes 786440 | tf_op jit(solution)/shard_map/ppermute | solution.py:29
  67.4 18.6 %collective-permute-start.20 = (bf16[2,256,256]{2,1,0:T(8,128)(2,1)S(1)}, bf16[2,256,256]{2,1,0:T(8,128)(2,1)S(1)}, u32[]{:S(2)}, u32[]{:S(2)}) collective-permute-start(bf16[2,256,256]{2,1,0:T(8,128)(2,1)S(1)} %get-tuple-element.87), channel_id=1, source_target_pairs={{0,232},{4,236},{8,240},{12,244},{16,248},{20,252},{24,0},{28,4},{... | collective-permute-start | bytes 786440 | tf_op jit(solution)/shard_map/ppermute | solution.py:29
  86.1 8.5 %collective-permute-start.22 = (bf16[4,168,256]{2,1,0:T(8,128)(2,1)S(1)}, bf16[4,168,256]{2,1,0:T(8,128)(2,1)S(1)}, u32[]{:S(2)}, u32[]{:S(2)}) collective-permute-start(bf16[4,168,256]{2,1,0:T(8,128)(2,1)S(1)} %fusion.1), channel_id=1, source_target_pairs={{0,8},{4,12},{8,0},{12,4},{16,24},{20,28},{24,16},{28,20},{32,40},... | collective-permute-start | bytes 1032200 | tf_op jit(solution)/shard_map/ppermute | solution.py:29
  86.3 9.0 %collective-permute-start.21 = (bf16[4,168,256]{2,1,0:T(8,128)(2,1)S(1)}, bf16[4,168,256]{2,1,0:T(8,128)(2,1)S(1)}, u32[]{:S(2)}, u32[]{:S(2)}) collective-permute-start(bf16[4,168,256]{2,1,0:T(8,128)(2,1)S(1)} %fusion), channel_id=1, source_target_pairs={{0,24},{4,28},{8,16},{12,20},{16,8},{20,12},{24,0},{28,4},{32,56},... | collective-permute-start | bytes 1032200 | tf_op jit(solution)/shard_map/ppermute | solution.py:29
  86.4 8.2 %collective-permute-start.23 = (bf16[2,256,256]{2,1,0:T(8,128)(2,1)S(1)}, bf16[2,256,256]{2,1,0:T(8,128)(2,1)S(1)}, u32[]{:S(2)}, u32[]{:S(2)}) collective-permute-start(bf16[2,256,256]{2,1,0:T(8,128)(2,1)S(1)} %get-tuple-element.96), channel_id=1, source_target_pairs={{0,224},{4,228},{8,232},{12,236},{16,240},{20,244},{24,248},{28,25... | collective-permute-start | bytes 786440 | tf_op jit(solution)/shard_map/ppermute | solution.py:29
  96.5 32.4 %all-to-all-start = ((bf16[16,84,256]{2,1,0:T(8,128)(2,1)}), bf16[16,84,256]{2,1,0:T(8,128)(2,1)S(1)}, u32[]{:S(2)}, u32[]{:S(2)}) async-start(bf16[16,84,256]{2,1,0:T(8,128)(2,1)} %projection_merge.1), calls=%async_computation | async-start | bytes 1441792 | tf_op jit(solution)/shard_map/all_to_all | solution.py:57
  107.5 1.3 %collective-permute-start.15 = (bf16[2,128,256]{2,1,0:T(8,128)(2,1)S(1)}, bf16[2,128,256]{2,1,0:T(8,128)(2,1)S(1)}, u32[]{:S(2)}, u32[]{:S(2)}) collective-permute-start(bf16[2,128,256]{2,1,0:T(8,128)(2,1)S(1)} %get-tuple-element.81), channel_id=1, source_target_pairs={{0,4},{4,0},{8,12},{12,8},{16,20},{20,16},{24,28},{28,24},{32,36},... | collective-permute-start | bytes 393224 | tf_op jit(solution)/shard_map/ppermute | solution.py:29
  107.9 1.7 %collective-permute-start.24 = (bf16[2,128,256]{2,1,0:T(8,128)(2,1)S(1)}, bf16[2,128,256]{2,1,0:T(8,128)(2,1)S(1)}, u32[]{:S(2)}, u32[]{:S(2)}) collective-permute-start(bf16[2,128,256]{2,1,0:T(8,128)(2,1)S(1)} %slice.52), channel_id=1, source_target_pairs={{0,4},{4,0},{8,12},{12,8},{16,20},{20,16},{24,28},{28,24},{32,36},... | collective-permute-start | bytes 393224 | tf_op jit(solution)/shard_map/ppermute | solution.py:29

commit v9 on v8

--- a/solution.py
+++ b/solution.py
@@ -50,10 +50,8 @@
 
 
 def z_exchange(blocks):
-    groups = [
-        [(z * CHIPS_Y + y) * CORES + core for z in range(CHIPS_Z) for core in range(CORES)]
-        for y in range(CHIPS_Y)
-    ]
+    lanes = CORES * CHIPS_Y
+    groups = [[z * lanes + lane for z in range(CHIPS_Z)] for lane in range(lanes)]
     return lax.all_to_all(blocks, "ctx", 0, 0, axis_index_groups=groups, tiled=True)
 
 
@@ -243,9 +241,10 @@
         dq_other[0, :, cols] = full[rows:]
 
 
-def merge_kernel(kept_a, got_a, last_a, kept_b, got_b, last_b, out):
+def merge_kernel(scalars, kept_a, got_a, last_a, kept_b, got_b, last_b, own, sent):
     half = kept_a.shape[1]
-    rows = out.shape[1]
+    rows = own.shape[1]
+    first = scalars[0] == 0
     for part, (kept, got, last) in enumerate(((kept_a, got_a, last_a), (kept_b, got_b, last_b))):
         for z in range(half):
             total = (
@@ -253,44 +252,55 @@
                 + got[0, z].astype(jnp.float32)
                 + last[z].astype(jnp.float32)
             )
-            for core in range(CORES):
-                slot = CORES * (half * part + z) + core
-                out[slot] = total[core * rows : (core + 1) * rows].astype(jnp.bfloat16)
-
-
-def finish_kernel(blocks, out):
-    width = blocks.shape[2]
-    for core in range(CORES):
-        total = blocks[core].astype(jnp.float32)
-        for z in range(1, CHIPS_Z):
-            total = total + blocks[CORES * z + core].astype(jnp.float32)
-        out[:, core * width : (core + 1) * width] = total
-
-
-def merge(kept_a, got_a, last_a, kept_b, got_b, last_b):
+            top, bottom = total[:rows], total[rows:]
+            own[half * part + z] = jnp.where(first, top, bottom).astype(jnp.bfloat16)
+            sent[half * part + z] = jnp.where(first, bottom, top).astype(jnp.bfloat16)
+
+
+def finish_kernel(scalars, blocks, out):
+    width = blocks.shape[2] // CORES
+    first = scalars[0] == 0
+    total = blocks[0].astype(jnp.float32)
+    for z in range(1, CHIPS_Z):
+        total = total + blocks[z].astype(jnp.float32)
+    own, other = total[:, :width], total[:, width:]
+    out[:, :width] = jnp.where(first, own, other)
+    out[:, width:] = jnp.where(first, other, own)
+
+
+def merge(scalars, kept_a, got_a, last_a, kept_b, got_b, last_b):
     _, half, rows, width = kept_a.shape
-    front = pl.BlockSpec((1, half, rows, width), lambda i: (0, 0, 0, 0))
-    flat = pl.BlockSpec((half, rows, width), lambda i: (0, 0, 0))
-    shape = (CORES * 2 * half, rows // CORES, width)
+    front = pl.BlockSpec((1, half, rows, width), lambda i, *_: (0, 0, 0, 0))
+    flat = pl.BlockSpec((half, rows, width), lambda i, *_: (0, 0, 0))
+    shape = (2 * half, rows // CORES, width)
     return pl.pallas_call(
         merge_kernel,
-        out_shape=jax.ShapeDtypeStruct(shape, jnp.bfloat16),
-        grid=(1,),
-        in_specs=[front, front, flat] * 2,
-        out_specs=pl.BlockSpec(shape, lambda i: (0, 0, 0)),
+        out_shape=(jax.ShapeDtypeStruct(shape, jnp.bfloat16),) * 2,
+        grid_spec=pltpu.PrefetchScalarGridSpec(
+            num_scalar_prefetch=1,
+            grid=(1,),
+            in_specs=[front, front, flat] * 2,
+            out_specs=[pl.BlockSpec(shape, lambda i, *_: (0, 0, 0))] * 2,
+        ),
         compiler_params=pltpu.CompilerParams(vmem_limit_bytes=16 << 20),
         name="projection_merge",
-    )(kept_a, got_a, last_a, kept_b, got_b, last_b)
-
-
-def finish(blocks):
-    count, rows, width = blocks.shape
+    )(scalars, kept_a, got_a, last_a, kept_b, got_b, last_b)
+
+
+def finish(scalars, blocks):
+    _, rows, width = blocks.shape
     return pl.pallas_call(
         finish_kernel,
-        out_shape=jax.ShapeDtypeStruct((rows, CORES * width), jnp.float32),
+        out_shape=jax.ShapeDtypeStruct((rows, width), jnp.float32),
+        grid_spec=pltpu.PrefetchScalarGridSpec(
+            num_scalar_prefetch=1,
+            grid=(1,),
+            in_specs=[pl.BlockSpec(blocks.shape, lambda i, *_: (0, 0, 0))],
+            out_specs=pl.BlockSpec((rows, width), lambda i, *_: (0, 0)),
+        ),
         compiler_params=pltpu.CompilerParams(vmem_limit_bytes=16 << 20),
         name="projection_finish",
-    )(blocks)
+    )(scalars, blocks)
 
 
 def split_kernel(
@@ -530,8 +540,8 @@
     last_a = y_route(next_a, y_mirror)
     last_b = y_route(next_b, y_pair)
     last_a, last_b, g_far = lax.optimization_barrier((last_a, last_b, g_far))
-    w_sum = merge(kept_a, got_a, last_a, kept_b, got_b, last_b)
-    w_all = z_exchange(w_sum)
+    w_own, w_other = merge(scalars, kept_a, got_a, last_a, kept_b, got_b, last_b)
+    w_all = z_exchange(jnp.concatenate([w_own, to_sibling(w_other)], axis=-1))
 
     grads = added(g_own, *g_near, g_far).astype(jnp.bfloat16)
     g_mine = grads[:, :shard_rows]
@@ -546,7 +556,7 @@
         by_core(dq_mine, dq_recv),
         by_core(g_mine[..., :HEAD_SIZE], g_recv[..., :HEAD_SIZE]),
         by_core(g_mine[..., HEAD_SIZE:], g_recv[..., HEAD_SIZE:]),
-        finish(w_all),
+        finish(scalars, w_all),
     )
 
 

time: 130 us -> 133 us (1.023)
  waiting for transfers between devices: 56.2 us -> 59.3 us
    all_to_all x1, starting transfers between devices: 11.1 us -> 8.02 us  [z_exchange(): lax.all_to_all(blocks, 'ctx', 0, 0, axis_index_groups=groups, tiled=True)]
    ppermute x21 -> x22, starting transfers between devices: 26.6 us -> 29.6 us  [ctx_shift(): return lax.ppermute(block, 'ctx', [(i, move(i)) for i in range(count)])]
    ppermute x21 -> x22, waiting for transfers between devices: 31.9 us -> 34.5 us  [ctx_shift(): return lax.ppermute(block, 'ctx', [(i, move(i)) for i in range(count)])]
  transfers between devices with their start and end apart: 26 -> 27, of which waited for: 12 -> 13; matrix products, arithmetic and copies ran while one was open for 2% -> 2% of each run, Pallas kernels for 12% -> 12%
where the time goes in v9:
time: 133 us
  waiting for transfers between devices  59.3 us (45%)
  starting transfers between devices  41.8 us (31%)
  Pallas kernels  22.6 us (17%)
  local copies, waits for them, and re-layouts  5.4 us (4%)
  other arithmetic  2.97 us (2%)
    ppermute x22, waiting for transfers between devices, ctx_shift(): return lax.ppermute(block, 'ctx', [(i, move(i)) for i in range(count)])  34.5 us
    ppermute x22, starting transfers between devices, ctx_shift(): return lax.ppermute(block, 'ctx', [(i, move(i)) for i in range(count)])  29.6 us
    all_to_all x1, waiting for transfers between devices, z_exchange(): lax.all_to_all(blocks, 'ctx', 0, 0, axis_index_groups=groups, tiled=True)  19 us
    all_to_all x1, starting transfers between devices, z_exchange(): lax.all_to_all(blocks, 'ctx', 0, 0, axis_index_groups=groups, tiled=True)  8.02 us
    pallas_call x2, Pallas kernels, early_projection(): pl.pallas_call(early_kernel, out_shape=outs, grid_spec=pltpu.PrefetchScal...  7.51 us
    ppermute x4, waiting for transfers between devices, tp_ahead(): lax.ppermute(block, 'tp', [(i, (i + distance) % TP) for i in range(TP)])  5.87 us
    unnamed x14, local copies, waits for them, and re-layouts  5.33 us
    pallas_call x1, Pallas kernels, forward(): pl.pallas_call(forward_kernel, out_shape=outs, grid_spec=pltpu.PrefetchSc...  4.24 us
  transfers between devices with their start and end apart: 27, of which 13 were waited for; matrix products, arithmetic and copies ran while one was open for 2% of the time, Pallas kernels for 12%

profile of v9, /device:TPU:1, one launch (start us, length us, event | category | flops | bytes accessed | tf_op | source)
XLA Modules:
  0.0 132.9 jit_solution(6973328874158248707)
XLA Ops:
  0.6 3.3 %collective-permute-start.2 = (bf16[2,32,5376]{2,1,0:T(8,128)(2,1)}, bf16[2,32,5376]{2,1,0:T(8,128)(2,1)S(1)}, u32[]{:S(2)}, u32[]{:S(2)}) collective-permute-start(bf16[2,32,5376]{2,1,0:T(8,128)(2,1)} %refs_0_.1), channel_id=1, source_target_pairs={{0,4},{4,0},{8,12},{12,8},{16,20},{20,16},{24,28},{28,24},{32,36},... | collective-permute-start | bytes 2064392 | tf_op jit(solution)/shard_map/ppermute | solution.py:29
  4.0 0.9 copy-done.2
  5.0 0.9 copy-done.3
  5.9 0.9 copy-done.4
  6.8 0.7 split_heads.1
  7.6 0.5 collective-permute-start.1
  8.1 0.8 collective-permute-start.3
  8.8 0.7 collective-permute-start.4
  9.6 1.0 collective-permute-start.6
  10.6 1.3 collective-permute-start.5
  11.9 2.6 %copy-done = bf16[5376,512]{1,0:T(8,128)(2,1)S(1)} copy-done((bf16[5376,512]{1,0:T(8,128)(2,1)S(1)}, bf16[5376,512]{1,0:T(8,128)(2,1)}, u32[]{:S(2)}) %copy-start) | copy-done | bytes 5505048
  14.5 3.3 %projection_early.2 = (bf16[128,256]{1,0:T(8,128)(2,1)S(1)}, bf16[5376,128]{1,0:T(8,128)(2,1)S(1)}) custom-call(s32[4]{0:T(128)S(1)} %pad_add_fusion.scalars, bf16[2,32,5376]{2,1,0:T(8,128)(2,1)S(1)} %copy-done.5, bf16[2,32,5376]{2,1,0:T(8,128)(2,1)S(1)} %collective-permute-done.2.refs_1_, bf16[5376,512]{1,0:T(8,128)(2,1)S(1)} %copy-done), custom_call_target="tpu_custom_call" | custom-call | flops 3523215360 | bytes 12582912 | tf_op jit(solution)/shard_map/projection_early/pallas_call | solution.py:390
  17.8 3.2 %collective-permute-done.6.kv4 = bf16[2,256,256]{2,1,0:T(8,128)(2,1)S(1)} collective-permute-done((bf16[2,256,256]{2,1,0:T(8,128)(2,1)S(1)}, bf16[2,256,256]{2,1,0:T(8,128)(2,1)S(1)}, u32[]{:S(2)}, u32[]{:S(2)}) %collective-permute-start.6) | collective-permute-done | bytes 262176 | tf_op jit(solution)/shard_map/ppermute | solution.py:29
  21.0 4.2 %collective-permute-done.3.refs_0_ = bf16[2,32,5376]{2,1,0:T(8,128)(2,1)S(1)} collective-permute-done((bf16[2,32,5376]{2,1,0:T(8,128)(2,1)}, bf16[2,32,5376]{2,1,0:T(8,128)(2,1)S(1)}, u32[]{:S(2)}, u32[]{:S(2)}) %collective-permute-start.3) | collective-permute-done | bytes 688160 | tf_op jit(solution)/shard_map/ppermute | solution.py:68
  25.3 1.6 %collective-permute-done.4.refs_1_ = bf16[2,32,5376]{2,1,0:T(8,128)(2,1)S(1)} collective-permute-done((bf16[2,32,5376]{2,1,0:T(8,128)(2,1)}, bf16[2,32,5376]{2,1,0:T(8,128)(2,1)S(1)}, u32[]{:S(2)}, u32[]{:S(2)}) %collective-permute-start.4) | collective-permute-done | bytes 688160 | tf_op jit(solution)/shard_map/ppermute | solution.py:68
  26.9 2.1 %collective-permute-done.5.kv1 = bf16[2,256,256]{2,1,0:T(8,128)(2,1)S(1)} collective-permute-done((bf16[2,256,256]{2,1,0:T(8,128)(2,1)S(1)}, bf16[2,256,256]{2,1,0:T(8,128)(2,1)S(1)}, u32[]{:S(2)}, u32[]{:S(2)}) %collective-permute-start.5) | collective-permute-done | bytes 262176 | tf_op jit(solution)/shard_map/ppermute | solution.py:29
  29.0 0.9 collective-permute-start.7
  29.9 1.2 collective-permute-start.11
  31.2 0.8 collective-permute-start.12
  31.9 2.7 %collective-permute-start.10 = (bf16[1,32,5376]{2,1,0:T(8,128)(2,1)S(1)}, bf16[1,32,5376]{2,1,0:T(8,128)(2,1)S(1)}, u32[]{:S(2)}, u32[]{:S(2)}) collective-permute-start(bf16[1,32,5376]{2,1,0:T(8,128)(2,1)S(1)} %slice.41), channel_id=1, source_target_pairs={{0,3},{1,0},{2,1},{3,2},{4,7},{5,4},{6,5},{7,6},{8,11},{9,8},{10,9... | collective-permute-start | bytes 1032200 | tf_op jit(solution)/shard_map/ppermute | solution.py:68
  34.6 4.2 %projection_early.3 = (bf16[256,256]{1,0:T(8,128)(2,1)S(1)}, bf16[5376,256]{1,0:T(8,128)(2,1)S(1)}) custom-call(s32[4]{0:T(128)S(1)} %pad_add_fusion.scalars, bf16[2,32,5376]{2,1,0:T(8,128)(2,1)S(1)} %collective-permute-done.3.refs_0_, bf16[2,32,5376]{2,1,0:T(8,128)(2,1)S(1)} %collective-permute-done.4.refs_1_, ...), custom_call_target="tpu_custom_call" | custom-call | flops 7046430720 | bytes 12582912 | tf_op jit(solution)/shard_map/projection_early/pallas_call | solution.py:390
  38.9 4.2 %collective-permute-done.12.kv3 = bf16[2,256,256]{2,1,0:T(8,128)(2,1)S(1)} collective-permute-done((bf16[2,256,256]{2,1,0:T(8,128)(2,1)S(1)}, bf16[2,256,256]{2,1,0:T(8,128)(2,1)S(1)}, u32[]{:S(2)}, u32[]{:S(2)}) %collective-permute-start.12) | collective-permute-done | bytes 262176 | tf_op jit(solution)/shard_map/ppermute | solution.py:29
  43.1 1.4 %collective-permute-start.13 = (bf16[1,32,5376]{2,1,0:T(8,128)(2,1)S(1)}, bf16[1,32,5376]{2,1,0:T(8,128)(2,1)S(1)}, u32[]{:S(2)}, u32[]{:S(2)}) collective-permute-start(bf16[1,32,5376]{2,1,0:T(8,128)(2,1)S(1)} %collective-permute-done.9.r2a), channel_id=1, source_target_pairs={{0,4},{4,0},{8,12},{12,8},{16,20},{20,16},{24,28},{28,24},{32,36},... | collective-permute-start | bytes 1032200 | tf_op jit(solution)/shard_map/ppermute | solution.py:29
  44.5 0.3 collective-permute-start.14
  44.8 4.2 %attention_forward.1 = (bf16[2,256,256]{2,1,0:T(8,128)(2,1)S(1)}, bf16[2,2,1280,256]{3,2,1,0:T(8,128)(2,1)S(1)}) custom-call(s32[4]{0:T(128)S(1)} %pad_add_fusion.scalars, bf16[2,128,256]{2,1,0:T(8,128)(2,1)S(1)} %get-tuple-element.56.mine, bf16[2,128,512]{2,1,0:T(8,128)(2,1)S(1)} %collective-permute-done.recv, ...), custom_call_target="tpu_custom_call" | custom-call | flops 671088640 | bytes 8388608 | tf_op jit(solution)/shard_map/attention_forward/pallas_call | solution.py:359
  49.0 4.1 %projection_late.1 = (bf16[2,256,256]{2,1,0:T(8,128)(2,1)S(1)}, bf16[2,4,168,256]{3,2,1,0:T(8,128)(2,1)S(1)}, bf16[2,4,168,256]{3,2,1,0:T(8,128)(2,1)S(1)}, bf16...) custom-call(s32[4]{0:T(128)S(1)} %pad_add_fusion.scalars, ...), custom_call_target="tpu_custom_call" | custom-call | flops 2113929216 | bytes 12582912 | tf_op jit(solution)/shard_map/projection_late/pallas_call | solution.py:424
  53.2 1.0 collective-permute-start.16
  54.1 1.5 %collective-permute-start.17 = (bf16[2,4,168,256]{3,2,1,0:T(8,128)(2,1)S(1)}, bf16[2,4,168,256]{3,2,1,0:T(8,128)(2,1)S(1)}, u32[]{:S(2)}, u32[]{:S(2)}) collective-permute-start(bf16[2,4,168,256]{3,2,1,0:T(8,128)(2,1)S(1)} %get-tuple-element.85), channel_id=1, source_target_pairs={{0,24},{4,28},{8,16},{12,20},{16,8},{20,12},{24,0},{28,4},{32,56},... | collective-permute-start | bytes 2064392 | tf_op jit(solution)/shard_map/ppermute | solution.py:29
  55.7 3.8 %attention_backward.1 = (bf16[2,128,256]{2,1,0:T(8,128)(2,1)S(1)}, bf16[2,128,256]{2,1,0:T(8,128)(2,1)S(1)}, f32[2,256,256]{2,1,0:T(8,128)S(1)}, bf16[2,256,256]...) custom-call(bf16[2,128,256]{2,1,0:T(8,128)(2,1)S(1)} %get-tuple-elem, ...), custom_call_target="tpu_custom_call" | custom-call | flops 1677721600 | bytes 8388608 | tf_op jit(solution)/shard_map/attention_backward/pallas_call | solution.py:460
  59.5 6.5 %collective-permute-start.18 = (bf16[2,256,256]{2,1,0:T(8,128)(2,1)S(1)}, bf16[2,256,256]{2,1,0:T(8,128)(2,1)S(1)}, u32[]{:S(2)}, u32[]{:S(2)}) collective-permute-start(bf16[2,256,256]{2,1,0:T(8,128)(2,1)S(1)} %get-tuple-element.87), channel_id=1, source_target_pairs={{0,248},{4,252},{8,0},{12,4},{16,8},{20,12},{24,16},{28,20},{32,24... | collective-permute-start | bytes 786440 | tf_op jit(solution)/shard_map/ppermute | solution.py:29
  66.0 1.4 %collective-permute-start.19 = (bf16[2,256,256]{2,1,0:T(8,128)(2,1)S(1)}, bf16[2,256,256]{2,1,0:T(8,128)(2,1)S(1)}, u32[]{:S(2)}, u32[]{:S(2)}) collective-permute-start(bf16[2,256,256]{2,1,0:T(8,128)(2,1)S(1)} %get-tuple-element.88), channel_id=1, source_target_pairs={{0,240},{4,244},{8,248},{12,252},{16,0},{20,4},{24,8},{28,12},{32,... | collective-permute-start | bytes 786440 | tf_op jit(solution)/shard_map/ppermute | solution.py:29
  67.4 13.9 %collective-permute-done.18 = bf16[2,256,256]{2,1,0:T(8,128)(2,1)S(1)} collective-permute-done((bf16[2,256,256]{2,1,0:T(8,128)(2,1)S(1)}, bf16[2,256,256]{2,1,0:T(8,128)(2,1)S(1)}, u32[]{:S(2)}, u32[]{:S(2)}) %collective-permute-start.18) | collective-permute-done | bytes 262176 | tf_op jit(solution)/shard_map/ppermute | solution.py:29
  81.3 2.1 %collective-permute-done.19 = bf16[2,256,256]{2,1,0:T(8,128)(2,1)S(1)} collective-permute-done((bf16[2,256,256]{2,1,0:T(8,128)(2,1)S(1)}, bf16[2,256,256]{2,1,0:T(8,128)(2,1)S(1)}, u32[]{:S(2)}, u32[]{:S(2)}) %collective-permute-start.19) | collective-permute-done | bytes 262176 | tf_op jit(solution)/shard_map/ppermute | solution.py:29
  83.4 2.7 %collective-permute-done.20 = bf16[2,256,256]{2,1,0:T(8,128)(2,1)S(1)} collective-permute-done((bf16[2,256,256]{2,1,0:T(8,128)(2,1)S(1)}, bf16[2,256,256]{2,1,0:T(8,128)(2,1)S(1)}, u32[]{:S(2)}, u32[]{:S(2)}) %collective-permute-start.20) | collective-permute-done | bytes 262176 | tf_op jit(solution)/shard_map/ppermute | solution.py:29
  86.4 4.7 %collective-permute-start.23 = (bf16[2,256,256]{2,1,0:T(8,128)(2,1)S(1)}, bf16[2,256,256]{2,1,0:T(8,128)(2,1)S(1)}, u32[]{:S(2)}, u32[]{:S(2)}) collective-permute-start(bf16[2,256,256]{2,1,0:T(8,128)(2,1)S(1)} %get-tuple-element.98), channel_id=1, source_target_pairs={{0,224},{4,228},{8,232},{12,236},{16,240},{20,244},{24,248},{28,25... | collective-permute-start | bytes 786440 | tf_op jit(solution)/shard_map/ppermute | solution.py:29
  91.1 3.6 %collective-permute-done.23 = bf16[2,256,256]{2,1,0:T(8,128)(2,1)S(1)} collective-permute-done((bf16[2,256,256]{2,1,0:T(8,128)(2,1)S(1)}, bf16[2,256,256]{2,1,0:T(8,128)(2,1)S(1)}, u32[]{:S(2)}, u32[]{:S(2)}) %collective-permute-start.23) | collective-permute-done | bytes 262176 | tf_op jit(solution)/shard_map/ppermute | solution.py:29
  94.6 0.7 collective-permute-done.21.last_a
  95.4 1.0 projection_merge.1
  96.4 2.8 %collective-permute-start.25 = (bf16[8,84,256]{2,1,0:T(8,128)(2,1)S(1)}, bf16[8,84,256]{2,1,0:T(8,128)(2,1)S(1)}, u32[]{:S(2)}, u32[]{:S(2)}) collective-permute-start(bf16[8,84,256]{2,1,0:T(8,128)(2,1)S(1)} %get-tuple-element.103), channel_id=1, source_target_pairs={{0,4},{4,0},{8,12},{12,8},{16,20},{20,16},{24,28},{28,24},{32,36},... | collective-permute-start | bytes 1032200 | tf_op jit(solution)/shard_map/ppermute | solution.py:29
  99.2 1.3 collective-permute-done.25
  100.5 0.9 pad_maximum_fusion
  101.4 8.0 %all-to-all-start = ((bf16[8,84,512]{2,1,0:T(8,128)(2,1)}), bf16[8,84,512]{2,1,0:T(8,128)(2,1)S(1)}, u32[]{:S(2)}, u32[]{:S(2)}) async-start(bf16[8,84,512]{2,1,0:T(8,128)(2,1)} %pad_maximum_fusion), calls=%async_computation | async-start | bytes 1441792 | tf_op jit(solution)/shard_map/all_to_all | solution.py:55
  109.4 0.7 collective-permute-start.15
  110.4 0.7 collective-permute-done.15
  111.1 0.7 pad_maximum_fusion.2
  111.8 0.7 pad_maximum_fusion.3
  112.6 19.0 %all-to-all-done.blocks = bf16[8,84,512]{2,1,0:T(8,128)(2,1)S(1)} async-done(((bf16[8,84,512]{2,1,0:T(8,128)(2,1)}), bf16[8,84,512]{2,1,0:T(8,128)(2,1)S(1)}, u32[]{:S(2)}, u32[]{:S(2)}) %all-to-all-start) | async-done | bytes 688160 | tf_op jit(solution)/shard_map/all_to_all | solution.py:55
  131.6 1.3 projection_finish.1
  (43 shorter events, 1.2 us)
Async XLA Ops:
  0.6 8.9 %collective-permute-start.2 = (bf16[2,32,5376]{2,1,0:T(8,128)(2,1)}, bf16[2,32,5376]{2,1,0:T(8,128)(2,1)S(1)}, u32[]{:S(2)}, u32[]{:S(2)}) collective-permute-start(bf16[2,32,5376]{2,1,0:T(8,128)(2,1)} %refs_0_.1), channel_id=1, source_target_pairs={{0,4},{4,0},{8,12},{12,8},{16,20},{20,16},{24,28},{28,24},{32,36},... | collective-permute-start | bytes 2064392 | tf_op jit(solution)/shard_map/ppermute | solution.py:29
  4.0 1.0 copy-start.2
  5.0 0.9 copy-start.3
  5.9 0.9 copy-start.4
  6.8 5.1 %copy-start.5 = (bf16[2,32,5376]{2,1,0:T(8,128)(2,1)S(1)}, bf16[2,32,5376]{2,1,0:T(8,128)(2,1)}, u32[]{:S(2)}) copy-start(bf16[2,32,5376]{2,1,0:T(8,128)(2,1)} %refs_0_.1) | copy-start | bytes 2064388
  7.5 2.1 %collective-permute-start = (bf16[2,128,512]{2,1,0:T(8,128)(2,1)S(1)}, bf16[2,128,512]{2,1,0:T(8,128)(2,1)S(1)}, u32[]{:S(2)}, u32[]{:S(2)}) collective-permute-start(bf16[2,128,512]{2,1,0:T(8,128)(2,1)S(1)} %get-tuple-element.54), channel_id=1, source_target_pairs={{0,4},{4,0},{8,12},{12,8},{16,20},{20,16},{24,28},{28,24},{32,36},... | collective-permute-start | bytes 786440 | tf_op jit(solution)/shard_map/ppermute | solution.py:29
  7.6 1.9 %collective-permute-start.1 = (s32[2,1,128]{2,1,0:T(1,128)}, s32[2,1,128]{2,1,0:T(1,128)S(1)}, u32[]{:S(2)}, u32[]{:S(2)}) collective-permute-start(s32[2,1,128]{2,1,0:T(1,128)} %bitcast.9), channel_id=1, source_target_pairs={{0,4},{4,0},{8,12},{12,8},{16,20},{20,16},{24,28},{28,24},{32,36},... | collective-permute-start | bytes 3080 | tf_op jit(solution)/shard_map/ppermute | solution.py:29
  8.1 17.2 %collective-permute-start.3 = (bf16[2,32,5376]{2,1,0:T(8,128)(2,1)}, bf16[2,32,5376]{2,1,0:T(8,128)(2,1)S(1)}, u32[]{:S(2)}, u32[]{:S(2)}) collective-permute-start(bf16[2,32,5376]{2,1,0:T(8,128)(2,1)} %refs_0_.1), channel_id=1, source_target_pairs={{0,3},{1,0},{2,1},{3,2},{4,7},{5,4},{6,5},{7,6},{8,11},{9,8},{10,9... | collective-permute-start | bytes 2064392 | tf_op jit(solution)/shard_map/ppermute | solution.py:68
  8.8 18.1 %collective-permute-start.4 = (bf16[2,32,5376]{2,1,0:T(8,128)(2,1)}, bf16[2,32,5376]{2,1,0:T(8,128)(2,1)S(1)}, u32[]{:S(2)}, u32[]{:S(2)}) collective-permute-start(bf16[2,32,5376]{2,1,0:T(8,128)(2,1)} %refs_0_.1), channel_id=1, source_target_pairs={{0,1},{1,2},{2,3},{3,0},{4,5},{5,6},{6,7},{7,4},{8,9},{9,10},{10,1... | collective-permute-start | bytes 2064392 | tf_op jit(solution)/shard_map/ppermute | solution.py:68
  9.6 11.3 %collective-permute-start.6 = (bf16[2,256,256]{2,1,0:T(8,128)(2,1)S(1)}, bf16[2,256,256]{2,1,0:T(8,128)(2,1)S(1)}, u32[]{:S(2)}, u32[]{:S(2)}) collective-permute-start(bf16[2,256,256]{2,1,0:T(8,128)(2,1)S(1)} %pad_maximum_fusion.1.kv0), channel_id=1, source_target_pairs={{0,32},{4,36},{8,40},{12,44},{16,48},{20,52},{24,56},{28,60},{32,6... | collective-permute-start | bytes 786440 | tf_op jit(solution)/shard_map/ppermute | solution.py:29
  10.6 18.4 %collective-permute-start.5 = (bf16[2,256,256]{2,1,0:T(8,128)(2,1)S(1)}, bf16[2,256,256]{2,1,0:T(8,128)(2,1)S(1)}, u32[]{:S(2)}, u32[]{:S(2)}) collective-permute-start(bf16[2,256,256]{2,1,0:T(8,128)(2,1)S(1)} %pad_maximum_fusion.1.kv0), channel_id=1, source_target_pairs={{0,8},{4,12},{8,16},{12,20},{16,24},{20,28},{24,32},{28,36},{32,40... | collective-permute-start | bytes 786440 | tf_op jit(solution)/shard_map/ppermute | solution.py:29
  11.9 2.6 %copy-start = (bf16[5376,512]{1,0:T(8,128)(2,1)S(1)}, bf16[5376,512]{1,0:T(8,128)(2,1)}, u32[]{:S(2)}) copy-start(bf16[5376,512]{1,0:T(8,128)(2,1)} %o_weight.1) | copy-start | bytes 16515076
  14.5 20.2 %copy-start.1 = (bf16[5376,512]{1,0:T(8,128)(2,1)S(1)}, bf16[5376,512]{1,0:T(8,128)(2,1)}, u32[]{:S(2)}) copy-start(bf16[5376,512]{1,0:T(8,128)(2,1)} %o_weight.1) | copy-start | bytes 16515076
  29.0 3.0 %collective-permute-start.7 = (bf16[2,32,5376]{2,1,0:T(8,128)(2,1)S(1)}, bf16[2,32,5376]{2,1,0:T(8,128)(2,1)S(1)}, u32[]{:S(2)}, u32[]{:S(2)}) collective-permute-start(bf16[2,32,5376]{2,1,0:T(8,128)(2,1)S(1)} %collective-permute-done.3.refs_0_), channel_id=1, source_target_pairs={{0,4},{4,0},{8,12},{12,8},{16,20},{20,16},{24,28},{28,24},{32,36},... | collective-permute-start | bytes 2064392 | tf_op jit(solution)/shard_map/ppermute | solution.py:29
  29.9 4.8 %collective-permute-start.8 = (bf16[2,32,5376]{2,1,0:T(8,128)(2,1)S(1)}, bf16[2,32,5376]{2,1,0:T(8,128)(2,1)S(1)}, u32[]{:S(2)}, u32[]{:S(2)}) collective-permute-start(bf16[2,32,5376]{2,1,0:T(8,128)(2,1)S(1)} %collective-permute-done.4.refs_1_), channel_id=1, source_target_pairs={{0,4},{4,0},{8,12},{12,8},{16,20},{20,16},{24,28},{28,24},{32,36},... | collective-permute-start | bytes 2064392 | tf_op jit(solution)/shard_map/ppermute | solution.py:29
  29.9 14.8 %copy-start.6 = (s32[2,128]{1,0:T(2,128)S(1)}, s32[2,128]{1,0:T(2,128)}, u32[]{:S(2)}) copy-start(s32[2,128]{1,0:T(2,128)} %param.11) | copy-start | bytes 3076
  29.9 9.0 %collective-permute-start.11 = (bf16[2,256,256]{2,1,0:T(8,128)(2,1)S(1)}, bf16[2,256,256]{2,1,0:T(8,128)(2,1)S(1)}, u32[]{:S(2)}, u32[]{:S(2)}) collective-permute-start(bf16[2,256,256]{2,1,0:T(8,128)(2,1)S(1)} %get-tuple-element.68), channel_id=1, source_target_pairs={{0,16},{4,20},{8,24},{12,28},{16,0},{20,4},{24,8},{28,12},{32,48},... | collective-permute-start | bytes 786440 | tf_op jit(solution)/shard_map/ppermute | solution.py:29
  31.2 12.0 %collective-permute-start.12 = (bf16[2,256,256]{2,1,0:T(8,128)(2,1)S(1)}, bf16[2,256,256]{2,1,0:T(8,128)(2,1)S(1)}, u32[]{:S(2)}, u32[]{:S(2)}) collective-permute-start(bf16[2,256,256]{2,1,0:T(8,128)(2,1)S(1)} %get-tuple-element.69), channel_id=1, source_target_pairs={{0,24},{4,28},{8,0},{12,4},{16,8},{20,12},{24,16},{28,20},{32,56},... | collective-permute-start | bytes 786440 | tf_op jit(solution)/shard_map/ppermute | solution.py:29
  31.9 11.2 %collective-permute-start.9 = (bf16[1,32,5376]{2,1,0:T(8,128)(2,1)S(1)}, bf16[1,32,5376]{2,1,0:T(8,128)(2,1)S(1)}, u32[]{:S(2)}, u32[]{:S(2)}) collective-permute-start(bf16[1,32,5376]{2,1,0:T(8,128)(2,1)S(1)} %slice.40), channel_id=1, source_target_pairs={{0,1},{1,2},{2,3},{3,0},{4,5},{5,6},{6,7},{7,4},{8,9},{9,10},{10,1... | collective-permute-start | bytes 1032200 | tf_op jit(solution)/shard_map/ppermute | solution.py:68
  31.9 11.2 %collective-permute-start.10 = (bf16[1,32,5376]{2,1,0:T(8,128)(2,1)S(1)}, bf16[1,32,5376]{2,1,0:T(8,128)(2,1)S(1)}, u32[]{:S(2)}, u32[]{:S(2)}) collective-permute-start(bf16[1,32,5376]{2,1,0:T(8,128)(2,1)S(1)} %slice.41), channel_id=1, source_target_pairs={{0,3},{1,0},{2,1},{3,2},{4,7},{5,4},{6,5},{7,6},{8,11},{9,8},{10,9... | collective-permute-start | bytes 1032200 | tf_op jit(solution)/shard_map/ppermute | solution.py:68
  43.1 5.9 %collective-permute-start.13 = (bf16[1,32,5376]{2,1,0:T(8,128)(2,1)S(1)}, bf16[1,32,5376]{2,1,0:T(8,128)(2,1)S(1)}, u32[]{:S(2)}, u32[]{:S(2)}) collective-permute-start(bf16[1,32,5376]{2,1,0:T(8,128)(2,1)S(1)} %collective-permute-done.9.r2a), channel_id=1, source_target_pairs={{0,4},{4,0},{8,12},{12,8},{16,20},{20,16},{24,28},{28,24},{32,36},... | collective-permute-start | bytes 1032200 | tf_op jit(solution)/shard_map/ppermute | solution.py:29
  44.5 4.5 %collective-permute-start.14 = (bf16[1,32,5376]{2,1,0:T(8,128)(2,1)S(1)}, bf16[1,32,5376]{2,1,0:T(8,128)(2,1)S(1)}, u32[]{:S(2)}, u32[]{:S(2)}) collective-permute-start(bf16[1,32,5376]{2,1,0:T(8,128)(2,1)S(1)} %collective-permute-done.10.r2b), channel_id=1, source_target_pairs={{0,4},{4,0},{8,12},{12,8},{16,20},{20,16},{24,28},{28,24},{32,36},... | collective-permute-start | bytes 1032200 | tf_op jit(solution)/shard_map/ppermute | solution.py:29
  53.2 32.9 %collective-permute-start.16 = (bf16[2,4,168,256]{3,2,1,0:T(8,128)(2,1)S(1)}, bf16[2,4,168,256]{3,2,1,0:T(8,128)(2,1)S(1)}, u32[]{:S(2)}, u32[]{:S(2)}) collective-permute-start(bf16[2,4,168,256]{3,2,1,0:T(8,128)(2,1)S(1)} %get-tuple-element.84), channel_id=1, source_target_pairs={{0,8},{4,12},{8,0},{12,4},{16,24},{20,28},{24,16},{28,20},{32,40},... | collective-permute-start | bytes 2064392 | tf_op jit(solution)/shard_map/ppermute | solution.py:29
  54.1 31.9 %collective-permute-start.17 = (bf16[2,4,168,256]{3,2,1,0:T(8,128)(2,1)S(1)}, bf16[2,4,168,256]{3,2,1,0:T(8,128)(2,1)S(1)}, u32[]{:S(2)}, u32[]{:S(2)}) collective-permute-start(bf16[2,4,168,256]{3,2,1,0:T(8,128)(2,1)S(1)} %get-tuple-element.85), channel_id=1, source_target_pairs={{0,24},{4,28},{8,16},{12,20},{16,8},{20,12},{24,0},{28,4},{32,56},... | collective-permute-start | bytes 2064392 | tf_op jit(solution)/shard_map/ppermute | solution.py:29
  59.5 21.8 %collective-permute-start.18 = (bf16[2,256,256]{2,1,0:T(8,128)(2,1)S(1)}, bf16[2,256,256]{2,1,0:T(8,128)(2,1)S(1)}, u32[]{:S(2)}, u32[]{:S(2)}) collective-permute-start(bf16[2,256,256]{2,1,0:T(8,128)(2,1)S(1)} %get-tuple-element.87), channel_id=1, source_target_pairs={{0,248},{4,252},{8,0},{12,4},{16,8},{20,12},{24,16},{28,20},{32,24... | collective-permute-start | bytes 786440 | tf_op jit(solution)/shard_map/ppermute | solution.py:29
  66.0 17.4 %collective-permute-start.19 = (bf16[2,256,256]{2,1,0:T(8,128)(2,1)S(1)}, bf16[2,256,256]{2,1,0:T(8,128)(2,1)S(1)}, u32[]{:S(2)}, u32[]{:S(2)}) collective-permute-start(bf16[2,256,256]{2,1,0:T(8,128)(2,1)S(1)} %get-tuple-element.88), channel_id=1, source_target_pairs={{0,240},{4,244},{8,248},{12,252},{16,0},{20,4},{24,8},{28,12},{32,... | collective-permute-start | bytes 786440 | tf_op jit(solution)/shard_map/ppermute | solution.py:29
  67.4 18.6 %collective-permute-start.20 = (bf16[2,256,256]{2,1,0:T(8,128)(2,1)S(1)}, bf16[2,256,256]{2,1,0:T(8,128)(2,1)S(1)}, u32[]{:S(2)}, u32[]{:S(2)}) collective-permute-start(bf16[2,256,256]{2,1,0:T(8,128)(2,1)S(1)} %get-tuple-element.89), channel_id=1, source_target_pairs={{0,232},{4,236},{8,240},{12,244},{16,248},{20,252},{24,0},{28,4},{... | collective-permute-start | bytes 786440 | tf_op jit(solution)/shard_map/ppermute | solution.py:29
  86.1 8.5 %collective-permute-start.22 = (bf16[4,168,256]{2,1,0:T(8,128)(2,1)S(1)}, bf16[4,168,256]{2,1,0:T(8,128)(2,1)S(1)}, u32[]{:S(2)}, u32[]{:S(2)}) collective-permute-start(bf16[4,168,256]{2,1,0:T(8,128)(2,1)S(1)} %fusion.1), channel_id=1, source_target_pairs={{0,8},{4,12},{8,0},{12,4},{16,24},{20,28},{24,16},{28,20},{32,40},... | collective-permute-start | bytes 1032200 | tf_op jit(solution)/shard_map/ppermute | solution.py:29
  86.3 9.1 %collective-permute-start.21 = (bf16[4,168,256]{2,1,0:T(8,128)(2,1)S(1)}, bf16[4,168,256]{2,1,0:T(8,128)(2,1)S(1)}, u32[]{:S(2)}, u32[]{:S(2)}) collective-permute-start(bf16[4,168,256]{2,1,0:T(8,128)(2,1)S(1)} %fusion), channel_id=1, source_target_pairs={{0,24},{4,28},{8,16},{12,20},{16,8},{20,12},{24,0},{28,4},{32,56},... | collective-permute-start | bytes 1032200 | tf_op jit(solution)/shard_map/ppermute | solution.py:29
  86.4 8.2 %collective-permute-start.23 = (bf16[2,256,256]{2,1,0:T(8,128)(2,1)S(1)}, bf16[2,256,256]{2,1,0:T(8,128)(2,1)S(1)}, u32[]{:S(2)}, u32[]{:S(2)}) collective-permute-start(bf16[2,256,256]{2,1,0:T(8,128)(2,1)S(1)} %get-tuple-element.98), channel_id=1, source_target_pairs={{0,224},{4,228},{8,232},{12,236},{16,240},{20,244},{24,248},{28,25... | collective-permute-start | bytes 786440 | tf_op jit(solution)/shard_map/ppermute | solution.py:29
  96.4 4.1 %collective-permute-start.25 = (bf16[8,84,256]{2,1,0:T(8,128)(2,1)S(1)}, bf16[8,84,256]{2,1,0:T(8,128)(2,1)S(1)}, u32[]{:S(2)}, u32[]{:S(2)}) collective-permute-start(bf16[8,84,256]{2,1,0:T(8,128)(2,1)S(1)} %get-tuple-element.103), channel_id=1, source_target_pairs={{0,4},{4,0},{8,12},{12,8},{16,20},{20,16},{24,28},{28,24},{32,36},... | collective-permute-start | bytes 1032200 | tf_op jit(solution)/shard_map/ppermute | solution.py:29
  101.4 30.2 %all-to-all-start = ((bf16[8,84,512]{2,1,0:T(8,128)(2,1)}), bf16[8,84,512]{2,1,0:T(8,128)(2,1)S(1)}, u32[]{:S(2)}, u32[]{:S(2)}) async-start(bf16[8,84,512]{2,1,0:T(8,128)(2,1)} %pad_maximum_fusion), calls=%async_computation | async-start | bytes 1441792 | tf_op jit(solution)/shard_map/all_to_all | solution.py:55
  109.4 1.6 %collective-permute-start.15 = (bf16[2,128,256]{2,1,0:T(8,128)(2,1)S(1)}, bf16[2,128,256]{2,1,0:T(8,128)(2,1)S(1)}, u32[]{:S(2)}, u32[]{:S(2)}) collective-permute-start(bf16[2,128,256]{2,1,0:T(8,128)(2,1)S(1)} %get-tuple-element.83), channel_id=1, source_target_pairs={{0,4},{4,0},{8,12},{12,8},{16,20},{20,16},{24,28},{28,24},{32,36},... | collective-permute-start | bytes 393224 | tf_op jit(solution)/shard_map/ppermute | solution.py:29
  110.3 1.5 %collective-permute-start.24 = (bf16[2,128,256]{2,1,0:T(8,128)(2,1)S(1)}, bf16[2,128,256]{2,1,0:T(8,128)(2,1)S(1)}, u32[]{:S(2)}, u32[]{:S(2)}) collective-permute-start(bf16[2,128,256]{2,1,0:T(8,128)(2,1)S(1)} %slice.52), channel_id=1, source_target_pairs={{0,4},{4,0},{8,12},{12,8},{16,20},{20,16},{24,28},{28,24},{32,36},... | collective-permute-start | bytes 393224 | tf_op jit(solution)/shard_map/ppermute | solution.py:29

commit v10 on v8

--- a/solution.py
+++ b/solution.py
@@ -481,25 +481,24 @@
     doc_mine = doc_start[:, None, :]
     doc_recv = to_sibling(doc_mine)
     t0 = to_sibling(d_out)
-    recv, doc_recv, t0, scalars, first, one_row, two_rows = lax.optimization_barrier(
-        (recv, doc_recv, t0, scalars, first, y < 1, y < 2)
+    recv, doc_recv, t0, scalars, first, one_row = lax.optimization_barrier(
+        (recv, doc_recv, t0, scalars, first, y < 1)
     )
     kv0 = jnp.concatenate([kv_mine, recv[..., -2 * HEAD_SIZE :]], axis=1)
-    kv4, kv1 = (chips_ahead(kv0, d) for d in (4, 1))
+    kv4, kv2, kv1 = (chips_ahead(kv0, d) for d in (4, 2, 1))
     own, own_t = early_projection(scalars, [d_out, t0], o_weight)
 
-    kv_two = jnp.where(two_rows, kv0, kv4)
     kv_three = jnp.where(one_row, kv0, kv4)
-    r1, r3, own, kv1, kv_two, kv_three = lax.optimization_barrier(
-        (r1, r3, own, kv1, kv_two, kv_three)
-    )
-    kv2, kv3 = y_ahead(kv_two, 2), y_ahead(kv_three, 3)
+    r1, r3, own, kv1, kv2, kv_three = lax.optimization_barrier(
+        (r1, r3, own, kv1, kv2, kv_three)
+    )
+    kv3 = y_ahead(kv_three, 3)
     r2a = tp_ahead(r3[:1], 1)
     r2b = tp_ahead(r1[1:], -1)
     near, near_t = early_projection(
         scalars, [r1, r3, to_sibling(r1), to_sibling(r3)], o_weight
     )
-    near, r2a, r2b, kv2, kv3 = lax.optimization_barrier((near, r2a, r2b, kv2, kv3))
+    near, r2a, r2b, kv3 = lax.optimization_barrier((near, r2a, r2b, kv3))
     kvs = [kv0, kv1, kv2, kv3, kv4]
     attn, weights = forward(scalars, q_mine, recv, kvs, doc_mine, doc_recv)
     d_attn, sent_a, kept_a, sent_b, kept_b = late_projection(

time: 130 us -> 131 us (level)
  waiting for transfers between devices: 56.2 us -> 65 us
  starting transfers between devices: 41.9 us -> 34.4 us
    ppermute x21, waiting for transfers between devices: 31.9 us -> 39.2 us  [ctx_shift(): return lax.ppermute(block, 'ctx', [(i, move(i)) for i in range(count)])]
    ppermute x21, starting transfers between devices: 26.6 us -> 20.8 us  [ctx_shift(): return lax.ppermute(block, 'ctx', [(i, move(i)) for i in range(count)])]
    all_to_all x1, starting transfers between devices: 11.1 us -> 8.89 us  [z_exchange(): lax.all_to_all(blocks, 'ctx', 0, 0, axis_index_groups=groups, tiled=True)]
    ppermute x4, waiting for transfers between devices: 5.87 us -> 7.39 us  [tp_ahead(): lax.ppermute(block, 'tp', [(i, (i + distance) % TP) for i in range(TP)])]
  transfers between devices with their start and end apart: 26 -> 26, of which waited for: 12 -> 14; matrix products, arithmetic and copies ran while one was open for 2% -> 1% of each run, Pallas kernels for 12% -> 12%
where the time goes in v10:
time: 131 us
  waiting for transfers between devices  65 us (50%)
  starting transfers between devices  34.4 us (26%)
  Pallas kernels  22.3 us (17%)
  local copies, waits for them, and re-layouts  6.49 us (5%)
  other arithmetic  1.98 us (2%)
    ppermute x21, waiting for transfers between devices, ctx_shift(): return lax.ppermute(block, 'ctx', [(i, move(i)) for i in range(count)])  39.2 us
    ppermute x21, starting transfers between devices, ctx_shift(): return lax.ppermute(block, 'ctx', [(i, move(i)) for i in range(count)])  20.8 us
    all_to_all x1, waiting for transfers between devices, z_exchange(): lax.all_to_all(blocks, 'ctx', 0, 0, axis_index_groups=groups, tiled=True)  18.5 us
    all_to_all x1, starting transfers between devices, z_exchange(): lax.all_to_all(blocks, 'ctx', 0, 0, axis_index_groups=groups, tiled=True)  8.89 us
    pallas_call x2, Pallas kernels, early_projection(): pl.pallas_call(early_kernel, out_shape=outs, grid_spec=pltpu.PrefetchScal...  7.51 us
    ppermute x4, waiting for transfers between devices, tp_ahead(): lax.ppermute(block, 'tp', [(i, (i + distance) % TP) for i in range(TP)])  7.39 us
    unnamed x14, local copies, waits for them, and re-layouts  6.43 us
    ppermute x4, starting transfers between devices, tp_ahead(): lax.ppermute(block, 'tp', [(i, (i + distance) % TP) for i in range(TP)])  4.63 us
  transfers between devices with their start and end apart: 26, of which 14 were waited for; matrix products, arithmetic and copies ran while one was open for 1% of the time, Pallas kernels for 12%

profile of v10, /device:TPU:1, one launch (start us, length us, event | category | flops | bytes accessed | tf_op | source)
XLA Modules:
  0.0 130.9 jit_solution(4032112580294678827)
XLA Ops:
  0.6 3.3 %collective-permute-start.2 = (bf16[2,32,5376]{2,1,0:T(8,128)(2,1)}, bf16[2,32,5376]{2,1,0:T(8,128)(2,1)S(1)}, u32[]{:S(2)}, u32[]{:S(2)}) collective-permute-start(bf16[2,32,5376]{2,1,0:T(8,128)(2,1)} %refs_0_.1), channel_id=1, source_target_pairs={{0,4},{4,0},{8,12},{12,8},{16,20},{20,16},{24,28},{28,24},{32,36},... | collective-permute-start | bytes 2064392 | tf_op jit(solution)/shard_map/ppermute | solution.py:29
  4.0 0.9 copy-done.2
  5.0 0.9 copy-done.3
  5.9 0.9 copy-done.4
  6.8 0.7 split_heads.1
  7.6 0.8 collective-permute-start.3
  8.4 0.7 collective-permute-start.4
  9.1 1.0 collective-permute-start.1
  10.1 1.0 collective-permute-done.1.doc_recv
  11.2 0.7 collective-permute-start.7
  11.9 2.9 %collective-permute-start.6 = (bf16[2,256,256]{2,1,0:T(8,128)(2,1)S(1)}, bf16[2,256,256]{2,1,0:T(8,128)(2,1)S(1)}, u32[]{:S(2)}, u32[]{:S(2)}) collective-permute-start(bf16[2,256,256]{2,1,0:T(8,128)(2,1)S(1)} %pad_maximum_fusion.kv0), channel_id=1, source_target_pairs={{0,16},{4,20},{8,24},{12,28},{16,32},{20,36},{24,40},{28,44},{32,4... | collective-permute-start | bytes 786440 | tf_op jit(solution)/shard_map/ppermute | solution.py:29
  14.8 0.4 collective-permute-start.5
  15.2 2.6 %copy-done = bf16[5376,512]{1,0:T(8,128)(2,1)S(1)} copy-done((bf16[5376,512]{1,0:T(8,128)(2,1)S(1)}, bf16[5376,512]{1,0:T(8,128)(2,1)}, u32[]{:S(2)}) %copy-start) | copy-done | bytes 5505048
  17.7 1.1 copy-done.5
  18.8 3.3 %projection_early.2 = (bf16[128,256]{1,0:T(8,128)(2,1)S(1)}, bf16[5376,128]{1,0:T(8,128)(2,1)S(1)}) custom-call(s32[4]{0:T(128)S(1)} %pad_add_fusion.scalars, bf16[2,32,5376]{2,1,0:T(8,128)(2,1)S(1)} %copy-done.5, bf16[2,32,5376]{2,1,0:T(8,128)(2,1)S(1)} %collective-permute-done.2.refs_1_, bf16[5376,512]{1,0:T(8,128)(2,1)S(1)} %copy-done), custom_call_target="tpu_custom_call" | custom-call | flops 3523215360 | bytes 12582912 | tf_op jit(solution)/shard_map/projection_early/pallas_call | solution.py:380
  22.3 2.1 %collective-permute-done.3.refs_0_ = bf16[2,32,5376]{2,1,0:T(8,128)(2,1)S(1)} collective-permute-done((bf16[2,32,5376]{2,1,0:T(8,128)(2,1)}, bf16[2,32,5376]{2,1,0:T(8,128)(2,1)S(1)}, u32[]{:S(2)}, u32[]{:S(2)}) %collective-permute-start.3) | collective-permute-done | bytes 688160 | tf_op jit(solution)/shard_map/ppermute | solution.py:70
  24.4 1.6 %collective-permute-done.4.refs_1_ = bf16[2,32,5376]{2,1,0:T(8,128)(2,1)S(1)} collective-permute-done((bf16[2,32,5376]{2,1,0:T(8,128)(2,1)}, bf16[2,32,5376]{2,1,0:T(8,128)(2,1)S(1)}, u32[]{:S(2)}, u32[]{:S(2)}) %collective-permute-start.4) | collective-permute-done | bytes 688160 | tf_op jit(solution)/shard_map/ppermute | solution.py:70
  26.1 4.4 %collective-permute-done.6.kv2 = bf16[2,256,256]{2,1,0:T(8,128)(2,1)S(1)} collective-permute-done((bf16[2,256,256]{2,1,0:T(8,128)(2,1)S(1)}, bf16[2,256,256]{2,1,0:T(8,128)(2,1)S(1)}, u32[]{:S(2)}, u32[]{:S(2)}) %collective-permute-start.6) | collective-permute-done | bytes 262176 | tf_op jit(solution)/shard_map/ppermute | solution.py:29
  30.5 5.6 %collective-permute-done.5.kv1 = bf16[2,256,256]{2,1,0:T(8,128)(2,1)S(1)} collective-permute-done((bf16[2,256,256]{2,1,0:T(8,128)(2,1)S(1)}, bf16[2,256,256]{2,1,0:T(8,128)(2,1)S(1)}, u32[]{:S(2)}, u32[]{:S(2)}) %collective-permute-start.5) | collective-permute-done | bytes 262176 | tf_op jit(solution)/shard_map/ppermute | solution.py:29
  36.1 0.9 collective-permute-start.8
  37.1 0.6 collective-permute-start.10
  37.7 2.6 %collective-permute-start.11 = (bf16[1,32,5376]{2,1,0:T(8,128)(2,1)S(1)}, bf16[1,32,5376]{2,1,0:T(8,128)(2,1)S(1)}, u32[]{:S(2)}, u32[]{:S(2)}) collective-permute-start(bf16[1,32,5376]{2,1,0:T(8,128)(2,1)S(1)} %slice.41), channel_id=1, source_target_pairs={{0,3},{1,0},{2,1},{3,2},{4,7},{5,4},{6,5},{7,6},{8,11},{9,8},{10,9... | collective-permute-start | bytes 1032200 | tf_op jit(solution)/shard_map/ppermute | solution.py:70
  40.2 4.2 %projection_early.3 = (bf16[256,256]{1,0:T(8,128)(2,1)S(1)}, bf16[5376,256]{1,0:T(8,128)(2,1)S(1)}) custom-call(s32[4]{0:T(128)S(1)} %pad_add_fusion.scalars, bf16[2,32,5376]{2,1,0:T(8,128)(2,1)S(1)} %collective-permute-done.3.refs_0_, bf16[2,32,5376]{2,1,0:T(8,128)(2,1)S(1)} %collective-permute-done.4.refs_1_, ...), custom_call_target="tpu_custom_call" | custom-call | flops 7046430720 | bytes 12582912 | tf_op jit(solution)/shard_map/projection_early/pallas_call | solution.py:380
  44.5 3.6 %collective-permute-done.10.r2a = bf16[1,32,5376]{2,1,0:T(8,128)(2,1)S(1)} collective-permute-done((bf16[1,32,5376]{2,1,0:T(8,128)(2,1)S(1)}, bf16[1,32,5376]{2,1,0:T(8,128)(2,1)S(1)}, u32[]{:S(2)}, u32[]{:S(2)}) %collective-permute-start.10) | collective-permute-done | bytes 344096 | tf_op jit(solution)/shard_map/ppermute | solution.py:70
  48.1 1.0 collective-permute-start.13
  49.2 4.2 %attention_forward.1 = (bf16[2,256,256]{2,1,0:T(8,128)(2,1)S(1)}, bf16[2,2,1280,256]{3,2,1,0:T(8,128)(2,1)S(1)}) custom-call(s32[4]{0:T(128)S(1)} %pad_add_fusion.scalars, bf16[2,128,256]{2,1,0:T(8,128)(2,1)S(1)} %get-tuple-element.52.mine, bf16[2,128,512]{2,1,0:T(8,128)(2,1)S(1)} %collective-permute-done.recv, ...), custom_call_target="tpu_custom_call" | custom-call | flops 671088640 | bytes 8388608 | tf_op jit(solution)/shard_map/attention_forward/pallas_call | solution.py:349
  53.4 4.1 %projection_late.1 = (bf16[2,256,256]{2,1,0:T(8,128)(2,1)S(1)}, bf16[2,4,168,256]{3,2,1,0:T(8,128)(2,1)S(1)}, bf16[2,4,168,256]{3,2,1,0:T(8,128)(2,1)S(1)}, bf16...) custom-call(s32[4]{0:T(128)S(1)} %pad_add_fusion.scalars, ...), custom_call_target="tpu_custom_call" | custom-call | flops 2113929216 | bytes 12582912 | tf_op jit(solution)/shard_map/projection_late/pallas_call | solution.py:414
  57.5 1.5 %collective-permute-start.16 = (bf16[2,4,168,256]{3,2,1,0:T(8,128)(2,1)S(1)}, bf16[2,4,168,256]{3,2,1,0:T(8,128)(2,1)S(1)}, u32[]{:S(2)}, u32[]{:S(2)}) collective-permute-start(bf16[2,4,168,256]{3,2,1,0:T(8,128)(2,1)S(1)} %get-tuple-element.78), channel_id=1, source_target_pairs={{0,8},{4,12},{8,0},{12,4},{16,24},{20,28},{24,16},{28,20},{32,40},... | collective-permute-start | bytes 2064392 | tf_op jit(solution)/shard_map/ppermute | solution.py:29
  59.0 3.8 %attention_backward.1 = (bf16[2,128,256]{2,1,0:T(8,128)(2,1)S(1)}, bf16[2,128,256]{2,1,0:T(8,128)(2,1)S(1)}, f32[2,256,256]{2,1,0:T(8,128)S(1)}, bf16[2,256,256]...) custom-call(bf16[2,128,256]{2,1,0:T(8,128)(2,1)S(1)} %get-tuple-elem, ...), custom_call_target="tpu_custom_call" | custom-call | flops 1677721600 | bytes 8388608 | tf_op jit(solution)/shard_map/attention_backward/pallas_call | solution.py:450
  62.8 3.9 %collective-permute-start.18 = (bf16[2,256,256]{2,1,0:T(8,128)(2,1)S(1)}, bf16[2,256,256]{2,1,0:T(8,128)(2,1)S(1)}, u32[]{:S(2)}, u32[]{:S(2)}) collective-permute-start(bf16[2,256,256]{2,1,0:T(8,128)(2,1)S(1)} %get-tuple-element.81), channel_id=1, source_target_pairs={{0,248},{4,252},{8,0},{12,4},{16,8},{20,12},{24,16},{28,20},{32,24... | collective-permute-start | bytes 786440 | tf_op jit(solution)/shard_map/ppermute | solution.py:29
  66.7 1.2 collective-permute-start.20
  68.0 17.4 %collective-permute-done.18 = bf16[2,256,256]{2,1,0:T(8,128)(2,1)S(1)} collective-permute-done((bf16[2,256,256]{2,1,0:T(8,128)(2,1)S(1)}, bf16[2,256,256]{2,1,0:T(8,128)(2,1)S(1)}, u32[]{:S(2)}, u32[]{:S(2)}) %collective-permute-start.18) | collective-permute-done | bytes 262176 | tf_op jit(solution)/shard_map/ppermute | solution.py:29
  85.4 2.3 %collective-permute-done.20 = bf16[2,256,256]{2,1,0:T(8,128)(2,1)S(1)} collective-permute-done((bf16[2,256,256]{2,1,0:T(8,128)(2,1)S(1)}, bf16[2,256,256]{2,1,0:T(8,128)(2,1)S(1)}, u32[]{:S(2)}, u32[]{:S(2)}) %collective-permute-start.20) | collective-permute-done | bytes 262176 | tf_op jit(solution)/shard_map/ppermute | solution.py:29
  87.7 2.3 %collective-permute-start.22 = (bf16[4,168,256]{2,1,0:T(8,128)(2,1)S(1)}, bf16[4,168,256]{2,1,0:T(8,128)(2,1)S(1)}, u32[]{:S(2)}, u32[]{:S(2)}) collective-permute-start(bf16[4,168,256]{2,1,0:T(8,128)(2,1)S(1)} %fusion.1), channel_id=1, source_target_pairs={{0,8},{4,12},{8,0},{12,4},{16,24},{20,28},{24,16},{28,20},{32,40},... | collective-permute-start | bytes 1032200 | tf_op jit(solution)/shard_map/ppermute | solution.py:29
  90.3 0.7 collective-permute-start.23
  91.0 4.9 %collective-permute-done.23 = bf16[2,256,256]{2,1,0:T(8,128)(2,1)S(1)} collective-permute-done((bf16[2,256,256]{2,1,0:T(8,128)(2,1)S(1)}, bf16[2,256,256]{2,1,0:T(8,128)(2,1)S(1)}, u32[]{:S(2)}, u32[]{:S(2)}) %collective-permute-start.23) | collective-permute-done | bytes 262176 | tf_op jit(solution)/shard_map/ppermute | solution.py:29
  95.9 0.6 collective-permute-done.22.last_b
  96.5 2.3 %collective-permute-done.21.last_a = bf16[4,168,256]{2,1,0:T(8,128)(2,1)S(1)} collective-permute-done((bf16[4,168,256]{2,1,0:T(8,128)(2,1)S(1)}, bf16[4,168,256]{2,1,0:T(8,128)(2,1)S(1)}, u32[]{:S(2)}, u32[]{:S(2)}) %collective-permute-start.21) | collective-permute-done | bytes 344096 | tf_op jit(solution)/shard_map/ppermute | solution.py:29
  98.8 1.2 projection_merge.1
  99.9 8.9 %all-to-all-start = ((bf16[16,84,256]{2,1,0:T(8,128)(2,1)}), bf16[16,84,256]{2,1,0:T(8,128)(2,1)S(1)}, u32[]{:S(2)}, u32[]{:S(2)}) async-start(bf16[16,84,256]{2,1,0:T(8,128)(2,1)} %projection_merge.1), calls=%async_computation | async-start | bytes 1441792 | tf_op jit(solution)/shard_map/all_to_all | solution.py:57
  108.8 0.2 collective-permute-start.15
  109.0 0.1 add_convert_fusion.2
  109.2 0.4 collective-permute-start.24
  109.6 0.6 collective-permute-done.15
  110.2 0.7 pad_maximum_fusion.1
  111.0 0.7 pad_maximum_fusion.2
  111.7 18.5 %all-to-all-done.blocks = bf16[16,84,256]{2,1,0:T(8,128)(2,1)S(1)} async-done(((bf16[16,84,256]{2,1,0:T(8,128)(2,1)}), bf16[16,84,256]{2,1,0:T(8,128)(2,1)S(1)}, u32[]{:S(2)}, u32[]{:S(2)}) %all-to-all-start) | async-done | bytes 688160 | tf_op jit(solution)/shard_map/all_to_all | solution.py:57
  130.2 0.8 projection_finish.1
  (40 shorter events, 0.9 us)
Async XLA Ops:
  0.6 10.5 %collective-permute-start.2 = (bf16[2,32,5376]{2,1,0:T(8,128)(2,1)}, bf16[2,32,5376]{2,1,0:T(8,128)(2,1)S(1)}, u32[]{:S(2)}, u32[]{:S(2)}) collective-permute-start(bf16[2,32,5376]{2,1,0:T(8,128)(2,1)} %refs_0_.1), channel_id=1, source_target_pairs={{0,4},{4,0},{8,12},{12,8},{16,20},{20,16},{24,28},{28,24},{32,36},... | collective-permute-start | bytes 2064392 | tf_op jit(solution)/shard_map/ppermute | solution.py:29
  4.0 1.0 copy-start.2
  5.0 0.9 copy-start.3
  5.9 0.9 copy-start.4
  7.5 3.7 %collective-permute-start = (bf16[2,128,512]{2,1,0:T(8,128)(2,1)S(1)}, bf16[2,128,512]{2,1,0:T(8,128)(2,1)S(1)}, u32[]{:S(2)}, u32[]{:S(2)}) collective-permute-start(bf16[2,128,512]{2,1,0:T(8,128)(2,1)S(1)} %get-tuple-element.50), channel_id=1, source_target_pairs={{0,4},{4,0},{8,12},{12,8},{16,20},{20,16},{24,28},{28,24},{32,36},... | collective-permute-start | bytes 786440 | tf_op jit(solution)/shard_map/ppermute | solution.py:29
  7.6 16.8 %collective-permute-start.3 = (bf16[2,32,5376]{2,1,0:T(8,128)(2,1)}, bf16[2,32,5376]{2,1,0:T(8,128)(2,1)S(1)}, u32[]{:S(2)}, u32[]{:S(2)}) collective-permute-start(bf16[2,32,5376]{2,1,0:T(8,128)(2,1)} %refs_0_.1), channel_id=1, source_target_pairs={{0,3},{1,0},{2,1},{3,2},{4,7},{5,4},{6,5},{7,6},{8,11},{9,8},{10,9... | collective-permute-start | bytes 2064392 | tf_op jit(solution)/shard_map/ppermute | solution.py:70
  8.4 17.7 %collective-permute-start.4 = (bf16[2,32,5376]{2,1,0:T(8,128)(2,1)}, bf16[2,32,5376]{2,1,0:T(8,128)(2,1)S(1)}, u32[]{:S(2)}, u32[]{:S(2)}) collective-permute-start(bf16[2,32,5376]{2,1,0:T(8,128)(2,1)} %refs_0_.1), channel_id=1, source_target_pairs={{0,1},{1,2},{2,3},{3,0},{4,5},{5,6},{6,7},{7,4},{8,9},{9,10},{10,1... | collective-permute-start | bytes 2064392 | tf_op jit(solution)/shard_map/ppermute | solution.py:70
  9.1 2.0 %collective-permute-start.1 = (s32[2,1,128]{2,1,0:T(1,128)}, s32[2,1,128]{2,1,0:T(1,128)S(1)}, u32[]{:S(2)}, u32[]{:S(2)}) collective-permute-start(s32[2,1,128]{2,1,0:T(1,128)} %bitcast.9), channel_id=1, source_target_pairs={{0,4},{4,0},{8,12},{12,8},{16,20},{20,16},{24,28},{28,24},{32,36},... | collective-permute-start | bytes 3080 | tf_op jit(solution)/shard_map/ppermute | solution.py:29
  11.2 11.1 %collective-permute-start.7 = (bf16[2,256,256]{2,1,0:T(8,128)(2,1)S(1)}, bf16[2,256,256]{2,1,0:T(8,128)(2,1)S(1)}, u32[]{:S(2)}, u32[]{:S(2)}) collective-permute-start(bf16[2,256,256]{2,1,0:T(8,128)(2,1)S(1)} %pad_maximum_fusion.kv0), channel_id=1, source_target_pairs={{0,32},{4,36},{8,40},{12,44},{16,48},{20,52},{24,56},{28,60},{32,6... | collective-permute-start | bytes 786440 | tf_op jit(solution)/shard_map/ppermute | solution.py:29
  11.9 18.6 %collective-permute-start.6 = (bf16[2,256,256]{2,1,0:T(8,128)(2,1)S(1)}, bf16[2,256,256]{2,1,0:T(8,128)(2,1)S(1)}, u32[]{:S(2)}, u32[]{:S(2)}) collective-permute-start(bf16[2,256,256]{2,1,0:T(8,128)(2,1)S(1)} %pad_maximum_fusion.kv0), channel_id=1, source_target_pairs={{0,16},{4,20},{8,24},{12,28},{16,32},{20,36},{24,40},{28,44},{32,4... | collective-permute-start | bytes 786440 | tf_op jit(solution)/shard_map/ppermute | solution.py:29
  14.8 21.3 %collective-permute-start.5 = (bf16[2,256,256]{2,1,0:T(8,128)(2,1)S(1)}, bf16[2,256,256]{2,1,0:T(8,128)(2,1)S(1)}, u32[]{:S(2)}, u32[]{:S(2)}) collective-permute-start(bf16[2,256,256]{2,1,0:T(8,128)(2,1)S(1)} %pad_maximum_fusion.kv0), channel_id=1, source_target_pairs={{0,8},{4,12},{8,16},{12,20},{16,24},{20,28},{24,32},{28,36},{32,40... | collective-permute-start | bytes 786440 | tf_op jit(solution)/shard_map/ppermute | solution.py:29
  15.2 2.6 %copy-start = (bf16[5376,512]{1,0:T(8,128)(2,1)S(1)}, bf16[5376,512]{1,0:T(8,128)(2,1)}, u32[]{:S(2)}) copy-start(bf16[5376,512]{1,0:T(8,128)(2,1)} %o_weight.1) | copy-start | bytes 16515076
  17.7 1.1 copy-start.5
  18.8 21.4 %copy-start.1 = (bf16[5376,512]{1,0:T(8,128)(2,1)S(1)}, bf16[5376,512]{1,0:T(8,128)(2,1)}, u32[]{:S(2)}) copy-start(bf16[5376,512]{1,0:T(8,128)(2,1)} %o_weight.1) | copy-start | bytes 16515076
  36.1 4.2 %collective-permute-start.8 = (bf16[2,32,5376]{2,1,0:T(8,128)(2,1)S(1)}, bf16[2,32,5376]{2,1,0:T(8,128)(2,1)S(1)}, u32[]{:S(2)}, u32[]{:S(2)}) collective-permute-start(bf16[2,32,5376]{2,1,0:T(8,128)(2,1)S(1)} %collective-permute-done.3.refs_0_), channel_id=1, source_target_pairs={{0,4},{4,0},{8,12},{12,8},{16,20},{20,16},{24,28},{28,24},{32,36},... | collective-permute-start | bytes 2064392 | tf_op jit(solution)/shard_map/ppermute | solution.py:29
  36.9 3.3 %collective-permute-start.9 = (bf16[2,32,5376]{2,1,0:T(8,128)(2,1)S(1)}, bf16[2,32,5376]{2,1,0:T(8,128)(2,1)S(1)}, u32[]{:S(2)}, u32[]{:S(2)}) collective-permute-start(bf16[2,32,5376]{2,1,0:T(8,128)(2,1)S(1)} %collective-permute-done.4.refs_1_), channel_id=1, source_target_pairs={{0,4},{4,0},{8,12},{12,8},{16,20},{20,16},{24,28},{28,24},{32,36},... | collective-permute-start | bytes 2064392 | tf_op jit(solution)/shard_map/ppermute | solution.py:29
  37.0 12.2 %copy-start.6 = (s32[2,128]{1,0:T(2,128)S(1)}, s32[2,128]{1,0:T(2,128)}, u32[]{:S(2)}) copy-start(s32[2,128]{1,0:T(2,128)} %param.11) | copy-start | bytes 3076
  37.0 7.5 %collective-permute-start.12 = (bf16[2,256,256]{2,1,0:T(8,128)(2,1)S(1)}, bf16[2,256,256]{2,1,0:T(8,128)(2,1)S(1)}, u32[]{:S(2)}, u32[]{:S(2)}) collective-permute-start(bf16[2,256,256]{2,1,0:T(8,128)(2,1)S(1)} %broadcast_select_fusion), channel_id=1, source_target_pairs={{0,24},{4,28},{8,0},{12,4},{16,8},{20,12},{24,16},{28,20},{32,56},... | collective-permute-start | bytes 786440 | tf_op jit(solution)/shard_map/ppermute | solution.py:29
  37.1 11.0 %collective-permute-start.10 = (bf16[1,32,5376]{2,1,0:T(8,128)(2,1)S(1)}, bf16[1,32,5376]{2,1,0:T(8,128)(2,1)S(1)}, u32[]{:S(2)}, u32[]{:S(2)}) collective-permute-start(bf16[1,32,5376]{2,1,0:T(8,128)(2,1)S(1)} %slice.40), channel_id=1, source_target_pairs={{0,1},{1,2},{2,3},{3,0},{4,5},{5,6},{6,7},{7,4},{8,9},{9,10},{10,1... | collective-permute-start | bytes 1032200 | tf_op jit(solution)/shard_map/ppermute | solution.py:70
  37.7 10.5 %collective-permute-start.11 = (bf16[1,32,5376]{2,1,0:T(8,128)(2,1)S(1)}, bf16[1,32,5376]{2,1,0:T(8,128)(2,1)S(1)}, u32[]{:S(2)}, u32[]{:S(2)}) collective-permute-start(bf16[1,32,5376]{2,1,0:T(8,128)(2,1)S(1)} %slice.41), channel_id=1, source_target_pairs={{0,3},{1,0},{2,1},{3,2},{4,7},{5,4},{6,5},{7,6},{8,11},{9,8},{10,9... | collective-permute-start | bytes 1032200 | tf_op jit(solution)/shard_map/ppermute | solution.py:70
  48.1 5.3 %collective-permute-start.13 = (bf16[1,32,5376]{2,1,0:T(8,128)(2,1)S(1)}, bf16[1,32,5376]{2,1,0:T(8,128)(2,1)S(1)}, u32[]{:S(2)}, u32[]{:S(2)}) collective-permute-start(bf16[1,32,5376]{2,1,0:T(8,128)(2,1)S(1)} %collective-permute-done.10.r2a), channel_id=1, source_target_pairs={{0,4},{4,0},{8,12},{12,8},{16,20},{20,16},{24,28},{28,24},{32,36},... | collective-permute-start | bytes 1032200 | tf_op jit(solution)/shard_map/ppermute | solution.py:29
  49.2 4.3 %collective-permute-start.14 = (bf16[1,32,5376]{2,1,0:T(8,128)(2,1)S(1)}, bf16[1,32,5376]{2,1,0:T(8,128)(2,1)S(1)}, u32[]{:S(2)}, u32[]{:S(2)}) collective-permute-start(bf16[1,32,5376]{2,1,0:T(8,128)(2,1)S(1)} %collective-permute-done.11.r2b), channel_id=1, source_target_pairs={{0,4},{4,0},{8,12},{12,8},{16,20},{20,16},{24,28},{28,24},{32,36},... | collective-permute-start | bytes 1032200 | tf_op jit(solution)/shard_map/ppermute | solution.py:29
  57.5 30.1 %collective-permute-start.16 = (bf16[2,4,168,256]{3,2,1,0:T(8,128)(2,1)S(1)}, bf16[2,4,168,256]{3,2,1,0:T(8,128)(2,1)S(1)}, u32[]{:S(2)}, u32[]{:S(2)}) collective-permute-start(bf16[2,4,168,256]{3,2,1,0:T(8,128)(2,1)S(1)} %get-tuple-element.78), channel_id=1, source_target_pairs={{0,8},{4,12},{8,0},{12,4},{16,24},{20,28},{24,16},{28,20},{32,40},... | collective-permute-start | bytes 2064392 | tf_op jit(solution)/shard_map/ppermute | solution.py:29
  59.0 28.6 %collective-permute-start.17 = (bf16[2,4,168,256]{3,2,1,0:T(8,128)(2,1)S(1)}, bf16[2,4,168,256]{3,2,1,0:T(8,128)(2,1)S(1)}, u32[]{:S(2)}, u32[]{:S(2)}) collective-permute-start(bf16[2,4,168,256]{3,2,1,0:T(8,128)(2,1)S(1)} %get-tuple-element.79), channel_id=1, source_target_pairs={{0,24},{4,28},{8,16},{12,20},{16,8},{20,12},{24,0},{28,4},{32,56},... | collective-permute-start | bytes 2064392 | tf_op jit(solution)/shard_map/ppermute | solution.py:29
  62.8 22.5 %collective-permute-start.18 = (bf16[2,256,256]{2,1,0:T(8,128)(2,1)S(1)}, bf16[2,256,256]{2,1,0:T(8,128)(2,1)S(1)}, u32[]{:S(2)}, u32[]{:S(2)}) collective-permute-start(bf16[2,256,256]{2,1,0:T(8,128)(2,1)S(1)} %get-tuple-element.81), channel_id=1, source_target_pairs={{0,248},{4,252},{8,0},{12,4},{16,8},{20,12},{24,16},{28,20},{32,24... | collective-permute-start | bytes 786440 | tf_op jit(solution)/shard_map/ppermute | solution.py:29
  66.7 18.6 %collective-permute-start.19 = (bf16[2,256,256]{2,1,0:T(8,128)(2,1)S(1)}, bf16[2,256,256]{2,1,0:T(8,128)(2,1)S(1)}, u32[]{:S(2)}, u32[]{:S(2)}) collective-permute-start(bf16[2,256,256]{2,1,0:T(8,128)(2,1)S(1)} %get-tuple-element.82), channel_id=1, source_target_pairs={{0,240},{4,244},{8,248},{12,252},{16,0},{20,4},{24,8},{28,12},{32,... | collective-permute-start | bytes 786440 | tf_op jit(solution)/shard_map/ppermute | solution.py:29
  66.7 20.9 %collective-permute-start.20 = (bf16[2,256,256]{2,1,0:T(8,128)(2,1)S(1)}, bf16[2,256,256]{2,1,0:T(8,128)(2,1)S(1)}, u32[]{:S(2)}, u32[]{:S(2)}) collective-permute-start(bf16[2,256,256]{2,1,0:T(8,128)(2,1)S(1)} %get-tuple-element.83), channel_id=1, source_target_pairs={{0,232},{4,236},{8,240},{12,244},{16,248},{20,252},{24,0},{28,4},{... | collective-permute-start | bytes 786440 | tf_op jit(solution)/shard_map/ppermute | solution.py:29
  87.7 8.8 %collective-permute-start.22 = (bf16[4,168,256]{2,1,0:T(8,128)(2,1)S(1)}, bf16[4,168,256]{2,1,0:T(8,128)(2,1)S(1)}, u32[]{:S(2)}, u32[]{:S(2)}) collective-permute-start(bf16[4,168,256]{2,1,0:T(8,128)(2,1)S(1)} %fusion.1), channel_id=1, source_target_pairs={{0,8},{4,12},{8,0},{12,4},{16,24},{20,28},{24,16},{28,20},{32,40},... | collective-permute-start | bytes 1032200 | tf_op jit(solution)/shard_map/ppermute | solution.py:29
  90.2 8.6 %collective-permute-start.21 = (bf16[4,168,256]{2,1,0:T(8,128)(2,1)S(1)}, bf16[4,168,256]{2,1,0:T(8,128)(2,1)S(1)}, u32[]{:S(2)}, u32[]{:S(2)}) collective-permute-start(bf16[4,168,256]{2,1,0:T(8,128)(2,1)S(1)} %fusion), channel_id=1, source_target_pairs={{0,24},{4,28},{8,16},{12,20},{16,8},{20,12},{24,0},{28,4},{32,56},... | collective-permute-start | bytes 1032200 | tf_op jit(solution)/shard_map/ppermute | solution.py:29
  90.3 5.6 %collective-permute-start.23 = (bf16[2,256,256]{2,1,0:T(8,128)(2,1)S(1)}, bf16[2,256,256]{2,1,0:T(8,128)(2,1)S(1)}, u32[]{:S(2)}, u32[]{:S(2)}) collective-permute-start(bf16[2,256,256]{2,1,0:T(8,128)(2,1)S(1)} %get-tuple-element.92), channel_id=1, source_target_pairs={{0,224},{4,228},{8,232},{12,236},{16,240},{20,244},{24,248},{28,25... | collective-permute-start | bytes 786440 | tf_op jit(solution)/shard_map/ppermute | solution.py:29
  99.9 30.2 %all-to-all-start = ((bf16[16,84,256]{2,1,0:T(8,128)(2,1)}), bf16[16,84,256]{2,1,0:T(8,128)(2,1)S(1)}, u32[]{:S(2)}, u32[]{:S(2)}) async-start(bf16[16,84,256]{2,1,0:T(8,128)(2,1)} %projection_merge.1), calls=%async_computation | async-start | bytes 1441792 | tf_op jit(solution)/shard_map/all_to_all | solution.py:57
  108.8 1.3 %collective-permute-start.15 = (bf16[2,128,256]{2,1,0:T(8,128)(2,1)S(1)}, bf16[2,128,256]{2,1,0:T(8,128)(2,1)S(1)}, u32[]{:S(2)}, u32[]{:S(2)}) collective-permute-start(bf16[2,128,256]{2,1,0:T(8,128)(2,1)S(1)} %get-tuple-element.77), channel_id=1, source_target_pairs={{0,4},{4,0},{8,12},{12,8},{16,20},{20,16},{24,28},{28,24},{32,36},... | collective-permute-start | bytes 393224 | tf_op jit(solution)/shard_map/ppermute | solution.py:29
  109.2 1.7 %collective-permute-start.24 = (bf16[2,128,256]{2,1,0:T(8,128)(2,1)S(1)}, bf16[2,128,256]{2,1,0:T(8,128)(2,1)S(1)}, u32[]{:S(2)}, u32[]{:S(2)}) collective-permute-start(bf16[2,128,256]{2,1,0:T(8,128)(2,1)S(1)} %slice.52), channel_id=1, source_target_pairs={{0,4},{4,0},{8,12},{12,8},{16,20},{20,16},{24,28},{28,24},{32,36},... | collective-permute-start | bytes 393224 | tf_op jit(solution)/shard_map/ppermute | solution.py:29

commit v11 on v8

--- a/solution.py
+++ b/solution.py
@@ -516,8 +516,10 @@
         q_mine, recv, kvs, weights, attn, d_attn
     )
     *g_near, g_far = (chips_ahead(g, -d) for d, g in enumerate(g_sent, 1))
-    got_a, got_b, g_own, *g_near = lax.optimization_barrier((got_a, got_b, g_own, *g_near))
     dq_recv = to_sibling(dq_other)
+    got_a, got_b, g_own, g_far, dq_recv, *g_near = lax.optimization_barrier(
+        (got_a, got_b, g_own, g_far, dq_recv, *g_near)
+    )
 
     def added(*blocks):
         total = blocks[0].astype(jnp.float32)
@@ -529,7 +531,6 @@
     next_b = added(kept_b[1], got_b[1]).astype(jnp.bfloat16)
     last_a = y_route(next_a, y_mirror)
     last_b = y_route(next_b, y_pair)
-    last_a, last_b, g_far = lax.optimization_barrier((last_a, last_b, g_far))
     w_sum = merge(kept_a, got_a, last_a, kept_b, got_b, last_b)
     w_all = z_exchange(w_sum)
 

time: 130 us -> 135 us (1.038)
  waiting for transfers between devices: 56.2 us -> 62.1 us
    ppermute x21, waiting for transfers between devices: 31.9 us -> 37.2 us  [ctx_shift(): return lax.ppermute(block, 'ctx', [(i, move(i)) for i in range(count)])]
    all_to_all x1, starting transfers between devices: 11.1 us -> 6.68 us  [z_exchange(): lax.all_to_all(blocks, 'ctx', 0, 0, axis_index_groups=groups, tiled=True)]
    ppermute x21, starting transfers between devices: 26.6 us -> 29.9 us  [ctx_shift(): return lax.ppermute(block, 'ctx', [(i, move(i)) for i in range(count)])]
  transfers between devices with their start and end apart: 26 -> 26, of which waited for: 12 -> 13; matrix products, arithmetic and copies ran while one was open for 2% -> 1% of each run, Pallas kernels for 12% -> 12%
where the time goes in v11:
time: 135 us; the launch traced here: 134 us
  waiting for transfers between devices  62.1 us (46%)
  starting transfers between devices  40.7 us (30%)
  Pallas kernels  22.2 us (16%)
  local copies, waits for them, and re-layouts  6.5 us (5%)
  other arithmetic  2.02 us (1%)
    ppermute x21, waiting for transfers between devices, ctx_shift(): return lax.ppermute(block, 'ctx', [(i, move(i)) for i in range(count)])  37.2 us
    ppermute x21, starting transfers between devices, ctx_shift(): return lax.ppermute(block, 'ctx', [(i, move(i)) for i in range(count)])  29.9 us
    all_to_all x1, waiting for transfers between devices, z_exchange(): lax.all_to_all(blocks, 'ctx', 0, 0, axis_index_groups=groups, tiled=True)  19 us
    pallas_call x2, Pallas kernels, early_projection(): pl.pallas_call(early_kernel, out_shape=outs, grid_spec=pltpu.PrefetchScal...  7.51 us
    all_to_all x1, starting transfers between devices, z_exchange(): lax.all_to_all(blocks, 'ctx', 0, 0, axis_index_groups=groups, tiled=True)  6.68 us
    unnamed x14, local copies, waits for them, and re-layouts  6.43 us
    ppermute x4, waiting for transfers between devices, tp_ahead(): lax.ppermute(block, 'tp', [(i, (i + distance) % TP) for i in range(TP)])  5.87 us
    pallas_call x1, Pallas kernels, forward(): pl.pallas_call(forward_kernel, out_shape=outs, grid_spec=pltpu.PrefetchSc...  4.23 us
  transfers between devices with their start and end apart: 26, of which 13 were waited for; matrix products, arithmetic and copies ran while one was open for 1% of the time, Pallas kernels for 12%

profile of v11, /device:TPU:1, one launch (start us, length us, event | category | flops | bytes accessed | tf_op | source)
XLA Modules:
  0.0 134.4 jit_solution(14705571514490857890)
XLA Ops:
  0.6 3.3 %collective-permute-start.2 = (bf16[2,32,5376]{2,1,0:T(8,128)(2,1)}, bf16[2,32,5376]{2,1,0:T(8,128)(2,1)S(1)}, u32[]{:S(2)}, u32[]{:S(2)}) collective-permute-start(bf16[2,32,5376]{2,1,0:T(8,128)(2,1)} %refs_0_.1), channel_id=1, source_target_pairs={{0,4},{4,0},{8,12},{12,8},{16,20},{20,16},{24,28},{28,24},{32,36},... | collective-permute-start | bytes 2064392 | tf_op jit(solution)/shard_map/ppermute | solution.py:29
  4.0 0.9 copy-done.2
  5.0 0.9 copy-done.3
  5.9 0.9 copy-done.4
  6.8 0.7 split_heads.1
  7.6 0.5 collective-permute-start.1
  8.1 0.8 collective-permute-start.3
  8.8 0.7 collective-permute-start.4
  9.6 1.0 collective-permute-start.6
  10.6 1.3 collective-permute-start.5
  11.9 2.6 %copy-done = bf16[5376,512]{1,0:T(8,128)(2,1)S(1)} copy-done((bf16[5376,512]{1,0:T(8,128)(2,1)S(1)}, bf16[5376,512]{1,0:T(8,128)(2,1)}, u32[]{:S(2)}) %copy-start) | copy-done | bytes 5505048
  14.5 1.1 copy-done.5
  15.6 3.3 %projection_early.2 = (bf16[128,256]{1,0:T(8,128)(2,1)S(1)}, bf16[5376,128]{1,0:T(8,128)(2,1)S(1)}) custom-call(s32[4]{0:T(128)S(1)} %pad_add_fusion.scalars, bf16[2,32,5376]{2,1,0:T(8,128)(2,1)S(1)} %copy-done.5, bf16[2,32,5376]{2,1,0:T(8,128)(2,1)S(1)} %collective-permute-done.2.refs_1_, bf16[5376,512]{1,0:T(8,128)(2,1)S(1)} %copy-done), custom_call_target="tpu_custom_call" | custom-call | flops 3523215360 | bytes 12582912 | tf_op jit(solution)/shard_map/projection_early/pallas_call | solution.py:380
  18.9 2.1 %collective-permute-done.6.kv4 = bf16[2,256,256]{2,1,0:T(8,128)(2,1)S(1)} collective-permute-done((bf16[2,256,256]{2,1,0:T(8,128)(2,1)S(1)}, bf16[2,256,256]{2,1,0:T(8,128)(2,1)S(1)}, u32[]{:S(2)}, u32[]{:S(2)}) %collective-permute-start.6) | collective-permute-done | bytes 262176 | tf_op jit(solution)/shard_map/ppermute | solution.py:29
  21.0 4.2 %collective-permute-done.3.refs_0_ = bf16[2,32,5376]{2,1,0:T(8,128)(2,1)S(1)} collective-permute-done((bf16[2,32,5376]{2,1,0:T(8,128)(2,1)}, bf16[2,32,5376]{2,1,0:T(8,128)(2,1)S(1)}, u32[]{:S(2)}, u32[]{:S(2)}) %collective-permute-start.3) | collective-permute-done | bytes 688160 | tf_op jit(solution)/shard_map/ppermute | solution.py:70
  25.3 1.6 %collective-permute-done.4.refs_1_ = bf16[2,32,5376]{2,1,0:T(8,128)(2,1)S(1)} collective-permute-done((bf16[2,32,5376]{2,1,0:T(8,128)(2,1)}, bf16[2,32,5376]{2,1,0:T(8,128)(2,1)S(1)}, u32[]{:S(2)}, u32[]{:S(2)}) %collective-permute-start.4) | collective-permute-done | bytes 688160 | tf_op jit(solution)/shard_map/ppermute | solution.py:70
  26.9 2.1 %collective-permute-done.5.kv1 = bf16[2,256,256]{2,1,0:T(8,128)(2,1)S(1)} collective-permute-done((bf16[2,256,256]{2,1,0:T(8,128)(2,1)S(1)}, bf16[2,256,256]{2,1,0:T(8,128)(2,1)S(1)}, u32[]{:S(2)}, u32[]{:S(2)}) %collective-permute-start.5) | collective-permute-done | bytes 262176 | tf_op jit(solution)/shard_map/ppermute | solution.py:29
  29.0 0.9 collective-permute-start.7
  29.9 1.2 collective-permute-start.11
  31.2 0.8 collective-permute-start.12
  31.9 2.7 %collective-permute-start.10 = (bf16[1,32,5376]{2,1,0:T(8,128)(2,1)S(1)}, bf16[1,32,5376]{2,1,0:T(8,128)(2,1)S(1)}, u32[]{:S(2)}, u32[]{:S(2)}) collective-permute-start(bf16[1,32,5376]{2,1,0:T(8,128)(2,1)S(1)} %slice.41), channel_id=1, source_target_pairs={{0,3},{1,0},{2,1},{3,2},{4,7},{5,4},{6,5},{7,6},{8,11},{9,8},{10,9... | collective-permute-start | bytes 1032200 | tf_op jit(solution)/shard_map/ppermute | solution.py:70
  34.6 4.2 %projection_early.3 = (bf16[256,256]{1,0:T(8,128)(2,1)S(1)}, bf16[5376,256]{1,0:T(8,128)(2,1)S(1)}) custom-call(s32[4]{0:T(128)S(1)} %pad_add_fusion.scalars, bf16[2,32,5376]{2,1,0:T(8,128)(2,1)S(1)} %collective-permute-done.3.refs_0_, bf16[2,32,5376]{2,1,0:T(8,128)(2,1)S(1)} %collective-permute-done.4.refs_1_, ...), custom_call_target="tpu_custom_call" | custom-call | flops 7046430720 | bytes 12582912 | tf_op jit(solution)/shard_map/projection_early/pallas_call | solution.py:380
  38.9 4.2 %collective-permute-done.12.kv3 = bf16[2,256,256]{2,1,0:T(8,128)(2,1)S(1)} collective-permute-done((bf16[2,256,256]{2,1,0:T(8,128)(2,1)S(1)}, bf16[2,256,256]{2,1,0:T(8,128)(2,1)S(1)}, u32[]{:S(2)}, u32[]{:S(2)}) %collective-permute-start.12) | collective-permute-done | bytes 262176 | tf_op jit(solution)/shard_map/ppermute | solution.py:29
  43.1 1.4 %collective-permute-start.13 = (bf16[1,32,5376]{2,1,0:T(8,128)(2,1)S(1)}, bf16[1,32,5376]{2,1,0:T(8,128)(2,1)S(1)}, u32[]{:S(2)}, u32[]{:S(2)}) collective-permute-start(bf16[1,32,5376]{2,1,0:T(8,128)(2,1)S(1)} %collective-permute-done.9.r2a), channel_id=1, source_target_pairs={{0,4},{4,0},{8,12},{12,8},{16,20},{20,16},{24,28},{28,24},{32,36},... | collective-permute-start | bytes 1032200 | tf_op jit(solution)/shard_map/ppermute | solution.py:29
  44.8 4.2 %attention_forward.1 = (bf16[2,256,256]{2,1,0:T(8,128)(2,1)S(1)}, bf16[2,2,1280,256]{3,2,1,0:T(8,128)(2,1)S(1)}) custom-call(s32[4]{0:T(128)S(1)} %pad_add_fusion.scalars, bf16[2,128,256]{2,1,0:T(8,128)(2,1)S(1)} %get-tuple-element.53.mine, bf16[2,128,512]{2,1,0:T(8,128)(2,1)S(1)} %collective-permute-done.recv, ...), custom_call_target="tpu_custom_call" | custom-call | flops 671088640 | bytes 8388608 | tf_op jit(solution)/shard_map/attention_forward/pallas_call | solution.py:349
  49.0 4.1 %projection_late.1 = (bf16[2,256,256]{2,1,0:T(8,128)(2,1)S(1)}, bf16[2,4,168,256]{3,2,1,0:T(8,128)(2,1)S(1)}, bf16[2,4,168,256]{3,2,1,0:T(8,128)(2,1)S(1)}, bf16...) custom-call(s32[4]{0:T(128)S(1)} %pad_add_fusion.scalars, ...), custom_call_target="tpu_custom_call" | custom-call | flops 2113929216 | bytes 12582912 | tf_op jit(solution)/shard_map/projection_late/pallas_call | solution.py:414
  53.2 1.0 collective-permute-start.15
  54.2 1.5 %collective-permute-start.16 = (bf16[2,4,168,256]{3,2,1,0:T(8,128)(2,1)S(1)}, bf16[2,4,168,256]{3,2,1,0:T(8,128)(2,1)S(1)}, u32[]{:S(2)}, u32[]{:S(2)}) collective-permute-start(bf16[2,4,168,256]{3,2,1,0:T(8,128)(2,1)S(1)} %get-tuple-element.81), channel_id=1, source_target_pairs={{0,24},{4,28},{8,16},{12,20},{16,8},{20,12},{24,0},{28,4},{32,56},... | collective-permute-start | bytes 2064392 | tf_op jit(solution)/shard_map/ppermute | solution.py:29
  55.7 3.8 %attention_backward.1 = (bf16[2,128,256]{2,1,0:T(8,128)(2,1)S(1)}, bf16[2,128,256]{2,1,0:T(8,128)(2,1)S(1)}, f32[2,256,256]{2,1,0:T(8,128)S(1)}, bf16[2,256,256]...) custom-call(bf16[2,128,256]{2,1,0:T(8,128)(2,1)S(1)} %get-tuple-elem, ...), custom_call_target="tpu_custom_call" | custom-call | flops 1677721600 | bytes 8388608 | tf_op jit(solution)/shard_map/attention_backward/pallas_call | solution.py:450
  59.5 5.7 %collective-permute-start.17 = (bf16[2,256,256]{2,1,0:T(8,128)(2,1)S(1)}, bf16[2,256,256]{2,1,0:T(8,128)(2,1)S(1)}, u32[]{:S(2)}, u32[]{:S(2)}) collective-permute-start(bf16[2,256,256]{2,1,0:T(8,128)(2,1)S(1)} %get-tuple-element.83), channel_id=1, source_target_pairs={{0,224},{4,228},{8,232},{12,236},{16,240},{20,244},{24,248},{28,25... | collective-permute-start | bytes 786440 | tf_op jit(solution)/shard_map/ppermute | solution.py:29
  65.1 0.8 collective-permute-start.18
  65.9 1.9 %collective-permute-start.19 = (bf16[2,256,256]{2,1,0:T(8,128)(2,1)S(1)}, bf16[2,256,256]{2,1,0:T(8,128)(2,1)S(1)}, u32[]{:S(2)}, u32[]{:S(2)}) collective-permute-start(bf16[2,256,256]{2,1,0:T(8,128)(2,1)S(1)} %get-tuple-element.85), channel_id=1, source_target_pairs={{0,248},{4,252},{8,0},{12,4},{16,8},{20,12},{24,16},{28,20},{32,24... | collective-permute-start | bytes 786440 | tf_op jit(solution)/shard_map/ppermute | solution.py:29
  67.8 1.4 %collective-permute-start.20 = (bf16[2,256,256]{2,1,0:T(8,128)(2,1)S(1)}, bf16[2,256,256]{2,1,0:T(8,128)(2,1)S(1)}, u32[]{:S(2)}, u32[]{:S(2)}) collective-permute-start(bf16[2,256,256]{2,1,0:T(8,128)(2,1)S(1)} %get-tuple-element.86), channel_id=1, source_target_pairs={{0,240},{4,244},{8,248},{12,252},{16,0},{20,4},{24,8},{28,12},{32,... | collective-permute-start | bytes 786440 | tf_op jit(solution)/shard_map/ppermute | solution.py:29
  69.2 1.1 collective-permute-done.17
  70.3 3.6 %collective-permute-start.21 = (bf16[2,256,256]{2,1,0:T(8,128)(2,1)S(1)}, bf16[2,256,256]{2,1,0:T(8,128)(2,1)S(1)}, u32[]{:S(2)}, u32[]{:S(2)}) collective-permute-start(bf16[2,256,256]{2,1,0:T(8,128)(2,1)S(1)} %get-tuple-element.87), channel_id=1, source_target_pairs={{0,232},{4,236},{8,240},{12,244},{16,248},{20,252},{24,0},{28,4},{... | collective-permute-start | bytes 786440 | tf_op jit(solution)/shard_map/ppermute | solution.py:29
  73.9 7.4 %collective-permute-done.19 = bf16[2,256,256]{2,1,0:T(8,128)(2,1)S(1)} collective-permute-done((bf16[2,256,256]{2,1,0:T(8,128)(2,1)S(1)}, bf16[2,256,256]{2,1,0:T(8,128)(2,1)S(1)}, u32[]{:S(2)}, u32[]{:S(2)}) %collective-permute-start.19) | collective-permute-done | bytes 262176 | tf_op jit(solution)/shard_map/ppermute | solution.py:29
  81.3 2.1 %collective-permute-done.20 = bf16[2,256,256]{2,1,0:T(8,128)(2,1)S(1)} collective-permute-done((bf16[2,256,256]{2,1,0:T(8,128)(2,1)S(1)}, bf16[2,256,256]{2,1,0:T(8,128)(2,1)S(1)}, u32[]{:S(2)}, u32[]{:S(2)}) %collective-permute-start.20) | collective-permute-done | bytes 262176 | tf_op jit(solution)/shard_map/ppermute | solution.py:29
  83.4 8.0 %collective-permute-done.21 = bf16[2,256,256]{2,1,0:T(8,128)(2,1)S(1)} collective-permute-done((bf16[2,256,256]{2,1,0:T(8,128)(2,1)S(1)}, bf16[2,256,256]{2,1,0:T(8,128)(2,1)S(1)}, u32[]{:S(2)}, u32[]{:S(2)}) %collective-permute-start.21) | collective-permute-done | bytes 262176 | tf_op jit(solution)/shard_map/ppermute | solution.py:29
  91.5 3.1 %collective-permute-start.24 = (bf16[4,168,256]{2,1,0:T(8,128)(2,1)S(1)}, bf16[4,168,256]{2,1,0:T(8,128)(2,1)S(1)}, u32[]{:S(2)}, u32[]{:S(2)}) collective-permute-start(bf16[4,168,256]{2,1,0:T(8,128)(2,1)S(1)} %fusion.1), channel_id=1, source_target_pairs={{0,8},{4,12},{8,0},{12,4},{16,24},{20,28},{24,16},{28,20},{32,40},... | collective-permute-start | bytes 1032200 | tf_op jit(solution)/shard_map/ppermute | solution.py:29
  94.8 7.4 %collective-permute-done.24.last_b = bf16[4,168,256]{2,1,0:T(8,128)(2,1)S(1)} collective-permute-done((bf16[4,168,256]{2,1,0:T(8,128)(2,1)S(1)}, bf16[4,168,256]{2,1,0:T(8,128)(2,1)S(1)}, u32[]{:S(2)}, u32[]{:S(2)}) %collective-permute-start.24) | collective-permute-done | bytes 344096 | tf_op jit(solution)/shard_map/ppermute | solution.py:29
  102.2 2.2 %collective-permute-done.23.last_a = bf16[4,168,256]{2,1,0:T(8,128)(2,1)S(1)} collective-permute-done((bf16[4,168,256]{2,1,0:T(8,128)(2,1)S(1)}, bf16[4,168,256]{2,1,0:T(8,128)(2,1)S(1)}, u32[]{:S(2)}, u32[]{:S(2)}) %collective-permute-start.23) | collective-permute-done | bytes 344096 | tf_op jit(solution)/shard_map/ppermute | solution.py:29
  104.4 1.2 projection_merge.1
  105.6 6.7 %all-to-all-start = ((bf16[16,84,256]{2,1,0:T(8,128)(2,1)}), bf16[16,84,256]{2,1,0:T(8,128)(2,1)S(1)}, u32[]{:S(2)}, u32[]{:S(2)}) async-start(bf16[16,84,256]{2,1,0:T(8,128)(2,1)} %projection_merge.1), calls=%async_computation | async-start | bytes 1441792 | tf_op jit(solution)/shard_map/all_to_all | solution.py:57
  112.7 0.7 pad_maximum_fusion.1
  113.4 0.5 collective-permute-done.22
  113.9 0.7 pad_maximum_fusion.2
  114.6 19.0 %all-to-all-done.blocks = bf16[16,84,256]{2,1,0:T(8,128)(2,1)S(1)} async-done(((bf16[16,84,256]{2,1,0:T(8,128)(2,1)}), bf16[16,84,256]{2,1,0:T(8,128)(2,1)S(1)}, u32[]{:S(2)}, u32[]{:S(2)}) %all-to-all-start) | async-done | bytes 688160 | tf_op jit(solution)/shard_map/all_to_all | solution.py:57
  133.6 0.8 projection_finish.1
  (40 shorter events, 1.4 us)
Async XLA Ops:
  0.6 8.9 %collective-permute-start.2 = (bf16[2,32,5376]{2,1,0:T(8,128)(2,1)}, bf16[2,32,5376]{2,1,0:T(8,128)(2,1)S(1)}, u32[]{:S(2)}, u32[]{:S(2)}) collective-permute-start(bf16[2,32,5376]{2,1,0:T(8,128)(2,1)} %refs_0_.1), channel_id=1, source_target_pairs={{0,4},{4,0},{8,12},{12,8},{16,20},{20,16},{24,28},{28,24},{32,36},... | collective-permute-start | bytes 2064392 | tf_op jit(solution)/shard_map/ppermute | solution.py:29
  4.0 1.0 copy-start.2
  5.0 0.9 copy-start.3
  5.9 0.9 copy-start.4
  7.5 2.1 %collective-permute-start = (bf16[2,128,512]{2,1,0:T(8,128)(2,1)S(1)}, bf16[2,128,512]{2,1,0:T(8,128)(2,1)S(1)}, u32[]{:S(2)}, u32[]{:S(2)}) collective-permute-start(bf16[2,128,512]{2,1,0:T(8,128)(2,1)S(1)} %get-tuple-element.51), channel_id=1, source_target_pairs={{0,4},{4,0},{8,12},{12,8},{16,20},{20,16},{24,28},{28,24},{32,36},... | collective-permute-start | bytes 786440 | tf_op jit(solution)/shard_map/ppermute | solution.py:29
  7.6 1.9 %collective-permute-start.1 = (s32[2,1,128]{2,1,0:T(1,128)}, s32[2,1,128]{2,1,0:T(1,128)S(1)}, u32[]{:S(2)}, u32[]{:S(2)}) collective-permute-start(s32[2,1,128]{2,1,0:T(1,128)} %bitcast.9), channel_id=1, source_target_pairs={{0,4},{4,0},{8,12},{12,8},{16,20},{20,16},{24,28},{28,24},{32,36},... | collective-permute-start | bytes 3080 | tf_op jit(solution)/shard_map/ppermute | solution.py:29
  8.1 17.2 %collective-permute-start.3 = (bf16[2,32,5376]{2,1,0:T(8,128)(2,1)}, bf16[2,32,5376]{2,1,0:T(8,128)(2,1)S(1)}, u32[]{:S(2)}, u32[]{:S(2)}) collective-permute-start(bf16[2,32,5376]{2,1,0:T(8,128)(2,1)} %refs_0_.1), channel_id=1, source_target_pairs={{0,3},{1,0},{2,1},{3,2},{4,7},{5,4},{6,5},{7,6},{8,11},{9,8},{10,9... | collective-permute-start | bytes 2064392 | tf_op jit(solution)/shard_map/ppermute | solution.py:70
  8.8 18.1 %collective-permute-start.4 = (bf16[2,32,5376]{2,1,0:T(8,128)(2,1)}, bf16[2,32,5376]{2,1,0:T(8,128)(2,1)S(1)}, u32[]{:S(2)}, u32[]{:S(2)}) collective-permute-start(bf16[2,32,5376]{2,1,0:T(8,128)(2,1)} %refs_0_.1), channel_id=1, source_target_pairs={{0,1},{1,2},{2,3},{3,0},{4,5},{5,6},{6,7},{7,4},{8,9},{9,10},{10,1... | collective-permute-start | bytes 2064392 | tf_op jit(solution)/shard_map/ppermute | solution.py:70
  9.6 11.3 %collective-permute-start.6 = (bf16[2,256,256]{2,1,0:T(8,128)(2,1)S(1)}, bf16[2,256,256]{2,1,0:T(8,128)(2,1)S(1)}, u32[]{:S(2)}, u32[]{:S(2)}) collective-permute-start(bf16[2,256,256]{2,1,0:T(8,128)(2,1)S(1)} %pad_maximum_fusion.kv0), channel_id=1, source_target_pairs={{0,32},{4,36},{8,40},{12,44},{16,48},{20,52},{24,56},{28,60},{32,6... | collective-permute-start | bytes 786440 | tf_op jit(solution)/shard_map/ppermute | solution.py:29
  10.6 18.4 %collective-permute-start.5 = (bf16[2,256,256]{2,1,0:T(8,128)(2,1)S(1)}, bf16[2,256,256]{2,1,0:T(8,128)(2,1)S(1)}, u32[]{:S(2)}, u32[]{:S(2)}) collective-permute-start(bf16[2,256,256]{2,1,0:T(8,128)(2,1)S(1)} %pad_maximum_fusion.kv0), channel_id=1, source_target_pairs={{0,8},{4,12},{8,16},{12,20},{16,24},{20,28},{24,32},{28,36},{32,40... | collective-permute-start | bytes 786440 | tf_op jit(solution)/shard_map/ppermute | solution.py:29
  11.9 2.6 %copy-start = (bf16[5376,512]{1,0:T(8,128)(2,1)S(1)}, bf16[5376,512]{1,0:T(8,128)(2,1)}, u32[]{:S(2)}) copy-start(bf16[5376,512]{1,0:T(8,128)(2,1)} %o_weight.1) | copy-start | bytes 16515076
  14.5 1.1 copy-start.5
  15.6 19.1 %copy-start.1 = (bf16[5376,512]{1,0:T(8,128)(2,1)S(1)}, bf16[5376,512]{1,0:T(8,128)(2,1)}, u32[]{:S(2)}) copy-start(bf16[5376,512]{1,0:T(8,128)(2,1)} %o_weight.1) | copy-start | bytes 16515076
  29.0 3.0 %collective-permute-start.7 = (bf16[2,32,5376]{2,1,0:T(8,128)(2,1)S(1)}, bf16[2,32,5376]{2,1,0:T(8,128)(2,1)S(1)}, u32[]{:S(2)}, u32[]{:S(2)}) collective-permute-start(bf16[2,32,5376]{2,1,0:T(8,128)(2,1)S(1)} %collective-permute-done.3.refs_0_), channel_id=1, source_target_pairs={{0,4},{4,0},{8,12},{12,8},{16,20},{20,16},{24,28},{28,24},{32,36},... | collective-permute-start | bytes 2064392 | tf_op jit(solution)/shard_map/ppermute | solution.py:29
  29.9 4.8 %collective-permute-start.8 = (bf16[2,32,5376]{2,1,0:T(8,128)(2,1)S(1)}, bf16[2,32,5376]{2,1,0:T(8,128)(2,1)S(1)}, u32[]{:S(2)}, u32[]{:S(2)}) collective-permute-start(bf16[2,32,5376]{2,1,0:T(8,128)(2,1)S(1)} %collective-permute-done.4.refs_1_), channel_id=1, source_target_pairs={{0,4},{4,0},{8,12},{12,8},{16,20},{20,16},{24,28},{28,24},{32,36},... | collective-permute-start | bytes 2064392 | tf_op jit(solution)/shard_map/ppermute | solution.py:29
  29.9 14.8 %copy-start.6 = (s32[2,128]{1,0:T(2,128)S(1)}, s32[2,128]{1,0:T(2,128)}, u32[]{:S(2)}) copy-start(s32[2,128]{1,0:T(2,128)} %param.11) | copy-start | bytes 3076
  29.9 9.0 %collective-permute-start.11 = (bf16[2,256,256]{2,1,0:T(8,128)(2,1)S(1)}, bf16[2,256,256]{2,1,0:T(8,128)(2,1)S(1)}, u32[]{:S(2)}, u32[]{:S(2)}) collective-permute-start(bf16[2,256,256]{2,1,0:T(8,128)(2,1)S(1)} %get-tuple-element.65), channel_id=1, source_target_pairs={{0,16},{4,20},{8,24},{12,28},{16,0},{20,4},{24,8},{28,12},{32,48},... | collective-permute-start | bytes 786440 | tf_op jit(solution)/shard_map/ppermute | solution.py:29
  31.2 12.0 %collective-permute-start.12 = (bf16[2,256,256]{2,1,0:T(8,128)(2,1)S(1)}, bf16[2,256,256]{2,1,0:T(8,128)(2,1)S(1)}, u32[]{:S(2)}, u32[]{:S(2)}) collective-permute-start(bf16[2,256,256]{2,1,0:T(8,128)(2,1)S(1)} %get-tuple-element.66), channel_id=1, source_target_pairs={{0,24},{4,28},{8,0},{12,4},{16,8},{20,12},{24,16},{28,20},{32,56},... | collective-permute-start | bytes 786440 | tf_op jit(solution)/shard_map/ppermute | solution.py:29
  31.9 11.2 %collective-permute-start.9 = (bf16[1,32,5376]{2,1,0:T(8,128)(2,1)S(1)}, bf16[1,32,5376]{2,1,0:T(8,128)(2,1)S(1)}, u32[]{:S(2)}, u32[]{:S(2)}) collective-permute-start(bf16[1,32,5376]{2,1,0:T(8,128)(2,1)S(1)} %slice.40), channel_id=1, source_target_pairs={{0,1},{1,2},{2,3},{3,0},{4,5},{5,6},{6,7},{7,4},{8,9},{9,10},{10,1... | collective-permute-start | bytes 1032200 | tf_op jit(solution)/shard_map/ppermute | solution.py:70
  31.9 11.2 %collective-permute-start.10 = (bf16[1,32,5376]{2,1,0:T(8,128)(2,1)S(1)}, bf16[1,32,5376]{2,1,0:T(8,128)(2,1)S(1)}, u32[]{:S(2)}, u32[]{:S(2)}) collective-permute-start(bf16[1,32,5376]{2,1,0:T(8,128)(2,1)S(1)} %slice.41), channel_id=1, source_target_pairs={{0,3},{1,0},{2,1},{3,2},{4,7},{5,4},{6,5},{7,6},{8,11},{9,8},{10,9... | collective-permute-start | bytes 1032200 | tf_op jit(solution)/shard_map/ppermute | solution.py:70
  43.1 5.9 %collective-permute-start.13 = (bf16[1,32,5376]{2,1,0:T(8,128)(2,1)S(1)}, bf16[1,32,5376]{2,1,0:T(8,128)(2,1)S(1)}, u32[]{:S(2)}, u32[]{:S(2)}) collective-permute-start(bf16[1,32,5376]{2,1,0:T(8,128)(2,1)S(1)} %collective-permute-done.9.r2a), channel_id=1, source_target_pairs={{0,4},{4,0},{8,12},{12,8},{16,20},{20,16},{24,28},{28,24},{32,36},... | collective-permute-start | bytes 1032200 | tf_op jit(solution)/shard_map/ppermute | solution.py:29
  44.5 4.5 %collective-permute-start.14 = (bf16[1,32,5376]{2,1,0:T(8,128)(2,1)S(1)}, bf16[1,32,5376]{2,1,0:T(8,128)(2,1)S(1)}, u32[]{:S(2)}, u32[]{:S(2)}) collective-permute-start(bf16[1,32,5376]{2,1,0:T(8,128)(2,1)S(1)} %collective-permute-done.10.r2b), channel_id=1, source_target_pairs={{0,4},{4,0},{8,12},{12,8},{16,20},{20,16},{24,28},{28,24},{32,36},... | collective-permute-start | bytes 1032200 | tf_op jit(solution)/shard_map/ppermute | solution.py:29
  53.2 38.3 %collective-permute-start.15 = (bf16[2,4,168,256]{3,2,1,0:T(8,128)(2,1)S(1)}, bf16[2,4,168,256]{3,2,1,0:T(8,128)(2,1)S(1)}, u32[]{:S(2)}, u32[]{:S(2)}) collective-permute-start(bf16[2,4,168,256]{3,2,1,0:T(8,128)(2,1)S(1)} %get-tuple-element.80), channel_id=1, source_target_pairs={{0,8},{4,12},{8,0},{12,4},{16,24},{20,28},{24,16},{28,20},{32,40},... | collective-permute-start | bytes 2064392 | tf_op jit(solution)/shard_map/ppermute | solution.py:29
  54.2 37.3 %collective-permute-start.16 = (bf16[2,4,168,256]{3,2,1,0:T(8,128)(2,1)S(1)}, bf16[2,4,168,256]{3,2,1,0:T(8,128)(2,1)S(1)}, u32[]{:S(2)}, u32[]{:S(2)}) collective-permute-start(bf16[2,4,168,256]{3,2,1,0:T(8,128)(2,1)S(1)} %get-tuple-element.81), channel_id=1, source_target_pairs={{0,24},{4,28},{8,16},{12,20},{16,8},{20,12},{24,0},{28,4},{32,56},... | collective-permute-start | bytes 2064392 | tf_op jit(solution)/shard_map/ppermute | solution.py:29
  59.5 10.8 %collective-permute-start.17 = (bf16[2,256,256]{2,1,0:T(8,128)(2,1)S(1)}, bf16[2,256,256]{2,1,0:T(8,128)(2,1)S(1)}, u32[]{:S(2)}, u32[]{:S(2)}) collective-permute-start(bf16[2,256,256]{2,1,0:T(8,128)(2,1)S(1)} %get-tuple-element.83), channel_id=1, source_target_pairs={{0,224},{4,228},{8,232},{12,236},{16,240},{20,244},{24,248},{28,25... | collective-permute-start | bytes 786440 | tf_op jit(solution)/shard_map/ppermute | solution.py:29
  65.1 2.7 %collective-permute-start.18 = (bf16[2,128,256]{2,1,0:T(8,128)(2,1)S(1)}, bf16[2,128,256]{2,1,0:T(8,128)(2,1)S(1)}, u32[]{:S(2)}, u32[]{:S(2)}) collective-permute-start(bf16[2,128,256]{2,1,0:T(8,128)(2,1)S(1)} %get-tuple-element.84), channel_id=1, source_target_pairs={{0,4},{4,0},{8,12},{12,8},{16,20},{20,16},{24,28},{28,24},{32,36},... | collective-permute-start | bytes 393224 | tf_op jit(solution)/shard_map/ppermute | solution.py:29
  65.9 15.3 %collective-permute-start.19 = (bf16[2,256,256]{2,1,0:T(8,128)(2,1)S(1)}, bf16[2,256,256]{2,1,0:T(8,128)(2,1)S(1)}, u32[]{:S(2)}, u32[]{:S(2)}) collective-permute-start(bf16[2,256,256]{2,1,0:T(8,128)(2,1)S(1)} %get-tuple-element.85), channel_id=1, source_target_pairs={{0,248},{4,252},{8,0},{12,4},{16,8},{20,12},{24,16},{28,20},{32,24... | collective-permute-start | bytes 786440 | tf_op jit(solution)/shard_map/ppermute | solution.py:29
  67.8 15.6 %collective-permute-start.20 = (bf16[2,256,256]{2,1,0:T(8,128)(2,1)S(1)}, bf16[2,256,256]{2,1,0:T(8,128)(2,1)S(1)}, u32[]{:S(2)}, u32[]{:S(2)}) collective-permute-start(bf16[2,256,256]{2,1,0:T(8,128)(2,1)S(1)} %get-tuple-element.86), channel_id=1, source_target_pairs={{0,240},{4,244},{8,248},{12,252},{16,0},{20,4},{24,8},{28,12},{32,... | collective-permute-start | bytes 786440 | tf_op jit(solution)/shard_map/ppermute | solution.py:29
  70.3 21.1 %collective-permute-start.21 = (bf16[2,256,256]{2,1,0:T(8,128)(2,1)S(1)}, bf16[2,256,256]{2,1,0:T(8,128)(2,1)S(1)}, u32[]{:S(2)}, u32[]{:S(2)}) collective-permute-start(bf16[2,256,256]{2,1,0:T(8,128)(2,1)S(1)} %get-tuple-element.87), channel_id=1, source_target_pairs={{0,232},{4,236},{8,240},{12,244},{16,248},{20,252},{24,0},{28,4},{... | collective-permute-start | bytes 786440 | tf_op jit(solution)/shard_map/ppermute | solution.py:29
  91.5 10.7 %collective-permute-start.24 = (bf16[4,168,256]{2,1,0:T(8,128)(2,1)S(1)}, bf16[4,168,256]{2,1,0:T(8,128)(2,1)S(1)}, u32[]{:S(2)}, u32[]{:S(2)}) collective-permute-start(bf16[4,168,256]{2,1,0:T(8,128)(2,1)S(1)} %fusion.1), channel_id=1, source_target_pairs={{0,8},{4,12},{8,0},{12,4},{16,24},{20,28},{24,16},{28,20},{32,40},... | collective-permute-start | bytes 1032200 | tf_op jit(solution)/shard_map/ppermute | solution.py:29
  94.7 9.7 %collective-permute-start.23 = (bf16[4,168,256]{2,1,0:T(8,128)(2,1)S(1)}, bf16[4,168,256]{2,1,0:T(8,128)(2,1)S(1)}, u32[]{:S(2)}, u32[]{:S(2)}) collective-permute-start(bf16[4,168,256]{2,1,0:T(8,128)(2,1)S(1)} %fusion), channel_id=1, source_target_pairs={{0,24},{4,28},{8,16},{12,20},{16,8},{20,12},{24,0},{28,4},{32,56},... | collective-permute-start | bytes 1032200 | tf_op jit(solution)/shard_map/ppermute | solution.py:29
  105.6 28.0 %all-to-all-start = ((bf16[16,84,256]{2,1,0:T(8,128)(2,1)}), bf16[16,84,256]{2,1,0:T(8,128)(2,1)S(1)}, u32[]{:S(2)}, u32[]{:S(2)}) async-start(bf16[16,84,256]{2,1,0:T(8,128)(2,1)} %projection_merge.1), calls=%async_computation | async-start | bytes 1441792 | tf_op jit(solution)/shard_map/all_to_all | solution.py:57
  112.4 1.4 %collective-permute-start.22 = (bf16[2,128,256]{2,1,0:T(8,128)(2,1)S(1)}, bf16[2,128,256]{2,1,0:T(8,128)(2,1)S(1)}, u32[]{:S(2)}, u32[]{:S(2)}) collective-permute-start(bf16[2,128,256]{2,1,0:T(8,128)(2,1)S(1)} %slice.52), channel_id=1, source_target_pairs={{0,4},{4,0},{8,12},{12,8},{16,20},{20,16},{24,28},{28,24},{32,36},... | collective-permute-start | bytes 393224 | tf_op jit(solution)/shard_map/ppermute | solution.py:29
